TPU v7x, 32 devices: a whole 2x2x4 slice. The times are simulated.
32 devices in a mesh: dp: 16 (over z, x, core), tensor: 2 (over y).
Axes of the slice: x: 2, y: 2, z: 4, core: 2. Of those that a mesh axis runs over, the one named last changes fastest.
Arguments:
- layer_input: bfloat16 [8192, 2048], P('dp'), may hold values from -6 to 6
- cotangent: bfloat16 [8192, 2048], P('dp', 'tensor'), may hold values from -6 to 6
- attention_norm_gain: float32 [2048], replicated, may hold values from 0.1 to 1.9
- expert_norm_gain: float32 [2048], replicated, may hold values from 0.1 to 1.9
- query_norm_gain: float32 [128], replicated, may hold values from 0.1 to 1.9
- key_norm_gain: float32 [128], replicated, may hold values from 0.1 to 1.9
- query_weight_matrix: bfloat16 [2048, 2048], P(None, 'tensor'), may hold values from -0.125 to 0.125
- key_weight_matrix: bfloat16 [2048, 2048], P(None, 'tensor'), may hold values from -0.125 to 0.125
- value_weight_matrix: bfloat16 [2048, 2048], P(None, 'tensor'), may hold values from -0.125 to 0.125
- output_weight_matrix: bfloat16 [2048, 2048], P('tensor'), may hold values from -0.75 to 0.75
- adapter_projection_down: bfloat16 [3, 8, 2048, 16], replicated, may hold values from -0.125 to 0.125
- adapter_projection_up: bfloat16 [3, 8, 16, 2048], P(None, None, None, 'tensor'), may hold values from -1.5 to 1.5
- adapter_output_down: bfloat16 [8, 2048, 16], P(None, 'tensor'), may hold values from -0.75 to 0.75
- adapter_output_up: bfloat16 [8, 16, 2048], replicated, may hold values from -1.5 to 1.5
- router: bfloat16 [2048, 64], replicated, may hold values from -0.0625 to 0.0625
- expert_gate_weight: bfloat16 [64, 2048, 1024], P('dp', None, 'tensor'), may hold values from -0.125 to 0.125
- expert_up_weight: bfloat16 [64, 2048, 1024], P('dp', None, 'tensor'), may hold values from -0.125 to 0.125
- expert_down_weight: bfloat16 [64, 1024, 2048], P('dp', 'tensor'), may hold values from -1 to 1
- segments: int32 [16, 512], P('dp'), may hold values from 0 to 15, never falling along the last dimension, each value on 1 to 256 neighbouring positions
- sequence_adapter_index: int32 [16], P('dp'), may hold values from 0 to 7
- routes: int32 [8192, 8], P('dp'), may hold values from 0 to 63, all different within a row; in each aligned block of 512 rows (0 to 511, 512 to 1023, ...) at most 80 rows name the same one
Outputs:
- layer_out: bfloat16 [8192, 2048], P('dp', 'tensor')
- grad_input: float32 [8192, 2048], P('dp', 'tensor')
- grad_down_qkv: float32 [3, 8, 2048, 16], replicated
- grad_up_qkv: float32 [3, 8, 16, 2048], P(None, None, None, 'tensor')
- grad_down_out: float32 [8, 2048, 16], P(None, 'tensor')
- grad_up_out: float32 [8, 16, 2048], P(None, None, 'tensor')
Inputs may be any that keep to these rules, and one draw needn't show every extreme that they name: `routes`: each row names 8 different experts. Among the rows of one index of dp no expert is named by more than 80 rows, a bound that some block reaches. `segments`: within a sequence the document numbers never fall; a document holds at most 256 positions, and one holds exactly that many.
All inputs are finite; a program needn't handle non-finite values.
Results may differ from a plain program's by a relative error of at most 0.02.
Values may be sent and summed in bfloat16 or wider, within the bound.
No kernel may reach another device: no remote copies, remote signals or barrier semaphores. Data moves between devices by JAX's collectives and lax.ppermute only.
A program may use at most 320 MiB of HBM per device.

v0:
```python
import jax
import jax.numpy as jnp
from jax import lax
from jax.sharding import PartitionSpec as P

MODEL_WIDTH = 2048
HEAD_WIDTH = 128
TOP = 8
LEN = 512
ADAPTER_RANK = 16
ADAPTER_CHOICES = 8


norm_eps = 1e-05
head_eps = 1e-06
rope_base = 50000.0


def rms_scale(values, gain_vec, epsilon):
    return (
        values * lax.rsqrt(jnp.mean(values * values, axis=-1, keepdims=True) + epsilon) * gain_vec
    )


def rotate(values, positions):
    half_dim = values.shape[-1] // 2
    inverse = rope_base ** (-(jnp.arange(half_dim, dtype=jnp.float32) * 2.0 / values.shape[-1]))
    angles = positions.astype(jnp.float32)[:, None, None] * inverse[None, None, :]
    cosine = jnp.cos(angles)
    sine_val = jnp.sin(angles)
    first_half = values[..., :half_dim]
    second_half = values[..., half_dim:]
    return jnp.concatenate(
        [
            first_half * cosine - second_half * sine_val,
            second_half * cosine + first_half * sine_val,
        ],
        axis=-1,
    )


def head_prep(projected, gain_vec, positions):
    shaped = projected.reshape(projected.shape[0], projected.shape[1] // HEAD_WIDTH, HEAD_WIDTH)
    return rotate(rms_scale(shaped, gain_vec, head_eps), positions)


def swiglu(pre_gate, pre_up):
    return pre_gate * jax.nn.sigmoid(pre_gate) * pre_up


def down_factor_layout(adapter_down_factor):
    return adapter_down_factor.transpose(1, 0, 2).reshape(
        adapter_down_factor.shape[1], adapter_down_factor.shape[0] * adapter_down_factor.shape[2]
    )


def local(
    layer_input,
    cotangent,
    attention_norm_gain,
    expert_norm_gain,
    query_norm_gain,
    key_norm_gain,
    query_weight_matrix,
    key_weight_matrix,
    value_weight_matrix,
    output_weight_matrix,
    adapter_projection_down,
    adapter_projection_up,
    adapter_output_down,
    adapter_output_up,
    router,
    expert_gate_weight,
    expert_up_weight,
    expert_down_weight,
    segments,
    sequence_adapter_index,
    routes,
):
    tok_count = layer_input.shape[0]
    tensor_count = lax.axis_size("tensor")
    data_count = lax.axis_size("dp")
    col_width = MODEL_WIDTH // tensor_count
    col_start = lax.axis_index("tensor") * col_width
    shard_local_width = query_weight_matrix.shape[1]
    local_heads = shard_local_width // HEAD_WIDTH
    local_experts = expert_gate_weight.shape[0]
    expert_total = local_experts * data_count
    capacity = 5 * tok_count * TOP // (4 * expert_total)
    device_lane_count = ADAPTER_CHOICES * ADAPTER_RANK
    flat_count = tok_count * TOP
    block_rows = min(512, LEN)
    block_count = tok_count // block_rows
    score_scale = HEAD_WIDTH ** (-0.5)
    half_type = jnp.bfloat16
    token_ids = jnp.arange(tok_count, dtype=jnp.int32)
    seq_of = token_ids // LEN
    positions = token_ids % LEN
    seq_hot = seq_of[:, None] == jnp.arange(tok_count // LEN, dtype=jnp.int32)[None, :]
    token_adapter = jnp.sum(jnp.where(seq_hot, sequence_adapter_index[None, :], 0), axis=1)
    adapter_mask = (
        token_adapter[:, None]
        == (jnp.arange(device_lane_count, dtype=jnp.int32) // ADAPTER_RANK)[None, :]
    )
    mask_float = adapter_mask.astype(jnp.float32)
    mask_half = adapter_mask.astype(half_type)
    doc_flat = segments.reshape(-1)
    hidden32 = layer_input.astype(jnp.float32)
    normed32, norm1_back = jax.vjp(
        lambda values: rms_scale(values, attention_norm_gain, norm_eps), hidden32
    )
    normed = normed32.astype(half_type)
    w_proj = [query_weight_matrix, key_weight_matrix, value_weight_matrix]
    down_factor_rows = [
        down_factor_layout(adapter_projection_down[projection_index])
        for projection_index in range(3)
    ]
    up_factor_rows = [
        adapter_projection_up[projection_index].reshape(device_lane_count, shard_local_width)
        for projection_index in range(3)
    ]
    latents = []
    raw_proj = []
    for projection_index in range(3):
        latent = jnp.dot(
            normed, down_factor_rows[projection_index], preferred_element_type=jnp.float32
        ).astype(half_type)
        latents.append(latent * mask_half)
        raw_proj.append(
            jnp.dot(normed, w_proj[projection_index], preferred_element_type=jnp.float32)
            + jnp.dot(
                latent * mask_half,
                up_factor_rows[projection_index],
                preferred_element_type=jnp.float32,
            )
        )
    query_f, query_back = jax.vjp(
        lambda projected: head_prep(projected, query_norm_gain, positions), raw_proj[0]
    )
    key_f, key_back = jax.vjp(
        lambda projected: head_prep(projected, key_norm_gain, positions), raw_proj[1]
    )
    queries = query_f.astype(half_type)
    keys = key_f.astype(half_type)
    values = raw_proj[2].reshape(tok_count, local_heads, HEAD_WIDTH).astype(half_type)

    def block_scores():
        scores = (
            jnp.einsum("qhd,khd->hqk", queries, keys, preferred_element_type=jnp.float32)
            * score_scale
        )
        same_doc = (doc_flat[:, None] == doc_flat[None, :])[None]
        return (jnp.where(same_doc, scores, -1e30), same_doc, queries, keys, values)

    def forward_block(block_index):
        scores, same_doc, query_block, key_seq, value_seq = block_scores()
        top_score = jnp.max(scores, axis=-1, keepdims=True)
        exp_scores = jnp.exp(scores - top_score)
        row_total = jnp.sum(exp_scores, axis=-1, keepdims=True)
        prob_half = (exp_scores / row_total).astype(half_type)
        out_block = jnp.einsum(
            "hqk,khd->qhd", prob_half, value_seq, preferred_element_type=jnp.float32
        )
        return (out_block, top_score[..., 0] + jnp.log(row_total[..., 0]))

    attended_blocks, log_totals = lax.map(forward_block, jnp.arange(block_count, dtype=jnp.int32))
    attended = attended_blocks.reshape(tok_count, shard_local_width).astype(half_type)
    output_down_rows = down_factor_layout(adapter_output_down)
    output_up_rows = adapter_output_up.reshape(device_lane_count, MODEL_WIDTH)
    proj_part = jnp.dot(attended, output_weight_matrix, preferred_element_type=jnp.float32)
    latent_part = jnp.dot(attended, output_down_rows, preferred_element_type=jnp.float32)
    attn_total, latent_total = lax.psum((proj_part, latent_part), "tensor")
    latent_out = latent_total.astype(half_type) * mask_half
    mixed_rows = (
        hidden32
        + attn_total
        + jnp.dot(latent_out, output_up_rows, preferred_element_type=jnp.float32)
    )
    moe_in32, norm2_back = jax.vjp(
        lambda values: rms_scale(values, expert_norm_gain, norm_eps), mixed_rows
    )
    moe_in = moe_in32.astype(half_type)
    logits = jnp.dot(moe_in, router, preferred_element_type=jnp.float32)

    def gate_fn(logit_rows):
        chosen = jnp.take_along_axis(logit_rows, routes, axis=1)
        chosen_exp = jnp.exp(chosen - jnp.max(chosen, axis=1, keepdims=True))
        return chosen_exp / jnp.sum(chosen_exp, axis=1, keepdims=True)

    gate_vals, gate_back = jax.vjp(gate_fn, logits)
    flat_routes = routes.reshape(-1)
    route_hot = (flat_routes[:, None] == jnp.arange(expert_total, dtype=jnp.int32)[None, :]).astype(
        jnp.int32
    )
    slot_of = jnp.sum(
        (jnp.cumsum(route_hot, axis=0, dtype=jnp.int32) - route_hot) * route_hot,
        axis=1,
        dtype=jnp.int32,
    )
    slot_place = flat_routes * capacity + slot_of
    source = (
        jnp.full((expert_total * capacity,), flat_count, jnp.int32)
        .at[slot_place]
        .set(jnp.arange(flat_count, dtype=jnp.int32))
    )
    token_of = source // TOP
    moe_padded = jnp.concatenate([moe_in, jnp.zeros((1, MODEL_WIDTH), half_type)], axis=0)
    slot_tokens = moe_padded[token_of].reshape(expert_total, capacity, MODEL_WIDTH)
    gate_use, up_use, down_use = (expert_gate_weight, expert_up_weight, expert_down_weight)
    received = lax.all_to_all(slot_tokens, "dp", split_axis=0, concat_axis=0, tiled=True)
    received = received.reshape(data_count, local_experts, capacity, MODEL_WIDTH)
    pre_gate = jnp.einsum("secd,edh->sech", received, gate_use, preferred_element_type=jnp.float32)
    pre_up = jnp.einsum("secd,edh->sech", received, up_use, preferred_element_type=jnp.float32)
    activated, swiglu_back = jax.vjp(swiglu, pre_gate, pre_up)
    activated_half = activated.astype(half_type)
    expert_part = jnp.einsum(
        "sech,ehd->secd", activated_half, down_use, preferred_element_type=jnp.float32
    )
    expert_cols = lax.psum_scatter(expert_part, "tensor", scatter_dimension=3, tiled=True)
    expert_half = expert_cols.astype(half_type).reshape(
        expert_total, capacity, expert_cols.shape[3]
    )
    came_back = lax.all_to_all(expert_half, "dp", split_axis=0, concat_axis=0, tiled=True)
    came_back = came_back.reshape(expert_total * capacity, col_width)
    route_out = came_back[slot_place].reshape(tok_count, TOP, col_width)
    mixed_cols = lax.dynamic_slice_in_dim(mixed_rows, col_start, col_width, 1)
    layer_out = (
        mixed_cols + jnp.sum(gate_vals[:, :, None] * route_out.astype(jnp.float32), axis=1)
    ).astype(half_type)
    grad_cols = cotangent.astype(jnp.float32)
    gate_part = jnp.einsum("tkd,td->tk", route_out, cotangent, preferred_element_type=jnp.float32)
    grad_gate = lax.psum(gate_part, "tensor")
    route_grad = (
        (gate_vals[:, :, None] * grad_cols[:, None, :])
        .astype(half_type)
        .reshape(flat_count, col_width)
    )
    route_grad_pad = jnp.concatenate([route_grad, jnp.zeros((1, col_width), half_type)], axis=0)
    grad_out = route_grad_pad[source].reshape(expert_total, capacity, col_width)
    grad_arrived = lax.all_to_all(grad_out, "dp", split_axis=0, concat_axis=0, tiled=True)
    grad_expert = lax.all_gather(grad_arrived, "tensor", axis=2, tiled=True)
    grad_expert = grad_expert.reshape(data_count, local_experts, capacity, MODEL_WIDTH)
    grad_act = jnp.einsum(
        "secd,ehd->sech", grad_expert, down_use, preferred_element_type=jnp.float32
    ).astype(half_type)
    grad_pre_gate, grad_pre_up = swiglu_back(grad_act.astype(jnp.float32))
    grad_in_part = jnp.einsum(
        "sech,edh->secd",
        grad_pre_gate.astype(half_type),
        gate_use,
        preferred_element_type=jnp.float32,
    )
    grad_in_part = grad_in_part + jnp.einsum(
        "sech,edh->secd", grad_pre_up.astype(half_type), up_use, preferred_element_type=jnp.float32
    )
    grad_in_cols = lax.psum_scatter(grad_in_part, "tensor", scatter_dimension=3, tiled=True)
    grad_in_cols = grad_in_cols.reshape(expert_total, capacity, grad_in_cols.shape[3])
    grad_home = lax.all_to_all(grad_in_cols, "dp", split_axis=0, concat_axis=0, tiled=True)
    grad_home = grad_home.reshape(expert_total * capacity, col_width)
    grad_moe_cols = jnp.sum(grad_home[slot_place].reshape(tok_count, TOP, col_width), axis=1)
    grad_moe_expert, grad_full = (
        lax.all_gather(grad_moe_cols, "tensor", axis=1, tiled=True),
        lax.all_gather(grad_cols, "tensor", axis=1, tiled=True),
    )
    grad_logits = gate_back(grad_gate)[0].astype(half_type)
    grad_moe_in = grad_moe_expert + jnp.einsum(
        "te,de->td", grad_logits, router, preferred_element_type=jnp.float32
    )
    grad_mixed = grad_full + norm2_back(grad_moe_in)[0]
    grad_branch = grad_mixed.astype(half_type)
    grad_latent_out = (
        jnp.einsum("td,ad->ta", grad_branch, output_up_rows, preferred_element_type=jnp.float32)
        * mask_float
    ).astype(half_type)
    branch_cols = lax.dynamic_slice_in_dim(grad_branch, col_start, col_width, 1)
    grad_up_out = jnp.einsum(
        "ta,td->ad", latent_out, branch_cols, preferred_element_type=jnp.float32
    ).reshape(ADAPTER_CHOICES, ADAPTER_RANK, col_width)
    grad_attended = jnp.einsum(
        "td,cd->tc", grad_branch, output_weight_matrix, preferred_element_type=jnp.float32
    )
    grad_attended = grad_attended + jnp.einsum(
        "ta,ca->tc", grad_latent_out, output_down_rows, preferred_element_type=jnp.float32
    )
    grad_heads = grad_attended.astype(half_type).reshape(tok_count, local_heads, HEAD_WIDTH)
    grad_down_out = jnp.einsum(
        "tc,ta->ca", attended, grad_latent_out, preferred_element_type=jnp.float32
    )
    grad_down_out = grad_down_out.reshape(
        shard_local_width, ADAPTER_CHOICES, ADAPTER_RANK
    ).transpose(1, 0, 2)

    def backward_block(block_index):
        scores, same_doc, query_block, key_seq, value_seq = block_scores()
        prob_block = jnp.where(same_doc, jnp.exp(scores - log_totals[block_index][:, :, None]), 0.0)
        grad_prob = jnp.einsum(
            "qhd,khd->hqk", grad_heads, value_seq, preferred_element_type=jnp.float32
        )
        row_delta = jnp.sum(prob_block * grad_prob, axis=-1, keepdims=True)
        grad_scores = (prob_block * (grad_prob - row_delta)).astype(half_type)
        grad_query = (
            jnp.einsum("hqk,khd->qhd", grad_scores, key_seq, preferred_element_type=jnp.float32)
            * score_scale
        )
        grad_key = (
            jnp.einsum("hqk,qhd->khd", grad_scores, query_block, preferred_element_type=jnp.float32)
            * score_scale
        )
        grad_value = jnp.einsum(
            "hqk,qhd->khd",
            prob_block.astype(half_type),
            grad_heads,
            preferred_element_type=jnp.float32,
        )
        return (grad_query, grad_key, grad_value)

    grad_query_blocks, grad_key_blocks, grad_value_blocks = lax.map(
        backward_block, jnp.arange(block_count, dtype=jnp.int32)
    )
    seq_count = tok_count // LEN
    grad_queries = grad_query_blocks.reshape(tok_count, local_heads, HEAD_WIDTH)
    grad_keys = (
        grad_key_blocks.reshape(seq_count, LEN // block_rows, LEN, local_heads, HEAD_WIDTH)
        .sum(axis=1)
        .reshape(tok_count, local_heads, HEAD_WIDTH)
    )
    grad_values = (
        grad_value_blocks.reshape(seq_count, LEN // block_rows, LEN, local_heads, HEAD_WIDTH)
        .sum(axis=1)
        .reshape(tok_count, shard_local_width)
    )
    grad_raw = [
        query_back(grad_queries)[0].astype(half_type),
        key_back(grad_keys)[0].astype(half_type),
        grad_values.astype(half_type),
    ]
    grad_normed_part = jnp.zeros((tok_count, MODEL_WIDTH), jnp.float32)
    latent_parts = []
    for projection_index in range(3):
        grad_normed_part = grad_normed_part + jnp.einsum(
            "tc,dc->td",
            grad_raw[projection_index],
            w_proj[projection_index],
            preferred_element_type=jnp.float32,
        )
        latent_parts.append(
            jnp.einsum(
                "tc,ac->ta",
                grad_raw[projection_index],
                up_factor_rows[projection_index],
                preferred_element_type=jnp.float32,
            )
        )
    grad_normed_sum, grad_latent_sum = (
        lax.psum(grad_normed_part.astype(jnp.bfloat16), "tensor").astype(jnp.float32),
        lax.psum(jnp.stack(latent_parts).astype(jnp.bfloat16), "tensor").astype(jnp.float32),
    )
    grad_latent = (grad_latent_sum * mask_float[None]).astype(half_type)
    grad_normed = grad_normed_sum
    grad_down_list = []
    grad_up_list = []
    for projection_index in range(3):
        grad_normed = grad_normed + jnp.einsum(
            "ta,da->td",
            grad_latent[projection_index],
            down_factor_rows[projection_index],
            preferred_element_type=jnp.float32,
        )
        grad_down = jnp.einsum(
            "td,ta->da", normed, grad_latent[projection_index], preferred_element_type=jnp.float32
        )
        grad_down_list.append(
            grad_down.reshape(MODEL_WIDTH, ADAPTER_CHOICES, ADAPTER_RANK).transpose(1, 0, 2)
        )
        grad_up = jnp.einsum(
            "ta,tc->ac",
            latents[projection_index],
            grad_raw[projection_index],
            preferred_element_type=jnp.float32,
        )
        grad_up_list.append(grad_up.reshape(ADAPTER_CHOICES, ADAPTER_RANK, shard_local_width))
    grad_hidden_in = grad_mixed + norm1_back(grad_normed)[0]
    grad_input = lax.dynamic_slice_in_dim(grad_hidden_in, col_start, col_width, 1)
    summed = (
        lax.psum(jnp.stack(grad_down_list).astype(jnp.bfloat16), "dp").astype(jnp.float32),
        lax.psum(jnp.stack(grad_up_list).astype(jnp.bfloat16), "dp").astype(jnp.float32),
        lax.psum(grad_down_out.astype(jnp.bfloat16), "dp").astype(jnp.float32),
        lax.psum(grad_up_out.astype(jnp.bfloat16), "dp").astype(jnp.float32),
    )
    return (layer_out, grad_input, summed[0], summed[1], summed[2], summed[3])


def solution(mesh):
    return jax.shard_map(
        local,
        mesh=mesh,
        in_specs=(
            P("dp", None),
            P("dp", "tensor"),
            P(),
            P(),
            P(),
            P(),
            P(None, "tensor"),
            P(None, "tensor"),
            P(None, "tensor"),
            P("tensor", None),
            P(),
            P(None, None, None, "tensor"),
            P(None, "tensor", None),
            P(),
            P(),
            P("dp", None, "tensor"),
            P("dp", None, "tensor"),
            P("dp", "tensor", None),
            P("dp", None),
            P("dp"),
            P("dp", None),
        ),
        out_specs=(
            P("dp", "tensor"),
            P("dp", "tensor"),
            P(),
            P(None, None, None, "tensor"),
            P(None, "tensor", None),
            P(None, None, "tensor"),
        ),
        check_vma=False,
    )
```

profile of v0, /device:TPU:0, one launch (start us, length us, event | category | flops | bytes accessed | tf_op | source)
XLA Modules:
  0.0 3438.3 jit_solution(5603803381122716451)
XLA Ops:
  25.8 4.6 fusion.148
  36.7 5.3 fusion.146
  55.2 4.4 fusion.149
  61.3 28.8 reduce-window.6
  98.1 15.5 scatter_custom_fusion
  114.3 15.6 all-reduce.18
  129.9 42.0 %all-reduce.13.cloned.1.call-done = f32[512,2048]{1,0:T(8,128)} async-done(((f32[512,2048]{1,0:T(8,128)}), f32[512,2048]{1,0:T(8,128)}) %all-reduce.13.cloned.1.call-update) | async-done | bytes 4194320 | tf_op jit(solution)/shard_map/psum | solution.py:172
  178.0 25.9 gather_fusion
  203.8 458.3 %all_to_all.20 = bf16[64,80,2048]{2,1,0:T(8,128)(2,1)} all-to-all(bf16[64,80,2048]{2,1,0:T(8,128)(2,1)} %bitcast.341), channel_id=1, replica_groups=mesh['dp'=16,'tensor'=2] {'dp'}, dimensions={0} | all-to-all | bytes 41943040 | tf_op jit(solution)/shard_map/all_to_all | solution.py:210
  662.1 19.8 fusion.2
  681.9 19.9 fusion.4
  701.8 26.6 convolution_bitcast_fusion
  728.4 459.0 %reduce-scatter.3.cloned.1.call-done = f32[16,4,80,1024]{3,2,0,1:T(8,128)} async-done(((f32[16,4,80,2048]{3,2,0,1:T(8,128)}), f32[16,4,80,1024]{3,2,0,1:T(8,128)}) %reduce-scatter.3.cloned.1.call-update) | async-done | bytes 20971536 | tf_op jit(solution)/shard_map/reduce_scatter | solution.py:219
  1187.4 12.6 convert_element_type.256
  1199.9 10.2 copy.217
  1210.2 5.8 all-to-all-start.1
  1220.9 33.0 gather_fusion.4
  1254.3 148.9 %all-to-all-done.1 = bf16[64,80,1024]{2,1,0:T(8,128)(2,1)} async-done(((bf16[64,80,1024]{2,1,0:T(8,128)(2,1)}), bf16[64,80,1024]{2,1,0:T(8,128)(2,1)}, u32[]{:S(2)}, u32[]{:S(2)}) %all-to-all-start.1) | async-done | bytes 10485792 | tf_op jit(solution)/shard_map/all_to_all | solution.py:223
  1403.2 26.3 gather_fusion.1
  1429.5 8.2 fusion.22
  1437.8 7.2 psum.65
  1446.0 4.1 fusion.6
  1450.1 7.6 concatenate.17
  1457.7 30.4 gather_fusion.2
  1488.0 272.1 %all_to_all.21 = bf16[64,80,1024]{2,1,0:T(8,128)(2,1)} all-to-all(bf16[64,80,1024]{2,1,0:T(8,128)(2,1)} %bitcast.346), channel_id=1, replica_groups=mesh['dp'=16,'tensor'=2] {'dp'}, dimensions={0} | all-to-all | bytes 20971520 | tf_op jit(solution)/shard_map/all_to_all | solution.py:240
  1760.2 248.7 %all-gather.6.cloned.1.call-done = bf16[64,80,2048]{2,1,0:T(8,128)(2,1)} async-done(((bf16[64,80,1024]{2,1,0:T(8,128)(2,1)}), bf16[64,80,2048]{2,1,0:T(8,128)(2,1)}) %all-gather.6.cloned.1.call-update) | async-done | bytes 20971536 | tf_op jit(solution)/shard_map/all_gather | solution.py:241
  2008.9 18.3 fusion.34
  2027.2 28.5 fusion.17
  2055.7 35.9 %add_bitcast_fusion = f32[16,4,80,2048]{3,2,0,1:T(8,128)} fusion(f32[4,16,80,2048]{3,2,1,0:T(8,128)} %fusion.17, bf16[4,2048,512]{2,1,0:T(8,128)(2,1)} %param.37, bf16[4,16,80,512]{3,2,1,0:T(8,128)(2,1)} %fusion.34, f32[4,16,80,512]{3,2,1,0:T(8,128)} %fusion.4), kind=kOutput, calls=%fused_computation.7 | convolution fusion | flops 10766254080 | bytes 108003328 | tf_op jit(solution)/shard_map/sech,edh->secd/dot_general | solution.py:253
  2091.7 459.0 %reduce-scatter.5.cloned.1.call-done = f32[16,4,80,1024]{3,2,0,1:T(8,128)} async-done(((f32[16,4,80,2048]{3,2,0,1:T(8,128)}), f32[16,4,80,1024]{3,2,0,1:T(8,128)}) %reduce-scatter.5.cloned.1.call-update) | async-done | bytes 20971536 | tf_op jit(solution)/shard_map/reduce_scatter | solution.py:256
  2550.7 8.1 copy.220
  2558.8 457.5 %all_to_all.22 = f32[64,80,1024]{2,1,0:T(8,128)} all-to-all(f32[64,80,1024]{2,1,0:T(8,128)S(1)} %bitcast.340), channel_id=1, replica_groups=mesh['dp'=16,'tensor'=2] {'dp'}, dimensions={0} | all-to-all | bytes 41943040 | tf_op jit(solution)/shard_map/all_to_all | solution.py:258
  3016.3 29.4 gather_fusion.3
  3045.7 9.4 bitcast_reduce_fusion
  3056.6 21.9 scatter_custom_fusion.1
  3078.6 34.7 %all-gather.8.cloned.1.call-done = f32[512,2048]{1,0:T(8,128)} async-done(((f32[512,1024]{1,0:T(8,128)}), f32[512,2048]{1,0:T(8,128)}) %all-gather.8.cloned.1.call-update) | async-done | bytes 4194320 | tf_op jit(solution)/shard_map/all_gather | solution.py:262
  3113.3 6.2 multiply_reduce_fusion.3
  3119.5 52.1 %all-gather.4.cloned.1.call-done = f32[512,2048]{1,0:T(8,128)} async-done(((f32[512,1024]{1,0:T(8,128)}), f32[512,2048]{1,0:T(8,128)}) %all-gather.4.cloned.1.call-update) | async-done | bytes 4194320 | tf_op jit(solution)/shard_map/all_gather | solution.py:263
  3171.6 7.8 fusion.141
  3185.4 6.1 multiply_reduce_fusion.1
  3197.8 3.7 fusion.54
  3210.7 7.1 fusion.152
  3223.9 5.0 fusion.153
  3229.9 3.7 add_convert_fusion
  3238.9 10.6 multiply_reduce_fusion
  3249.5 3.7 add_convert_fusion.2
  3258.0 48.3 %all-reduce.17.cloned.1.call-done = (bf16[3,512,128]{2,1,0:T(8,128)(2,1)}, bf16[512,2048]{1,0:T(8,128)(2,1)}) async-done(((bf16[3,512,128]{2,1,0:T(8,128)(2,1)}, bf16[512,2048]{1,0:T(8,128)(2,1)}), (bf16[3,512,128]{2,1,0:T(8,128)(2,1)}, bf16[512,2048]{1,0:T(8,128)(2,1)})) %all-reduce.17.cloned.1.call-update) | async-done | bytes 2490384 | tf_op jit(solution)/shard_map/psum | solution.py:356
  3330.7 94.0 %all-reduce.15.cloned.1.call-done = (bf16[3,8,2048,16]{2,3,1,0:T(8,128)(2,1)}, bf16[3,8,16,1024]{3,2,1,0:T(8,128)(2,1)}, bf16[8,1024,16]{1,2,0:T(8,128)(2,1)}, bf16[8,16,1024]{2,1,0:T(8,128)(2,1)}) async-done(((bf16[3,8,2048,16]{2,3,1,0:T(8,128)(2,1)}, bf16[3,8,16,1024]{3,2,1,0:T(8,128)(2,1)}, bf16[8,1024,16]{1,2,0:T(8,128)(2,1)}, bf16[8,16,1024]{2,1,0:T(8,128)(2,1)}), (bf16[3,8,2048,16]{2,3,1,0:T(8,128)(2,1)}, ...) | async-done | bytes 2883600 | tf_op jit(solution)/shard_map/psum | solution.py:385
  (406 shorter events, 129.8 us)
Async XLA Ops:
  7.2 164.7 %copy-start = (bf16[8,16,2048]{2,1,0:T(8,128)(2,1)S(1)}, bf16[8,16,2048]{2,1,0:T(8,128)(2,1)}, u32[]{:S(2)}) copy-start(bf16[8,16,2048]{2,1,0:T(8,128)(2,1)} %param.34) | copy-start | bytes 1572868
  7.2 164.7 %all-reduce.13.cloned.1.call-start = ((), (), s32[]{:S(2)}) async-start(), calls=%async_computation.6 | async-start | bytes 8388608 | tf_op jit(solution)/shard_map/psum | solution.py:172
  7.3 164.6 %copy-start.108 = (s32[128]{0:T(128)}, s32[128]{0:T(128)S(1)}, u32[]{:S(2)}) copy-start(s32[128]{0:T(128)S(1)} %and_select_fusion.1) | copy-start | bytes 1540
  11.8 22.3 copy-start.37
  18.2 153.6 %copy-start.82 = (s32[512]{0:T(512)}, s32[512]{0:T(512)S(1)}, u32[]{:S(2)}) copy-start(s32[512]{0:T(512)S(1)} %fusion.119) | copy-start | bytes 6148
  19.0 31.7 copy-start.49
  23.9 19.4 copy-start.88
  31.0 12.4 copy-start.3
  33.8 8.2 copy-start.93
  33.9 9.5 copy-start.86
  34.1 17.2 copy-start.43
  36.6 14.1 copy-start.61
  36.7 6.7 copy-start.6
  36.7 6.7 copy-start.119
  36.7 6.7 copy-start.121
  59.7 1127.7 %reduce-scatter.3.cloned.1.call-start = ((), (), s32[]{:S(2)}) async-start(), calls=%async_computation.7 | async-start | bytes 62914560 | tf_op jit(solution)/shard_map/reduce_scatter | solution.py:219
  90.1 81.8 %copy-start.9 = (bf16[512,2048]{1,0:T(8,128)(2,1)S(1)}, bf16[512,2048]{1,0:T(8,128)(2,1)}, u32[]{:S(2)}) copy-start(bf16[512,2048]{1,0:T(8,128)(2,1)} %param.21) | copy-start | bytes 6291460
  98.1 77.1 %copy-start.102 = (s32[4096,1]{0,1:T(1,128)}, s32[4096,1]{0,1:T(1,128)S(1)}, u32[]{:S(2)}) copy-start(s32[4096,1]{0,1:T(1,128)S(1)} %compare_select_fusion.12) | copy-start | bytes 49156
  129.9 45.2 %copy-start.63 = (bf16[512,128]{0,1:T(8,128)(2,1)}, bf16[512,128]{0,1:T(8,128)(2,1)S(1)}, u32[]{:S(2)}) copy-start(bf16[512,128]{0,1:T(8,128)(2,1)S(1)} %all-reduce.18) | copy-start | bytes 393220
  1210.2 7.6 copy-start.103
  1210.2 7.6 copy-start.67
  1210.2 193.0 %all-to-all-start.1 = ((bf16[64,80,1024]{2,1,0:T(8,128)(2,1)}), bf16[64,80,1024]{2,1,0:T(8,128)(2,1)}, u32[]{:S(2)}, u32[]{:S(2)}) async-start(bf16[64,80,1024]{2,1,0:T(8,128)(2,1)} %bitcast.347), calls=%async_computation.2 | async-start | bytes 20971520 | tf_op jit(solution)/shard_map/all_to_all | solution.py:223
  1216.0 792.9 %all-gather.6.cloned.1.call-start = ((), (), s32[]{:S(2)}) async-start(), calls=%async_computation.9 | async-start | bytes 31457280 | tf_op jit(solution)/shard_map/all_gather | solution.py:241
  1217.8 228.2 %copy-start.13 = (f32[512,1024]{1,0:T(8,128)}, f32[512,1024]{1,0:T(8,128)S(1)}, u32[]{:S(2)}) copy-start(f32[512,1024]{1,0:T(8,128)S(1)} %convert_element_type.259) | copy-start | bytes 6291460
  1217.9 185.4 %copy-start.90 = (s32[4096]{0:T(1024)}, s32[4096]{0:T(1024)S(1)}, u32[]{:S(2)}) copy-start(s32[4096]{0:T(1024)S(1)} %broadcast_clamp_fusion) | copy-start | bytes 49156
  1450.1 7.6 copy-start.98
  1760.2 790.5 %reduce-scatter.5.cloned.1.call-start = ((), (), s32[]{:S(2)}) async-start(), calls=%async_computation.10 | async-start | bytes 62914560 | tf_op jit(solution)/shard_map/reduce_scatter | solution.py:256
  2091.6 1021.7 %all-gather.8.cloned.1.call-start = ((), (), s32[]{:S(2)}) async-start(), calls=%async_computation.11 | async-start | bytes 6291456 | tf_op jit(solution)/shard_map/all_gather | solution.py:262
  2558.8 457.5 %copy-start.91 = (s32[4096]{0:T(1024)S(1)}, s32[4096]{0:T(1024)}, u32[]{:S(2)}) copy-start(s32[4096]{0:T(1024)} %copy-done.90) | copy-start | bytes 49156
  3055.1 58.2 %copy-start.68 = (bf16[2048,64]{0,1:T(8,128)(2,1)S(1)}, bf16[2048,64]{0,1:T(8,128)(2,1)}, u32[]{:S(2)}) copy-start(bf16[2048,64]{0,1:T(8,128)(2,1)} %param.35) | copy-start | bytes 786436
  3055.1 58.2 %copy-start.105 = (f32[2048]{0:T(1024)S(1)}, f32[2048]{0:T(1024)}, u32[]{:S(2)}) copy-start(f32[2048]{0:T(1024)} %param.24) | copy-start | bytes 24580
  3055.1 116.4 %all-gather.4.cloned.1.call-start = ((), (), s32[]{:S(2)}) async-start(), calls=%async_computation.8 | async-start | bytes 6291456 | tf_op jit(solution)/shard_map/all_gather | solution.py:263
  3055.7 250.6 %all-reduce.17.cloned.1.call-start = ((), (), s32[]{:S(2)}) async-start(), calls=%async_computation.13 | async-start | bytes 4980736 | tf_op jit(solution)/shard_map/psum | solution.py:356
  3078.6 40.9 %copy-start.117 = (f32[512]{0:T(512)S(1)}, f32[512]{0:T(512)}, u32[]{:S(2)}) copy-start(f32[512]{0:T(512)} %copy-done.116) | copy-start | bytes 6148
  3078.6 93.0 %copy-start.111 = (f32[512]{0:T(512)S(1)}, f32[512]{0:T(512)}, u32[]{:S(2)}) copy-start(f32[512]{0:T(512)} %copy-done.110) | copy-start | bytes 6148
  3171.6 7.8 copy-start.58
  3171.6 7.8 copy-start.60
  3171.6 7.8 copy-start.62
  3171.6 7.8 copy-start.83
  3171.6 7.8 copy-start.109
  3171.6 9.3 copy-start.20
  3210.7 7.1 copy-start.22
  3210.7 7.1 copy-start.54
  3210.7 7.6 copy-start.4
  3210.7 7.6 copy-start.15
  3210.7 7.6 copy-start.122
  3234.5 190.2 %all-reduce.15.cloned.1.call-start = ((), (), s32[]{:S(2)}) async-start(), calls=%async_computation.12 | async-start | bytes 5767168 | tf_op jit(solution)/shard_map/psum | solution.py:385
  3254.3 53.9 %copy-start.40 = (bf16[1,8,2048,16]{2,3,1,0:T(8,128)(2,1)S(1)}, bf16[1,8,2048,16]{2,3,1,0:T(8,128)(2,1)}, u32[]{:S(2)}) copy-start(bf16[1,8,2048,16]{2,3,1,0:T(8,128)(2,1)} %copy-done.39) | copy-start | bytes 1572868
  (91 other events, 292.3 us)
Sparse Core Ops, SparseCore 0:
  59.8 112.0 all-reduce.12
  728.5 458.7 reduce-scatter.2
  1760.3 248.5 all-gather.5
  2091.8 458.9 reduce-scatter.4
  3055.3 58.0 all-gather.7
  3114.8 56.7 all-gather.3
  3234.6 71.6 all-reduce.16
  3322.1 102.5 all-reduce.14
where the time goes:
time: 3450 us; the launch traced here: 3440 us
  waiting for transfers between devices  1590 us (46%)
  blocking collectives  1210 us (35%)
  matrix products  253 us (7%)
  local copies, waits for them, and re-layouts  219 us (6%)
  other arithmetic  146 us (4%)
    reduce_scatter x1, waiting for transfers between devices, local(): lax.psum_scatter(grad_in_part, 'tensor', scatter_dimension=3, tiled=True)  459 us
    reduce_scatter x1, waiting for transfers between devices, local(): lax.psum_scatter(expert_part, 'tensor', scatter_dimension=3, tiled=True)  459 us
    all_to_all x1, blocking collectives, local(): lax.all_to_all(slot_tokens, 'dp', split_axis=0, concat_axis=0, tiled=True)  458 us
    all_to_all x1, blocking collectives, local(): lax.all_to_all(grad_in_cols, 'dp', split_axis=0, concat_axis=0, tiled=True)  458 us
    all_to_all x1, blocking collectives, local(): lax.all_to_all(grad_out, 'dp', split_axis=0, concat_axis=0, tiled=True)  272 us
    all_gather x1, waiting for transfers between devices, local(): grad_expert = lax.all_gather(grad_arrived, 'tensor', axis=2, tiled=True)  249 us
    all_to_all x1, waiting for transfers between devices, local(): lax.all_to_all(expert_half, 'dp', split_axis=0, concat_axis=0, tiled=True)  149 us
    psum x1, waiting for transfers between devices, local(): lax.psum(jnp.stack(grad_down_list).astype(jnp.bfloat16), 'dp')  94 us
  transfers between devices with their start and end apart: 9, of which 9 were waited for; matrix products, arithmetic and copies ran while one was open for 4% of the time, Pallas kernels for 0%

commit v1 on v0

v1 whole, which is shorter than its diff:
```python
import functools

import jax
import jax.numpy as jnp
from jax import lax
from jax.experimental import pallas as pl
from jax.experimental.pallas import tpu as pltpu
from jax.sharding import PartitionSpec as P

MODEL_WIDTH = 2048
HEAD_WIDTH = 128
TOP = 8
LEN = 512
ADAPTER_RANK = 16
ADAPTER_CHOICES = 8
QUAD = 4

norm_eps = 1e-05
head_eps = 1e-06
rope_base = 50000.0
half_type = jnp.bfloat16
VMEM_LIMIT = 56 * 1024 * 1024


def rms_scale(values, gain_vec, epsilon):
    return (
        values * lax.rsqrt(jnp.mean(values * values, axis=-1, keepdims=True) + epsilon) * gain_vec
    )


def rotate(values, positions):
    half_dim = values.shape[-1] // 2
    inverse = rope_base ** (-(jnp.arange(half_dim, dtype=jnp.float32) * 2.0 / values.shape[-1]))
    angles = positions.astype(jnp.float32)[:, None, None] * inverse[None, None, :]
    cosine = jnp.cos(angles)
    sine_val = jnp.sin(angles)
    first_half = values[..., :half_dim]
    second_half = values[..., half_dim:]
    return jnp.concatenate(
        [
            first_half * cosine - second_half * sine_val,
            second_half * cosine + first_half * sine_val,
        ],
        axis=-1,
    )


def head_prep(projected, gain_vec, positions):
    shaped = projected.reshape(projected.shape[0], projected.shape[1] // HEAD_WIDTH, HEAD_WIDTH)
    return rotate(rms_scale(shaped, gain_vec, head_eps), positions)


def down_factor_layout(adapter_down_factor):
    return adapter_down_factor.transpose(1, 0, 2).reshape(
        adapter_down_factor.shape[1], adapter_down_factor.shape[0] * adapter_down_factor.shape[2]
    )


def nt_dot(left, right):
    return lax.dot_general(
        left, right, (((1,), (1,)), ((), ())), preferred_element_type=jnp.float32
    )


def start_blocks(block_refs, buffer_ref, sems, flip):
    for b in range(QUAD):
        for r in range(2):
            pltpu.make_async_copy(
                block_refs[2 * b + r], buffer_ref.at[b, r ^ flip], sems.at[b, r]
            ).start()


def wait_block(block_refs, buffer_ref, sems, b):
    for r in range(2):
        pltpu.make_async_copy(block_refs[0], buffer_ref.at[b, r], sems.at[b, r]).wait()


def pick_rows(place_ref, buffer_ref, rows_ref, b, experts, cap, tile):
    toks = buffer_ref.shape[2]
    slot = lax.broadcasted_iota(jnp.int32, (cap, toks), 0)
    picks = jnp.concatenate(
        [jnp.where(slot == place_ref[b, e], 1.0, 0.0) for e in range(experts)], axis=0
    ).astype(half_type)
    half = buffer_ref.shape[3]
    for h in range(2):
        for start in range(0, half, tile):
            rows = jnp.dot(
                picks,
                buffer_ref[b, h, :, start : start + tile],
                preferred_element_type=jnp.float32,
            ).astype(half_type)
            for e in range(experts):
                rows_ref[e, h, b, :, start : start + tile] = rows[e * cap : (e + 1) * cap]


def add_rows(target_ref, rows_ref, out_ref, b, flip, experts, cap, tile):
    target = target_ref[b]
    toks = target.shape[0]
    lane = lax.broadcasted_iota(jnp.int32, (toks, experts * cap), 1)
    hit = lane == target[:, 0:1]
    for e in range(1, experts):
        hit = jnp.logical_or(hit, lane == target[:, e : e + 1])
    spread = jnp.where(hit, 1.0, 0.0).astype(half_type)
    half = rows_ref.shape[4]
    for h in range(2):
        for start in range(0, half, tile):
            rows = jnp.concatenate(
                [rows_ref[e, h, b, :, start : start + tile] for e in range(experts)], axis=0
            )
            out_ref[0, h ^ flip, :, start : start + tile] = jnp.dot(
                spread, rows, preferred_element_type=jnp.float32
            ).astype(half_type)


def grad_rows_kernel(experts, cap, flip_ref, place_ref, down_ref, *refs):
    block_refs = refs[: 2 * QUAD]
    out_ref, buffer_ref, rows_ref, sems = refs[2 * QUAD :]
    step = pl.program_id(0)
    half = buffer_ref.shape[3]

    @pl.when(step == 0)
    def _():
        start_blocks(block_refs, buffer_ref, sems, flip_ref[0])

    @pl.when(step < QUAD)
    def _():
        wait_block(block_refs, buffer_ref, sems, step)
        pick_rows(place_ref, buffer_ref, rows_ref, step, experts, cap, 512)

    @pl.when(step >= QUAD)
    def _():
        e = step - QUAD
        total = nt_dot(rows_ref[e, 0].reshape(QUAD * cap, half), down_ref[0, :, :half])
        total += nt_dot(rows_ref[e, 1].reshape(QUAD * cap, half), down_ref[0, :, half:])
        out_ref[0] = total.astype(half_type)


def expert_kernel(experts, cap, flip_ref, place_ref, gate_ref, target_ref, wg_ref, wu_ref, dh_ref, *refs):
    block_refs = refs[: 2 * QUAD]
    send_ref, keep_ref, hidden_ref, dgate_ref, buffer_ref, rows_ref, sems = refs[2 * QUAD :]
    step = pl.program_id(0)
    half = buffer_ref.shape[3]
    toks = buffer_ref.shape[2]

    @pl.when(step == 0)
    def _():
        start_blocks(block_refs, buffer_ref, sems, flip_ref[0])

    @pl.when(step < QUAD)
    def _():
        wait_block(block_refs, buffer_ref, sems, step)
        pick_rows(place_ref, buffer_ref, rows_ref, step, experts, cap, 512)

    @pl.when(jnp.logical_and(step >= QUAD, step < QUAD + experts))
    def _():
        e = step - QUAD
        first = rows_ref[e, 0].reshape(QUAD * cap, half)
        second = rows_ref[e, 1].reshape(QUAD * cap, half)
        pre_gate = jnp.dot(first, wg_ref[0, :half], preferred_element_type=jnp.float32)
        pre_gate += jnp.dot(second, wg_ref[0, half:], preferred_element_type=jnp.float32)
        pre_up = jnp.dot(first, wu_ref[0, :half], preferred_element_type=jnp.float32)
        pre_up += jnp.dot(second, wu_ref[0, half:], preferred_element_type=jnp.float32)
        sig = lax.logistic(pre_gate)
        silu = pre_gate * sig
        act = silu * pre_up
        d_raw = dh_ref[0].astype(jnp.float32)
        slot = lax.broadcasted_iota(jnp.int32, (cap, toks), 0)
        gate_parts = []
        for b in range(QUAD):
            hit = slot == place_ref[b, e]
            gate_parts.append(
                jnp.sum(jnp.where(hit, gate_ref[b, e], 0.0), axis=1, keepdims=True)
            )
        gate_col = jnp.concatenate(gate_parts, axis=0)
        hidden_ref[0] = (act * gate_col).astype(half_type)
        d_col = jnp.sum(act * d_raw, axis=1, keepdims=True)
        for b in range(QUAD):
            hit = slot == place_ref[b, e]
            dgate_ref[e, b] = jnp.sum(
                jnp.where(hit, d_col[b * cap : (b + 1) * cap], 0.0), axis=0, keepdims=True
            )
        d_hidden = d_raw * gate_col
        d_up = (d_hidden * silu).astype(half_type)
        d_gate = (d_hidden * pre_up * (sig * (1.0 + pre_gate * (1.0 - sig)))).astype(half_type)
        for h in range(2):
            d_in = nt_dot(d_gate, wg_ref[0, h * half : (h + 1) * half])
            d_in += nt_dot(d_up, wu_ref[0, h * half : (h + 1) * half])
            rows_ref[e, h] = d_in.astype(half_type).reshape(QUAD, cap, half)

    for which, out_ref in ((0, send_ref), (1, keep_ref)):
        first_step = QUAD + experts + 2 * which

        @pl.when(jnp.logical_and(step >= first_step, step < first_step + 2))
        def _():
            b = 2 * (step - first_step) + 1 - which
            add_rows(target_ref, rows_ref, out_ref, b, flip_ref[0], experts, cap, 512)


def output_kernel(experts, cap, flip_ref, target_ref, down_ref, hidden_ref, send_ref, keep_ref, rows_ref):
    step = pl.program_id(0)
    half = rows_ref.shape[4]

    @pl.when(step < experts)
    def _():
        for h in range(2):
            out = jnp.dot(
                hidden_ref[0],
                down_ref[0, :, h * half : (h + 1) * half],
                preferred_element_type=jnp.float32,
            )
            rows_ref[step, h] = out.astype(half_type).reshape(QUAD, cap, half)

    for which, out_ref in ((0, send_ref), (1, keep_ref)):
        first_step = experts + 2 * which

        @pl.when(jnp.logical_and(step >= first_step, step < first_step + 2))
        def _():
            b = 2 * (step - first_step) + 1 - which
            add_rows(target_ref, rows_ref, out_ref, b, flip_ref[0], experts, cap, 512)


def whole(shape):
    return pl.BlockSpec(shape, lambda i, *_: (0,) * len(shape), pipeline_mode=pl.Buffered(1))


def per_step(shape, first, count):
    return pl.BlockSpec(
        (1,) + shape[1:], lambda i, *_: (jnp.clip(i - first, 0, count - 1),) + (0,) * (len(shape) - 1)
    )


def block_scratch(toks, half, experts, cap, with_buffer):
    rows = pltpu.VMEM((experts, 2, QUAD, cap, half), half_type)
    if not with_buffer:
        return [rows]
    return [
        pltpu.VMEM((QUAD, 2, toks, half), half_type),
        rows,
        pltpu.SemaphoreType.DMA((QUAD, 2)),
    ]


def call_grad_rows(flip, place, down, halves, cap):
    experts, hidden_units, width = down.shape
    toks, half = halves[0].shape
    rows = QUAD * cap
    return pl.pallas_call(
        functools.partial(grad_rows_kernel, experts, cap),
        out_shape=jax.ShapeDtypeStruct((experts, rows, hidden_units), half_type),
        grid_spec=pltpu.PrefetchScalarGridSpec(
            num_scalar_prefetch=1,
            grid=(QUAD + experts,),
            in_specs=[whole(place.shape), per_step(down.shape, QUAD, experts)]
            + [pl.BlockSpec(memory_space=pl.ANY)] * (2 * QUAD),
            out_specs=per_step((experts, rows, hidden_units), QUAD, experts),
            scratch_shapes=block_scratch(toks, half, experts, cap, True),
        ),
        compiler_params=pltpu.CompilerParams(
            dimension_semantics=("arbitrary",), vmem_limit_bytes=VMEM_LIMIT
        ),
        cost_estimate=pl.CostEstimate(
            flops=2 * experts * rows * width * (toks + hidden_units),
            bytes_accessed=2 * (down.size + 2 * QUAD * toks * half + experts * rows * hidden_units),
            transcendentals=0,
        ),
        name="grad_rows",
    )(flip, place, down, *halves)


def call_experts(flip, place, gate, target, gate_w, up_w, d_raw, halves, cap):
    experts, width, hidden_units = gate_w.shape
    toks, half = halves[0].shape
    rows = QUAD * cap
    blocks = (2, 2, toks, half)
    return pl.pallas_call(
        functools.partial(expert_kernel, experts, cap),
        out_shape=(
            jax.ShapeDtypeStruct(blocks, half_type),
            jax.ShapeDtypeStruct(blocks, half_type),
            jax.ShapeDtypeStruct((experts, rows, hidden_units), half_type),
            jax.ShapeDtypeStruct((experts, QUAD, 1, toks), jnp.float32),
        ),
        grid_spec=pltpu.PrefetchScalarGridSpec(
            num_scalar_prefetch=1,
            grid=(2 * QUAD + experts,),
            in_specs=[
                whole(place.shape),
                whole(gate.shape),
                whole(target.shape),
                per_step(gate_w.shape, QUAD, experts),
                per_step(up_w.shape, QUAD, experts),
                per_step(d_raw.shape, QUAD, experts),
            ]
            + [pl.BlockSpec(memory_space=pl.ANY)] * (2 * QUAD),
            out_specs=(
                per_step(blocks, QUAD + experts, 2),
                per_step(blocks, QUAD + experts + 2, 2),
                per_step((experts, rows, hidden_units), QUAD, experts),
                whole((experts, QUAD, 1, toks)),
            ),
            scratch_shapes=block_scratch(toks, half, experts, cap, True),
        ),
        compiler_params=pltpu.CompilerParams(
            dimension_semantics=("arbitrary",), vmem_limit_bytes=VMEM_LIMIT
        ),
        cost_estimate=pl.CostEstimate(
            flops=4 * experts * rows * width * (toks + 2 * hidden_units),
            bytes_accessed=2 * (2 * gate_w.size + 4 * QUAD * toks * half),
            transcendentals=experts * rows * hidden_units,
        ),
        name="experts",
    )(flip, place, gate, target, gate_w, up_w, d_raw, *halves)


def call_output(flip, target, down, hidden, cap, half):
    experts, hidden_units, width = down.shape
    toks = target.shape[1]
    rows = QUAD * cap
    blocks = (2, 2, toks, half)
    return pl.pallas_call(
        functools.partial(output_kernel, experts, cap),
        out_shape=(
            jax.ShapeDtypeStruct(blocks, half_type),
            jax.ShapeDtypeStruct(blocks, half_type),
        ),
        grid_spec=pltpu.PrefetchScalarGridSpec(
            num_scalar_prefetch=1,
            grid=(QUAD + experts,),
            in_specs=[
                whole(target.shape),
                per_step(down.shape, 0, experts),
                per_step(hidden.shape, 0, experts),
            ],
            out_specs=(per_step(blocks, experts, 2), per_step(blocks, experts + 2, 2)),
            scratch_shapes=block_scratch(toks, half, experts, cap, False),
        ),
        compiler_params=pltpu.CompilerParams(
            dimension_semantics=("arbitrary",), vmem_limit_bytes=VMEM_LIMIT
        ),
        cost_estimate=pl.CostEstimate(
            flops=2 * experts * rows * width * (toks + hidden_units),
            bytes_accessed=2 * (down.size + 2 * QUAD * toks * half),
            transcendentals=0,
        ),
        name="outputs",
    )(flip, target, down, hidden)


def swap(values, data_count, bit):
    return lax.ppermute(values, "dp", [(i, i ^ bit) for i in range(data_count)])


def onward(values, data_count):
    return lax.ppermute(values, "dp", [(i, (i + QUAD) % data_count) for i in range(data_count)])


def other_side(values):
    return lax.ppermute(values, "tensor", [(0, 1), (1, 0)])


def gather_groups(first, second, data_count, pair):
    groups = []
    for j in range(data_count // QUAD):
        core_first = swap(first, data_count, 1)
        core_second = swap(second, data_count, 1)
        across_first = swap(first, data_count, 2)
        across_second = other_side(across_first) if pair else swap(second, data_count, 2)
        groups.append(
            [
                first,
                second,
                core_first,
                core_second,
                across_first,
                across_second,
                swap(across_first, data_count, 1),
                swap(across_second, data_count, 1),
            ]
        )
        if j + 1 < data_count // QUAD:
            first = onward(first, data_count)
            second = onward(second, data_count)
    return groups


def plus(left, right):
    return (left.astype(jnp.float32) + right.astype(jnp.float32)).astype(half_type)


def reduce_group(send, keep, data_count, pair):
    got = swap(send, data_count, 1)
    if pair:
        away = plus(keep[1, 1], got[1, 1])
        near = keep[1, 0].astype(jnp.float32) + got[1, 0].astype(jnp.float32)
        near = (near + other_side(away).astype(jnp.float32)).astype(half_type)
        first = (
            keep[0, 0].astype(jnp.float32)
            + got[0, 0].astype(jnp.float32)
            + swap(near, data_count, 2).astype(jnp.float32)
        ).astype(half_type)
        return first, plus(keep[0, 1], got[0, 1])
    across = plus(keep[1], got[1])
    total = (
        keep[0].astype(jnp.float32)
        + got[0].astype(jnp.float32)
        + swap(across, data_count, 2).astype(jnp.float32)
    ).astype(half_type)
    return total[0], total[1]


def reduce_groups(parts, data_count, pair):
    sums = [reduce_group(send, keep, data_count, pair) for send, keep in parts]
    count = len(sums)
    first, second = sums[1 % count]
    for j in range(2, count + 1):
        first = plus(onward(first, data_count), sums[j % count][0])
        second = plus(onward(second, data_count), sums[j % count][1])
    return first, second


def local(
    layer_input,
    cotangent,
    attention_norm_gain,
    expert_norm_gain,
    query_norm_gain,
    key_norm_gain,
    query_weight_matrix,
    key_weight_matrix,
    value_weight_matrix,
    output_weight_matrix,
    adapter_projection_down,
    adapter_projection_up,
    adapter_output_down,
    adapter_output_up,
    router,
    expert_gate_weight,
    expert_up_weight,
    expert_down_weight,
    segments,
    sequence_adapter_index,
    routes,
):
    tok_count = layer_input.shape[0]
    tensor_count = lax.axis_size("tensor")
    data_count = lax.axis_size("dp")
    pair = tensor_count == 2
    ring_count = data_count // QUAD
    col_width = MODEL_WIDTH // tensor_count
    half_width = MODEL_WIDTH // 2
    side = lax.axis_index("tensor")
    col_start = side * col_width
    place_dp = lax.axis_index("dp")
    flip = side.astype(jnp.int32) if pair else jnp.int32(0)
    flip_arr = flip.reshape(1)
    shard_local_width = query_weight_matrix.shape[1]
    local_heads = shard_local_width // HEAD_WIDTH
    local_experts = expert_gate_weight.shape[0]
    expert_total = local_experts * data_count
    capacity = 5 * tok_count * TOP // (4 * expert_total)
    device_lane_count = ADAPTER_CHOICES * ADAPTER_RANK
    score_scale = HEAD_WIDTH ** (-0.5)
    token_ids = jnp.arange(tok_count, dtype=jnp.int32)

    def to_sides(full):
        if pair:
            low_cols, high_cols = full[:, :half_width], full[:, half_width:]
            return (
                jnp.where(flip == 0, low_cols, high_cols),
                jnp.where(flip == 0, high_cols, low_cols),
            )
        return full[:, :half_width], full[:, half_width:]

    def from_sides(first, second):
        if pair:
            return jnp.concatenate(
                [jnp.where(flip == 0, first, second), jnp.where(flip == 0, second, first)], axis=1
            )
        return jnp.concatenate([first, second], axis=1)

    routes_t = routes.T
    expert_ids = jnp.arange(expert_total, dtype=jnp.int32)
    chosen_mask = jnp.any(routes_t[:, None, :] == expert_ids[None, :, None], axis=0)
    earlier = (token_ids[:, None] < token_ids[None, :]).astype(half_type)
    rank = jnp.dot(chosen_mask.astype(half_type), earlier, preferred_element_type=jnp.float32)
    place_own = jnp.where(chosen_mask, rank, -1.0).astype(jnp.int32)
    place_all = lax.all_to_all(
        place_own.reshape(data_count, local_experts, tok_count), "dp", 0, 0, tiled=True
    )
    ring_at, quad_at = place_dp // QUAD, place_dp % QUAD
    group_ids = jnp.arange(data_count, dtype=jnp.int32)
    order = ((ring_at - group_ids // QUAD) % ring_count) * QUAD + (quad_at ^ (group_ids % QUAD))
    place_all = place_all[order]
    target_all = jnp.where(
        place_all >= 0,
        place_all + capacity * jnp.arange(local_experts, dtype=jnp.int32)[None, :, None],
        -1,
    ).transpose(0, 2, 1)

    def group_of(values, j):
        return values[j * QUAD : (j + 1) * QUAD]

    if pair:
        g_first = cotangent
        g_second = other_side(cotangent)
    else:
        g_full = lax.all_gather(cotangent, "tensor", axis=1, tiled=True)
        g_first, g_second = g_full[:, :half_width], g_full[:, half_width:]
    g_groups = gather_groups(g_first, g_second, data_count, pair)
    d_raw = [
        call_grad_rows(
            flip_arr,
            group_of(place_all, j)[:, :, None, :],
            expert_down_weight,
            g_groups[j],
            capacity,
        )
        for j in range(ring_count)
    ]

    seq_of = token_ids // LEN
    positions = token_ids % LEN
    seq_hot = seq_of[:, None] == jnp.arange(tok_count // LEN, dtype=jnp.int32)[None, :]
    token_adapter = jnp.sum(jnp.where(seq_hot, sequence_adapter_index[None, :], 0), axis=1)
    adapter_mask = (
        token_adapter[:, None]
        == (jnp.arange(device_lane_count, dtype=jnp.int32) // ADAPTER_RANK)[None, :]
    )
    mask_float = adapter_mask.astype(jnp.float32)
    mask_half = adapter_mask.astype(half_type)
    doc_flat = segments.reshape(-1) + 16 * 1024 * seq_of
    hidden32 = layer_input.astype(jnp.float32)
    normed32, norm1_back = jax.vjp(
        lambda values: rms_scale(values, attention_norm_gain, norm_eps), hidden32
    )
    normed = normed32.astype(half_type)
    w_proj = [query_weight_matrix, key_weight_matrix, value_weight_matrix]
    down_factor_rows = [
        down_factor_layout(adapter_projection_down[projection_index])
        for projection_index in range(3)
    ]
    up_factor_rows = [
        adapter_projection_up[projection_index].reshape(device_lane_count, shard_local_width)
        for projection_index in range(3)
    ]
    latents = []
    raw_proj = []
    for projection_index in range(3):
        latent = jnp.dot(
            normed, down_factor_rows[projection_index], preferred_element_type=jnp.float32
        ).astype(half_type)
        latents.append(latent * mask_half)
        raw_proj.append(
            jnp.dot(normed, w_proj[projection_index], preferred_element_type=jnp.float32)
            + jnp.dot(
                latent * mask_half,
                up_factor_rows[projection_index],
                preferred_element_type=jnp.float32,
            )
        )
    query_f, query_back = jax.vjp(
        lambda projected: head_prep(projected, query_norm_gain, positions), raw_proj[0]
    )
    key_f, key_back = jax.vjp(
        lambda projected: head_prep(projected, key_norm_gain, positions), raw_proj[1]
    )
    queries = query_f.astype(half_type)
    keys = key_f.astype(half_type)
    values = raw_proj[2].reshape(tok_count, local_heads, HEAD_WIDTH).astype(half_type)

    same_doc = (doc_flat[:, None] == doc_flat[None, :])[None]

    def block_scores():
        scores = (
            jnp.einsum("qhd,khd->hqk", queries, keys, preferred_element_type=jnp.float32)
            * score_scale
        )
        return jnp.where(same_doc, scores, -1e30)

    scores = block_scores()
    top_score = jnp.max(scores, axis=-1, keepdims=True)
    exp_scores = jnp.exp(scores - top_score)
    row_total = jnp.sum(exp_scores, axis=-1, keepdims=True)
    prob_half = (exp_scores / row_total).astype(half_type)
    attended = jnp.einsum("hqk,khd->qhd", prob_half, values, preferred_element_type=jnp.float32)
    log_totals = top_score[..., 0] + jnp.log(row_total[..., 0])
    attended = attended.reshape(tok_count, shard_local_width).astype(half_type)
    output_down_rows = down_factor_layout(adapter_output_down)
    output_up_rows = adapter_output_up.reshape(device_lane_count, MODEL_WIDTH)
    proj_part = jnp.dot(attended, output_weight_matrix, preferred_element_type=jnp.float32)
    latent_part = jnp.dot(attended, output_down_rows, preferred_element_type=jnp.float32)

    def tensor_sum(part):
        part = part.astype(half_type)
        if pair:
            return part.astype(jnp.float32) + other_side(part).astype(jnp.float32)
        return lax.psum(part, "tensor").astype(jnp.float32)

    attn_total = tensor_sum(proj_part)
    latent_total = tensor_sum(latent_part)
    latent_out = latent_total.astype(half_type) * mask_half
    mixed_rows = (
        hidden32
        + attn_total
        + jnp.dot(latent_out, output_up_rows, preferred_element_type=jnp.float32)
    )
    moe_in32, norm2_back = jax.vjp(
        lambda values: rms_scale(values, expert_norm_gain, norm_eps), mixed_rows
    )
    moe_in = moe_in32.astype(half_type)
    x_groups = gather_groups(*to_sides(moe_in), data_count, pair)

    logits_t = lax.dot_general(
        router, moe_in, (((0,), (1,)), ((), ())), preferred_element_type=jnp.float32
    )
    top_logit = jnp.max(jnp.where(chosen_mask, logits_t, -jnp.inf), axis=0, keepdims=True)
    gate_exp = jnp.where(chosen_mask, jnp.exp(jnp.minimum(logits_t - top_logit, 0.0)), 0.0)
    gates_t = gate_exp / jnp.sum(gate_exp, axis=0, keepdims=True)
    gates_all = lax.all_to_all(
        gates_t.reshape(data_count, local_experts, tok_count), "dp", 0, 0, tiled=True
    )[order]

    grad_parts = []
    out_hidden = []
    d_gate_parts = []
    for j in range(ring_count):
        send, keep, hidden, d_gate = call_experts(
            flip_arr,
            group_of(place_all, j)[:, :, None, :],
            group_of(gates_all, j)[:, :, None, :],
            group_of(target_all, j),
            expert_gate_weight,
            expert_up_weight,
            d_raw[j],
            x_groups[j],
            capacity,
        )
        grad_parts.append((send, keep))
        out_hidden.append(hidden)
        d_gate_parts.append(d_gate[:, :, 0, :].transpose(1, 0, 2))

    d_gate_all = jnp.concatenate(d_gate_parts, axis=0)
    back_order = ((ring_at - group_ids // QUAD) % ring_count) * QUAD + (
        quad_at ^ (group_ids % QUAD)
    )
    d_gate_home = lax.all_to_all(d_gate_all[back_order], "dp", 0, 0, tiled=True)
    d_gate_home = d_gate_home.reshape(expert_total, tok_count)
    if pair:
        d_gate_home = d_gate_home + other_side(d_gate_home)
    else:
        d_gate_home = lax.psum(d_gate_home, "tensor")
    weighted = gates_t * d_gate_home
    grad_logits_t = (
        gates_t * (d_gate_home - jnp.sum(weighted, axis=0, keepdims=True))
    ).astype(half_type)

    grad_first, grad_second = reduce_groups(grad_parts, data_count, pair)
    if pair:
        got_first = other_side(grad_first)
        got_second = other_side(grad_second)
        full_first = grad_first.astype(jnp.float32) + got_second.astype(jnp.float32)
        full_second = grad_second.astype(jnp.float32) + got_first.astype(jnp.float32)
        grad_moe_expert = from_sides(full_first, full_second)
        grad_full = from_sides(g_first, g_second).astype(jnp.float32)
    else:
        grad_moe_expert = lax.psum(from_sides(grad_first, grad_second), "tensor").astype(
            jnp.float32
        )
        grad_full = g_full.astype(jnp.float32)
    grad_moe_in = grad_moe_expert + lax.dot_general(
        grad_logits_t, router, (((0,), (1,)), ((), ())), preferred_element_type=jnp.float32
    )

    out_parts = [
        call_output(
            flip_arr,
            group_of(target_all, j),
            expert_down_weight,
            out_hidden[j],
            capacity,
            half_width,
        )
        for j in range(ring_count)
    ]
    out_first, out_second = reduce_groups(out_parts, data_count, pair)
    if pair:
        moe_cols = out_first.astype(jnp.float32) + other_side(out_second).astype(jnp.float32)
    else:
        moe_cols = lax.psum_scatter(
            from_sides(out_first, out_second), "tensor", scatter_dimension=1, tiled=True
        ).astype(jnp.float32)
    mixed_cols = lax.dynamic_slice_in_dim(mixed_rows, col_start, col_width, 1)
    layer_out = (mixed_cols + moe_cols).astype(half_type)

    grad_mixed = grad_full + norm2_back(grad_moe_in)[0]
    grad_branch = grad_mixed.astype(half_type)
    grad_latent_out = (
        jnp.einsum("td,ad->ta", grad_branch, output_up_rows, preferred_element_type=jnp.float32)
        * mask_float
    ).astype(half_type)
    branch_cols = lax.dynamic_slice_in_dim(grad_branch, col_start, col_width, 1)
    grad_up_out = jnp.einsum(
        "ta,td->ad", latent_out, branch_cols, preferred_element_type=jnp.float32
    ).reshape(ADAPTER_CHOICES, ADAPTER_RANK, col_width)
    grad_attended = jnp.einsum(
        "td,cd->tc", grad_branch, output_weight_matrix, preferred_element_type=jnp.float32
    )
    grad_attended = grad_attended + jnp.einsum(
        "ta,ca->tc", grad_latent_out, output_down_rows, preferred_element_type=jnp.float32
    )
    grad_heads = grad_attended.astype(half_type).reshape(tok_count, local_heads, HEAD_WIDTH)
    grad_down_out = jnp.einsum(
        "tc,ta->ca", attended, grad_latent_out, preferred_element_type=jnp.float32
    )
    grad_down_out = grad_down_out.reshape(
        shard_local_width, ADAPTER_CHOICES, ADAPTER_RANK
    ).transpose(1, 0, 2)

    prob_block = jnp.where(same_doc, jnp.exp(block_scores() - log_totals[:, :, None]), 0.0)
    grad_prob = jnp.einsum("qhd,khd->hqk", grad_heads, values, preferred_element_type=jnp.float32)
    row_delta = jnp.sum(prob_block * grad_prob, axis=-1, keepdims=True)
    grad_scores = (prob_block * (grad_prob - row_delta)).astype(half_type)
    grad_queries = (
        jnp.einsum("hqk,khd->qhd", grad_scores, keys, preferred_element_type=jnp.float32)
        * score_scale
    )
    grad_keys = (
        jnp.einsum("hqk,qhd->khd", grad_scores, queries, preferred_element_type=jnp.float32)
        * score_scale
    )
    grad_values = jnp.einsum(
        "hqk,qhd->khd",
        prob_block.astype(half_type),
        grad_heads,
        preferred_element_type=jnp.float32,
    ).reshape(tok_count, shard_local_width)
    grad_raw = [
        query_back(grad_queries)[0].astype(half_type),
        key_back(grad_keys)[0].astype(half_type),
        grad_values.astype(half_type),
    ]
    grad_normed_part = jnp.zeros((tok_count, MODEL_WIDTH), jnp.float32)
    latent_parts = []
    for projection_index in range(3):
        grad_normed_part = grad_normed_part + jnp.einsum(
            "tc,dc->td",
            grad_raw[projection_index],
            w_proj[projection_index],
            preferred_element_type=jnp.float32,
        )
        latent_parts.append(
            jnp.einsum(
                "tc,ac->ta",
                grad_raw[projection_index],
                up_factor_rows[projection_index],
                preferred_element_type=jnp.float32,
            )
        )
    grad_latent_sum = tensor_sum(jnp.stack(latent_parts))
    grad_normed = tensor_sum(grad_normed_part)
    grad_latent = (grad_latent_sum * mask_float[None]).astype(half_type)
    grad_down_list = []
    grad_up_list = []
    for projection_index in range(3):
        grad_normed = grad_normed + jnp.einsum(
            "ta,da->td",
            grad_latent[projection_index],
            down_factor_rows[projection_index],
            preferred_element_type=jnp.float32,
        )
        grad_down = jnp.einsum(
            "td,ta->da", normed, grad_latent[projection_index], preferred_element_type=jnp.float32
        )
        grad_down_list.append(
            grad_down.reshape(MODEL_WIDTH, ADAPTER_CHOICES, ADAPTER_RANK).transpose(1, 0, 2)
        )
        grad_up = jnp.einsum(
            "ta,tc->ac",
            latents[projection_index],
            grad_raw[projection_index],
            preferred_element_type=jnp.float32,
        )
        grad_up_list.append(grad_up.reshape(ADAPTER_CHOICES, ADAPTER_RANK, shard_local_width))
    grad_hidden_in = grad_mixed + norm1_back(grad_normed)[0]
    grad_input = lax.dynamic_slice_in_dim(grad_hidden_in, col_start, col_width, 1)
    summed = (
        lax.psum(jnp.stack(grad_down_list).astype(jnp.bfloat16), "dp").astype(jnp.float32),
        lax.psum(jnp.stack(grad_up_list).astype(jnp.bfloat16), "dp").astype(jnp.float32),
        lax.psum(grad_down_out.astype(jnp.bfloat16), "dp").astype(jnp.float32),
        lax.psum(grad_up_out.astype(jnp.bfloat16), "dp").astype(jnp.float32),
    )
    return (layer_out, grad_input, summed[0], summed[1], summed[2], summed[3])


def solution(mesh):
    return jax.shard_map(
        local,
        mesh=mesh,
        in_specs=(
            P("dp", None),
            P("dp", "tensor"),
            P(),
            P(),
            P(),
            P(),
            P(None, "tensor"),
            P(None, "tensor"),
            P(None, "tensor"),
            P("tensor", None),
            P(),
            P(None, None, None, "tensor"),
            P(None, "tensor", None),
            P(),
            P(),
            P("dp", None, "tensor"),
            P("dp", None, "tensor"),
            P("dp", "tensor", None),
            P("dp", None),
            P("dp"),
            P("dp", None),
        ),
        out_specs=(
            P("dp", "tensor"),
            P("dp", "tensor"),
            P(),
            P(None, None, None, "tensor"),
            P(None, "tensor", None),
            P(None, None, "tensor"),
        ),
        check_vma=False,
    )
```

time: 3450 us -> 1260 us (0.37)
  blocking collectives: 1210 us -> 0 us
  waiting for transfers between devices: 1590 us -> 663 us
  Pallas kernels: 0 us -> 231 us
  local copies, waits for them, and re-layouts: 219 us -> 42.9 us
  matrix products: 253 us -> 84.9 us
  starting transfers between devices: 6.27 us -> 82.4 us
    all_to_all x3 -> x0, blocking collectives: 1190 us -> none  [the longest x1 458 us: local(): lax.all_to_all(slot_tokens, 'dp', split_axis=0, concat_axis=0, tiled=True)]
    reduce_scatter x2 -> x0, waiting for transfers between devices: 918 us -> none  [the longest x1 459 us: local(): lax.psum_scatter(grad_in_part, 'tensor', scatter_dimension=3, tiled=True)]
    ppermute x0 -> x105, waiting for transfers between devices: none -> 500 us  [the longest x24 299 us: onward(): lax.ppermute(values, 'dp', [(i, (i + QUAD) % data_count) for i in range(d...]
    all_gather x3 -> x0, waiting for transfers between devices: 335 us -> none  [the longest x1 249 us: local(): grad_expert = lax.all_gather(grad_arrived, 'tensor', axis=2, tiled=True)]
    pallas_call x0 -> x12, Pallas kernels: none -> 231 us  [the longest x4 119 us: call_experts(): pl.pallas_call(functools.partial(expert_kernel, experts, cap), out_shape=...]
    dot_general x14 -> x8, matrix products: 182 us -> 17.5 us  [the longest x1 5.78 us: local(): jnp.einsum('qhd,khd->hqk', grad_heads, values, preferred_element_type=jnp...]
    gather x10 -> x3, local copies, waits for them, and re-layouts: 145 us -> 2.52 us  [the longest x1 1.27 us: local(): d_gate_home = lax.all_to_all(d_gate_all[back_order], 'dp', 0, 0, tiled=True)]
    psum x2 -> x0, waiting for transfers between devices: 90.3 us -> none  [the longest x1 48.3 us: local(): lax.psum(jnp.stack(latent_parts).astype(jnp.bfloat16), 'tensor')]
  transfers between devices with their start and end apart: 9 -> 109, of which waited for: 9 -> 36; matrix products, arithmetic and copies ran while one was open for 4% -> 15% of each run, Pallas kernels for 0% -> 19%
where the time goes in v1:
time: 1260 us; the launch traced here: 1250 us
  waiting for transfers between devices  663 us (53%)
  Pallas kernels  231 us (18%)
  other arithmetic  124 us (10%)
  matrix products  84.9 us (7%)
  starting transfers between devices  82.4 us (7%)
  local copies, waits for them, and re-layouts  42.9 us (3%)
  between operations  17.4 us (1%)
    ppermute x24, waiting for transfers between devices, onward(): lax.ppermute(values, 'dp', [(i, (i + QUAD) % data_count) for i in range(d...  299 us
    ppermute x25, waiting for transfers between devices, other_side(): return lax.ppermute(values, 'tensor', [(0, 1), (1, 0)])  157 us
    pallas_call x4, Pallas kernels, call_experts(): pl.pallas_call(functools.partial(expert_kernel, experts, cap), out_shape=...  119 us
    psum x1, waiting for transfers between devices, local(): lax.psum(jnp.stack(grad_down_list).astype(jnp.bfloat16), 'dp')  87.4 us
    pallas_call x4, Pallas kernels, call_output(): pl.pallas_call(functools.partial(output_kernel, experts, cap), out_shape=...  61.1 us
    pallas_call x4, Pallas kernels, call_grad_rows(): pl.pallas_call(functools.partial(grad_rows_kernel, experts, cap), out_sha...  50.6 us
    all_to_all x1, waiting for transfers between devices, local(): lax.all_to_all(place_own.reshape(data_count, local_experts, tok_count), '...  45 us
    ppermute x56, waiting for transfers between devices, swap(): return lax.ppermute(values, 'dp', [(i, i ^ bit) for i in range(data_count)])  44.3 us
  transfers between devices with their start and end apart: 109, of which 36 were waited for; matrix products, arithmetic and copies ran while one was open for 15% of the time, Pallas kernels for 19%

profile of v1, /device:TPU:0, one launch (start us, length us, event | category | flops | bytes accessed | tf_op | source)
XLA Modules:
  0.0 1246.3 jit_solution(12694617511308338108)
XLA Ops:
  67.8 44.0 %collective-permute-done.1 = bf16[512,128]{0,1:T(8,128)(2,1)S(1)} collective-permute-done((bf16[512,128]{0,1:T(8,128)(2,1)S(1)}, bf16[512,128]{0,1:T(8,128)(2,1)S(1)}, u32[]{:S(2)}, u32[]{:S(2)}) %collective-permute-start.1) | collective-permute-done | bytes 131104 | tf_op jit(solution)/shard_map/ppermute | solution.py:358
  119.6 14.0 %collective-permute-done.3.refs_1_ = bf16[512,1024]{1,0:T(8,128)(2,1)} collective-permute-done((bf16[512,1024]{1,0:T(8,128)(2,1)}, bf16[512,1024]{1,0:T(8,128)(2,1)}, u32[]{:S(2)}, u32[]{:S(2)}) %collective-permute-start.3) | collective-permute-done | bytes 1048608 | tf_op jit(solution)/shard_map/ppermute | solution.py:358
  135.6 5.2 collective-permute-done.23.refs_0_
  143.2 19.7 %collective-permute-done.4.refs_1_ = bf16[512,1024]{1,0:T(8,128)(2,1)S(1)} collective-permute-done((bf16[512,1024]{1,0:T(8,128)(2,1)}, bf16[512,1024]{1,0:T(8,128)(2,1)S(1)}, u32[]{:S(2)}, u32[]{:S(2)}) %collective-permute-start.4) | collective-permute-done | bytes 1048608 | tf_op jit(solution)/shard_map/ppermute | solution.py:354
  169.4 21.3 %collective-permute-done.11.refs_0_ = bf16[512,1024]{1,0:T(8,128)(2,1)S(1)} collective-permute-done((bf16[512,1024]{1,0:T(8,128)(2,1)S(1)}, bf16[512,1024]{1,0:T(8,128)(2,1)S(1)}, u32[]{:S(2)}, u32[]{:S(2)}) %collective-permute-start.11) | collective-permute-done | bytes 1048608 | tf_op jit(solution)/shard_map/ppermute | solution.py:354
  190.7 22.5 %collective-permute-done.12.refs_1_ = bf16[512,1024]{1,0:T(8,128)(2,1)S(1)} collective-permute-done((bf16[512,1024]{1,0:T(8,128)(2,1)S(1)}, bf16[512,1024]{1,0:T(8,128)(2,1)S(1)}, u32[]{:S(2)}, u32[]{:S(2)}) %collective-permute-start.12) | collective-permute-done | bytes 1048608 | tf_op jit(solution)/shard_map/ppermute | solution.py:354
  214.7 20.9 %collective-permute-done.43.refs_0_ = bf16[512,1024]{1,0:T(8,128)(2,1)S(1)} collective-permute-done((bf16[512,1024]{1,0:T(8,128)(2,1)}, bf16[512,1024]{1,0:T(8,128)(2,1)S(1)}, u32[]{:S(2)}, u32[]{:S(2)}) %collective-permute-start.43) | collective-permute-done | bytes 1048608 | tf_op jit(solution)/shard_map/ppermute | solution.py:354
  235.7 22.0 %collective-permute-done.24.refs_1_ = bf16[512,1024]{1,0:T(8,128)(2,1)S(1)} collective-permute-done((bf16[512,1024]{1,0:T(8,128)(2,1)S(1)}, bf16[512,1024]{1,0:T(8,128)(2,1)S(1)}, u32[]{:S(2)}, u32[]{:S(2)}) %collective-permute-start.24) | collective-permute-done | bytes 1048608 | tf_op jit(solution)/shard_map/ppermute | solution.py:354
  260.3 23.0 %collective-permute-done.71.refs_4_ = bf16[512,1024]{1,0:T(8,128)(2,1)} collective-permute-done((bf16[512,1024]{1,0:T(8,128)(2,1)S(1)}, bf16[512,1024]{1,0:T(8,128)(2,1)}, u32[]{:S(2)}, u32[]{:S(2)}) %collective-permute-start.71) | collective-permute-done | bytes 1048608 | tf_op jit(solution)/shard_map/ppermute | solution.py:350
  289.0 22.4 %collective-permute-done.32.refs_1_ = bf16[512,1024]{1,0:T(8,128)(2,1)} collective-permute-done((bf16[512,1024]{1,0:T(8,128)(2,1)S(1)}, bf16[512,1024]{1,0:T(8,128)(2,1)}, u32[]{:S(2)}, u32[]{:S(2)}) %collective-permute-start.32) | collective-permute-done | bytes 1048608 | tf_op jit(solution)/shard_map/ppermute | solution.py:354
  311.9 20.5 %collective-permute-done.44.refs_1_ = bf16[512,1024]{1,0:T(8,128)(2,1)S(1)} collective-permute-done((bf16[512,1024]{1,0:T(8,128)(2,1)S(1)}, bf16[512,1024]{1,0:T(8,128)(2,1)S(1)}, u32[]{:S(2)}, u32[]{:S(2)}) %collective-permute-start.44) | collective-permute-done | bytes 1048608 | tf_op jit(solution)/shard_map/ppermute | solution.py:354
  336.1 20.2 %collective-permute-done.15.refs_4_ = bf16[512,1024]{1,0:T(8,128)(2,1)S(1)} collective-permute-done((bf16[512,1024]{1,0:T(8,128)(2,1)S(1)}, bf16[512,1024]{1,0:T(8,128)(2,1)S(1)}, u32[]{:S(2)}, u32[]{:S(2)}) %collective-permute-start.15) | collective-permute-done | bytes 1048608 | tf_op jit(solution)/shard_map/ppermute | solution.py:350
  358.8 5.6 all-to-all-start
  364.4 45.0 %all-to-all-done = s32[16,4,512]{2,1,0:T(4,128)S(1)} async-done(((s32[16,4,512]{2,1,0:T(4,128)}), s32[16,4,512]{2,1,0:T(4,128)S(1)}, u32[]{:S(2)}, u32[]{:S(2)}) %all-to-all-start) | async-done | bytes 131104 | tf_op jit(solution)/shard_map/all_to_all | solution.py:487
  427.9 16.1 %all-to-all-done.1 = f32[16,4,512]{2,1,0:T(4,128)S(1)} async-done(((f32[16,4,512]{2,1,0:T(4,128)}), f32[16,4,512]{2,1,0:T(4,128)S(1)}, u32[]{:S(2)}, u32[]{:S(2)}) %all-to-all-start.1) | async-done | bytes 131104 | tf_op jit(solution)/shard_map/all_to_all | solution.py:619
  448.9 12.6 %grad_rows.7.dh_ref = bf16[4,320,512]{2,1,0:T(8,128)(2,1)} custom-call(s32[1]{0:T(128)} %bitcast.21.flip_ref, s32[4,4,1,512]{3,2,1,0:T(1,128)} %broadcast_in_dim.134.place_ref, bf16[4,512,2048]{2,1,0:T(8,128)(2,1)} %down_ref.15, bf16[512,1024]{1,0:T(8,128)(2,1)} %refs_0_.1, bf16[512,1024]{1,0:T(8,128)(2,1)} %collective-permute-done.3.refs_1_, ...), custom_call_target="tpu_custom_call" | custom-call | flops 5368709120 | bytes 18087936 | tf_op jit(solution)/shard_map/grad_rows/pallas_call | solution.py:247
  461.5 12.7 %grad_rows.4.dh_ref = bf16[4,320,512]{2,1,0:T(8,128)(2,1)} custom-call(s32[1]{0:T(128)} %bitcast.21.flip_ref, s32[4,4,1,512]{3,2,1,0:T(1,128)} %broadcast_in_dim.127.place_ref, bf16[4,512,2048]{2,1,0:T(8,128)(2,1)} %down_ref.15, bf16[512,1024]{1,0:T(8,128)(2,1)} %collective-permute-done.2.refs_0_, bf16[512,1024]{1,0:T(8,128)(2,1)} %copy-done.133, ...), custom_call_target="tpu_custom_call" | custom-call | flops 5368709120 | bytes 18087936 | tf_op jit(solution)/shard_map/grad_rows/pallas_call | solution.py:247
  474.2 12.7 %grad_rows.5.dh_ref = bf16[4,320,512]{2,1,0:T(8,128)(2,1)} custom-call(s32[1]{0:T(128)} %bitcast.21.flip_ref, s32[4,4,1,512]{3,2,1,0:T(1,128)} %broadcast_in_dim.130.place_ref, bf16[4,512,2048]{2,1,0:T(8,128)(2,1)} %down_ref.15, bf16[512,1024]{1,0:T(8,128)(2,1)} %collective-permute-done.23.refs_0_, bf16[512,1024]{1,0:T(8,128)(2,1)} %copy-done.141, ...), custom_call_target="tpu_custom_call" | custom-call | flops 5368709120 | bytes 18087936 | tf_op jit(solution)/shard_map/grad_rows/pallas_call | solution.py:247
  489.8 29.7 %experts.7 = (bf16[2,2,512,1024]{3,2,1,0:T(8,128)(2,1)}, bf16[2,2,512,1024]{3,2,1,0:T(8,128)(2,1)}, bf16[4,320,512]{2,1,0:T(8,128)(2,1)}, f32[4,4,1,512]{3,2,1,0:T(1,128)}) custom-call(s32[1]{0:T(128)} %bitcast.21.flip_ref, s32[4,4,1,512]{3,2,1,0:T(1,128)} %broadcast_in_dim.134.place_ref, f32[4,4,1,512]{3,2,1,0:T(1,128)} %broadcast_in_dim.135.gate_ref, ...), custom_call_target="tpu_custom_call" | custom-call | flops 16106127360 | bytes 33554432 | tf_op jit(solution)/shard_map/experts/pallas_call | solution.py:275
  521.1 29.9 %experts.4 = (bf16[2,2,512,1024]{3,2,1,0:T(8,128)(2,1)}, bf16[2,2,512,1024]{3,2,1,0:T(8,128)(2,1)}, bf16[4,320,512]{2,1,0:T(8,128)(2,1)}, f32[4,4,1,512]{3,2,1,0:T(1,128)}) custom-call(s32[1]{0:T(128)} %bitcast.21.flip_ref, s32[4,4,1,512]{3,2,1,0:T(1,128)} %broadcast_in_dim.127.place_ref, f32[4,4,1,512]{3,2,1,0:T(1,128)} %copy.218.gate_ref, ...), custom_call_target="tpu_custom_call" | custom-call | flops 16106127360 | bytes 33554432 | tf_op jit(solution)/shard_map/experts/pallas_call | solution.py:275
  551.0 15.2 %outputs.4 = (bf16[2,2,512,1024]{3,2,1,0:T(8,128)(2,1)}, bf16[2,2,512,1024]{3,2,1,0:T(8,128)(2,1)}) custom-call(s32[1]{0:T(128)} %bitcast.21.flip_ref, s32[4,512,4]{2,1,0:T(8,128)} %get-tuple-element.83.target_ref, bf16[4,512,2048]{2,1,0:T(8,128)(2,1)} %down_ref.15, bf16[4,320,512]{2,1,0:T(8,128)(2,1)} %get-tuple-element.30.hidden_ref), custom_call_target="tpu_custom_call" | custom-call | flops 5368709120 | bytes 16777216 | tf_op jit(solution)/shard_map/outputs/pallas_call | solution.py:320
  566.2 12.6 %grad_rows.6.dh_ref = bf16[4,320,512]{2,1,0:T(8,128)(2,1)} custom-call(s32[1]{0:T(128)} %bitcast.21.flip_ref, s32[4,4,1,512]{3,2,1,0:T(1,128)} %broadcast_in_dim.132.place_ref, bf16[4,512,2048]{2,1,0:T(8,128)(2,1)} %down_ref.15, bf16[512,1024]{1,0:T(8,128)(2,1)} %copy-done.128, bf16[512,1024]{1,0:T(8,128)(2,1)} %copy-done.137, ...), custom_call_target="tpu_custom_call" | custom-call | flops 5368709120 | bytes 18087936 | tf_op jit(solution)/shard_map/grad_rows/pallas_call | solution.py:247
  580.0 30.0 %experts.5 = (bf16[2,2,512,1024]{3,2,1,0:T(8,128)(2,1)}, bf16[2,2,512,1024]{3,2,1,0:T(8,128)(2,1)}, bf16[4,320,512]{2,1,0:T(8,128)(2,1)}, f32[4,4,1,512]{3,2,1,0:T(1,128)}) custom-call(s32[1]{0:T(128)} %bitcast.21.flip_ref, s32[4,4,1,512]{3,2,1,0:T(1,128)} %broadcast_in_dim.130.place_ref, f32[4,4,1,512]{3,2,1,0:T(1,128)} %copy.219.gate_ref, ...), custom_call_target="tpu_custom_call" | custom-call | flops 16106127360 | bytes 33554432 | tf_op jit(solution)/shard_map/experts/pallas_call | solution.py:275
  610.1 15.2 %outputs.5 = (bf16[2,2,512,1024]{3,2,1,0:T(8,128)(2,1)}, bf16[2,2,512,1024]{3,2,1,0:T(8,128)(2,1)}) custom-call(s32[1]{0:T(128)} %bitcast.21.flip_ref, s32[4,512,4]{2,1,0:T(8,128)} %get-tuple-element.82.target_ref, bf16[4,512,2048]{2,1,0:T(8,128)(2,1)} %down_ref.15, bf16[4,320,512]{2,1,0:T(8,128)(2,1)} %get-tuple-element.33.hidden_ref), custom_call_target="tpu_custom_call" | custom-call | flops 5368709120 | bytes 16777216 | tf_op jit(solution)/shard_map/outputs/pallas_call | solution.py:320
  629.4 29.8 %experts.6 = (bf16[2,2,512,1024]{3,2,1,0:T(8,128)(2,1)}, bf16[2,2,512,1024]{3,2,1,0:T(8,128)(2,1)}, bf16[4,320,512]{2,1,0:T(8,128)(2,1)}, f32[4,4,1,512]{3,2,1,0:T(1,128)}) custom-call(s32[1]{0:T(128)} %bitcast.21.flip_ref, s32[4,4,1,512]{3,2,1,0:T(1,128)} %broadcast_in_dim.132.place_ref, f32[4,4,1,512]{3,2,1,0:T(1,128)} %copy.220.gate_ref, ...), custom_call_target="tpu_custom_call" | custom-call | flops 16106127360 | bytes 33554432 | tf_op jit(solution)/shard_map/experts/pallas_call | solution.py:275
  659.4 15.3 %outputs.6 = (bf16[2,2,512,1024]{3,2,1,0:T(8,128)(2,1)}, bf16[2,2,512,1024]{3,2,1,0:T(8,128)(2,1)}) custom-call(s32[1]{0:T(128)} %bitcast.21.flip_ref, s32[4,512,4]{2,1,0:T(8,128)} %get-tuple-element.81.target_ref, bf16[4,512,2048]{2,1,0:T(8,128)(2,1)} %down_ref.15, bf16[4,320,512]{2,1,0:T(8,128)(2,1)} %get-tuple-element.36.hidden_ref), custom_call_target="tpu_custom_call" | custom-call | flops 5368709120 | bytes 16777216 | tf_op jit(solution)/shard_map/outputs/pallas_call | solution.py:320
  681.5 24.8 %collective-permute-done.83 = bf16[512,1024]{1,0:T(8,128)(2,1)S(1)} collective-permute-done((bf16[512,1024]{1,0:T(8,128)(2,1)S(1)}, bf16[512,1024]{1,0:T(8,128)(2,1)S(1)}, u32[]{:S(2)}, u32[]{:S(2)}) %collective-permute-start.83) | collective-permute-done | bytes 1048608 | tf_op jit(solution)/shard_map/ppermute | solution.py:358
  712.6 15.4 %outputs.7 = (bf16[2,2,512,1024]{3,2,1,0:T(8,128)(2,1)}, bf16[2,2,512,1024]{3,2,1,0:T(8,128)(2,1)}) custom-call(s32[1]{0:T(128)} %bitcast.21.flip_ref, s32[4,512,4]{2,1,0:T(8,128)} %get-tuple-element.80.target_ref, bf16[4,512,2048]{2,1,0:T(8,128)(2,1)} %down_ref.15, bf16[4,320,512]{2,1,0:T(8,128)(2,1)} %get-tuple-element.39.hidden_ref), custom_call_target="tpu_custom_call" | custom-call | flops 5368709120 | bytes 16777216 | tf_op jit(solution)/shard_map/outputs/pallas_call | solution.py:320
  744.9 15.6 %collective-permute-done.87 = bf16[512,1024]{1,0:T(8,128)(2,1)S(1)} collective-permute-done((bf16[512,1024]{1,0:T(8,128)(2,1)S(1)}, bf16[512,1024]{1,0:T(8,128)(2,1)S(1)}, u32[]{:S(2)}, u32[]{:S(2)}) %collective-permute-start.87) | collective-permute-done | bytes 1048608 | tf_op jit(solution)/shard_map/ppermute | solution.py:358
  767.5 15.5 %collective-permute-done.40 = bf16[512,1024]{1,0:T(8,128)(2,1)S(1)} collective-permute-done((bf16[512,1024]{1,0:T(8,128)(2,1)S(1)}, bf16[512,1024]{1,0:T(8,128)(2,1)S(1)}, u32[]{:S(2)}, u32[]{:S(2)}) %collective-permute-start.40) | collective-permute-done | bytes 1048608 | tf_op jit(solution)/shard_map/ppermute | solution.py:358
  787.0 16.9 %collective-permute-done.91 = bf16[512,1024]{1,0:T(8,128)(2,1)S(1)} collective-permute-done((bf16[512,1024]{1,0:T(8,128)(2,1)S(1)}, bf16[512,1024]{1,0:T(8,128)(2,1)S(1)}, u32[]{:S(2)}, u32[]{:S(2)}) %collective-permute-start.91) | collective-permute-done | bytes 1048608 | tf_op jit(solution)/shard_map/ppermute | solution.py:358
  816.4 16.9 %collective-permute-done.78 = bf16[512,1024]{1,0:T(8,128)(2,1)S(1)} collective-permute-done((bf16[512,1024]{1,0:T(8,128)(2,1)S(1)}, bf16[512,1024]{1,0:T(8,128)(2,1)S(1)}, u32[]{:S(2)}, u32[]{:S(2)}) %collective-permute-start.78) | collective-permute-done | bytes 1048608 | tf_op jit(solution)/shard_map/ppermute | solution.py:354
  836.9 18.9 %collective-permute-done.22 = bf16[512,1024]{1,0:T(8,128)(2,1)S(1)} collective-permute-done((bf16[512,1024]{1,0:T(8,128)(2,1)}, bf16[512,1024]{1,0:T(8,128)(2,1)S(1)}, u32[]{:S(2)}, u32[]{:S(2)}) %collective-permute-start.22) | collective-permute-done | bytes 1048608 | tf_op jit(solution)/shard_map/ppermute | solution.py:354
  865.6 12.6 %collective-permute-done.89 = bf16[512,1024]{1,0:T(8,128)(2,1)S(1)} collective-permute-done((bf16[512,1024]{1,0:T(8,128)(2,1)S(1)}, bf16[512,1024]{1,0:T(8,128)(2,1)S(1)}, u32[]{:S(2)}, u32[]{:S(2)}) %collective-permute-start.89) | collective-permute-done | bytes 1048608 | tf_op jit(solution)/shard_map/ppermute | solution.py:354
  878.3 22.5 %collective-permute-done.98 = bf16[512,1024]{1,0:T(8,128)(2,1)S(1)} collective-permute-done((bf16[512,1024]{1,0:T(8,128)(2,1)S(1)}, bf16[512,1024]{1,0:T(8,128)(2,1)S(1)}, u32[]{:S(2)}, u32[]{:S(2)}) %collective-permute-start.98) | collective-permute-done | bytes 1048608 | tf_op jit(solution)/shard_map/ppermute | solution.py:354
  917.7 5.8 collective-permute-done.42
  924.0 22.0 %collective-permute-done.79 = bf16[512,1024]{1,0:T(8,128)(2,1)} collective-permute-done((bf16[512,1024]{1,0:T(8,128)(2,1)}, bf16[512,1024]{1,0:T(8,128)(2,1)}, u32[]{:S(2)}, u32[]{:S(2)}) %collective-permute-start.79) | collective-permute-done | bytes 1048608 | tf_op jit(solution)/shard_map/ppermute | solution.py:354
  946.0 5.9 add_convert_fusion.20
  952.0 16.4 %collective-permute-done.93 = bf16[512,1024]{1,0:T(8,128)(2,1)} collective-permute-done((bf16[512,1024]{1,0:T(8,128)(2,1)}, bf16[512,1024]{1,0:T(8,128)(2,1)}, u32[]{:S(2)}, u32[]{:S(2)}) %collective-permute-start.93) | collective-permute-done | bytes 1048608 | tf_op jit(solution)/shard_map/ppermute | solution.py:354
  968.5 22.4 %collective-permute-done.99 = bf16[512,1024]{1,0:T(8,128)(2,1)} collective-permute-done((bf16[512,1024]{1,0:T(8,128)(2,1)}, bf16[512,1024]{1,0:T(8,128)(2,1)}, u32[]{:S(2)}, u32[]{:S(2)}) %collective-permute-start.99) | collective-permute-done | bytes 1048608 | tf_op jit(solution)/shard_map/ppermute | solution.py:354
  997.2 14.7 %all-to-all-done.2 = f32[16,4,512]{2,1,0:T(4,128)S(1)} async-done(((f32[16,4,512]{2,1,0:T(4,128)}), f32[16,4,512]{2,1,0:T(4,128)S(1)}, u32[]{:S(2)}, u32[]{:S(2)}) %all-to-all-start.2) | async-done | bytes 131104 | tf_op jit(solution)/shard_map/all_to_all | solution.py:646
  1014.6 22.9 %collective-permute-done.102 = f32[64,512]{1,0:T(8,128)S(1)} collective-permute-done((f32[64,512]{1,0:T(8,128)S(1)}, f32[64,512]{1,0:T(8,128)S(1)}, u32[]{:S(2)}, u32[]{:S(2)}) %collective-permute-start.102) | collective-permute-done | bytes 131104 | tf_op jit(solution)/shard_map/ppermute | solution.py:358
  1037.6 5.0 fusion.34
  1059.7 5.8 multiply_reduce_fusion
  1086.2 7.0 fusion.161
  1099.3 4.7 fusion.162
  1124.7 5.0 add_convert_fusion.13
  1135.2 87.4 %all-reduce.7.cloned.1.call-done = (bf16[3,8,2048,16]{2,3,1,0:T(8,128)(2,1)}, bf16[3,8,16,1024]{3,2,1,0:T(8,128)(2,1)}, bf16[8,1024,16]{1,2,0:T(8,128)(2,1)}, bf16[8,16,1024]{2,1,0:T(8,128)(2,1)}) async-done(((bf16[3,8,2048,16]{2,3,1,0:T(8,128)(2,1)}, bf16[3,8,16,1024]{3,2,1,0:T(8,128)(2,1)}, bf16[8,1024,16]{1,2,0:T(8,128)(2,1)}, bf16[8,16,1024]{2,1,0:T(8,128)(2,1)}), (bf16[3,8,2048,16]{2,3,1,0:T(8,128)(2,1)}, ...) | async-done | bytes 2883600 | tf_op jit(solution)/shard_map/psum | solution.py:787
  (662 shorter events, 306.7 us)
Async XLA Ops:
  59.4 55.0 %collective-permute-start = (bf16[512,2048]{1,0:T(8,128)(2,1)}, bf16[512,2048]{1,0:T(8,128)(2,1)}, u32[]{:S(2)}, u32[]{:S(2)}) collective-permute-start(bf16[512,2048]{1,0:T(8,128)(2,1)} %convolution_convert_fusion), channel_id=1, source_target_pairs={{0,1},{1,0},{2,3},{3,2},{4,5},{5,4},{6,7},{7,6},{8,9},{9,8},{10,11... | collective-permute-start | bytes 6291464 | tf_op jit(solution)/shard_map/ppermute | solution.py:358
  62.4 49.5 %collective-permute-start.2 = (bf16[512,1024]{1,0:T(8,128)(2,1)}, bf16[512,1024]{1,0:T(8,128)(2,1)}, u32[]{:S(2)}, u32[]{:S(2)}) collective-permute-start(bf16[512,1024]{1,0:T(8,128)(2,1)} %refs_0_.1), channel_id=1, source_target_pairs={{0,8},{2,10},{4,12},{6,14},{8,16},{10,18},{12,20},{14,22},{16,24},... | collective-permute-start | bytes 3145736 | tf_op jit(solution)/shard_map/ppermute | solution.py:354
  64.3 47.6 %collective-permute-start.1 = (bf16[512,128]{0,1:T(8,128)(2,1)S(1)}, bf16[512,128]{0,1:T(8,128)(2,1)S(1)}, u32[]{:S(2)}, u32[]{:S(2)}) collective-permute-start(bf16[512,128]{0,1:T(8,128)(2,1)S(1)} %convolution_convert_fusion.15), channel_id=1, source_target_pairs={{0,1},{1,0},{2,3},{3,2},{4,5},{5,4},{6,7},{7,6},{8,9},{9,8},{10,11... | collective-permute-start | bytes 393224 | tf_op jit(solution)/shard_map/ppermute | solution.py:358
  64.8 68.7 %collective-permute-start.3 = (bf16[512,1024]{1,0:T(8,128)(2,1)}, bf16[512,1024]{1,0:T(8,128)(2,1)}, u32[]{:S(2)}, u32[]{:S(2)}) collective-permute-start(bf16[512,1024]{1,0:T(8,128)(2,1)} %refs_0_.1), channel_id=1, source_target_pairs={{0,1},{1,0},{2,3},{3,2},{4,5},{5,4},{6,7},{7,6},{8,9},{9,8},{10,11... | collective-permute-start | bytes 3145736 | tf_op jit(solution)/shard_map/ppermute | solution.py:358
  66.4 67.2 %collective-permute-start.65 = (bf16[512,1024]{1,0:T(8,128)(2,1)}, bf16[512,1024]{1,0:T(8,128)(2,1)}, u32[]{:S(2)}, u32[]{:S(2)}) collective-permute-start(bf16[512,1024]{1,0:T(8,128)(2,1)} %refs_0_.1), channel_id=1, source_target_pairs={{0,4},{2,6},{4,0},{6,2},{8,12},{10,14},{12,8},{14,10},{16,20},{18,... | collective-permute-start | bytes 3145736 | tf_op jit(solution)/shard_map/ppermute | solution.py:350
  114.4 48.5 %collective-permute-start.7 = (bf16[512,1024]{1,0:T(8,128)(2,1)}, bf16[512,1024]{1,0:T(8,128)(2,1)S(1)}, u32[]{:S(2)}, u32[]{:S(2)}) collective-permute-start(bf16[512,1024]{1,0:T(8,128)(2,1)} %collective-permute-done.2.refs_0_), channel_id=1, source_target_pairs={{0,4},{2,6},{4,0},{6,2},{8,12},{10,14},{12,8},{14,10},{16,20},{18,... | collective-permute-start | bytes 3145736 | tf_op jit(solution)/shard_map/ppermute | solution.py:350
  163.0 50.2 %collective-permute-start.12 = (bf16[512,1024]{1,0:T(8,128)(2,1)S(1)}, bf16[512,1024]{1,0:T(8,128)(2,1)S(1)}, u32[]{:S(2)}, u32[]{:S(2)}) collective-permute-start(bf16[512,1024]{1,0:T(8,128)(2,1)S(1)} %get-tuple-element.94.refs_1_), channel_id=1, source_target_pairs={{0,8},{2,10},{4,12},{6,14},{8,16},{10,18},{12,20},{14,22},{16,24},... | collective-permute-start | bytes 3145736 | tf_op jit(solution)/shard_map/ppermute | solution.py:354
  165.6 70.0 %collective-permute-start.43 = (bf16[512,1024]{1,0:T(8,128)(2,1)}, bf16[512,1024]{1,0:T(8,128)(2,1)S(1)}, u32[]{:S(2)}, u32[]{:S(2)}) collective-permute-start(bf16[512,1024]{1,0:T(8,128)(2,1)} %collective-permute-done.23.refs_0_), channel_id=1, source_target_pairs={{0,8},{2,10},{4,12},{6,14},{8,16},{10,18},{12,20},{14,22},{16,24},... | collective-permute-start | bytes 3145736 | tf_op jit(solution)/shard_map/ppermute | solution.py:354
  165.9 91.8 %collective-permute-start.24 = (bf16[512,1024]{1,0:T(8,128)(2,1)S(1)}, bf16[512,1024]{1,0:T(8,128)(2,1)S(1)}, u32[]{:S(2)}, u32[]{:S(2)}) collective-permute-start(bf16[512,1024]{1,0:T(8,128)(2,1)S(1)} %collective-permute-done.4.refs_1_), channel_id=1, source_target_pairs={{0,8},{2,10},{4,12},{6,14},{8,16},{10,18},{12,20},{14,22},{16,24},... | collective-permute-start | bytes 3145736 | tf_op jit(solution)/shard_map/ppermute | solution.py:354
  167.9 89.8 %collective-permute-start.27 = (bf16[512,1024]{1,0:T(8,128)(2,1)}, bf16[512,1024]{1,0:T(8,128)(2,1)S(1)}, u32[]{:S(2)}, u32[]{:S(2)}) collective-permute-start(bf16[512,1024]{1,0:T(8,128)(2,1)} %collective-permute-done.23.refs_0_), channel_id=1, source_target_pairs={{0,4},{2,6},{4,0},{6,2},{8,12},{10,14},{12,8},{14,10},{16,20},{18,... | collective-permute-start | bytes 3145736 | tf_op jit(solution)/shard_map/ppermute | solution.py:350
  190.7 68.5 %collective-permute-start.25 = (bf16[512,1024]{1,0:T(8,128)(2,1)}, bf16[512,1024]{1,0:T(8,128)(2,1)}, u32[]{:S(2)}, u32[]{:S(2)}) collective-permute-start(bf16[512,1024]{1,0:T(8,128)(2,1)} %collective-permute-done.23.refs_0_), channel_id=1, source_target_pairs={{0,2},{2,0},{4,6},{6,4},{8,10},{10,8},{12,14},{14,12},{16,18},{18,... | collective-permute-start | bytes 3145736 | tf_op jit(solution)/shard_map/ppermute | solution.py:350
  285.0 47.4 %collective-permute-start.44 = (bf16[512,1024]{1,0:T(8,128)(2,1)S(1)}, bf16[512,1024]{1,0:T(8,128)(2,1)S(1)}, u32[]{:S(2)}, u32[]{:S(2)}) collective-permute-start(bf16[512,1024]{1,0:T(8,128)(2,1)S(1)} %collective-permute-done.24.refs_1_), channel_id=1, source_target_pairs={{0,8},{2,10},{4,12},{6,14},{8,16},{10,18},{12,20},{14,22},{16,24},... | collective-permute-start | bytes 3145736 | tf_op jit(solution)/shard_map/ppermute | solution.py:354
  286.0 47.9 %collective-permute-start.45 = (bf16[512,1024]{1,0:T(8,128)(2,1)S(1)}, bf16[512,1024]{1,0:T(8,128)(2,1)S(1)}, u32[]{:S(2)}, u32[]{:S(2)}) collective-permute-start(bf16[512,1024]{1,0:T(8,128)(2,1)S(1)} %collective-permute-done.43.refs_0_), channel_id=1, source_target_pairs={{0,2},{2,0},{4,6},{6,4},{8,10},{10,8},{12,14},{14,12},{16,18},{18,... | collective-permute-start | bytes 3145736 | tf_op jit(solution)/shard_map/ppermute | solution.py:350
  334.5 82.4 %collective-permute-start.72 = (bf16[512,1024]{1,0:T(8,128)(2,1)}, bf16[512,1024]{1,0:T(8,128)(2,1)}, u32[]{:S(2)}, u32[]{:S(2)}) collective-permute-start(bf16[512,1024]{1,0:T(8,128)(2,1)} %collective-permute-done.71.refs_4_), channel_id=1, source_target_pairs={{0,1},{1,0},{2,3},{3,2},{4,5},{5,4},{6,7},{7,6},{8,9},{9,8},{10,11... | collective-permute-start | bytes 3145736 | tf_op jit(solution)/shard_map/ppermute | solution.py:358
  336.0 80.9 %collective-permute-start.73 = (bf16[512,1024]{1,0:T(8,128)(2,1)}, bf16[512,1024]{1,0:T(8,128)(2,1)}, u32[]{:S(2)}, u32[]{:S(2)}) collective-permute-start(bf16[512,1024]{1,0:T(8,128)(2,1)} %collective-permute-done.71.refs_4_), channel_id=1, source_target_pairs={{0,2},{2,0},{4,6},{6,4},{8,10},{10,8},{12,14},{14,12},{16,18},{18,... | collective-permute-start | bytes 3145736 | tf_op jit(solution)/shard_map/ppermute | solution.py:350
  356.2 59.2 %collective-permute-start.10 = (bf16[512,1024]{1,0:T(8,128)(2,1)}, bf16[512,1024]{1,0:T(8,128)(2,1)}, u32[]{:S(2)}, u32[]{:S(2)}) collective-permute-start(bf16[512,1024]{1,0:T(8,128)(2,1)} %collective-permute-done.8.refs_5_), channel_id=1, source_target_pairs={{0,2},{2,0},{4,6},{6,4},{8,10},{10,8},{12,14},{14,12},{16,18},{18,... | collective-permute-start | bytes 3145736 | tf_op jit(solution)/shard_map/ppermute | solution.py:350
  356.2 61.6 %collective-permute-start.51 = (bf16[512,1024]{1,0:T(8,128)(2,1)}, bf16[512,1024]{1,0:T(8,128)(2,1)}, u32[]{:S(2)}, u32[]{:S(2)}) collective-permute-start(bf16[512,1024]{1,0:T(8,128)(2,1)} %collective-permute-done.31.refs_0_), channel_id=1, source_target_pairs={{0,8},{2,10},{4,12},{6,14},{8,16},{10,18},{12,20},{14,22},{16,24},... | collective-permute-start | bytes 3145736 | tf_op jit(solution)/shard_map/ppermute | solution.py:354
  356.3 61.6 %collective-permute-start.52 = (bf16[512,1024]{1,0:T(8,128)(2,1)}, bf16[512,1024]{1,0:T(8,128)(2,1)}, u32[]{:S(2)}, u32[]{:S(2)}) collective-permute-start(bf16[512,1024]{1,0:T(8,128)(2,1)} %collective-permute-done.32.refs_1_), channel_id=1, source_target_pairs={{0,8},{2,10},{4,12},{6,14},{8,16},{10,18},{12,20},{14,22},{16,24},... | collective-permute-start | bytes 3145736 | tf_op jit(solution)/shard_map/ppermute | solution.py:354
  358.8 50.7 %all-to-all-start = ((s32[16,4,512]{2,1,0:T(4,128)}), s32[16,4,512]{2,1,0:T(4,128)S(1)}, u32[]{:S(2)}, u32[]{:S(2)}) async-start(s32[16,4,512]{2,1,0:T(4,128)} %reshape.634), calls=%async_computation | async-start | bytes 262144 | tf_op jit(solution)/shard_map/all_to_all | solution.py:487
  519.5 105.8 %collective-permute-start.94 = (bf16[2,2,512,1024]{3,2,1,0:T(8,128)(2,1)}, bf16[2,2,512,1024]{3,2,1,0:T(8,128)(2,1)}, u32[]{:S(2)}, u32[]{:S(2)}) collective-permute-start(bf16[2,2,512,1024]{3,2,1,0:T(8,128)(2,1)} %get-tuple-element.49), channel_id=1, source_target_pairs={{0,2},{2,0},{4,6},{6,4},{8,10},{10,8},{12,14},{14,12},{16,18},{18,... | collective-permute-start | bytes 12582920 | tf_op jit(solution)/shard_map/ppermute | solution.py:350
  520.1 59.3 %collective-permute-start.37 = (bf16[512,1024]{1,0:T(8,128)(2,1)}, bf16[512,1024]{1,0:T(8,128)(2,1)}, u32[]{:S(2)}, u32[]{:S(2)}) collective-permute-start(bf16[512,1024]{1,0:T(8,128)(2,1)} %collective-permute-done.35.refs_4_), channel_id=1, source_target_pairs={{0,2},{2,0},{4,6},{6,4},{8,10},{10,8},{12,14},{14,12},{16,18},{18,... | collective-permute-start | bytes 3145736 | tf_op jit(solution)/shard_map/ppermute | solution.py:350
  520.2 58.7 %collective-permute-start.54 = (bf16[512,1024]{1,0:T(8,128)(2,1)}, bf16[512,1024]{1,0:T(8,128)(2,1)S(1)}, u32[]{:S(2)}, u32[]{:S(2)}) collective-permute-start(bf16[512,1024]{1,0:T(8,128)(2,1)} %collective-permute-done.52.refs_1_), channel_id=1, source_target_pairs={{0,2},{2,0},{4,6},{6,4},{8,10},{10,8},{12,14},{14,12},{16,18},{18,... | collective-permute-start | bytes 3145736 | tf_op jit(solution)/shard_map/ppermute | solution.py:350
  520.6 58.9 %collective-permute-start.56 = (bf16[512,1024]{1,0:T(8,128)(2,1)}, bf16[512,1024]{1,0:T(8,128)(2,1)}, u32[]{:S(2)}, u32[]{:S(2)}) collective-permute-start(bf16[512,1024]{1,0:T(8,128)(2,1)} %collective-permute-done.55.refs_4_), channel_id=1, source_target_pairs={{0,1},{1,0},{2,3},{3,2},{4,5},{5,4},{6,7},{7,6},{8,9},{9,8},{10,11... | collective-permute-start | bytes 3145736 | tf_op jit(solution)/shard_map/ppermute | solution.py:358
  521.1 58.8 %collective-permute-start.38 = (bf16[512,1024]{1,0:T(8,128)(2,1)S(1)}, bf16[512,1024]{1,0:T(8,128)(2,1)}, u32[]{:S(2)}, u32[]{:S(2)}) collective-permute-start(bf16[512,1024]{1,0:T(8,128)(2,1)S(1)} %collective-permute-done.36.refs_5_), channel_id=1, source_target_pairs={{0,2},{2,0},{4,6},{6,4},{8,10},{10,8},{12,14},{14,12},{16,18},{18,... | collective-permute-start | bytes 3145736 | tf_op jit(solution)/shard_map/ppermute | solution.py:350
  578.9 95.9 %collective-permute-start.82 = (bf16[2,2,512,1024]{3,2,1,0:T(8,128)(2,1)}, bf16[2,2,512,1024]{3,2,1,0:T(8,128)(2,1)S(1)}, u32[]{:S(2)}, u32[]{:S(2)}) collective-permute-start(bf16[2,2,512,1024]{3,2,1,0:T(8,128)(2,1)} %get-tuple-element.43), channel_id=1, source_target_pairs={{0,2},{2,0},{4,6},{6,4},{8,10},{10,8},{12,14},{14,12},{16,18},{18,... | collective-permute-start | bytes 12582920 | tf_op jit(solution)/shard_map/ppermute | solution.py:350
  579.4 101.6 %collective-permute-start.19 = (bf16[2,2,512,1024]{3,2,1,0:T(8,128)(2,1)}, bf16[2,2,512,1024]{3,2,1,0:T(8,128)(2,1)}, u32[]{:S(2)}, u32[]{:S(2)}) collective-permute-start(bf16[2,2,512,1024]{3,2,1,0:T(8,128)(2,1)} %get-tuple-element.32), channel_id=1, source_target_pairs={{0,2},{2,0},{4,6},{6,4},{8,10},{10,8},{12,14},{14,12},{16,18},{18,... | collective-permute-start | bytes 12582920 | tf_op jit(solution)/shard_map/ppermute | solution.py:350
  579.5 48.2 %collective-permute-start.57 = (bf16[512,1024]{1,0:T(8,128)(2,1)}, bf16[512,1024]{1,0:T(8,128)(2,1)}, u32[]{:S(2)}, u32[]{:S(2)}) collective-permute-start(bf16[512,1024]{1,0:T(8,128)(2,1)} %collective-permute-done.55.refs_4_), channel_id=1, source_target_pairs={{0,2},{2,0},{4,6},{6,4},{8,10},{10,8},{12,14},{14,12},{16,18},{18,... | collective-permute-start | bytes 3145736 | tf_op jit(solution)/shard_map/ppermute | solution.py:350
  579.9 47.9 %collective-permute-start.58 = (bf16[512,1024]{1,0:T(8,128)(2,1)}, bf16[512,1024]{1,0:T(8,128)(2,1)}, u32[]{:S(2)}, u32[]{:S(2)}) collective-permute-start(bf16[512,1024]{1,0:T(8,128)(2,1)} %collective-permute-done.56.refs_5_), channel_id=1, source_target_pairs={{0,2},{2,0},{4,6},{6,4},{8,10},{10,8},{12,14},{14,12},{16,18},{18,... | collective-permute-start | bytes 3145736 | tf_op jit(solution)/shard_map/ppermute | solution.py:350
  625.3 86.8 %collective-permute-start.86 = (bf16[2,2,512,1024]{3,2,1,0:T(8,128)(2,1)}, bf16[2,2,512,1024]{3,2,1,0:T(8,128)(2,1)}, u32[]{:S(2)}, u32[]{:S(2)}) collective-permute-start(bf16[2,2,512,1024]{3,2,1,0:T(8,128)(2,1)} %get-tuple-element.45), channel_id=1, source_target_pairs={{0,2},{2,0},{4,6},{6,4},{8,10},{10,8},{12,14},{14,12},{16,18},{18,... | collective-permute-start | bytes 12582920 | tf_op jit(solution)/shard_map/ppermute | solution.py:350
  627.7 108.8 %collective-permute-start.39 = (bf16[2,2,512,1024]{3,2,1,0:T(8,128)(2,1)}, bf16[2,2,512,1024]{3,2,1,0:T(8,128)(2,1)}, u32[]{:S(2)}, u32[]{:S(2)}) collective-permute-start(bf16[2,2,512,1024]{3,2,1,0:T(8,128)(2,1)} %get-tuple-element.35), channel_id=1, source_target_pairs={{0,2},{2,0},{4,6},{6,4},{8,10},{10,8},{12,14},{14,12},{16,18},{18,... | collective-permute-start | bytes 12582920 | tf_op jit(solution)/shard_map/ppermute | solution.py:350
  659.2 83.9 %collective-permute-start.90 = (bf16[2,2,512,1024]{3,2,1,0:T(8,128)(2,1)}, bf16[2,2,512,1024]{3,2,1,0:T(8,128)(2,1)}, u32[]{:S(2)}, u32[]{:S(2)}) collective-permute-start(bf16[2,2,512,1024]{3,2,1,0:T(8,128)(2,1)} %get-tuple-element.47), channel_id=1, source_target_pairs={{0,2},{2,0},{4,6},{6,4},{8,10},{10,8},{12,14},{14,12},{16,18},{18,... | collective-permute-start | bytes 12582920 | tf_op jit(solution)/shard_map/ppermute | solution.py:350
  674.7 89.7 %collective-permute-start.59 = (bf16[2,2,512,1024]{3,2,1,0:T(8,128)(2,1)}, bf16[2,2,512,1024]{3,2,1,0:T(8,128)(2,1)}, u32[]{:S(2)}, u32[]{:S(2)}) collective-permute-start(bf16[2,2,512,1024]{3,2,1,0:T(8,128)(2,1)} %get-tuple-element.38), channel_id=1, source_target_pairs={{0,2},{2,0},{4,6},{6,4},{8,10},{10,8},{12,14},{14,12},{16,18},{18,... | collective-permute-start | bytes 12582920 | tf_op jit(solution)/shard_map/ppermute | solution.py:350
  743.1 162.3 %collective-permute-start.75 = (bf16[2,2,512,1024]{3,2,1,0:T(8,128)(2,1)}, bf16[2,2,512,1024]{3,2,1,0:T(8,128)(2,1)}, u32[]{:S(2)}, u32[]{:S(2)}) collective-permute-start(bf16[2,2,512,1024]{3,2,1,0:T(8,128)(2,1)} %get-tuple-element.41), channel_id=1, source_target_pairs={{0,2},{2,0},{4,6},{6,4},{8,10},{10,8},{12,14},{14,12},{16,18},{18,... | collective-permute-start | bytes 12582920 | tf_op jit(solution)/shard_map/ppermute | solution.py:350
  834.6 66.2 %collective-permute-start.98 = (bf16[512,1024]{1,0:T(8,128)(2,1)S(1)}, bf16[512,1024]{1,0:T(8,128)(2,1)S(1)}, u32[]{:S(2)}, u32[]{:S(2)}) collective-permute-start(bf16[512,1024]{1,0:T(8,128)(2,1)S(1)} %get-tuple-element.67), channel_id=1, source_target_pairs={{0,8},{2,10},{4,12},{6,14},{8,16},{10,18},{12,20},{14,22},{16,24},... | collective-permute-start | bytes 3145736 | tf_op jit(solution)/shard_map/ppermute | solution.py:354
  855.8 49.8 %collective-permute-start.61 = (bf16[512,1024]{1,0:T(8,128)(2,1)S(1)}, bf16[512,1024]{1,0:T(8,128)(2,1)S(1)}, u32[]{:S(2)}, u32[]{:S(2)}) collective-permute-start(bf16[512,1024]{1,0:T(8,128)(2,1)S(1)} %fusion.36), channel_id=1, source_target_pairs={{0,4},{2,6},{4,0},{6,2},{8,12},{10,14},{12,8},{14,10},{16,20},{18,... | collective-permute-start | bytes 3145736 | tf_op jit(solution)/shard_map/ppermute | solution.py:350
  864.8 87.2 %collective-permute-start.96 = (bf16[512,1024]{1,0:T(8,128)(2,1)}, bf16[512,1024]{1,0:T(8,128)(2,1)S(1)}, u32[]{:S(2)}, u32[]{:S(2)}) collective-permute-start(bf16[512,1024]{1,0:T(8,128)(2,1)} %fusion.26), channel_id=1, source_target_pairs={{0,4},{2,6},{4,0},{6,2},{8,12},{10,14},{12,8},{14,10},{16,20},{18,... | collective-permute-start | bytes 3145736 | tf_op jit(solution)/shard_map/ppermute | solution.py:350
  905.5 63.0 %collective-permute-start.93 = (bf16[512,1024]{1,0:T(8,128)(2,1)}, bf16[512,1024]{1,0:T(8,128)(2,1)}, u32[]{:S(2)}, u32[]{:S(2)}) collective-permute-start(bf16[512,1024]{1,0:T(8,128)(2,1)} %get-tuple-element.64), channel_id=1, source_target_pairs={{0,8},{2,10},{4,12},{6,14},{8,16},{10,18},{12,20},{14,22},{16,24},... | collective-permute-start | bytes 3145736 | tf_op jit(solution)/shard_map/ppermute | solution.py:354
  905.6 85.3 %collective-permute-start.99 = (bf16[512,1024]{1,0:T(8,128)(2,1)}, bf16[512,1024]{1,0:T(8,128)(2,1)}, u32[]{:S(2)}, u32[]{:S(2)}) collective-permute-start(bf16[512,1024]{1,0:T(8,128)(2,1)} %get-tuple-element.65), channel_id=1, source_target_pairs={{0,8},{2,10},{4,12},{6,14},{8,16},{10,18},{12,20},{14,22},{16,24},... | collective-permute-start | bytes 3145736 | tf_op jit(solution)/shard_map/ppermute | solution.py:354
  910.4 101.6 %all-to-all-start.2 = ((f32[16,4,512]{2,1,0:T(4,128)}), f32[16,4,512]{2,1,0:T(4,128)S(1)}, u32[]{:S(2)}, u32[]{:S(2)}) async-start(f32[16,4,512]{2,1,0:T(4,128)} %gather_fusion.2), calls=%async_computation.2 | async-start | bytes 262144 | tf_op jit(solution)/shard_map/all_to_all | solution.py:646
  914.8 307.9 %all-reduce.7.cloned.1.call-start = ((), (), s32[]{:S(2)}) async-start(), calls=%async_computation.3 | async-start | bytes 5767168 | tf_op jit(solution)/shard_map/psum | solution.py:787
  923.5 114.0 %collective-permute-start.76 = (bf16[512,1024]{1,0:T(8,128)(2,1)}, bf16[512,1024]{1,0:T(8,128)(2,1)}, u32[]{:S(2)}, u32[]{:S(2)}) collective-permute-start(bf16[512,1024]{1,0:T(8,128)(2,1)} %fusion.60), channel_id=1, source_target_pairs={{0,1},{1,0},{2,3},{3,2},{4,5},{5,4},{6,7},{7,6},{8,9},{9,8},{10,11... | collective-permute-start | bytes 3145736 | tf_op jit(solution)/shard_map/ppermute | solution.py:358
  951.8 85.7 %collective-permute-start.80 = (bf16[512,1024]{1,0:T(8,128)(2,1)}, bf16[512,1024]{1,0:T(8,128)(2,1)}, u32[]{:S(2)}, u32[]{:S(2)}) collective-permute-start(bf16[512,1024]{1,0:T(8,128)(2,1)} %get-tuple-element.73), channel_id=1, source_target_pairs={{0,8},{2,10},{4,12},{6,14},{8,16},{10,18},{12,20},{14,22},{16,24},... | collective-permute-start | bytes 3145736 | tf_op jit(solution)/shard_map/ppermute | solution.py:354
  995.1 49.6 %collective-permute-start.100 = (bf16[512,1024]{1,0:T(8,128)(2,1)S(1)}, bf16[512,1024]{1,0:T(8,128)(2,1)}, u32[]{:S(2)}, u32[]{:S(2)}) collective-permute-start(bf16[512,1024]{1,0:T(8,128)(2,1)S(1)} %get-tuple-element.63), channel_id=1, source_target_pairs={{0,1},{1,0},{2,3},{3,2},{4,5},{5,4},{6,7},{7,6},{8,9},{9,8},{10,11... | collective-permute-start | bytes 3145736 | tf_op jit(solution)/shard_map/ppermute | solution.py:358
  995.7 49.0 %collective-permute-start.101 = (bf16[512,1024]{1,0:T(8,128)(2,1)S(1)}, bf16[512,1024]{1,0:T(8,128)(2,1)}, u32[]{:S(2)}, u32[]{:S(2)}) collective-permute-start(bf16[512,1024]{1,0:T(8,128)(2,1)S(1)} %get-tuple-element.62), channel_id=1, source_target_pairs={{0,1},{1,0},{2,3},{3,2},{4,5},{5,4},{6,7},{7,6},{8,9},{9,8},{10,11... | collective-permute-start | bytes 3145736 | tf_op jit(solution)/shard_map/ppermute | solution.py:358
  1037.5 86.2 %collective-permute-start.62 = (bf16[512,1024]{1,0:T(8,128)(2,1)}, bf16[512,1024]{1,0:T(8,128)(2,1)}, u32[]{:S(2)}, u32[]{:S(2)}) collective-permute-start(bf16[512,1024]{1,0:T(8,128)(2,1)} %get-tuple-element.72), channel_id=1, source_target_pairs={{0,8},{2,10},{4,12},{6,14},{8,16},{10,18},{12,20},{14,22},{16,24},... | collective-permute-start | bytes 3145736 | tf_op jit(solution)/shard_map/ppermute | solution.py:354
  1042.6 81.1 %collective-permute-start.77 = (bf16[512,1024]{1,0:T(8,128)(2,1)}, bf16[512,1024]{1,0:T(8,128)(2,1)}, u32[]{:S(2)}, u32[]{:S(2)}) collective-permute-start(bf16[512,1024]{1,0:T(8,128)(2,1)} %get-tuple-element.70), channel_id=1, source_target_pairs={{0,4},{2,6},{4,0},{6,2},{8,12},{10,14},{12,8},{14,10},{16,20},{18,... | collective-permute-start | bytes 3145736 | tf_op jit(solution)/shard_map/ppermute | solution.py:350
  1044.1 79.6 %collective-permute-start.81 = (bf16[512,1024]{1,0:T(8,128)(2,1)}, bf16[512,1024]{1,0:T(8,128)(2,1)}, u32[]{:S(2)}, u32[]{:S(2)}) collective-permute-start(bf16[512,1024]{1,0:T(8,128)(2,1)} %get-tuple-element.71), channel_id=1, source_target_pairs={{0,1},{1,0},{2,3},{3,2},{4,5},{5,4},{6,7},{7,6},{8,9},{9,8},{10,11... | collective-permute-start | bytes 3145736 | tf_op jit(solution)/shard_map/ppermute | solution.py:358
  1109.8 123.0 %collective-permute-start.103 = (bf16[512,2048]{1,0:T(8,128)(2,1)}, bf16[512,2048]{1,0:T(8,128)(2,1)}, u32[]{:S(2)}, u32[]{:S(2)}) collective-permute-start(bf16[512,2048]{1,0:T(8,128)(2,1)} %add_convert_fusion), channel_id=1, source_target_pairs={{0,1},{1,0},{2,3},{3,2},{4,5},{5,4},{6,7},{7,6},{8,9},{9,8},{10,11... | collective-permute-start | bytes 6291464 | tf_op jit(solution)/shard_map/ppermute | solution.py:358
  (224 other events, 5736.4 us)
Sparse Core Ops, SparseCore 0:
  1119.6 103.0 all-reduce.6

commit v2 on v1

v2 whole, which is shorter than its diff:
```python
import functools

import jax
import jax.numpy as jnp
from jax import lax
from jax.experimental import pallas as pl
from jax.experimental.pallas import tpu as pltpu
from jax.sharding import PartitionSpec as P

MODEL_WIDTH = 2048
HEAD_WIDTH = 128
TOP = 8
LEN = 512
ADAPTER_RANK = 16
ADAPTER_CHOICES = 8
QUAD = 4

norm_eps = 1e-05
head_eps = 1e-06
rope_base = 50000.0
half_type = jnp.bfloat16
VMEM_LIMIT = 56 * 1024 * 1024


def rms_scale(values, gain_vec, epsilon):
    return (
        values * lax.rsqrt(jnp.mean(values * values, axis=-1, keepdims=True) + epsilon) * gain_vec
    )


def rotate(values, positions):
    half_dim = values.shape[-1] // 2
    inverse = rope_base ** (-(jnp.arange(half_dim, dtype=jnp.float32) * 2.0 / values.shape[-1]))
    angles = positions.astype(jnp.float32)[:, None, None] * inverse[None, None, :]
    cosine = jnp.cos(angles)
    sine_val = jnp.sin(angles)
    first_half = values[..., :half_dim]
    second_half = values[..., half_dim:]
    return jnp.concatenate(
        [
            first_half * cosine - second_half * sine_val,
            second_half * cosine + first_half * sine_val,
        ],
        axis=-1,
    )


def head_prep(projected, gain_vec, positions):
    shaped = projected.reshape(projected.shape[0], projected.shape[1] // HEAD_WIDTH, HEAD_WIDTH)
    return rotate(rms_scale(shaped, gain_vec, head_eps), positions)


def nt_dot(left, right):
    return lax.dot_general(
        left, right, (((1,), (1,)), ((), ())), preferred_element_type=jnp.float32
    )


def start_blocks(pieces, buffer_ref, sems, flip):
    for b in range(QUAD):
        for r in range(2):
            pltpu.make_async_copy(
                pieces[2 * b + r], buffer_ref.at[b, r ^ flip], sems.at[b, r]
            ).start()


def wait_block(pieces, buffer_ref, sems, b):
    for r in range(2):
        pltpu.make_async_copy(pieces[0], buffer_ref.at[b, r], sems.at[b, r]).wait()


def pick_rows(place_ref, buffer_ref, rows_ref, b, experts, cap, tile):
    toks = buffer_ref.shape[2]
    slot = lax.broadcasted_iota(jnp.int32, (cap, toks), 0)
    picks = jnp.concatenate(
        [jnp.where(slot == place_ref[b, e], 1.0, 0.0) for e in range(experts)], axis=0
    ).astype(half_type)
    half = buffer_ref.shape[3]
    for h in range(2):
        for start in range(0, half, tile):
            rows = jnp.dot(
                picks,
                buffer_ref[b, h, :, start : start + tile],
                preferred_element_type=jnp.float32,
            ).astype(half_type)
            for e in range(experts):
                rows_ref[e, h, b, :, start : start + tile] = rows[e * cap : (e + 1) * cap]


def add_rows(target_ref, rows_ref, out_ref, b, flip, experts, cap, tile):
    target = target_ref[b]
    toks = target.shape[0]
    lane = lax.broadcasted_iota(jnp.int32, (toks, experts * cap), 1)
    hit = lane == target[:, 0:1]
    for e in range(1, experts):
        hit = jnp.logical_or(hit, lane == target[:, e : e + 1])
    spread = jnp.where(hit, 1.0, 0.0).astype(half_type)
    half = rows_ref.shape[4]
    for h in range(2):
        for start in range(0, half, tile):
            rows = jnp.concatenate(
                [rows_ref[e, h, b, :, start : start + tile] for e in range(experts)], axis=0
            )
            out_ref[0, h ^ flip, :, start : start + tile] = jnp.dot(
                spread, rows, preferred_element_type=jnp.float32
            ).astype(half_type)


def grad_rows_kernel(
    experts, cap, flip_ref, block_ids, place_ref, down_ref, all_ref, out_ref, buffer_ref, rows_ref, sems
):
    block_refs = [all_ref.at[block_ids[b], r] for b in range(QUAD) for r in range(2)]
    step = pl.program_id(0)
    half = buffer_ref.shape[3]

    @pl.when(step == 0)
    def _():
        start_blocks(block_refs, buffer_ref, sems, flip_ref[0])

    @pl.when(step < QUAD)
    def _():
        wait_block(block_refs, buffer_ref, sems, step)
        pick_rows(place_ref, buffer_ref, rows_ref, step, experts, cap, 512)

    @pl.when(step >= QUAD)
    def _():
        e = step - QUAD
        total = nt_dot(rows_ref[e, 0].reshape(QUAD * cap, half), down_ref[0, :, :half])
        total += nt_dot(rows_ref[e, 1].reshape(QUAD * cap, half), down_ref[0, :, half:])
        out_ref[0] = total.astype(half_type)


def expert_kernel(
    experts,
    cap,
    flip_ref,
    place_ref,
    gate_ref,
    target_ref,
    wg_ref,
    wu_ref,
    dh_ref,
    own_first_ref,
    own_second_ref,
    core_first_ref,
    core_second_ref,
    across_first_ref,
    across_second_ref,
    far_first_ref,
    far_second_ref,
    send_ref,
    keep_ref,
    hidden_ref,
    dgate_ref,
    buffer_ref,
    rows_ref,
    sems,
):
    block_refs = [
        own_first_ref,
        own_second_ref,
        core_first_ref,
        core_second_ref,
        across_first_ref,
        across_second_ref,
        far_first_ref,
        far_second_ref,
    ]
    step = pl.program_id(0)
    half = buffer_ref.shape[3]
    toks = buffer_ref.shape[2]

    @pl.when(step == 0)
    def _():
        start_blocks(block_refs, buffer_ref, sems, flip_ref[0])

    @pl.when(step < QUAD)
    def _():
        wait_block(block_refs, buffer_ref, sems, step)
        pick_rows(place_ref, buffer_ref, rows_ref, step, experts, cap, 512)

    @pl.when(jnp.logical_and(step >= QUAD, step < QUAD + experts))
    def _():
        e = step - QUAD
        first = rows_ref[e, 0].reshape(QUAD * cap, half)
        second = rows_ref[e, 1].reshape(QUAD * cap, half)
        pre_gate = jnp.dot(first, wg_ref[0, :half], preferred_element_type=jnp.float32)
        pre_gate += jnp.dot(second, wg_ref[0, half:], preferred_element_type=jnp.float32)
        pre_up = jnp.dot(first, wu_ref[0, :half], preferred_element_type=jnp.float32)
        pre_up += jnp.dot(second, wu_ref[0, half:], preferred_element_type=jnp.float32)
        sig = lax.logistic(pre_gate)
        silu = pre_gate * sig
        act = silu * pre_up
        d_raw = dh_ref[0].astype(jnp.float32)
        slot = lax.broadcasted_iota(jnp.int32, (cap, toks), 0)
        gate_parts = []
        for b in range(QUAD):
            hit = slot == place_ref[b, e]
            gate_parts.append(
                jnp.sum(jnp.where(hit, gate_ref[b, e], 0.0), axis=1, keepdims=True)
            )
        gate_col = jnp.concatenate(gate_parts, axis=0)
        hidden_ref[0] = (act * gate_col).astype(half_type)
        d_col = jnp.sum(act * d_raw, axis=1, keepdims=True)
        for b in range(QUAD):
            hit = slot == place_ref[b, e]
            dgate_ref[e, b] = jnp.sum(
                jnp.where(hit, d_col[b * cap : (b + 1) * cap], 0.0), axis=0, keepdims=True
            )
        d_hidden = d_raw * gate_col
        d_up = (d_hidden * silu).astype(half_type)
        d_gate = (d_hidden * pre_up * (sig * (1.0 + pre_gate * (1.0 - sig)))).astype(half_type)
        for h in range(2):
            d_in = nt_dot(d_gate, wg_ref[0, h * half : (h + 1) * half])
            d_in += nt_dot(d_up, wu_ref[0, h * half : (h + 1) * half])
            rows_ref[e, h] = d_in.astype(half_type).reshape(QUAD, cap, half)

    for which, out_ref in ((0, send_ref), (1, keep_ref)):
        first_step = QUAD + experts + 2 * which

        @pl.when(jnp.logical_and(step >= first_step, step < first_step + 2))
        def _():
            b = 2 * (step - first_step) + 1 - which
            add_rows(target_ref, rows_ref, out_ref, b, flip_ref[0], experts, cap, 512)


def output_kernel(experts, cap, flip_ref, target_ref, down_ref, hidden_ref, send_ref, keep_ref, rows_ref):
    step = pl.program_id(0)
    half = rows_ref.shape[4]

    @pl.when(step < experts)
    def _():
        for h in range(2):
            out = jnp.dot(
                hidden_ref[0],
                down_ref[0, :, h * half : (h + 1) * half],
                preferred_element_type=jnp.float32,
            )
            rows_ref[step, h] = out.astype(half_type).reshape(QUAD, cap, half)

    for which, out_ref in ((0, send_ref), (1, keep_ref)):
        first_step = experts + 2 * which

        @pl.when(jnp.logical_and(step >= first_step, step < first_step + 2))
        def _():
            b = 2 * (step - first_step) + 1 - which
            add_rows(target_ref, rows_ref, out_ref, b, flip_ref[0], experts, cap, 512)


def whole(shape):
    return pl.BlockSpec(shape, lambda i, *_: (0,) * len(shape), pipeline_mode=pl.Buffered(1))


def per_step(shape, first, count):
    return pl.BlockSpec(
        (1,) + shape[1:], lambda i, *_: (jnp.clip(i - first, 0, count - 1),) + (0,) * (len(shape) - 1)
    )


def block_scratch(toks, half, experts, cap, with_buffer):
    rows = pltpu.VMEM((experts, 2, QUAD, cap, half), half_type)
    if not with_buffer:
        return [rows]
    return [
        pltpu.VMEM((QUAD, 2, toks, half), half_type),
        rows,
        pltpu.SemaphoreType.DMA((QUAD, 2)),
    ]


def call_grad_rows(flip, block_ids, place, down, blocks, cap):
    experts, hidden_units, width = down.shape
    toks, half = blocks.shape[2:]
    rows = QUAD * cap
    return pl.pallas_call(
        functools.partial(grad_rows_kernel, experts, cap),
        out_shape=jax.ShapeDtypeStruct((experts, rows, hidden_units), half_type),
        grid_spec=pltpu.PrefetchScalarGridSpec(
            num_scalar_prefetch=2,
            grid=(QUAD + experts,),
            in_specs=[
                whole(place.shape),
                per_step(down.shape, QUAD, experts),
                pl.BlockSpec(memory_space=pl.ANY),
            ],
            out_specs=per_step((experts, rows, hidden_units), QUAD, experts),
            scratch_shapes=block_scratch(toks, half, experts, cap, True),
        ),
        compiler_params=pltpu.CompilerParams(
            dimension_semantics=("arbitrary",), vmem_limit_bytes=VMEM_LIMIT
        ),
        cost_estimate=pl.CostEstimate(flops=1, bytes_accessed=1, transcendentals=0),
        name="grad_rows",
    )(flip, block_ids, place, down, blocks)


def call_experts(flip, place, gate, target, gate_w, up_w, d_raw, pieces, cap):
    experts, width, hidden_units = gate_w.shape
    toks, half = pieces[0].shape
    rows = QUAD * cap
    blocks = (2, 2, toks, half)
    return pl.pallas_call(
        functools.partial(expert_kernel, experts, cap),
        out_shape=(
            jax.ShapeDtypeStruct(blocks, half_type),
            jax.ShapeDtypeStruct(blocks, half_type),
            jax.ShapeDtypeStruct((experts, rows, hidden_units), half_type),
            jax.ShapeDtypeStruct((experts, QUAD, 1, toks), jnp.float32),
        ),
        grid_spec=pltpu.PrefetchScalarGridSpec(
            num_scalar_prefetch=1,
            grid=(2 * QUAD + experts,),
            in_specs=[
                whole(place.shape),
                whole(gate.shape),
                whole(target.shape),
                per_step(gate_w.shape, QUAD, experts),
                per_step(up_w.shape, QUAD, experts),
                per_step(d_raw.shape, QUAD, experts),
            ]
            + [pl.BlockSpec(memory_space=pl.ANY)] * len(pieces),
            out_specs=(
                per_step(blocks, QUAD + experts, 2),
                per_step(blocks, QUAD + experts + 2, 2),
                per_step((experts, rows, hidden_units), QUAD, experts),
                whole((experts, QUAD, 1, toks)),
            ),
            scratch_shapes=block_scratch(toks, half, experts, cap, True),
        ),
        compiler_params=pltpu.CompilerParams(
            dimension_semantics=("arbitrary",), vmem_limit_bytes=VMEM_LIMIT
        ),
        cost_estimate=pl.CostEstimate(flops=1, bytes_accessed=1, transcendentals=0),
        name="experts",
    )(flip, place, gate, target, gate_w, up_w, d_raw, *pieces)


def call_output(flip, target, down, hidden, cap, half):
    experts, hidden_units, width = down.shape
    toks = target.shape[1]
    rows = QUAD * cap
    blocks = (2, 2, toks, half)
    return pl.pallas_call(
        functools.partial(output_kernel, experts, cap),
        out_shape=(
            jax.ShapeDtypeStruct(blocks, half_type),
            jax.ShapeDtypeStruct(blocks, half_type),
        ),
        grid_spec=pltpu.PrefetchScalarGridSpec(
            num_scalar_prefetch=1,
            grid=(QUAD + experts,),
            in_specs=[
                whole(target.shape),
                per_step(down.shape, 0, experts),
                per_step(hidden.shape, 0, experts),
            ],
            out_specs=(per_step(blocks, experts, 2), per_step(blocks, experts + 2, 2)),
            scratch_shapes=block_scratch(toks, half, experts, cap, False),
        ),
        compiler_params=pltpu.CompilerParams(
            dimension_semantics=("arbitrary",), vmem_limit_bytes=VMEM_LIMIT
        ),
        cost_estimate=pl.CostEstimate(
            flops=4 * experts * rows * width * (toks + hidden_units),
            bytes_accessed=2 * (down.size + 2 * QUAD * toks * half),
            transcendentals=0,
        ),
        name="outputs",
    )(flip, target, down, hidden)


def swap(values, data_count, bit):
    return lax.ppermute(values, "dp", [(i, i ^ bit) for i in range(data_count)])


def onward(values, data_count):
    return lax.ppermute(values, "dp", [(i, (i + QUAD) % data_count) for i in range(data_count)])


def other_side(values):
    return lax.ppermute(values, "tensor", [(0, 1), (1, 0)])


def fence(*values):
    return lax.optimization_barrier(values)


def plus(*terms):
    total = terms[0].astype(jnp.float32)
    for term in terms[1:]:
        total = total + term.astype(jnp.float32)
    return total.astype(half_type)


def local(
    layer_input,
    cotangent,
    attention_norm_gain,
    expert_norm_gain,
    query_norm_gain,
    key_norm_gain,
    query_weight_matrix,
    key_weight_matrix,
    value_weight_matrix,
    output_weight_matrix,
    adapter_projection_down,
    adapter_projection_up,
    adapter_output_down,
    adapter_output_up,
    router,
    expert_gate_weight,
    expert_up_weight,
    expert_down_weight,
    segments,
    sequence_adapter_index,
    routes,
):
    tok_count = layer_input.shape[0]
    tensor_count = lax.axis_size("tensor")
    data_count = lax.axis_size("dp")
    pair = tensor_count == 2
    ring_count = data_count // QUAD
    col_width = MODEL_WIDTH // tensor_count
    half_width = MODEL_WIDTH // 2
    side = lax.axis_index("tensor")
    col_start = side * col_width
    place_dp = lax.axis_index("dp")
    flip = side.astype(jnp.int32) if pair else jnp.int32(0)
    flip_arr = flip.reshape(1)
    shard_local_width = query_weight_matrix.shape[1]
    local_heads = shard_local_width // HEAD_WIDTH
    local_experts = expert_gate_weight.shape[0]
    expert_total = local_experts * data_count
    capacity = 5 * tok_count * TOP // (4 * expert_total)
    score_scale = HEAD_WIDTH ** (-0.5)
    token_ids = jnp.arange(tok_count, dtype=jnp.int32)
    positions = token_ids % LEN

    def to_sides(full):
        if pair:
            low_cols, high_cols = full[:, :half_width], full[:, half_width:]
            return (
                jnp.where(flip == 0, low_cols, high_cols),
                jnp.where(flip == 0, high_cols, low_cols),
            )
        return full[:, :half_width], full[:, half_width:]

    def from_sides(first, second):
        if pair:
            return jnp.concatenate(
                [jnp.where(flip == 0, first, second), jnp.where(flip == 0, second, first)], axis=1
            )
        return jnp.concatenate([first, second], axis=1)

    routes_t = routes.T
    expert_ids = jnp.arange(expert_total, dtype=jnp.int32)
    chosen_mask = jnp.any(routes_t[:, None, :] == expert_ids[None, :, None], axis=0)
    earlier = (token_ids[:, None] < token_ids[None, :]).astype(half_type)
    rank = jnp.dot(chosen_mask.astype(half_type), earlier, preferred_element_type=jnp.float32)
    place_own = jnp.where(chosen_mask, rank, -1.0).astype(jnp.int32)
    place_all = lax.all_to_all(
        place_own.reshape(data_count, local_experts, tok_count), "dp", 0, 0, tiled=True
    )
    ring_at, quad_at = place_dp // QUAD, place_dp % QUAD
    group_ids = jnp.arange(data_count, dtype=jnp.int32)
    order = ((ring_at - group_ids // QUAD) % ring_count) * QUAD + (quad_at ^ (group_ids % QUAD))
    place_all = place_all[order]
    target_all = jnp.where(
        place_all >= 0,
        place_all + capacity * jnp.arange(local_experts, dtype=jnp.int32)[None, :, None],
        -1,
    ).transpose(0, 2, 1)

    def group_of(values, j):
        return values[j * QUAD : (j + 1) * QUAD]

    if pair:
        g_first = cotangent
        g_second = other_side(cotangent)
    else:
        g_full = lax.all_gather(cotangent, "tensor", axis=1, tiled=True)
        g_first, g_second = g_full[:, :half_width], g_full[:, half_width:]
    adapter = sequence_adapter_index[0]

    def own_adapter(factors, axis):
        return lax.dynamic_index_in_dim(factors, adapter, axis, keepdims=False)

    down_rows = own_adapter(adapter_projection_down.transpose(0, 1, 3, 2), 1)
    down_rows = down_rows.reshape(3 * ADAPTER_RANK, MODEL_WIDTH)
    up_rows = own_adapter(adapter_projection_up, 1)
    out_down_rows = own_adapter(adapter_output_down.transpose(0, 2, 1), 0)
    out_up_rows = own_adapter(adapter_output_up, 0)
    doc_flat = segments.reshape(-1)
    hidden32 = layer_input.astype(jnp.float32)
    hidden_scale = lax.rsqrt(
        jnp.mean(hidden32 * hidden32, axis=-1, keepdims=True) + norm_eps
    )
    normed = (hidden32 * hidden_scale * attention_norm_gain).astype(half_type)
    w_proj = [query_weight_matrix, key_weight_matrix, value_weight_matrix]
    latents = nt_dot(normed, down_rows).astype(half_type)
    latents = [latents[:, p * ADAPTER_RANK : (p + 1) * ADAPTER_RANK] for p in range(3)]
    raw_proj = [
        jnp.dot(normed, w_proj[p], preferred_element_type=jnp.float32)
        + jnp.dot(latents[p], up_rows[p], preferred_element_type=jnp.float32)
        for p in range(3)
    ]
    g_blocks, raw_proj[2] = fence(jnp.stack([g_first, g_second]), raw_proj[2])
    g_all = lax.all_gather(g_blocks, "dp", axis=0)
    query_f, query_back = jax.vjp(
        lambda projected: head_prep(projected, query_norm_gain, positions), raw_proj[0]
    )
    key_f, key_back = jax.vjp(
        lambda projected: head_prep(projected, key_norm_gain, positions), raw_proj[1]
    )
    queries, place_all, target_all = lax.optimization_barrier(
        (query_f.astype(half_type), place_all, target_all)
    )
    keys = key_f.astype(half_type)
    values = raw_proj[2].reshape(tok_count, local_heads, HEAD_WIDTH).astype(half_type)

    same_doc = (doc_flat[:, None] == doc_flat[None, :])[None]

    def block_scores():
        scores = (
            jnp.einsum("qhd,khd->hqk", queries, keys, preferred_element_type=jnp.float32)
            * score_scale
        )
        return jnp.where(same_doc, scores, -1e30)

    scores = block_scores()
    top_score = jnp.max(scores, axis=-1, keepdims=True)
    exp_scores = jnp.exp(scores - top_score)
    row_total = jnp.sum(exp_scores, axis=-1, keepdims=True)
    prob_half = (exp_scores / row_total).astype(half_type)
    attended = jnp.einsum("hqk,khd->qhd", prob_half, values, preferred_element_type=jnp.float32)
    log_totals = top_score[..., 0] + jnp.log(row_total[..., 0])
    attended = attended.reshape(tok_count, shard_local_width).astype(half_type)
    proj_part = jnp.dot(attended, output_weight_matrix, preferred_element_type=jnp.float32)
    latent_part = nt_dot(attended, out_down_rows)

    def tensor_sum(part):
        if pair:
            return part.astype(jnp.float32) + other_side(part).astype(jnp.float32)
        return lax.psum(part, "tensor").astype(jnp.float32)

    def own_columns(part):
        if pair:
            first, second = to_sides(part)
            return first.astype(jnp.float32) + other_side(second.astype(half_type)).astype(
                jnp.float32
            )
        return lax.psum_scatter(
            part.astype(half_type), "tensor", scatter_dimension=1, tiled=True
        ).astype(jnp.float32)

    def columns_of(full):
        if pair:
            return to_sides(full)[0]
        return lax.dynamic_slice_in_dim(full, col_start, col_width, full.ndim - 1)

    def both_halves(cols):
        if pair:
            return cols, other_side(cols)
        full = lax.all_gather(cols, "tensor", axis=1, tiled=True)
        return full[:, :half_width], full[:, half_width:]

    attn_cols = own_columns(proj_part)
    latent_total = tensor_sum(latent_part.astype(half_type))
    latent_out = latent_total.astype(half_type)
    mixed_cols = (
        columns_of(layer_input).astype(jnp.float32)
        + attn_cols
        + jnp.dot(latent_out, columns_of(out_up_rows), preferred_element_type=jnp.float32)
    )
    expert_gain_cols = columns_of(expert_norm_gain[None, :])
    square_sum = tensor_sum(jnp.sum(mixed_cols * mixed_cols, axis=1, keepdims=True))
    mixed_scale = lax.rsqrt(square_sum / MODEL_WIDTH + norm_eps)
    moe_cols_in = (mixed_cols * mixed_scale * expert_gain_cols).astype(half_type)

    def gates_of(first, second):
        moe_in = from_sides(first, second)
        logits_t = lax.dot_general(
            router, moe_in, (((0,), (1,)), ((), ())), preferred_element_type=jnp.float32
        )
        top_logit = jnp.max(jnp.where(chosen_mask, logits_t, -jnp.inf), axis=0, keepdims=True)
        gate_exp = jnp.where(chosen_mask, jnp.exp(jnp.minimum(logits_t - top_logit, 0.0)), 0.0)
        return gate_exp / jnp.sum(gate_exp, axis=0, keepdims=True)

    def grad_rows_of(k, places):
        return call_grad_rows(
            flip_arr,
            group_of(order, k),
            group_of(places, k)[:, :, None, :],
            expert_down_weight,
            g_all,
            capacity,
        )

    def experts_of(k, d_raw, pieces):
        return call_experts(
            flip_arr,
            group_of(place_all, k)[:, :, None, :],
            group_of(gates_all, k)[:, :, None, :],
            group_of(target_all, k),
            expert_gate_weight,
            expert_up_weight,
            d_raw,
            pieces,
            capacity,
        )

    def outputs_of(k, hidden):
        return call_output(
            flip_arr,
            group_of(target_all, k),
            expert_down_weight,
            hidden,
            capacity,
            half_width,
        )

    quads = ring_count
    own0, own1, core0, core1 = ([None] * quads for _ in range(4))
    af, asec, ff, fs = ([None] * quads for _ in range(4))
    d_raw = [None] * quads
    send, keep, hidden, d_gate = ([None] * quads for _ in range(4))
    got, near, side_got, sums = ([None] * quads for _ in range(4))
    work_order = [(i + 1) % quads for i in range(quads)]
    sides_by_tensor = [pair and j != quads - 1 for j in range(quads)]
    places = place_all

    def move_first(j):
        own0[j + 1] = onward(own0[j], data_count)

    def move_second(j):
        own1[j + 1] = onward(own1[j], data_count)

    def send_across(j):
        af[j] = swap(own0[j], data_count, 2)
        core0[j] = swap(own0[j], data_count, 1)

    def send_rest(j):
        asec[j] = other_side(af[j]) if sides_by_tensor[j] else swap(own1[j], data_count, 2)
        core1[j] = swap(own1[j], data_count, 1)
        ff[j] = swap(af[j], data_count, 1)

    def send_last(j):
        fs[j] = swap(asec[j], data_count, 1)

    def run_experts(k):
        pieces = [own0[k], own1[k], core0[k], core1[k], af[k], asec[k], ff[k], fs[k]]
        send[k], keep[k], hidden[k], d_gate[k] = experts_of(k, d_raw[k], pieces)

    def sum_cores(k):
        got[k] = swap(send[k], data_count, 1)

    def sum_sides(k):
        if pair:
            near[k] = plus(keep[k][1, 0], got[k][1, 0])
            side_got[k] = other_side(plus(keep[k][1, 1], got[k][1, 1]))
        else:
            near[k] = plus(keep[k][1], got[k][1])

    def sum_across(k):
        if pair:
            arrived = swap(plus(near[k], side_got[k]), data_count, 2)
            first = plus(keep[k][0, 0], got[k][0, 0], arrived)
            sums[k] = jnp.stack([first, plus(keep[k][0, 1], got[k][0, 1])])
        else:
            sums[k] = plus(keep[k][0], got[k][0], swap(near[k], data_count, 2))

    def step_end(*more):
        groups = (
            own0, own1, core0, core1, af, asec, ff, fs, d_raw,
            send, keep, hidden, d_gate, got, near, side_got, sums,
        )
        fenced = fence(groups, more)
        for old, fresh in zip(groups, fenced[0]):
            old[:] = fresh
        return fenced[1]

    own0[0] = moe_cols_in if pair else both_halves(moe_cols_in)[0]
    own1[0] = both_halves(moe_cols_in)[1]
    move_first(0)
    send_across(0)
    step_end()
    gates_t = gates_of(own0[0], own1[0])
    move_second(0)
    send_rest(0)
    send_across(1)
    (gates_t,) = step_end(gates_t)
    gates_all = lax.all_gather(gates_t.reshape(data_count, local_experts, tok_count), "dp", axis=0)
    gates_all = lax.dynamic_index_in_dim(gates_all, place_dp, 1, keepdims=False)[order]
    move_first(1)
    send_rest(1)
    send_last(0)
    step_end()
    move_second(1)
    send_across(2)
    send_last(1)
    d_raw[1], d_raw[2] = grad_rows_of(1, places), grad_rows_of(2, places)
    (places,) = step_end(places)
    move_first(2)
    send_rest(2)
    run_experts(1)
    step_end()
    move_second(2)
    send_across(3)
    send_last(2)
    sum_cores(1)
    run_experts(2)
    step_end()
    send_rest(3)
    sum_sides(1)
    sum_cores(2)
    d_raw[3], d_raw[0] = grad_rows_of(3, places), grad_rows_of(0, places)
    step_end()
    send_last(3)
    sum_across(1)
    sum_sides(2)
    run_experts(3)
    step_end()
    total = onward(sums[1], data_count)
    sum_across(2)
    sum_cores(3)
    run_experts(0)
    (total,) = step_end(plus(total, sums[2]))
    out_send, out_keep, out_got, out_sums = ([None] * quads for _ in range(4))

    def out_near(k):
        return plus(out_keep[k][1], out_got[k][1])

    def out_sum(k, arrived):
        return plus(out_keep[k][0], out_got[k][0], arrived)

    passed = onward(total, data_count)
    sum_sides(3)
    sum_cores(0)
    out_send[1], out_keep[1] = outputs_of(1, hidden[1])
    out_send[2], out_keep[2] = outputs_of(2, hidden[2])
    out_send, out_keep = step_end(out_send, out_keep)
    sum_across(3)
    sum_sides(0)
    out_got[1] = swap(out_send[1], data_count, 1)
    out_got[2] = swap(out_send[2], data_count, 1)
    out_send[3], out_keep[3] = outputs_of(3, hidden[3])
    out_send[0], out_keep[0] = outputs_of(0, hidden[0])
    d_gate_all = jnp.concatenate([values[:, :, 0, :].transpose(1, 0, 2) for values in d_gate], axis=0)
    d_gate_all = lax.all_gather(d_gate_all, "dp", axis=0)
    total, out_send, out_keep, out_got = step_end(
        plus(passed, sums[3]), out_send, out_keep, out_got
    )
    passed = onward(total, data_count)
    sum_across(0)
    out_across = swap(out_near(1), data_count, 2)
    out_got[3] = swap(out_send[3], data_count, 1)
    out_got[0] = swap(out_send[0], data_count, 1)
    sender = jnp.arange(data_count, dtype=jnp.int32)
    mine = ((sender // QUAD - ring_at) % ring_count) * QUAD + ((sender % QUAD) ^ quad_at)
    d_gate_home = jnp.take_along_axis(d_gate_all, mine[:, None, None, None], axis=1)
    d_gate_home = d_gate_home.reshape(expert_total, tok_count)
    total, out_keep, out_got, out_across, d_gate_home = step_end(
        plus(passed, sums[0]), out_keep, out_got, out_across, d_gate_home
    )
    d_gate_home = tensor_sum(d_gate_home)
    if pair:
        grad_moe_cols = total[0].astype(jnp.float32) + other_side(total[1]).astype(jnp.float32)
    else:
        grad_moe_cols = own_columns(from_sides(total[0], total[1]))
    out_passed = onward(out_sum(1, out_across), data_count)
    out_next = swap(out_near(2), data_count, 2)
    d_gate_home, grad_moe_cols, out_got, out_keep = step_end(
        d_gate_home, grad_moe_cols, out_got, out_keep
    )

    weighted = gates_t * d_gate_home
    grad_logits_t = (
        gates_t * (d_gate_home - jnp.sum(weighted, axis=0, keepdims=True))
    ).astype(half_type)
    router_cols = router.T
    grad_moe_cols = grad_moe_cols + lax.dot_general(
        grad_logits_t,
        columns_of(router_cols),
        (((0,), (0,)), ((), ())),
        preferred_element_type=jnp.float32,
    )
    along = tensor_sum(
        jnp.sum(mixed_cols * expert_gain_cols * grad_moe_cols, axis=1, keepdims=True)
    )
    grad_mixed_cols = (
        cotangent.astype(jnp.float32)
        + expert_gain_cols * mixed_scale * grad_moe_cols
        - mixed_cols * (mixed_scale * mixed_scale * mixed_scale * (along / MODEL_WIDTH))
    )
    branch_cols = grad_mixed_cols.astype(half_type)
    grad_branch = from_sides(*both_halves(branch_cols))
    out_total = plus(out_passed, out_sum(2, out_next))
    grad_branch, out_total, out_got, out_keep = fence(grad_branch, out_total, out_got, out_keep)

    out_passed = onward(out_total, data_count)
    out_third = swap(out_near(3), data_count, 2)

    grad_latent_out = nt_dot(grad_branch, out_up_rows).astype(half_type)
    grad_up_out = lax.dot_general(
        latent_out, branch_cols, (((0,), (0,)), ((), ())), preferred_element_type=jnp.float32
    )
    grad_attended = nt_dot(grad_branch, output_weight_matrix) + jnp.dot(
        grad_latent_out, out_down_rows, preferred_element_type=jnp.float32
    )
    grad_heads = grad_attended.astype(half_type).reshape(tok_count, local_heads, HEAD_WIDTH)
    grad_down_out = lax.dot_general(
        grad_latent_out, attended, (((0,), (0,)), ((), ())), preferred_element_type=jnp.float32
    )

    prob_block = jnp.where(same_doc, jnp.exp(block_scores() - log_totals[:, :, None]), 0.0)
    grad_prob = jnp.einsum("qhd,khd->hqk", grad_heads, values, preferred_element_type=jnp.float32)
    row_delta = jnp.sum(prob_block * grad_prob, axis=-1, keepdims=True)
    grad_scores = (prob_block * (grad_prob - row_delta)).astype(half_type)
    out_total = plus(out_passed, out_sum(3, out_third))
    grad_scores, out_total = fence(grad_scores, out_total)
    out_passed = onward(out_total, data_count)
    out_fourth = swap(out_near(0), data_count, 2)
    grad_queries = (
        jnp.einsum("hqk,khd->qhd", grad_scores, keys, preferred_element_type=jnp.float32)
        * score_scale
    )
    grad_keys = (
        jnp.einsum("hqk,qhd->khd", grad_scores, queries, preferred_element_type=jnp.float32)
        * score_scale
    )
    grad_values = jnp.einsum(
        "hqk,qhd->khd",
        prob_block.astype(half_type),
        grad_heads,
        preferred_element_type=jnp.float32,
    ).reshape(tok_count, shard_local_width)
    grad_raw = [
        query_back(grad_queries)[0].astype(half_type),
        key_back(grad_keys)[0].astype(half_type),
        grad_values.astype(half_type),
    ]
    latent_parts = jnp.concatenate([nt_dot(grad_raw[p], up_rows[p]) for p in range(3)], axis=1)
    grad_latent = tensor_sum(latent_parts.astype(half_type)).astype(half_type)
    grad_up = [
        lax.dot_general(
            latents[p], grad_raw[p], (((0,), (0,)), ((), ())), preferred_element_type=jnp.float32
        )
        for p in range(3)
    ]
    grad_down = lax.dot_general(
        grad_latent, normed, (((0,), (0,)), ((), ())), preferred_element_type=jnp.float32
    )
    number = jnp.full((ADAPTER_RANK, shard_local_width), adapter.astype(half_type))
    first_part = jnp.concatenate(
        [grad_down_out.astype(half_type), grad_up_out.astype(half_type), number]
        + [part.astype(half_type) for part in grad_up],
        axis=0,
    )
    second_part = grad_down.astype(half_type)
    first_part, second_part = fence(first_part, second_part)
    first_all = lax.all_gather(first_part, "dp", axis=0)
    second_all = lax.all_gather(second_part, "dp", axis=0)
    numbers = first_all[:, 2 * ADAPTER_RANK, 0].astype(jnp.float32)
    holds = numbers[None, :] == jnp.arange(ADAPTER_CHOICES, dtype=jnp.float32)[:, None]
    holds = holds.astype(half_type)

    def by_adapter(parts):
        return jnp.einsum("as,src->arc", holds, parts, preferred_element_type=jnp.float32)

    first_sum = by_adapter(first_all)
    second_sum = by_adapter(second_all)

    def rows_at(i):
        return first_sum[:, i * ADAPTER_RANK : (i + 1) * ADAPTER_RANK]

    sum_down_qkv = jnp.stack(
        [second_sum[:, p * ADAPTER_RANK : (p + 1) * ADAPTER_RANK] for p in range(3)]
    ).transpose(0, 1, 3, 2)
    sum_up_qkv = jnp.stack([rows_at(3 + p) for p in range(3)])

    grad_normed_part = nt_dot(grad_raw[0], w_proj[0])
    grad_normed_part += nt_dot(grad_raw[1], w_proj[1])
    grad_normed_part += nt_dot(grad_raw[2], w_proj[2])
    grad_normed_cols = own_columns(grad_normed_part)
    out_total = plus(out_passed, out_sum(0, out_fourth))
    grad_normed_cols, out_total = fence(grad_normed_cols, out_total)
    if pair:
        moe_cols = out_total[0].astype(jnp.float32) + other_side(out_total[1]).astype(jnp.float32)
    else:
        moe_cols = own_columns(from_sides(out_total[0], out_total[1]))
    layer_out = (mixed_cols + moe_cols).astype(half_type)
    grad_normed_cols += jnp.dot(
        grad_latent, columns_of(down_rows), preferred_element_type=jnp.float32
    )
    attention_gain_cols = columns_of(attention_norm_gain[None, :])
    hidden_cols = columns_of(layer_input).astype(jnp.float32)
    along_in = tensor_sum(
        jnp.sum(hidden_cols * attention_gain_cols * grad_normed_cols, axis=1, keepdims=True)
    )
    grad_input = (
        grad_mixed_cols
        + attention_gain_cols * hidden_scale * grad_normed_cols
        - hidden_cols * (hidden_scale * hidden_scale * hidden_scale * (along_in / MODEL_WIDTH))
    )
    return (
        layer_out,
        grad_input,
        sum_down_qkv,
        sum_up_qkv,
        rows_at(0).transpose(0, 2, 1),
        rows_at(1),
    )


def solution(mesh):
    return jax.shard_map(
        local,
        mesh=mesh,
        in_specs=(
            P("dp", None),
            P("dp", "tensor"),
            P(),
            P(),
            P(),
            P(),
            P(None, "tensor"),
            P(None, "tensor"),
            P(None, "tensor"),
            P("tensor", None),
            P(),
            P(None, None, None, "tensor"),
            P(None, "tensor", None),
            P(),
            P(),
            P("dp", None, "tensor"),
            P("dp", None, "tensor"),
            P("dp", "tensor", None),
            P("dp", None),
            P("dp"),
            P("dp", None),
        ),
        out_specs=(
            P("dp", "tensor"),
            P("dp", "tensor"),
            P(),
            P(None, None, None, "tensor"),
            P(None, "tensor", None),
            P(None, None, "tensor"),
        ),
        check_vma=False,
    )
```

time: 1260 us -> 1020 us (0.81)
  waiting for transfers between devices: 663 us -> 433 us
  starting transfers between devices: 82.4 us -> 43.1 us
  matrix products: 84.9 us -> 99.4 us
  local copies, waits for them, and re-layouts: 42.9 us -> 56.8 us
    ppermute x24 -> x12, waiting for transfers between devices: 299 us -> 134 us  [onward(): lax.ppermute(values, 'dp', [(i, (i + QUAD) % data_count) for i in range(d...]
    ppermute x56 -> x37, waiting for transfers between devices: 44.3 us -> 199 us  [swap(): return lax.ppermute(values, 'dp', [(i, i ^ bit) for i in range(data_count)])]
    psum x1 -> x0, waiting for transfers between devices: 87.4 us -> none  [local(): lax.psum(jnp.stack(grad_down_list).astype(jnp.bfloat16), 'dp')]
    ppermute x25 -> x20, waiting for transfers between devices: 157 us -> 90.7 us  [other_side(): return lax.ppermute(values, 'tensor', [(0, 1), (1, 0)])]
    all_to_all x1, waiting for transfers between devices: 45 us -> 0.01 us  [local(): lax.all_to_all(place_own.reshape(data_count, local_experts, tok_count), '...]
    all_to_all x2 -> x0, waiting for transfers between devices: 30.9 us -> none  [the longest x1 16.1 us: local(): lax.all_to_all(gates_t.reshape(data_count, local_experts, tok_count), 'dp...]
    sub x0 -> x1, matrix products: none -> 14.3 us  [local(): grad_scores = (prob_block * (grad_prob - row_delta)).astype(half_type)]
    ppermute x56 -> x37, starting transfers between devices: 27.5 us -> 14.6 us  [swap(): return lax.ppermute(values, 'dp', [(i, i ^ bit) for i in range(data_count)])]
  transfers between devices with their start and end apart: 109 -> 75, of which waited for: 36 -> 25; matrix products, arithmetic and copies ran while one was open for 15% -> 20% of each run, Pallas kernels for 19% -> 23%
where the time goes in v2:
time: 1020 us; the launch traced here: 1010 us
  waiting for transfers between devices  433 us (42%)
  Pallas kernels  235 us (23%)
  other arithmetic  126 us (12%)
  matrix products  99.4 us (10%)
  local copies, waits for them, and re-layouts  56.8 us (6%)
  starting transfers between devices  43.1 us (4%)
  between operations  16.9 us (2%)
    ppermute x37, waiting for transfers between devices, swap(): return lax.ppermute(values, 'dp', [(i, i ^ bit) for i in range(data_count)])  199 us
    ppermute x12, waiting for transfers between devices, onward(): lax.ppermute(values, 'dp', [(i, (i + QUAD) % data_count) for i in range(d...  134 us
    pallas_call x4, Pallas kernels, call_experts(): pl.pallas_call(functools.partial(expert_kernel, experts, cap), out_shape=...  120 us
    ppermute x20, waiting for transfers between devices, other_side(): return lax.ppermute(values, 'tensor', [(0, 1), (1, 0)])  90.7 us
    convert_element_type x23, other arithmetic, plus(): return total.astype(half_type)  78.5 us
    pallas_call x4, Pallas kernels, call_output(): pl.pallas_call(functools.partial(output_kernel, experts, cap), out_shape=...  61.2 us
    pallas_call x4, Pallas kernels, call_grad_rows(): pl.pallas_call(functools.partial(grad_rows_kernel, experts, cap), out_sha...  53.8 us
    unnamed x258, local copies, waits for them, and re-layouts  25.7 us
  transfers between devices with their start and end apart: 75, of which 25 were waited for; matrix products, arithmetic and copies ran while one was open for 20% of the time, Pallas kernels for 23%

profile of v2, /device:TPU:0, one launch (start us, length us, event | category | flops | bytes accessed | tf_op | source)
XLA Modules:
  0.0 1010.2 jit_solution(14520335534491911376)
XLA Ops:
  16.2 4.6 fusion.159
  23.1 10.6 %collective-permute-done = bf16[512,1024]{1,0:T(8,128)(2,1)S(1)} collective-permute-done((bf16[512,1024]{1,0:T(8,128)(2,1)}, bf16[512,1024]{1,0:T(8,128)(2,1)S(1)}, u32[]{:S(2)}, u32[]{:S(2)}) %collective-permute-start) | collective-permute-done | bytes 1048608 | tf_op jit(solution)/shard_map/ppermute | solution.py:381
  37.5 6.2 all-to-all-start
  43.8 5.0 fusion.156
  51.2 5.2 fusion.154
  86.8 21.9 %collective-permute-done.2 = bf16[512,16]{0,1:T(8,128)(2,1)S(1)} collective-permute-done((bf16[512,16]{0,1:T(8,128)(2,1)S(1)}, bf16[512,16]{0,1:T(8,128)(2,1)S(1)}, u32[]{:S(2)}, u32[]{:S(2)}) %collective-permute-start.2) | collective-permute-done | bytes 16416 | tf_op jit(solution)/shard_map/ppermute | solution.py:381
  118.4 43.0 %collective-permute-done.7.across_first_ref = bf16[512,1024]{1,0:T(8,128)(2,1)S(1)} collective-permute-done((bf16[512,1024]{1,0:T(8,128)(2,1)S(1)}, bf16[512,1024]{1,0:T(8,128)(2,1)S(1)}, u32[]{:S(2)}, u32[]{:S(2)}) %collective-permute-start.7) | collective-permute-done | bytes 1048608 | tf_op jit(solution)/shard_map/ppermute | solution.py:373
  161.5 5.4 collective-permute-done.4.own_first_ref
  168.3 46.6 %collective-permute-done.11.across_first_ref = bf16[512,1024]{1,0:T(8,128)(2,1)S(1)} collective-permute-done((bf16[512,1024]{1,0:T(8,128)(2,1)S(1)}, bf16[512,1024]{1,0:T(8,128)(2,1)S(1)}, u32[]{:S(2)}, u32[]{:S(2)}) %collective-permute-start.11) | collective-permute-done | bytes 1048608 | tf_op jit(solution)/shard_map/ppermute | solution.py:373
  219.7 38.6 %collective-permute-done.8.own_second_ref = bf16[512,1024]{1,0:T(8,128)(2,1)} collective-permute-done((bf16[512,1024]{1,0:T(8,128)(2,1)S(1)}, bf16[512,1024]{1,0:T(8,128)(2,1)}, u32[]{:S(2)}, u32[]{:S(2)}) %collective-permute-start.8) | collective-permute-done | bytes 1048608 | tf_op jit(solution)/shard_map/ppermute | solution.py:377
  260.4 28.9 %collective-permute-done.14.own_first_ref = bf16[512,1024]{1,0:T(8,128)(2,1)S(1)} collective-permute-done((bf16[512,1024]{1,0:T(8,128)(2,1)}, bf16[512,1024]{1,0:T(8,128)(2,1)S(1)}, u32[]{:S(2)}, u32[]{:S(2)}) %collective-permute-start.14) | collective-permute-done | bytes 1048608 | tf_op jit(solution)/shard_map/ppermute | solution.py:377
  293.1 13.3 %grad_rows.4.dh_ref = bf16[4,320,512]{2,1,0:T(8,128)(2,1)} custom-call(s32[1]{0:T(128)} %bitcast.23.flip_ref, s32[4]{0:T(128)} %get-tuple-element.591.block_ids, s32[4,4,1,512]{3,2,1,0:T(1,128)} %broadcast_in_dim.138.place_ref, bf16[4,512,2048]{2,1,0:T(8,128)(2,1)} %down_ref.15, bf16[16,2,512,1024]{3,2,1,0:T(8,128)(2,1)} %bitcast.311), custom_call_target="tpu_custom_call" | custom-call | flops 1 | bytes 1 | tf_op jit(solution)/shard_map/grad_rows/pallas_call | solution.py:275
  306.4 13.3 %grad_rows.5.dh_ref = bf16[4,320,512]{2,1,0:T(8,128)(2,1)} custom-call(s32[1]{0:T(128)} %bitcast.23.flip_ref, s32[4]{0:T(128)} %get-tuple-element.590.block_ids, s32[4,4,1,512]{3,2,1,0:T(1,128)} %broadcast_in_dim.139.place_ref, bf16[4,512,2048]{2,1,0:T(8,128)(2,1)} %down_ref.15, bf16[16,2,512,1024]{3,2,1,0:T(8,128)(2,1)} %bitcast.312), custom_call_target="tpu_custom_call" | custom-call | flops 1 | bytes 1 | tf_op jit(solution)/shard_map/grad_rows/pallas_call | solution.py:275
  323.8 4.3 fusion.162
  330.7 29.8 %experts.4 = (bf16[2,2,512,1024]{3,2,1,0:T(8,128)(2,1)}, bf16[2,2,512,1024]{3,2,1,0:T(8,128)(2,1)}, bf16[4,320,512]{2,1,0:T(8,128)(2,1)}, f32[4,4,1,512]{3,2,1,0:T(1,128)}) custom-call(s32[1]{0:T(128)} %bitcast.23.flip_ref, s32[4,4,1,512]{3,2,1,0:T(1,128)} %broadcast_in_dim.138.place_ref, f32[4,4,1,512]{3,2,1,0:T(1,128)} %copy.234.gate_ref, ...), custom_call_target="tpu_custom_call" | custom-call | flops 1 | bytes 1 | tf_op jit(solution)/shard_map/experts/pallas_call | solution.py:302
  362.0 7.0 collective-permute-done.30.far_second_ref
  370.0 30.0 %experts.5 = (bf16[2,2,512,1024]{3,2,1,0:T(8,128)(2,1)}, bf16[2,2,512,1024]{3,2,1,0:T(8,128)(2,1)}, bf16[4,320,512]{2,1,0:T(8,128)(2,1)}, f32[4,4,1,512]{3,2,1,0:T(1,128)}) custom-call(s32[1]{0:T(128)} %bitcast.23.flip_ref, s32[4,4,1,512]{3,2,1,0:T(1,128)} %broadcast_in_dim.139.place_ref, f32[4,4,1,512]{3,2,1,0:T(1,128)} %copy.235.gate_ref, ...), custom_call_target="tpu_custom_call" | custom-call | flops 1 | bytes 1 | tf_op jit(solution)/shard_map/experts/pallas_call | solution.py:302
  408.2 13.3 %grad_rows.6.dh_ref = bf16[4,320,512]{2,1,0:T(8,128)(2,1)} custom-call(s32[1]{0:T(128)} %bitcast.23.flip_ref, s32[4]{0:T(128)} %get-tuple-element.589.block_ids, s32[4,4,1,512]{3,2,1,0:T(1,128)} %broadcast_in_dim.142.place_ref, bf16[4,512,2048]{2,1,0:T(8,128)(2,1)} %down_ref.15, bf16[16,2,512,1024]{3,2,1,0:T(8,128)(2,1)} %bitcast.313), custom_call_target="tpu_custom_call" | custom-call | flops 1 | bytes 1 | tf_op jit(solution)/shard_map/grad_rows/pallas_call | solution.py:275
  422.2 13.8 %grad_rows.7.dh_ref = bf16[4,320,512]{2,1,0:T(8,128)(2,1)} custom-call(s32[1]{0:T(128)} %bitcast.23.flip_ref, s32[4]{0:T(128)} %get-tuple-element.588.block_ids, s32[4,4,1,512]{3,2,1,0:T(1,128)} %broadcast_in_dim.143.place_ref, bf16[4,512,2048]{2,1,0:T(8,128)(2,1)} %down_ref.15, bf16[16,2,512,1024]{3,2,1,0:T(8,128)(2,1)} %bitcast.314), custom_call_target="tpu_custom_call" | custom-call | flops 1 | bytes 1 | tf_op jit(solution)/shard_map/grad_rows/pallas_call | solution.py:275
  448.5 30.1 %experts.6 = (bf16[2,2,512,1024]{3,2,1,0:T(8,128)(2,1)}, bf16[2,2,512,1024]{3,2,1,0:T(8,128)(2,1)}, bf16[4,320,512]{2,1,0:T(8,128)(2,1)}, f32[4,4,1,512]{3,2,1,0:T(1,128)}) custom-call(s32[1]{0:T(128)} %bitcast.23.flip_ref, s32[4,4,1,512]{3,2,1,0:T(1,128)} %broadcast_in_dim.144.place_ref, f32[4,4,1,512]{3,2,1,0:T(1,128)} %copy.236.gate_ref, ...), custom_call_target="tpu_custom_call" | custom-call | flops 1 | bytes 1 | tf_op jit(solution)/shard_map/experts/pallas_call | solution.py:302
  486.0 29.8 %experts.7 = (bf16[2,2,512,1024]{3,2,1,0:T(8,128)(2,1)}, bf16[2,2,512,1024]{3,2,1,0:T(8,128)(2,1)}, bf16[4,320,512]{2,1,0:T(8,128)(2,1)}, f32[4,4,1,512]{3,2,1,0:T(1,128)}) custom-call(s32[1]{0:T(128)} %bitcast.23.flip_ref, s32[4,4,1,512]{3,2,1,0:T(1,128)} %broadcast_in_dim.146.place_ref, f32[4,4,1,512]{3,2,1,0:T(1,128)} %broadcast_in_dim.147.gate_ref, ...), custom_call_target="tpu_custom_call" | custom-call | flops 1 | bytes 1 | tf_op jit(solution)/shard_map/experts/pallas_call | solution.py:302
  519.3 13.7 %collective-permute-done.42 = bf16[2,512,1024]{2,1,0:T(8,128)(2,1)} collective-permute-done((bf16[2,512,1024]{2,1,0:T(8,128)(2,1)}, bf16[2,512,1024]{2,1,0:T(8,128)(2,1)}, u32[]{:S(2)}, u32[]{:S(2)}) %collective-permute-start.42) | collective-permute-done | bytes 2097184 | tf_op jit(solution)/shard_map/ppermute | solution.py:377
  540.2 15.1 %outputs.4 = (bf16[2,2,512,1024]{3,2,1,0:T(8,128)(2,1)}, bf16[2,2,512,1024]{3,2,1,0:T(8,128)(2,1)}) custom-call(s32[1]{0:T(128)} %bitcast.23.flip_ref, s32[4,512,4]{2,1,0:T(8,128)} %get-tuple-element.551.target_ref, bf16[4,512,2048]{2,1,0:T(8,128)(2,1)} %down_ref.15, bf16[4,320,512]{2,1,0:T(8,128)(2,1)} %get-tuple-element.425.hidden_ref), custom_call_target="tpu_custom_call" | custom-call | flops 10737418240 | bytes 16777216 | tf_op jit(solution)/shard_map/outputs/pallas_call | solution.py:343
  555.4 15.4 %outputs.5 = (bf16[2,2,512,1024]{3,2,1,0:T(8,128)(2,1)}, bf16[2,2,512,1024]{3,2,1,0:T(8,128)(2,1)}) custom-call(s32[1]{0:T(128)} %bitcast.23.flip_ref, s32[4,512,4]{2,1,0:T(8,128)} %get-tuple-element.550.target_ref, bf16[4,512,2048]{2,1,0:T(8,128)(2,1)} %down_ref.15, bf16[4,320,512]{2,1,0:T(8,128)(2,1)} %get-tuple-element.426.hidden_ref), custom_call_target="tpu_custom_call" | custom-call | flops 10737418240 | bytes 16777216 | tf_op jit(solution)/shard_map/outputs/pallas_call | solution.py:343
  579.9 15.2 %outputs.6 = (bf16[2,2,512,1024]{3,2,1,0:T(8,128)(2,1)}, bf16[2,2,512,1024]{3,2,1,0:T(8,128)(2,1)}) custom-call(s32[1]{0:T(128)} %bitcast.23.flip_ref, s32[4,512,4]{2,1,0:T(8,128)} %get-tuple-element.548.target_ref, bf16[4,512,2048]{2,1,0:T(8,128)(2,1)} %down_ref.15, bf16[4,320,512]{2,1,0:T(8,128)(2,1)} %get-tuple-element.439.hidden_ref), custom_call_target="tpu_custom_call" | custom-call | flops 10737418240 | bytes 16777216 | tf_op jit(solution)/shard_map/outputs/pallas_call | solution.py:343
  595.0 15.5 %outputs.7 = (bf16[2,2,512,1024]{3,2,1,0:T(8,128)(2,1)}, bf16[2,2,512,1024]{3,2,1,0:T(8,128)(2,1)}) custom-call(s32[1]{0:T(128)} %bitcast.23.flip_ref, s32[4,512,4]{2,1,0:T(8,128)} %get-tuple-element.549.target_ref, bf16[4,512,2048]{2,1,0:T(8,128)(2,1)} %down_ref.15, bf16[4,320,512]{2,1,0:T(8,128)(2,1)} %get-tuple-element.440.hidden_ref), custom_call_target="tpu_custom_call" | custom-call | flops 10737418240 | bytes 16777216 | tf_op jit(solution)/shard_map/outputs/pallas_call | solution.py:343
  614.3 10.9 %collective-permute-done.47 = bf16[2,512,1024]{2,1,0:T(8,128)(2,1)} collective-permute-done((bf16[2,512,1024]{2,1,0:T(8,128)(2,1)S(1)}, bf16[2,512,1024]{2,1,0:T(8,128)(2,1)}, u32[]{:S(2)}, u32[]{:S(2)}) %collective-permute-start.47) | collective-permute-done | bytes 2097184 | tf_op jit(solution)/shard_map/ppermute | solution.py:377
  638.1 8.5 all-gather.14.cloned.1.call-done
  652.3 52.2 %collective-permute-done.50 = bf16[512,1024]{1,0:T(8,128)(2,1)} collective-permute-done((bf16[512,1024]{1,0:T(8,128)(2,1)S(1)}, bf16[512,1024]{1,0:T(8,128)(2,1)}, u32[]{:S(2)}, u32[]{:S(2)}) %collective-permute-start.50) | collective-permute-done | bytes 1048608 | tf_op jit(solution)/shard_map/ppermute | solution.py:373
  716.2 5.0 fusion.12
  721.4 15.6 %collective-permute-done.55 = f32[64,512]{1,0:T(8,128)S(1)} collective-permute-done((f32[64,512]{1,0:T(8,128)S(1)}, f32[64,512]{1,0:T(8,128)S(1)}, u32[]{:S(2)}, u32[]{:S(2)}) %collective-permute-start.55) | collective-permute-done | bytes 131104 | tf_op jit(solution)/shard_map/ppermute | solution.py:381
  745.3 16.9 %collective-permute-done.60 = bf16[2,512,1024]{2,1,0:T(8,128)(2,1)S(1)} collective-permute-done((bf16[2,512,1024]{2,1,0:T(8,128)(2,1)}, bf16[2,512,1024]{2,1,0:T(8,128)(2,1)S(1)}, u32[]{:S(2)}, u32[]{:S(2)}) %collective-permute-start.60) | collective-permute-done | bytes 2097184 | tf_op jit(solution)/shard_map/ppermute | solution.py:373
  762.2 7.2 collective-permute-done.59
  769.4 6.2 add_convert_fusion.4
  784.2 4.9 fusion.28
  792.3 6.0 fusion.45
  800.3 6.0 fusion.74
  806.3 14.3 %multiply_convert_fusion = bf16[8,512,512]{1,2,0:T(8,128)(2,1)} fusion(f32[8,512,512]{1,2,0:T(8,128)} %fusion.74, f32[8,512]{1,0:T(8,128)S(1)} %log_add_fusion, pred[512,512]{0,1:T(8,128)(4,1)S(1)} %copy-done.51, bf16[512,8,128]{2,0,1:T(8,128)(2,1)S(1)} %copy-done.19, bf16[512,8,64]{2,0,1:T(8,128)(2,1)S(1)} %copy-done.27, bf16[512,8,64]{2,0,1:T(8,128)(2,1)S(1)} %copy-done.25), kind=kOutput, calls=%fused_computation.4 | convolution fusion | flops 1103106560 | bytes 14958592 | tf_op jit(solution)/shard_map/sub | solution.py:818
  820.6 13.9 %collective-permute-done.62 = bf16[2,512,1024]{2,1,0:T(8,128)(2,1)} collective-permute-done((bf16[2,512,1024]{2,1,0:T(8,128)(2,1)}, bf16[2,512,1024]{2,1,0:T(8,128)(2,1)}, u32[]{:S(2)}, u32[]{:S(2)}) %collective-permute-start.62) | collective-permute-done | bytes 2097184 | tf_op jit(solution)/shard_map/ppermute | solution.py:373
  837.6 7.0 add_convert_fusion.2
  877.2 4.7 fusion.29
  882.3 4.4 fusion.169
  886.7 4.7 fusion.170
  895.4 19.6 %collective-permute-done.63 = bf16[512,1024]{1,0:T(8,128)(2,1)S(1)} collective-permute-done((bf16[512,1024]{1,0:T(8,128)(2,1)S(1)}, bf16[512,1024]{1,0:T(8,128)(2,1)S(1)}, u32[]{:S(2)}, u32[]{:S(2)}) %collective-permute-start.63) | collective-permute-done | bytes 1048608 | tf_op jit(solution)/shard_map/ppermute | solution.py:381
  915.7 19.7 %collective-permute-done.65 = bf16[2,512,1024]{2,1,0:T(8,128)(2,1)} collective-permute-done((bf16[2,512,1024]{2,1,0:T(8,128)(2,1)}, bf16[2,512,1024]{2,1,0:T(8,128)(2,1)}, u32[]{:S(2)}, u32[]{:S(2)}) %collective-permute-start.65) | collective-permute-done | bytes 2097184 | tf_op jit(solution)/shard_map/ppermute | solution.py:373
  935.4 23.0 %collective-permute-done.64 = bf16[2,512,1024]{2,1,0:T(8,128)(2,1)S(1)} collective-permute-done((bf16[2,512,1024]{2,1,0:T(8,128)(2,1)S(1)}, bf16[2,512,1024]{2,1,0:T(8,128)(2,1)S(1)}, u32[]{:S(2)}, u32[]{:S(2)}) %collective-permute-start.64) | collective-permute-done | bytes 2097184 | tf_op jit(solution)/shard_map/ppermute | solution.py:377
  965.6 15.2 %collective-permute-done.68 = f32[512,1]{0,1:T(1,128)S(1)} collective-permute-done((f32[512,1]{0,1:T(1,128)S(1)}, f32[512,1]{0,1:T(1,128)S(1)}, u32[]{:S(2)}, u32[]{:S(2)}) %collective-permute-start.68) | collective-permute-done | bytes 2080 | tf_op jit(solution)/shard_map/ppermute | solution.py:381
  989.3 5.6 fusion.18
  (541 shorter events, 246.5 us)
Async XLA Ops:
  7.2 285.9 %all-gather.12.cloned.1.call-start = ((), (), s32[]{:S(2)}) async-start(), calls=%async_computation.2 | async-start | bytes 35651584 | tf_op jit(solution)/shard_map/all_gather | solution.py:508
  43.7 284.3 %all-gather.10.cloned.1.call-start = ((), (), s32[]{:S(2)}) async-start(), calls=%async_computation.1 | async-start | bytes 2228224 | tf_op jit(solution)/shard_map/all_gather | solution.py:692
  113.6 47.8 %collective-permute-start.7 = (bf16[512,1024]{1,0:T(8,128)(2,1)S(1)}, bf16[512,1024]{1,0:T(8,128)(2,1)S(1)}, u32[]{:S(2)}, u32[]{:S(2)}) collective-permute-start(bf16[512,1024]{1,0:T(8,128)(2,1)S(1)} %multiply_convert_fusion.1.own_first_ref), channel_id=1, source_target_pairs={{0,4},{2,6},{4,0},{6,2},{8,12},{10,14},{12,8},{14,10},{16,20},{18,... | collective-permute-start | bytes 3145736 | tf_op jit(solution)/shard_map/ppermute | solution.py:373
  115.4 46.1 %collective-permute-start.6 = (bf16[512,1024]{1,0:T(8,128)(2,1)S(1)}, bf16[512,1024]{1,0:T(8,128)(2,1)S(1)}, u32[]{:S(2)}, u32[]{:S(2)}) collective-permute-start(bf16[512,1024]{1,0:T(8,128)(2,1)S(1)} %multiply_convert_fusion.1.own_first_ref), channel_id=1, source_target_pairs={{0,2},{2,0},{4,6},{6,4},{8,10},{10,8},{12,14},{14,12},{16,18},{18,... | collective-permute-start | bytes 3145736 | tf_op jit(solution)/shard_map/ppermute | solution.py:373
  115.4 46.1 %collective-permute-start.5 = (bf16[512,1024]{1,0:T(8,128)(2,1)S(1)}, bf16[512,1024]{1,0:T(8,128)(2,1)S(1)}, u32[]{:S(2)}, u32[]{:S(2)}) collective-permute-start(bf16[512,1024]{1,0:T(8,128)(2,1)S(1)} %multiply_convert_fusion.1.own_first_ref), channel_id=1, source_target_pairs={{0,1},{1,0},{2,3},{3,2},{4,5},{5,4},{6,7},{7,6},{8,9},{9,8},{10,11... | collective-permute-start | bytes 3145736 | tf_op jit(solution)/shard_map/ppermute | solution.py:381
  116.9 50.0 %collective-permute-start.4 = (bf16[512,1024]{1,0:T(8,128)(2,1)S(1)}, bf16[512,1024]{1,0:T(8,128)(2,1)S(1)}, u32[]{:S(2)}, u32[]{:S(2)}) collective-permute-start(bf16[512,1024]{1,0:T(8,128)(2,1)S(1)} %multiply_convert_fusion.1.own_first_ref), channel_id=1, source_target_pairs={{0,8},{2,10},{4,12},{6,14},{8,16},{10,18},{12,20},{14,22},{16,24},... | collective-permute-start | bytes 3145736 | tf_op jit(solution)/shard_map/ppermute | solution.py:377
  166.9 47.9 %collective-permute-start.11 = (bf16[512,1024]{1,0:T(8,128)(2,1)S(1)}, bf16[512,1024]{1,0:T(8,128)(2,1)S(1)}, u32[]{:S(2)}, u32[]{:S(2)}) collective-permute-start(bf16[512,1024]{1,0:T(8,128)(2,1)S(1)} %collective-permute-done.4.own_first_ref), channel_id=1, source_target_pairs={{0,4},{2,6},{4,0},{6,2},{8,12},{10,14},{12,8},{14,10},{16,20},{18,... | collective-permute-start | bytes 3145736 | tf_op jit(solution)/shard_map/ppermute | solution.py:373
  167.3 49.7 %collective-permute-start.9 = (bf16[512,1024]{1,0:T(8,128)(2,1)S(1)}, bf16[512,1024]{1,0:T(8,128)(2,1)S(1)}, u32[]{:S(2)}, u32[]{:S(2)}) collective-permute-start(bf16[512,1024]{1,0:T(8,128)(2,1)S(1)} %collective-permute-done.4.own_first_ref), channel_id=1, source_target_pairs={{0,2},{2,0},{4,6},{6,4},{8,10},{10,8},{12,14},{14,12},{16,18},{18,... | collective-permute-start | bytes 3145736 | tf_op jit(solution)/shard_map/ppermute | solution.py:373
  167.3 49.7 %collective-permute-start.13 = (bf16[512,1024]{1,0:T(8,128)(2,1)S(1)}, bf16[512,1024]{1,0:T(8,128)(2,1)S(1)}, u32[]{:S(2)}, u32[]{:S(2)}) collective-permute-start(bf16[512,1024]{1,0:T(8,128)(2,1)S(1)} %collective-permute-done.7.across_first_ref), channel_id=1, source_target_pairs={{0,2},{2,0},{4,6},{6,4},{8,10},{10,8},{12,14},{14,12},{16,18},{18,... | collective-permute-start | bytes 3145736 | tf_op jit(solution)/shard_map/ppermute | solution.py:373
  167.8 49.2 %collective-permute-start.12 = (bf16[512,1024]{1,0:T(8,128)(2,1)S(1)}, bf16[512,1024]{1,0:T(8,128)(2,1)S(1)}, u32[]{:S(2)}, u32[]{:S(2)}) collective-permute-start(bf16[512,1024]{1,0:T(8,128)(2,1)S(1)} %collective-permute-done.7.across_first_ref), channel_id=1, source_target_pairs={{0,1},{1,0},{2,3},{3,2},{4,5},{5,4},{6,7},{7,6},{8,9},{9,8},{10,11... | collective-permute-start | bytes 3145736 | tf_op jit(solution)/shard_map/ppermute | solution.py:381
  168.3 48.8 %collective-permute-start.10 = (bf16[512,1024]{1,0:T(8,128)(2,1)S(1)}, bf16[512,1024]{1,0:T(8,128)(2,1)S(1)}, u32[]{:S(2)}, u32[]{:S(2)}) collective-permute-start(bf16[512,1024]{1,0:T(8,128)(2,1)S(1)} %collective-permute-done.5.own_second_ref), channel_id=1, source_target_pairs={{0,2},{2,0},{4,6},{6,4},{8,10},{10,8},{12,14},{14,12},{16,18},{18,... | collective-permute-start | bytes 3145736 | tf_op jit(solution)/shard_map/ppermute | solution.py:373
  215.9 42.5 %collective-permute-start.8 = (bf16[512,1024]{1,0:T(8,128)(2,1)S(1)}, bf16[512,1024]{1,0:T(8,128)(2,1)}, u32[]{:S(2)}, u32[]{:S(2)}) collective-permute-start(bf16[512,1024]{1,0:T(8,128)(2,1)S(1)} %collective-permute-done.5.own_second_ref), channel_id=1, source_target_pairs={{0,8},{2,10},{4,12},{6,14},{8,16},{10,18},{12,20},{14,22},{16,24},... | collective-permute-start | bytes 3145736 | tf_op jit(solution)/shard_map/ppermute | solution.py:377
  259.1 387.5 %all-gather.14.cloned.1.call-start = ((), (), s32[]{:S(2)}) async-start(), calls=%async_computation.3 | async-start | bytes 2228224 | tf_op jit(solution)/shard_map/all_gather | solution.py:749
  323.1 37.4 %collective-permute-start.23 = (bf16[512,1024]{1,0:T(8,128)(2,1)S(1)}, bf16[512,1024]{1,0:T(8,128)(2,1)S(1)}, u32[]{:S(2)}, u32[]{:S(2)}) collective-permute-start(bf16[512,1024]{1,0:T(8,128)(2,1)S(1)} %collective-permute-done.14.own_first_ref), channel_id=1, source_target_pairs={{0,8},{2,10},{4,12},{6,14},{8,16},{10,18},{12,20},{14,22},{16,24},... | collective-permute-start | bytes 3145736 | tf_op jit(solution)/shard_map/ppermute | solution.py:377
  323.2 37.4 %collective-permute-start.24 = (bf16[512,1024]{1,0:T(8,128)(2,1)}, bf16[512,1024]{1,0:T(8,128)(2,1)}, u32[]{:S(2)}, u32[]{:S(2)}) collective-permute-start(bf16[512,1024]{1,0:T(8,128)(2,1)} %collective-permute-done.19.own_second_ref), channel_id=1, source_target_pairs={{0,2},{2,0},{4,6},{6,4},{8,10},{10,8},{12,14},{14,12},{16,18},{18,... | collective-permute-start | bytes 3145736 | tf_op jit(solution)/shard_map/ppermute | solution.py:373
  323.3 37.3 %collective-permute-start.26 = (bf16[512,1024]{1,0:T(8,128)(2,1)}, bf16[512,1024]{1,0:T(8,128)(2,1)}, u32[]{:S(2)}, u32[]{:S(2)}) collective-permute-start(bf16[512,1024]{1,0:T(8,128)(2,1)} %collective-permute-done.21.across_first_ref), channel_id=1, source_target_pairs={{0,2},{2,0},{4,6},{6,4},{8,10},{10,8},{12,14},{14,12},{16,18},{18,... | collective-permute-start | bytes 3145736 | tf_op jit(solution)/shard_map/ppermute | solution.py:373
  323.8 36.8 %collective-permute-start.25 = (bf16[512,1024]{1,0:T(8,128)(2,1)}, bf16[512,1024]{1,0:T(8,128)(2,1)}, u32[]{:S(2)}, u32[]{:S(2)}) collective-permute-start(bf16[512,1024]{1,0:T(8,128)(2,1)} %collective-permute-done.21.across_first_ref), channel_id=1, source_target_pairs={{0,1},{1,0},{2,3},{3,2},{4,5},{5,4},{6,7},{7,6},{8,9},{9,8},{10,11... | collective-permute-start | bytes 3145736 | tf_op jit(solution)/shard_map/ppermute | solution.py:381
  360.6 39.5 %collective-permute-start.31 = (bf16[2,2,512,1024]{3,2,1,0:T(8,128)(2,1)}, bf16[2,2,512,1024]{3,2,1,0:T(8,128)(2,1)}, u32[]{:S(2)}, u32[]{:S(2)}) collective-permute-start(bf16[2,2,512,1024]{3,2,1,0:T(8,128)(2,1)} %get-tuple-element.335), channel_id=1, source_target_pairs={{0,2},{2,0},{4,6},{6,4},{8,10},{10,8},{12,14},{14,12},{16,18},{18,... | collective-permute-start | bytes 12582920 | tf_op jit(solution)/shard_map/ppermute | solution.py:373
  361.1 38.8 %collective-permute-start.29 = (bf16[512,1024]{1,0:T(8,128)(2,1)S(1)}, bf16[512,1024]{1,0:T(8,128)(2,1)S(1)}, u32[]{:S(2)}, u32[]{:S(2)}) collective-permute-start(bf16[512,1024]{1,0:T(8,128)(2,1)S(1)} %collective-permute-done.23.own_first_ref), channel_id=1, source_target_pairs={{0,4},{2,6},{4,0},{6,2},{8,12},{10,14},{12,8},{14,10},{16,20},{18,... | collective-permute-start | bytes 3145736 | tf_op jit(solution)/shard_map/ppermute | solution.py:373
  361.4 38.6 %collective-permute-start.28 = (bf16[512,1024]{1,0:T(8,128)(2,1)S(1)}, bf16[512,1024]{1,0:T(8,128)(2,1)S(1)}, u32[]{:S(2)}, u32[]{:S(2)}) collective-permute-start(bf16[512,1024]{1,0:T(8,128)(2,1)S(1)} %collective-permute-done.23.own_first_ref), channel_id=1, source_target_pairs={{0,2},{2,0},{4,6},{6,4},{8,10},{10,8},{12,14},{14,12},{16,18},{18,... | collective-permute-start | bytes 3145736 | tf_op jit(solution)/shard_map/ppermute | solution.py:373
  361.4 38.6 %collective-permute-start.27 = (bf16[512,1024]{1,0:T(8,128)(2,1)}, bf16[512,1024]{1,0:T(8,128)(2,1)}, u32[]{:S(2)}, u32[]{:S(2)}) collective-permute-start(bf16[512,1024]{1,0:T(8,128)(2,1)} %collective-permute-done.19.own_second_ref), channel_id=1, source_target_pairs={{0,8},{2,10},{4,12},{6,14},{8,16},{10,18},{12,20},{14,22},{16,24},... | collective-permute-start | bytes 3145736 | tf_op jit(solution)/shard_map/ppermute | solution.py:377
  400.0 36.1 %collective-permute-start.35 = (bf16[2,2,512,1024]{3,2,1,0:T(8,128)(2,1)}, bf16[2,2,512,1024]{3,2,1,0:T(8,128)(2,1)}, u32[]{:S(2)}, u32[]{:S(2)}) collective-permute-start(bf16[2,2,512,1024]{3,2,1,0:T(8,128)(2,1)} %get-tuple-element.356), channel_id=1, source_target_pairs={{0,2},{2,0},{4,6},{6,4},{8,10},{10,8},{12,14},{14,12},{16,18},{18,... | collective-permute-start | bytes 12582920 | tf_op jit(solution)/shard_map/ppermute | solution.py:373
  400.5 35.6 %collective-permute-start.33 = (bf16[512,1024]{1,0:T(8,128)(2,1)}, bf16[512,1024]{1,0:T(8,128)(2,1)S(1)}, u32[]{:S(2)}, u32[]{:S(2)}) collective-permute-start(bf16[512,1024]{1,0:T(8,128)(2,1)} %collective-permute-done.27.own_second_ref), channel_id=1, source_target_pairs={{0,4},{2,6},{4,0},{6,2},{8,12},{10,14},{12,8},{14,10},{16,20},{18,... | collective-permute-start | bytes 3145736 | tf_op jit(solution)/shard_map/ppermute | solution.py:373
  400.8 35.3 %collective-permute-start.32 = (bf16[512,1024]{1,0:T(8,128)(2,1)}, bf16[512,1024]{1,0:T(8,128)(2,1)}, u32[]{:S(2)}, u32[]{:S(2)}) collective-permute-start(bf16[512,1024]{1,0:T(8,128)(2,1)} %collective-permute-done.27.own_second_ref), channel_id=1, source_target_pairs={{0,2},{2,0},{4,6},{6,4},{8,10},{10,8},{12,14},{14,12},{16,18},{18,... | collective-permute-start | bytes 3145736 | tf_op jit(solution)/shard_map/ppermute | solution.py:373
  401.0 35.1 %collective-permute-start.34 = (bf16[512,1024]{1,0:T(8,128)(2,1)S(1)}, bf16[512,1024]{1,0:T(8,128)(2,1)}, u32[]{:S(2)}, u32[]{:S(2)}) collective-permute-start(bf16[512,1024]{1,0:T(8,128)(2,1)S(1)} %collective-permute-done.29.across_first_ref), channel_id=1, source_target_pairs={{0,2},{2,0},{4,6},{6,4},{8,10},{10,8},{12,14},{14,12},{16,18},{18,... | collective-permute-start | bytes 3145736 | tf_op jit(solution)/shard_map/ppermute | solution.py:373
  439.1 39.4 %collective-permute-start.39 = (bf16[512,1024]{1,0:T(8,128)(2,1)}, bf16[512,1024]{1,0:T(8,128)(2,1)}, u32[]{:S(2)}, u32[]{:S(2)}) collective-permute-start(bf16[512,1024]{1,0:T(8,128)(2,1)} %add_convert_fusion.22), channel_id=1, source_target_pairs={{0,4},{2,6},{4,0},{6,2},{8,12},{10,14},{12,8},{14,10},{16,20},{18,... | collective-permute-start | bytes 3145736 | tf_op jit(solution)/shard_map/ppermute | solution.py:373
  444.3 38.4 %collective-permute-start.38 = (bf16[512,1024]{1,0:T(8,128)(2,1)}, bf16[512,1024]{1,0:T(8,128)(2,1)}, u32[]{:S(2)}, u32[]{:S(2)}) collective-permute-start(bf16[512,1024]{1,0:T(8,128)(2,1)} %get-tuple-element.544), channel_id=1, source_target_pairs={{0,1},{1,0},{2,3},{3,2},{4,5},{5,4},{6,7},{7,6},{8,9},{9,8},{10,11... | collective-permute-start | bytes 3145736 | tf_op jit(solution)/shard_map/ppermute | solution.py:381
  482.6 52.9 %collective-permute-start.40 = (bf16[2,2,512,1024]{3,2,1,0:T(8,128)(2,1)}, bf16[2,2,512,1024]{3,2,1,0:T(8,128)(2,1)}, u32[]{:S(2)}, u32[]{:S(2)}) collective-permute-start(bf16[2,2,512,1024]{3,2,1,0:T(8,128)(2,1)} %get-tuple-element.405), channel_id=1, source_target_pairs={{0,2},{2,0},{4,6},{6,4},{8,10},{10,8},{12,14},{14,12},{16,18},{18,... | collective-permute-start | bytes 12582920 | tf_op jit(solution)/shard_map/ppermute | solution.py:373
  482.6 50.4 %collective-permute-start.42 = (bf16[2,512,1024]{2,1,0:T(8,128)(2,1)}, bf16[2,512,1024]{2,1,0:T(8,128)(2,1)}, u32[]{:S(2)}, u32[]{:S(2)}) collective-permute-start(bf16[2,512,1024]{2,1,0:T(8,128)(2,1)} %pad_maximum_fusion.1), channel_id=1, source_target_pairs={{0,8},{2,10},{4,12},{6,14},{8,16},{10,18},{12,20},{14,22},{16,24},... | collective-permute-start | bytes 6291464 | tf_op jit(solution)/shard_map/ppermute | solution.py:377
  535.6 35.3 %collective-permute-start.43 = (bf16[2,2,512,1024]{3,2,1,0:T(8,128)(2,1)}, bf16[2,2,512,1024]{3,2,1,0:T(8,128)(2,1)}, u32[]{:S(2)}, u32[]{:S(2)}) collective-permute-start(bf16[2,2,512,1024]{3,2,1,0:T(8,128)(2,1)} %get-tuple-element.421), channel_id=1, source_target_pairs={{0,2},{2,0},{4,6},{6,4},{8,10},{10,8},{12,14},{14,12},{16,18},{18,... | collective-permute-start | bytes 12582920 | tf_op jit(solution)/shard_map/ppermute | solution.py:373
  570.8 58.3 %collective-permute-start.48 = (bf16[2,2,512,1024]{3,2,1,0:T(8,128)(2,1)}, bf16[2,2,512,1024]{3,2,1,0:T(8,128)(2,1)}, u32[]{:S(2)}, u32[]{:S(2)}) collective-permute-start(bf16[2,2,512,1024]{3,2,1,0:T(8,128)(2,1)} %get-tuple-element.451), channel_id=1, source_target_pairs={{0,2},{2,0},{4,6},{6,4},{8,10},{10,8},{12,14},{14,12},{16,18},{18,... | collective-permute-start | bytes 12582920 | tf_op jit(solution)/shard_map/ppermute | solution.py:373
  571.1 58.0 %collective-permute-start.49 = (bf16[2,2,512,1024]{3,2,1,0:T(8,128)(2,1)}, bf16[2,2,512,1024]{3,2,1,0:T(8,128)(2,1)}, u32[]{:S(2)}, u32[]{:S(2)}) collective-permute-start(bf16[2,2,512,1024]{3,2,1,0:T(8,128)(2,1)} %get-tuple-element.452), channel_id=1, source_target_pairs={{0,2},{2,0},{4,6},{6,4},{8,10},{10,8},{12,14},{14,12},{16,18},{18,... | collective-permute-start | bytes 12582920 | tf_op jit(solution)/shard_map/ppermute | solution.py:373
  571.4 53.9 %collective-permute-start.47 = (bf16[2,512,1024]{2,1,0:T(8,128)(2,1)S(1)}, bf16[2,512,1024]{2,1,0:T(8,128)(2,1)}, u32[]{:S(2)}, u32[]{:S(2)}) collective-permute-start(bf16[2,512,1024]{2,1,0:T(8,128)(2,1)S(1)} %add_convert_fusion.9), channel_id=1, source_target_pairs={{0,8},{2,10},{4,12},{6,14},{8,16},{10,18},{12,20},{14,22},{16,24},... | collective-permute-start | bytes 6291464 | tf_op jit(solution)/shard_map/ppermute | solution.py:377
  572.6 411.9 %all-gather.16.cloned.1.call-start = ((), (), s32[]{:S(2)}) async-start(), calls=%async_computation.4 | async-start | bytes 3342336 | tf_op jit(solution)/shard_map/all_gather | solution.py:861
  575.2 36.9 %collective-permute-start.46 = (bf16[512,1024]{1,0:T(8,128)(2,1)}, bf16[512,1024]{1,0:T(8,128)(2,1)}, u32[]{:S(2)}, u32[]{:S(2)}) collective-permute-start(bf16[512,1024]{1,0:T(8,128)(2,1)} %add_convert_fusion.14), channel_id=1, source_target_pairs={{0,4},{2,6},{4,0},{6,2},{8,12},{10,14},{12,8},{14,10},{16,20},{18,... | collective-permute-start | bytes 3145736 | tf_op jit(solution)/shard_map/ppermute | solution.py:373
  579.8 49.3 %collective-permute-start.45 = (bf16[512,1024]{1,0:T(8,128)(2,1)}, bf16[512,1024]{1,0:T(8,128)(2,1)}, u32[]{:S(2)}, u32[]{:S(2)}) collective-permute-start(bf16[512,1024]{1,0:T(8,128)(2,1)} %get-tuple-element.540), channel_id=1, source_target_pairs={{0,1},{1,0},{2,3},{3,2},{4,5},{5,4},{6,7},{7,6},{8,9},{9,8},{10,11... | collective-permute-start | bytes 3145736 | tf_op jit(solution)/shard_map/ppermute | solution.py:381
  629.1 80.6 %collective-permute-start.52 = (bf16[2,2,512,1024]{3,2,1,0:T(8,128)(2,1)}, bf16[2,2,512,1024]{3,2,1,0:T(8,128)(2,1)}, u32[]{:S(2)}, u32[]{:S(2)}) collective-permute-start(bf16[2,2,512,1024]{3,2,1,0:T(8,128)(2,1)} %get-tuple-element.467), channel_id=1, source_target_pairs={{0,2},{2,0},{4,6},{6,4},{8,10},{10,8},{12,14},{14,12},{16,18},{18,... | collective-permute-start | bytes 12582920 | tf_op jit(solution)/shard_map/ppermute | solution.py:373
  629.2 80.5 %collective-permute-start.53 = (bf16[2,2,512,1024]{3,2,1,0:T(8,128)(2,1)}, bf16[2,2,512,1024]{3,2,1,0:T(8,128)(2,1)}, u32[]{:S(2)}, u32[]{:S(2)}) collective-permute-start(bf16[2,2,512,1024]{3,2,1,0:T(8,128)(2,1)} %get-tuple-element.470), channel_id=1, source_target_pairs={{0,2},{2,0},{4,6},{6,4},{8,10},{10,8},{12,14},{14,12},{16,18},{18,... | collective-permute-start | bytes 12582920 | tf_op jit(solution)/shard_map/ppermute | solution.py:373
  629.7 77.2 %collective-permute-start.51 = (bf16[2,512,1024]{2,1,0:T(8,128)(2,1)}, bf16[2,512,1024]{2,1,0:T(8,128)(2,1)}, u32[]{:S(2)}, u32[]{:S(2)}) collective-permute-start(bf16[2,512,1024]{2,1,0:T(8,128)(2,1)} %add_convert_fusion.8), channel_id=1, source_target_pairs={{0,8},{2,10},{4,12},{6,14},{8,16},{10,18},{12,20},{14,22},{16,24},... | collective-permute-start | bytes 6291464 | tf_op jit(solution)/shard_map/ppermute | solution.py:377
  634.1 75.6 %collective-permute-start.54 = (bf16[2,512,1024]{2,1,0:T(8,128)(2,1)}, bf16[2,512,1024]{2,1,0:T(8,128)(2,1)}, u32[]{:S(2)}, u32[]{:S(2)}) collective-permute-start(bf16[2,512,1024]{2,1,0:T(8,128)(2,1)} %fusion.26), channel_id=1, source_target_pairs={{0,4},{2,6},{4,0},{6,2},{8,12},{10,14},{12,8},{14,10},{16,20},{18,... | collective-permute-start | bytes 6291464 | tf_op jit(solution)/shard_map/ppermute | solution.py:373
  636.1 68.4 %collective-permute-start.50 = (bf16[512,1024]{1,0:T(8,128)(2,1)S(1)}, bf16[512,1024]{1,0:T(8,128)(2,1)}, u32[]{:S(2)}, u32[]{:S(2)}) collective-permute-start(bf16[512,1024]{1,0:T(8,128)(2,1)S(1)} %add_convert_fusion.12), channel_id=1, source_target_pairs={{0,4},{2,6},{4,0},{6,2},{8,12},{10,14},{12,8},{14,10},{16,20},{18,... | collective-permute-start | bytes 3145736 | tf_op jit(solution)/shard_map/ppermute | solution.py:373
  715.8 46.4 %collective-permute-start.60 = (bf16[2,512,1024]{2,1,0:T(8,128)(2,1)}, bf16[2,512,1024]{2,1,0:T(8,128)(2,1)S(1)}, u32[]{:S(2)}, u32[]{:S(2)}) collective-permute-start(bf16[2,512,1024]{2,1,0:T(8,128)(2,1)} %fusion.27), channel_id=1, source_target_pairs={{0,4},{2,6},{4,0},{6,2},{8,12},{10,14},{12,8},{14,10},{16,20},{18,... | collective-permute-start | bytes 6291464 | tf_op jit(solution)/shard_map/ppermute | solution.py:373
  721.2 48.2 %collective-permute-start.59 = (bf16[2,512,1024]{2,1,0:T(8,128)(2,1)}, bf16[2,512,1024]{2,1,0:T(8,128)(2,1)}, u32[]{:S(2)}, u32[]{:S(2)}) collective-permute-start(bf16[2,512,1024]{2,1,0:T(8,128)(2,1)} %fusion.12), channel_id=1, source_target_pairs={{0,8},{2,10},{4,12},{6,14},{8,16},{10,18},{12,20},{14,22},{16,24},... | collective-permute-start | bytes 6291464 | tf_op jit(solution)/shard_map/ppermute | solution.py:377
  789.2 45.3 %collective-permute-start.62 = (bf16[2,512,1024]{2,1,0:T(8,128)(2,1)}, bf16[2,512,1024]{2,1,0:T(8,128)(2,1)}, u32[]{:S(2)}, u32[]{:S(2)}) collective-permute-start(bf16[2,512,1024]{2,1,0:T(8,128)(2,1)} %fusion.28), channel_id=1, source_target_pairs={{0,4},{2,6},{4,0},{6,2},{8,12},{10,14},{12,8},{14,10},{16,20},{18,... | collective-permute-start | bytes 6291464 | tf_op jit(solution)/shard_map/ppermute | solution.py:373
  790.8 46.8 %collective-permute-start.61 = (bf16[2,512,1024]{2,1,0:T(8,128)(2,1)}, bf16[2,512,1024]{2,1,0:T(8,128)(2,1)}, u32[]{:S(2)}, u32[]{:S(2)}) collective-permute-start(bf16[2,512,1024]{2,1,0:T(8,128)(2,1)} %add_convert_fusion.4), channel_id=1, source_target_pairs={{0,8},{2,10},{4,12},{6,14},{8,16},{10,18},{12,20},{14,22},{16,24},... | collective-permute-start | bytes 6291464 | tf_op jit(solution)/shard_map/ppermute | solution.py:377
  877.1 112.2 %all-gather.18.cloned.1.call-start = ((), (), s32[]{:S(2)}) async-start(), calls=%async_computation.5 | async-start | bytes 3342336 | tf_op jit(solution)/shard_map/all_gather | solution.py:862
  881.9 53.5 %collective-permute-start.65 = (bf16[2,512,1024]{2,1,0:T(8,128)(2,1)}, bf16[2,512,1024]{2,1,0:T(8,128)(2,1)}, u32[]{:S(2)}, u32[]{:S(2)}) collective-permute-start(bf16[2,512,1024]{2,1,0:T(8,128)(2,1)} %fusion.29), channel_id=1, source_target_pairs={{0,4},{2,6},{4,0},{6,2},{8,12},{10,14},{12,8},{14,10},{16,20},{18,... | collective-permute-start | bytes 6291464 | tf_op jit(solution)/shard_map/ppermute | solution.py:373
  891.5 66.9 %collective-permute-start.64 = (bf16[2,512,1024]{2,1,0:T(8,128)(2,1)S(1)}, bf16[2,512,1024]{2,1,0:T(8,128)(2,1)S(1)}, u32[]{:S(2)}, u32[]{:S(2)}) collective-permute-start(bf16[2,512,1024]{2,1,0:T(8,128)(2,1)S(1)} %copy-done.52), channel_id=1, source_target_pairs={{0,8},{2,10},{4,12},{6,14},{8,16},{10,18},{12,20},{14,22},{16,24},... | collective-permute-start | bytes 6291464 | tf_op jit(solution)/shard_map/ppermute | solution.py:377
  (149 other events, 2392.6 us)
Sparse Core Ops, SparseCore 0:
  35.3 215.5 all-gather.11
  259.2 66.7 all-gather.9
  572.7 73.8 all-gather.13
  877.2 58.2 all-gather.15
  938.2 44.4 all-gather.17

commit v3 on v2

v3 whole, which is shorter than its diff:
```python
import functools

import jax
import jax.numpy as jnp
from jax import lax
from jax.experimental import pallas as pl
from jax.experimental.pallas import tpu as pltpu
from jax.sharding import PartitionSpec as P

MODEL_WIDTH = 2048
HEAD_WIDTH = 128
TOP = 8
LEN = 512
ADAPTER_RANK = 16
ADAPTER_CHOICES = 8
QUAD = 4

norm_eps = 1e-05
head_eps = 1e-06
rope_base = 50000.0
half_type = jnp.bfloat16
VMEM_LIMIT = 56 * 1024 * 1024


def rotation(positions):
    half_dim = HEAD_WIDTH // 2
    inverse = rope_base ** (-(jnp.arange(half_dim, dtype=jnp.float32) * 2.0 / HEAD_WIDTH))
    angles = positions.astype(jnp.float32)[:, None] * inverse[None, :]
    cosine, sine = jnp.cos(angles), jnp.sin(angles)
    return (
        jnp.concatenate([cosine, cosine], axis=1),
        jnp.concatenate([-sine, sine], axis=1),
    )


def nt_dot(left, right):
    return lax.dot_general(
        left, right, (((1,), (1,)), ((), ())), preferred_element_type=jnp.float32
    )


def tn_dot(left, right):
    return lax.dot_general(
        left, right, (((0,), (0,)), ((), ())), preferred_element_type=jnp.float32
    )


def head_prep(raw, gain, cosine, sine):
    scale = lax.rsqrt(jnp.mean(raw * raw, axis=-1, keepdims=True) + head_eps)
    scaled = raw * scale * gain
    return scaled * cosine + pltpu.roll(scaled, HEAD_WIDTH // 2, 1) * sine


def head_prep_back(grad, raw, gain, cosine, sine):
    scale = lax.rsqrt(jnp.mean(raw * raw, axis=-1, keepdims=True) + head_eps)
    turned = (grad * cosine - pltpu.roll(grad, HEAD_WIDTH // 2, 1) * sine) * gain
    along = jnp.mean(raw * turned, axis=-1, keepdims=True)
    return scale * turned - raw * (scale * scale * scale * along)


def masked_exp(queries, keys, docs_col, docs_row):
    scores = nt_dot(queries, keys) * HEAD_WIDTH ** (-0.5)
    scores = jnp.where(docs_col == docs_row, scores, -1e30)
    exp_scores = jnp.exp(scores - jnp.max(scores, axis=-1, keepdims=True))
    return exp_scores, jnp.sum(exp_scores, axis=-1, keepdims=True)


def attend_kernel(
    raw_q, raw_k, raw_v, cosine, sine, gain_q, gain_k, docs_col, docs_row, out, queries, keys, values
):
    q = head_prep(raw_q[...], gain_q[...], cosine[...], sine[...]).astype(half_type)
    k = head_prep(raw_k[...], gain_k[...], cosine[...], sine[...]).astype(half_type)
    v = raw_v[...].astype(half_type)
    queries[...], keys[...], values[...] = q, k, v
    exp_scores, total = masked_exp(q, k, docs_col[...], docs_row[...])
    probs = (exp_scores / total).astype(half_type)
    out[...] = jnp.dot(probs, v, preferred_element_type=jnp.float32).astype(half_type)


def attend_back_kernel(
    raw_q, raw_k, queries, keys, values, grad, cosine, sine, gain_q, gain_k, docs_col, docs_row,
    grad_q, grad_k, grad_v,
):
    q, k, v, g = queries[...], keys[...], values[...], grad[...]
    score_scale = HEAD_WIDTH ** (-0.5)
    exp_scores, total = masked_exp(q, k, docs_col[...], docs_row[...])
    probs = exp_scores / total
    grad_v[...] = tn_dot(probs.astype(half_type), g).astype(half_type)
    grad_probs = nt_dot(g, v)
    delta = jnp.sum(probs * grad_probs, axis=-1, keepdims=True)
    grad_scores = (probs * (grad_probs - delta)).astype(half_type)
    d_q = jnp.dot(grad_scores, k, preferred_element_type=jnp.float32) * score_scale
    d_k = tn_dot(grad_scores, q) * score_scale
    grad_q[...] = head_prep_back(d_q, raw_q[...], gain_q[...], cosine[...], sine[...]).astype(
        half_type
    )
    grad_k[...] = head_prep_back(d_k, raw_k[...], gain_k[...], cosine[...], sine[...]).astype(
        half_type
    )


def call_heads(kernel, name, by_head, shared, out_count):
    toks, width = by_head[0].shape
    head = pl.BlockSpec((toks, HEAD_WIDTH), lambda h: (0, h))
    return pl.pallas_call(
        kernel,
        out_shape=[jax.ShapeDtypeStruct((toks, width), half_type)] * out_count,
        grid=(width // HEAD_WIDTH,),
        in_specs=[head] * len(by_head)
        + [pl.BlockSpec(v.shape, lambda h: (0, 0)) for v in shared],
        out_specs=[head] * out_count,
        compiler_params=pltpu.CompilerParams(
            dimension_semantics=("arbitrary",), vmem_limit_bytes=VMEM_LIMIT
        ),
        cost_estimate=pl.CostEstimate(
            flops=10 * toks * toks * width, bytes_accessed=8 * toks * width, transcendentals=toks * toks
        ),
        name=name,
    )(*by_head, *shared)


def start_blocks(pieces, buffer_ref, sems, flip):
    for b in range(QUAD):
        for r in range(2):
            pltpu.make_async_copy(
                pieces[2 * b + r], buffer_ref.at[b, r ^ flip], sems.at[b, r]
            ).start()


def wait_block(pieces, buffer_ref, sems, b):
    for r in range(2):
        pltpu.make_async_copy(pieces[0], buffer_ref.at[b, r], sems.at[b, r]).wait()


def pick_rows(place_ref, half_at, rows_ref, b, experts, cap, tile):
    toks = half_at(0).shape[0]
    slot = lax.broadcasted_iota(jnp.int32, (cap, toks), 0)
    picks = jnp.concatenate(
        [jnp.where(slot == place_ref[b, e], 1.0, 0.0) for e in range(experts)], axis=0
    ).astype(half_type)
    half = rows_ref.shape[4]
    for h in range(rows_ref.shape[1]):
        for start in range(0, half, tile):
            rows = jnp.dot(
                picks,
                half_at(h)[:, start : start + tile],
                preferred_element_type=jnp.float32,
            ).astype(half_type)
            for e in range(experts):
                rows_ref[e, h, b, :, start : start + tile] = rows[e * cap : (e + 1) * cap]


def add_rows(target_ref, rows_ref, out_ref, b, flip, experts, cap, tile):
    target = target_ref[b]
    toks = target.shape[0]
    lane = lax.broadcasted_iota(jnp.int32, (toks, experts * cap), 1)
    hit = lane == target[:, 0:1]
    for e in range(1, experts):
        hit = jnp.logical_or(hit, lane == target[:, e : e + 1])
    spread = jnp.where(hit, 1.0, 0.0).astype(half_type)
    half = rows_ref.shape[4]
    for h in range(2):
        for start in range(0, half, tile):
            rows = jnp.concatenate(
                [rows_ref[e, h, b, :, start : start + tile] for e in range(experts)], axis=0
            )
            out_ref[0, h ^ flip, :toks, start : start + tile] = jnp.dot(
                spread, rows, preferred_element_type=jnp.float32
            ).astype(half_type)


def add_gates(dgate_ref, out_ref, b, device, experts):
    toks, half = dgate_ref.shape[3], out_ref.shape[3]
    extra = out_ref.shape[2] - toks
    per_row = half // toks
    row = lax.broadcasted_iota(jnp.int32, (extra, half), 0)
    values = jnp.zeros((extra, half), jnp.float32)
    for i in range(experts // per_row):
        line = jnp.concatenate(
            [dgate_ref[i * per_row + n, b] for n in range(per_row)], axis=1
        )
        values = jnp.where(row == device * (experts // per_row) + i, line, values)
    for h in range(2):
        out_ref[0, h, toks:, :] = values.astype(half_type)


def grad_rows_kernel(experts, cap, block_ids, place_ref, down_ref, block_ref, out_ref, rows_ref):
    step = pl.program_id(0)
    sides, blocks, part = rows_ref.shape[1], rows_ref.shape[2], rows_ref.shape[4]

    @pl.when(step < blocks)
    def _():
        pick_rows(
            place_ref,
            lambda h: block_ref.at[0, h],
            rows_ref,
            step,
            experts,
            cap,
            min(part, 512),
        )

    @pl.when(step >= blocks)
    def _():
        e = step - blocks
        total = nt_dot(rows_ref[e, 0].reshape(blocks * cap, part), down_ref[0, :, :part])
        for h in range(1, sides):
            total += nt_dot(
                rows_ref[e, h].reshape(blocks * cap, part),
                down_ref[0, :, h * part : (h + 1) * part],
            )
        out_ref[0] = total.astype(half_type)


def expert_kernel(
    experts,
    cap,
    flip_ref,
    place_ref,
    gate_ref,
    target_ref,
    wg_ref,
    wu_ref,
    dh_ref,
    own_first_ref,
    own_second_ref,
    core_first_ref,
    core_second_ref,
    across_first_ref,
    across_second_ref,
    far_first_ref,
    far_second_ref,
    send_ref,
    keep_ref,
    hidden_ref,
    buffer_ref,
    rows_ref,
    dgate_ref,
    sems,
):
    block_refs = [
        own_first_ref,
        own_second_ref,
        core_first_ref,
        core_second_ref,
        across_first_ref,
        across_second_ref,
        far_first_ref,
        far_second_ref,
    ]
    step = pl.program_id(0)
    half = buffer_ref.shape[3]
    toks = buffer_ref.shape[2]

    @pl.when(step == 0)
    def _():
        start_blocks(block_refs, buffer_ref, sems, flip_ref[0])

    @pl.when(step < QUAD)
    def _():
        wait_block(block_refs, buffer_ref, sems, step)
        pick_rows(
            place_ref, lambda h: buffer_ref.at[step, h], rows_ref, step, experts, cap, 512
        )

    @pl.when(jnp.logical_and(step >= QUAD, step < QUAD + experts))
    def _():
        e = step - QUAD
        first = rows_ref[e, 0].reshape(QUAD * cap, half)
        second = rows_ref[e, 1].reshape(QUAD * cap, half)
        pre_gate = jnp.dot(first, wg_ref[0, :half], preferred_element_type=jnp.float32)
        pre_gate += jnp.dot(second, wg_ref[0, half:], preferred_element_type=jnp.float32)
        pre_up = jnp.dot(first, wu_ref[0, :half], preferred_element_type=jnp.float32)
        pre_up += jnp.dot(second, wu_ref[0, half:], preferred_element_type=jnp.float32)
        sig = lax.logistic(pre_gate)
        silu = pre_gate * sig
        act = silu * pre_up
        d_raw = dh_ref[0].astype(jnp.float32)
        slot = lax.broadcasted_iota(jnp.int32, (cap, toks), 0)
        gate_parts = []
        for b in range(QUAD):
            hit = slot == place_ref[b, e]
            gate_parts.append(
                jnp.sum(jnp.where(hit, gate_ref[b, e], 0.0), axis=1, keepdims=True)
            )
        gate_col = jnp.concatenate(gate_parts, axis=0)
        hidden_ref[0] = (act * gate_col).astype(half_type)
        d_col = jnp.sum(act * d_raw, axis=1, keepdims=True)
        for b in range(QUAD):
            hit = slot == place_ref[b, e]
            dgate_ref[e, b] = jnp.sum(
                jnp.where(hit, d_col[b * cap : (b + 1) * cap], 0.0), axis=0, keepdims=True
            )
        d_hidden = d_raw * gate_col
        d_up = (d_hidden * silu).astype(half_type)
        d_gate = (d_hidden * pre_up * (sig * (1.0 + pre_gate * (1.0 - sig)))).astype(half_type)
        for h in range(2):
            d_in = nt_dot(d_gate, wg_ref[0, h * half : (h + 1) * half])
            d_in += nt_dot(d_up, wu_ref[0, h * half : (h + 1) * half])
            rows_ref[e, h] = d_in.astype(half_type).reshape(QUAD, cap, half)

    for which, out_ref in ((0, send_ref), (1, keep_ref)):
        first_step = QUAD + experts + 2 * which

        @pl.when(jnp.logical_and(step >= first_step, step < first_step + 2))
        def _():
            b = 2 * (step - first_step) + 1 - which
            add_rows(target_ref, rows_ref, out_ref, b, flip_ref[0], experts, cap, 512)
            add_gates(dgate_ref, out_ref, b, flip_ref[1], experts)


def output_kernel(experts, cap, flip_ref, target_ref, down_ref, hidden_ref, send_ref, keep_ref, rows_ref):
    step = pl.program_id(0)
    half = rows_ref.shape[4]

    @pl.when(step < experts)
    def _():
        for h in range(2):
            out = jnp.dot(
                hidden_ref[0],
                down_ref[0, :, h * half : (h + 1) * half],
                preferred_element_type=jnp.float32,
            )
            rows_ref[step, h] = out.astype(half_type).reshape(QUAD, cap, half)

    for which, out_ref in ((0, send_ref), (1, keep_ref)):
        first_step = experts + 2 * which

        @pl.when(jnp.logical_and(step >= first_step, step < first_step + 2))
        def _():
            b = 2 * (step - first_step) + 1 - which
            add_rows(target_ref, rows_ref, out_ref, b, flip_ref[0], experts, cap, 512)


def whole(shape):
    return pl.BlockSpec(shape, lambda i, *_: (0,) * len(shape), pipeline_mode=pl.Buffered(1))


def per_step(shape, first, count):
    return pl.BlockSpec(
        (1,) + shape[1:], lambda i, *_: (jnp.clip(i - first, 0, count - 1),) + (0,) * (len(shape) - 1)
    )


def call_grad_rows(block_ids, place, down, blocks, cap):
    experts, hidden_units, width = down.shape
    count, sides, toks, half = blocks.shape
    rows = count * cap
    return pl.pallas_call(
        functools.partial(grad_rows_kernel, experts, cap),
        out_shape=jax.ShapeDtypeStruct((experts, rows, hidden_units), half_type),
        grid_spec=pltpu.PrefetchScalarGridSpec(
            num_scalar_prefetch=1,
            grid=(count + experts,),
            in_specs=[
                whole(place.shape),
                per_step(down.shape, count, experts),
                pl.BlockSpec(
                    (1, sides, toks, half),
                    lambda i, ids: (ids[jnp.minimum(i, count - 1)], 0, 0, 0),
                ),
            ],
            out_specs=per_step((experts, rows, hidden_units), count, experts),
            scratch_shapes=[pltpu.VMEM((experts, sides, count, cap, half), half_type)],
        ),
        compiler_params=pltpu.CompilerParams(
            dimension_semantics=("arbitrary",), vmem_limit_bytes=VMEM_LIMIT
        ),
        cost_estimate=pl.CostEstimate(
            flops=4 * experts * rows * width * (toks + hidden_units),
            bytes_accessed=2 * (down.size + blocks.size + experts * rows * hidden_units),
            transcendentals=0,
        ),
        name="grad_rows",
    )(block_ids, place, down, blocks)


def call_experts(group, flip, place, gate, target, gate_w, up_w, d_raw, pieces, cap, extra):
    experts, width, hidden_units = gate_w.shape
    toks, half = pieces[0].shape
    rows = QUAD * cap
    blocks = (2, 2, toks + extra, half)
    return pl.pallas_call(
        functools.partial(expert_kernel, experts, cap),
        out_shape=(
            jax.ShapeDtypeStruct(blocks, half_type),
            jax.ShapeDtypeStruct(blocks, half_type),
            jax.ShapeDtypeStruct((experts, rows, hidden_units), half_type),
        ),
        grid_spec=pltpu.PrefetchScalarGridSpec(
            num_scalar_prefetch=1,
            grid=(2 * QUAD + experts,),
            in_specs=[
                whole(place.shape),
                whole(gate.shape),
                whole(target.shape),
                per_step(gate_w.shape, QUAD, experts),
                per_step(up_w.shape, QUAD, experts),
                pl.BlockSpec(
                    (1, rows, hidden_units),
                    lambda i, *_: (jnp.clip(i - QUAD, 0, experts - 1), group, 0),
                ),
            ]
            + [pl.BlockSpec(memory_space=pl.ANY)] * len(pieces),
            out_specs=(
                per_step(blocks, QUAD + experts, 2),
                per_step(blocks, QUAD + experts + 2, 2),
                per_step((experts, rows, hidden_units), QUAD, experts),
            ),
            scratch_shapes=[
                pltpu.VMEM((QUAD, 2, toks, half), half_type),
                pltpu.VMEM((experts, 2, QUAD, cap, half), half_type),
                pltpu.VMEM((experts, QUAD, 1, toks), jnp.float32),
                pltpu.SemaphoreType.DMA((QUAD, 2)),
            ],
        ),
        compiler_params=pltpu.CompilerParams(
            dimension_semantics=("arbitrary",), vmem_limit_bytes=VMEM_LIMIT
        ),
        cost_estimate=pl.CostEstimate(
            flops=6 * experts * rows * width * (toks + 2 * hidden_units),
            bytes_accessed=2 * (2 * gate_w.size + 4 * QUAD * toks * half),
            transcendentals=experts * rows * hidden_units,
        ),
        name="experts",
    )(flip, place, gate, target, gate_w, up_w, d_raw, *pieces)


def call_output(flip, target, down, hidden, cap, half):
    experts, hidden_units, width = down.shape
    toks = target.shape[1]
    rows = QUAD * cap
    blocks = (2, 2, toks, half)
    return pl.pallas_call(
        functools.partial(output_kernel, experts, cap),
        out_shape=(
            jax.ShapeDtypeStruct(blocks, half_type),
            jax.ShapeDtypeStruct(blocks, half_type),
        ),
        grid_spec=pltpu.PrefetchScalarGridSpec(
            num_scalar_prefetch=1,
            grid=(QUAD + experts,),
            in_specs=[
                whole(target.shape),
                per_step(down.shape, 0, experts),
                per_step(hidden.shape, 0, experts),
            ],
            out_specs=(per_step(blocks, experts, 2), per_step(blocks, experts + 2, 2)),
            scratch_shapes=[pltpu.VMEM((experts, 2, QUAD, cap, half), half_type)],
        ),
        compiler_params=pltpu.CompilerParams(
            dimension_semantics=("arbitrary",), vmem_limit_bytes=VMEM_LIMIT
        ),
        cost_estimate=pl.CostEstimate(
            flops=4 * experts * rows * width * (toks + hidden_units),
            bytes_accessed=2 * (down.size + 2 * QUAD * toks * half),
            transcendentals=0,
        ),
        name="outputs",
    )(flip, target, down, hidden)


def swap(values, data_count, bit):
    return lax.ppermute(values, "dp", [(i, i ^ bit) for i in range(data_count)])


def onward(values, data_count):
    return lax.ppermute(values, "dp", [(i, (i + QUAD) % data_count) for i in range(data_count)])


def other_side(values):
    return lax.ppermute(values, "tensor", [(0, 1), (1, 0)])


def fence(*values):
    return lax.optimization_barrier(values)


def plus(*terms):
    total = terms[0].astype(jnp.float32)
    for term in terms[1:]:
        total = total + term.astype(jnp.float32)
    return total.astype(half_type)


def local(
    layer_input,
    cotangent,
    attention_norm_gain,
    expert_norm_gain,
    query_norm_gain,
    key_norm_gain,
    query_weight_matrix,
    key_weight_matrix,
    value_weight_matrix,
    output_weight_matrix,
    adapter_projection_down,
    adapter_projection_up,
    adapter_output_down,
    adapter_output_up,
    router,
    expert_gate_weight,
    expert_up_weight,
    expert_down_weight,
    segments,
    sequence_adapter_index,
    routes,
):
    tok_count = layer_input.shape[0]
    tensor_count = lax.axis_size("tensor")
    data_count = lax.axis_size("dp")
    pair = tensor_count == 2
    ring_count = data_count // QUAD
    col_width = MODEL_WIDTH // tensor_count
    half_width = MODEL_WIDTH // 2
    side = lax.axis_index("tensor")
    col_start = side * col_width
    place_dp = lax.axis_index("dp")
    flip = side.astype(jnp.int32) if pair else jnp.int32(0)
    flip_arr = jnp.stack([flip, place_dp.astype(jnp.int32)])
    shard_local_width = query_weight_matrix.shape[1]
    local_experts = expert_gate_weight.shape[0]
    expert_total = local_experts * data_count
    capacity = 5 * tok_count * TOP // (4 * expert_total)
    token_ids = jnp.arange(tok_count, dtype=jnp.int32)
    positions = token_ids % LEN

    def to_sides(full):
        if pair:
            low_cols, high_cols = full[:, :half_width], full[:, half_width:]
            return (
                jnp.where(flip == 0, low_cols, high_cols),
                jnp.where(flip == 0, high_cols, low_cols),
            )
        return full[:, :half_width], full[:, half_width:]

    def from_sides(first, second):
        if pair:
            return jnp.concatenate(
                [jnp.where(flip == 0, first, second), jnp.where(flip == 0, second, first)], axis=1
            )
        return jnp.concatenate([first, second], axis=1)

    routes_t = routes.T
    expert_ids = jnp.arange(expert_total, dtype=jnp.int32)
    chosen_mask = jnp.any(routes_t[:, None, :] == expert_ids[None, :, None], axis=0)
    earlier = (token_ids[:, None] < token_ids[None, :]).astype(half_type)
    rank = jnp.dot(chosen_mask.astype(half_type), earlier, preferred_element_type=jnp.float32)
    place_own = jnp.where(chosen_mask, rank, -1.0).astype(jnp.int32)
    number = jnp.broadcast_to(sequence_adapter_index[:1, None], (data_count, 1, tok_count))
    place_own = jnp.concatenate(
        [place_own.reshape(data_count, local_experts, tok_count), number], axis=1
    )
    place_all = lax.all_to_all(place_own, "dp", 0, 0, tiled=True)
    numbers = place_all[:, local_experts, 0]
    place_all = place_all[:, :local_experts]
    ring_at, quad_at = place_dp // QUAD, place_dp % QUAD
    group_ids = jnp.arange(data_count, dtype=jnp.int32)
    order = ((ring_at - group_ids // QUAD) % ring_count) * QUAD + (quad_at ^ (group_ids % QUAD))
    place_all = place_all[order]
    target_all = jnp.where(
        place_all >= 0,
        place_all + capacity * jnp.arange(local_experts, dtype=jnp.int32)[None, :, None],
        -1,
    ).transpose(0, 2, 1)

    def group_of(values, j):
        return values[j * QUAD : (j + 1) * QUAD]

    adapter = sequence_adapter_index[0]

    def own_adapter(factors, axis):
        return lax.dynamic_index_in_dim(factors, adapter, axis, keepdims=False)

    down_rows = own_adapter(adapter_projection_down.transpose(0, 1, 3, 2), 1)
    down_rows = down_rows.reshape(3 * ADAPTER_RANK, MODEL_WIDTH)
    up_rows = own_adapter(adapter_projection_up, 1)
    out_down_rows = own_adapter(adapter_output_down.transpose(0, 2, 1), 0)
    out_up_rows = own_adapter(adapter_output_up, 0)
    doc_flat = segments.reshape(-1)
    hidden32 = layer_input.astype(jnp.float32)
    hidden_scale = lax.rsqrt(
        jnp.mean(hidden32 * hidden32, axis=-1, keepdims=True) + norm_eps
    )
    normed = (hidden32 * hidden_scale * attention_norm_gain).astype(half_type)
    w_proj = [query_weight_matrix, key_weight_matrix, value_weight_matrix]
    latents = nt_dot(normed, down_rows).astype(half_type)
    latents = [latents[:, p * ADAPTER_RANK : (p + 1) * ADAPTER_RANK] for p in range(3)]
    raw_proj = [
        jnp.dot(normed, w_proj[p], preferred_element_type=jnp.float32)
        + jnp.dot(latents[p], up_rows[p], preferred_element_type=jnp.float32)
        for p in range(3)
    ]
    g_all = lax.all_gather(cotangent, ("dp", "tensor"), axis=0)
    g_all = g_all.reshape(data_count, tensor_count, tok_count, col_width)
    raw_proj[0], place_all, target_all = fence(raw_proj[0], place_all, target_all)
    head_shared = [
        *rotation(positions),
        query_norm_gain[None, :],
        key_norm_gain[None, :],
        doc_flat[:, None],
        doc_flat[None, :],
    ]
    attended, queries, keys, values = call_heads(
        attend_kernel, "attend", raw_proj, head_shared, 4
    )
    proj_part = jnp.dot(attended, output_weight_matrix, preferred_element_type=jnp.float32)
    latent_part = nt_dot(attended, out_down_rows)

    def tensor_sum(part):
        if pair:
            return part.astype(jnp.float32) + other_side(part).astype(jnp.float32)
        return lax.psum(part, "tensor").astype(jnp.float32)

    def split_columns(part):
        if pair:
            mine, theirs = to_sides(part)
            return mine.astype(jnp.float32), theirs.astype(half_type)
        return None, part.astype(half_type)

    def join_columns(mine, theirs):
        if pair:
            return mine + other_side(theirs).astype(jnp.float32)
        return lax.psum_scatter(theirs, "tensor", scatter_dimension=1, tiled=True).astype(
            jnp.float32
        )

    def own_columns(part):
        return join_columns(*split_columns(part))

    def columns_of(full):
        if pair:
            return to_sides(full)[0]
        return lax.dynamic_slice_in_dim(full, col_start, col_width, full.ndim - 1)

    def both_halves(cols):
        if pair:
            return cols, other_side(cols)
        full = lax.all_gather(cols, "tensor", axis=1, tiled=True)
        return full[:, :half_width], full[:, half_width:]

    attn_cols = own_columns(proj_part)
    latent_total = tensor_sum(latent_part.astype(half_type))
    latent_out = latent_total.astype(half_type)
    mixed_cols = (
        columns_of(layer_input).astype(jnp.float32)
        + attn_cols
        + jnp.dot(latent_out, columns_of(out_up_rows), preferred_element_type=jnp.float32)
    )
    expert_gain_cols = columns_of(expert_norm_gain[None, :])
    square_sum = tensor_sum(jnp.sum(mixed_cols * mixed_cols, axis=1, keepdims=True))
    mixed_scale = lax.rsqrt(square_sum / MODEL_WIDTH + norm_eps)
    moe_cols_in = (mixed_cols * mixed_scale * expert_gain_cols).astype(half_type)

    def gates_of(first, second):
        moe_in = from_sides(first, second)
        logits_t = lax.dot_general(
            router, moe_in, (((0,), (1,)), ((), ())), preferred_element_type=jnp.float32
        )
        top_logit = jnp.max(jnp.where(chosen_mask, logits_t, -jnp.inf), axis=0, keepdims=True)
        gate_exp = jnp.where(chosen_mask, jnp.exp(jnp.minimum(logits_t - top_logit, 0.0)), 0.0)
        return gate_exp / jnp.sum(gate_exp, axis=0, keepdims=True)

    def experts_of(k, pieces):
        return call_experts(
            k,
            flip_arr,
            group_of(place_all, k)[:, :, None, :],
            group_of(gates_all, k)[:, :, None, :],
            group_of(target_all, k),
            expert_gate_weight,
            expert_up_weight,
            d_raw[0],
            pieces,
            capacity,
            expert_total * tok_count // half_width,
        )

    def outputs_of(k, hidden):
        return call_output(
            flip_arr,
            group_of(target_all, k),
            expert_down_weight,
            hidden,
            capacity,
            half_width,
        )

    quads = ring_count
    own0, own1, core0, core1 = ([None] * quads for _ in range(4))
    af, asec, ff, fs = ([None] * quads for _ in range(4))
    d_raw = [None]
    sides_by_tensor = [pair and j != quads - 1 for j in range(quads)]
    hidden = [None] * quads

    def make_sums():
        return {
            name: [None] * quads for name in ("send", "keep", "got", "near", "side_got", "first")
        }

    grads, outs = make_sums(), make_sums()

    def move_first(j):
        own0[j + 1] = onward(own0[j], data_count)

    def move_second(j):
        own1[j + 1] = onward(own1[j], data_count)

    def send_across(j):
        af[j] = swap(own0[j], data_count, 2)
        core0[j] = swap(own0[j], data_count, 1)

    def send_rest(j):
        asec[j] = (
            other_side(af[j]) if sides_by_tensor[j] else swap(own1[j], data_count, 2)
        )
        core1[j] = swap(own1[j], data_count, 1)
        ff[j] = swap(af[j], data_count, 1)

    def send_last(j):
        fs[j] = swap(asec[j], data_count, 1)

    def run_experts(k):
        pieces = [own0[k], own1[k], core0[k], core1[k], af[k], asec[k], ff[k], fs[k]]
        grads["send"][k], grads["keep"][k], hidden[k] = experts_of(k, pieces)

    def run_outputs(k):
        outs["send"][k], outs["keep"][k] = outputs_of(k, hidden[k])

    def sum_cores(sums, k):
        sums["got"][k] = swap(sums["send"][k], data_count, 1)

    def sum_sides(sums, k):
        keep, got = sums["keep"][k], sums["got"][k]
        away = plus(keep[1, 1], got[1, 1])
        sums["side_got"][k] = other_side(away) if pair else swap(away, data_count, 2)
        sums["near"][k] = plus(keep[1, 0], got[1, 0])

    def sum_across(sums, k):
        keep, got, near = sums["keep"][k], sums["got"][k], sums["near"][k]
        if pair:
            near = plus(near, sums["side_got"][k])
        sums["first"][k] = plus(keep[0, 0], got[0, 0], swap(near, data_count, 2))

    def second_of(sums, k):
        terms = [sums["keep"][k][0, 1], sums["got"][k][0, 1]]
        return terms if pair else terms + [sums["side_got"][k]]

    def onward_sum(*terms):
        return onward(plus(*terms), data_count)

    def step_end(*more):
        groups = (
            own0, own1, core0, core1, af, asec, ff, fs, d_raw, hidden,
            *grads.values(), *outs.values(),
        )
        fenced = fence(groups, more)
        for old, fresh in zip(groups, fenced[0]):
            old[:] = fresh
        return fenced[1]

    own0[0] = moe_cols_in if pair else both_halves(moe_cols_in)[0]
    own1[0] = both_halves(moe_cols_in)[1]
    move_first(0)
    send_across(0)
    step_end()
    gates_t = gates_of(own0[0], own1[0])
    move_second(0)
    send_rest(0)
    send_across(1)
    (gates_t,) = step_end(gates_t)
    gates_all = lax.all_to_all(
        gates_t.reshape(data_count, local_experts, tok_count), "dp", 0, 0, tiled=True
    )[order]
    move_first(1)
    send_rest(1)
    send_last(0)
    step_end()
    move_second(1)
    send_across(2)
    send_last(1)
    d_raw[0] = call_grad_rows(
        order, place_all[:, :, None, :], expert_down_weight, g_all, capacity
    )
    (gates_all,) = step_end(gates_all)
    move_first(2)
    send_rest(2)
    run_experts(1)
    step_end()
    move_second(2)
    send_across(3)
    send_last(2)
    sum_cores(grads, 1)
    run_experts(0)
    step_end()
    send_rest(3)
    sum_sides(grads, 1)
    sum_cores(grads, 0)
    run_experts(2)
    step_end()
    send_last(3)
    sum_across(grads, 1)
    sum_sides(grads, 0)
    sum_cores(grads, 2)
    second = onward_sum(*second_of(grads, 1))
    run_experts(3)
    (second,) = step_end(second)
    sum_sides(grads, 2)
    sum_across(grads, 0)
    sum_cores(grads, 3)
    first = onward(grads["first"][1], data_count)
    second = onward_sum(second, *second_of(grads, 2))
    run_outputs(1)
    first, second = step_end(first, second)
    sum_sides(grads, 3)
    sum_across(grads, 2)
    second = onward_sum(second, *second_of(grads, 3))
    sum_cores(outs, 1)
    run_outputs(2)
    first, second = step_end(first, second)
    first = onward_sum(first, grads["first"][2])
    second = plus(second, *second_of(grads, 0))
    sum_across(grads, 3)
    sum_cores(outs, 2)
    sum_sides(outs, 1)
    run_outputs(3)
    first, second = step_end(first, second)
    first = onward_sum(first, grads["first"][3])
    sum_cores(outs, 3)
    sum_across(outs, 1)
    run_outputs(0)
    if pair:
        from_other = other_side(second).astype(jnp.float32)
        grad_moe_cols = first.astype(jnp.float32) + grads["first"][0].astype(jnp.float32) + from_other
    else:
        first = plus(first, grads["first"][0])
        grad_gates = tensor_sum(first[tok_count:])
        grad_moe_cols = own_columns(from_sides(first[:tok_count], second[:tok_count]))
        grad_moe_cols = jnp.pad(grad_moe_cols, ((0, 0), (0, half_width - col_width)))
        grad_moe_cols = jnp.concatenate([grad_moe_cols, grad_gates], axis=0)
    (grad_moe_cols,) = step_end(grad_moe_cols)
    sum_cores(outs, 0)
    sum_sides(outs, 2)
    out_second = onward_sum(*second_of(outs, 1))
    d_gate_home = grad_moe_cols[tok_count:].reshape(expert_total, tok_count)
    grad_moe_cols = grad_moe_cols[:tok_count, :col_width]

    weighted = gates_t * d_gate_home
    grad_logits_t = (
        gates_t * (d_gate_home - jnp.sum(weighted, axis=0, keepdims=True))
    ).astype(half_type)
    router_cols = router.T
    grad_moe_cols = grad_moe_cols + lax.dot_general(
        grad_logits_t,
        columns_of(router_cols),
        (((0,), (0,)), ((), ())),
        preferred_element_type=jnp.float32,
    )
    along = tensor_sum(
        jnp.sum(mixed_cols * expert_gain_cols * grad_moe_cols, axis=1, keepdims=True)
    )
    grad_mixed_cols = (
        cotangent.astype(jnp.float32)
        + expert_gain_cols * mixed_scale * grad_moe_cols
        - mixed_cols * (mixed_scale * mixed_scale * mixed_scale * (along / MODEL_WIDTH))
    )
    branch_cols = grad_mixed_cols.astype(half_type)
    branch_cols, out_second = step_end(branch_cols, out_second)
    sum_across(outs, 2)
    out_second = onward_sum(out_second, *second_of(outs, 2))
    grad_branch = from_sides(*both_halves(branch_cols))
    grad_branch, out_second = step_end(grad_branch, out_second)
    sum_sides(outs, 3)
    out_first = onward(outs["first"][1], data_count)

    grad_latent_out = nt_dot(grad_branch, out_up_rows).astype(half_type)
    grad_up_out = lax.dot_general(
        latent_out, branch_cols, (((0,), (0,)), ((), ())), preferred_element_type=jnp.float32
    )
    grad_attended = nt_dot(grad_branch, output_weight_matrix) + jnp.dot(
        grad_latent_out, out_down_rows, preferred_element_type=jnp.float32
    )
    grad_heads = grad_attended.astype(half_type)
    grad_down_out = lax.dot_general(
        grad_latent_out, attended, (((0,), (0,)), ((), ())), preferred_element_type=jnp.float32
    )

    grad_raw = call_heads(
        attend_back_kernel,
        "attend_back",
        [raw_proj[0], raw_proj[1], queries, keys, values, grad_heads],
        head_shared,
        3,
    )
    grad_raw, out_first = step_end(grad_raw, out_first)
    sum_sides(outs, 0)
    sum_across(outs, 3)
    out_first = onward_sum(out_first, outs["first"][2])
    latent_parts = jnp.concatenate([nt_dot(grad_raw[p], up_rows[p]) for p in range(3)], axis=1)
    grad_latent = tensor_sum(latent_parts.astype(half_type)).astype(half_type)
    grad_up = [
        lax.dot_general(
            latents[p], grad_raw[p], (((0,), (0,)), ((), ())), preferred_element_type=jnp.float32
        )
        for p in range(3)
    ]
    grad_down = lax.dot_general(
        grad_latent, normed, (((0,), (0,)), ((), ())), preferred_element_type=jnp.float32
    )
    parts = [grad_down_out, grad_up_out] + grad_up
    parts += [
        grad_down[:, i * shard_local_width : (i + 1) * shard_local_width]
        for i in range(tensor_count)
    ]
    parts = jnp.concatenate([part.astype(half_type) for part in parts], axis=0)
    parts_all = lax.all_gather(parts, "dp", axis=0)
    holds = numbers[None, :] == jnp.arange(ADAPTER_CHOICES, dtype=jnp.int32)[:, None]
    adapter_sums = jnp.einsum(
        "as,src->arc", holds.astype(half_type), parts_all, preferred_element_type=jnp.float32
    )

    def rows_at(i):
        return adapter_sums[:, i * ADAPTER_RANK : (i + 1) * ADAPTER_RANK]

    sum_up_qkv = jnp.stack([rows_at(2 + p) for p in range(3)])
    sum_down_qkv = jnp.stack(
        [
            jnp.concatenate([rows_at(5 + 3 * i + p) for i in range(tensor_count)], axis=2)
            for p in range(3)
        ]
    ).transpose(0, 1, 3, 2)

    grad_normed_part = nt_dot(grad_raw[0], w_proj[0])
    grad_normed_part += nt_dot(grad_raw[1], w_proj[1])
    grad_normed_part += nt_dot(grad_raw[2], w_proj[2])
    grad_normed_mine, grad_normed_other = split_columns(grad_normed_part)
    grad_normed_other, out_first = step_end(grad_normed_other, out_first)
    sum_across(outs, 0)
    out_second = onward_sum(out_second, *second_of(outs, 3))
    grad_normed_cols = join_columns(grad_normed_mine, grad_normed_other)
    grad_normed_cols, out_second = step_end(grad_normed_cols, out_second)
    out_first = plus(onward_sum(out_first, outs["first"][3]), outs["first"][0])
    out_second = plus(out_second, *second_of(outs, 0))
    if pair:
        moe_cols = out_first.astype(jnp.float32) + other_side(out_second).astype(jnp.float32)
    else:
        moe_cols = own_columns(from_sides(out_first, out_second))
    layer_out = (mixed_cols + moe_cols).astype(half_type)
    grad_normed_cols += jnp.dot(
        grad_latent, columns_of(down_rows), preferred_element_type=jnp.float32
    )
    attention_gain_cols = columns_of(attention_norm_gain[None, :])
    hidden_cols = columns_of(layer_input).astype(jnp.float32)
    along_in = tensor_sum(
        jnp.sum(hidden_cols * attention_gain_cols * grad_normed_cols, axis=1, keepdims=True)
    )
    grad_input = (
        grad_mixed_cols
        + attention_gain_cols * hidden_scale * grad_normed_cols
        - hidden_cols * (hidden_scale * hidden_scale * hidden_scale * (along_in / MODEL_WIDTH))
    )
    return (
        layer_out,
        grad_input,
        sum_down_qkv,
        sum_up_qkv,
        rows_at(0).transpose(0, 2, 1),
        rows_at(1),
    )


def solution(mesh):
    return jax.shard_map(
        local,
        mesh=mesh,
        in_specs=(
            P("dp", None),
            P("dp", "tensor"),
            P(),
            P(),
            P(),
            P(),
            P(None, "tensor"),
            P(None, "tensor"),
            P(None, "tensor"),
            P("tensor", None),
            P(),
            P(None, None, None, "tensor"),
            P(None, "tensor", None),
            P(),
            P(),
            P("dp", None, "tensor"),
            P("dp", None, "tensor"),
            P("dp", "tensor", None),
            P("dp", None),
            P("dp"),
            P("dp", None),
        ),
        out_specs=(
            P("dp", "tensor"),
            P("dp", "tensor"),
            P(),
            P(None, None, None, "tensor"),
            P(None, "tensor", None),
            P(None, None, "tensor"),
        ),
        check_vma=False,
    )
```

time: 1020 us -> 934 us (0.916)
  waiting for transfers between devices: 433 us -> 359 us
  starting transfers between devices: 43.1 us -> 89.5 us
  matrix products: 99.4 us -> 56.1 us
  Pallas kernels: 235 us -> 264 us
  other arithmetic: 126 us -> 103 us
  local copies, waits for them, and re-layouts: 56.8 us -> 36.3 us
    ppermute x37, waiting for transfers between devices: 199 us -> 138 us  [swap(): return lax.ppermute(values, 'dp', [(i, i ^ bit) for i in range(data_count)])]
    pallas_call x0 -> x2, Pallas kernels: none -> 41.9 us  [call_heads(): pl.pallas_call(kernel, out_shape=[jax.ShapeDtypeStruct((toks, width), hal...]
    ppermute x12 -> x18, starting transfers between devices: 2.49 us -> 34.1 us  [onward(): lax.ppermute(values, 'dp', [(i, (i + QUAD) % data_count) for i in range(d...]
    dot_general x8 -> x1, matrix products: 29.6 us -> 5.92 us  [local(): jnp.einsum('as,src->arc', holds.astype(half_type), parts_all, preferred_e...]
    ppermute x20 -> x22, waiting for transfers between devices: 90.7 us -> 68.5 us  [other_side(): return lax.ppermute(values, 'tensor', [(0, 1), (1, 0)])]
    pallas_call x4 -> x1, Pallas kernels: 53.8 us -> 35.7 us  [call_grad_rows(): pl.pallas_call(functools.partial(grad_rows_kernel, experts, cap), out_sha...]
    sub x1 -> x0, matrix products: 14.3 us -> none  [local(): grad_scores = (prob_block * (grad_prob - row_delta)).astype(half_type)]
    all_to_all x1 -> x2, waiting for transfers between devices: 0.01 us -> 12.9 us  [the longest x1 12.9 us: local(): lax.all_to_all(gates_t.reshape(data_count, local_experts, tok_count), 'dp...]
  transfers between devices with their start and end apart: 75 -> 81, of which waited for: 25 -> 26; matrix products, arithmetic and copies ran while one was open for 20% -> 18% of each run, Pallas kernels for 23% -> 29%
where the time goes in v3:
time: 934 us; the launch traced here: 924 us
  waiting for transfers between devices  359 us (38%)
  Pallas kernels  264 us (28%)
  other arithmetic  103 us (11%)
  starting transfers between devices  89.5 us (10%)
  matrix products  56.1 us (6%)
  local copies, waits for them, and re-layouts  36.3 us (4%)
  between operations  16.6 us (2%)
    ppermute x18, waiting for transfers between devices, onward(): lax.ppermute(values, 'dp', [(i, (i + QUAD) % data_count) for i in range(d...  139 us
    ppermute x37, waiting for transfers between devices, swap(): return lax.ppermute(values, 'dp', [(i, i ^ bit) for i in range(data_count)])  138 us
    pallas_call x4, Pallas kernels, call_experts(): pl.pallas_call(functools.partial(expert_kernel, experts, cap), out_shape=...  123 us
    convert_element_type x35, other arithmetic, plus(): return total.astype(half_type)  89 us
    ppermute x22, waiting for transfers between devices, other_side(): return lax.ppermute(values, 'tensor', [(0, 1), (1, 0)])  68.5 us
    pallas_call x4, Pallas kernels, call_output(): pl.pallas_call(functools.partial(output_kernel, experts, cap), out_shape=...  63.4 us
    pallas_call x2, Pallas kernels, call_heads(): pl.pallas_call(kernel, out_shape=[jax.ShapeDtypeStruct((toks, width), hal...  41.9 us
    pallas_call x1, Pallas kernels, call_grad_rows(): pl.pallas_call(functools.partial(grad_rows_kernel, experts, cap), out_sha...  35.7 us
  transfers between devices with their start and end apart: 81, of which 26 were waited for; matrix products, arithmetic and copies ran while one was open for 18% of the time, Pallas kernels for 29%

profile of v3, /device:TPU:0, one launch (start us, length us, event | category | flops | bytes accessed | tf_op | source)
XLA Modules:
  0.0 923.6 jit_solution(5740364951312008119)
XLA Ops:
  10.4 7.4 all-to-all-start
  42.7 19.5 %attend.1 = (bf16[512,1024]{1,0:T(8,128)(2,1)}, bf16[512,1024]{1,0:T(8,128)(2,1)}, bf16[512,1024]{1,0:T(8,128)(2,1)}, bf16[512,1024]{1,0:T(8,128)(2,1)}) custom-call(f32[512,1024]{1,0:T(8,128)} %convolution_add_fusion.2.raw_q, f32[512,1024]{1,0:T(8,128)} %convolution_add_fusion.1.raw_k, f32[512,1024]{1,0:T(8,128)} %convolution_add_fusion.raw_v, ...), custom_call_target="tpu_custom_call" | custom-call | flops 2684354560 | bytes 4194304 | tf_op jit(solution)/shard_map/attend/pallas_call | solution.py:105
  62.2 3.6 fusion.121
  70.6 24.2 %collective-permute-done.1 = bf16[512,16]{0,1:T(8,128)(2,1)S(1)} collective-permute-done((bf16[512,16]{0,1:T(8,128)(2,1)S(1)}, bf16[512,16]{0,1:T(8,128)(2,1)S(1)}, u32[]{:S(2)}, u32[]{:S(2)}) %collective-permute-start.1) | collective-permute-done | bytes 16416 | tf_op jit(solution)/shard_map/ppermute | solution.py:472
  103.3 34.8 %collective-permute-done.6.across_first_ref = bf16[512,1024]{1,0:T(8,128)(2,1)S(1)} collective-permute-done((bf16[512,1024]{1,0:T(8,128)(2,1)S(1)}, bf16[512,1024]{1,0:T(8,128)(2,1)S(1)}, u32[]{:S(2)}, u32[]{:S(2)}) %collective-permute-start.6) | collective-permute-done | bytes 1048608 | tf_op jit(solution)/shard_map/ppermute | solution.py:464
  138.1 4.0 collective-permute-done.4.own_second_ref
  147.0 45.7 %collective-permute-done.10.across_first_ref = bf16[512,1024]{1,0:T(8,128)(2,1)} collective-permute-done((bf16[512,1024]{1,0:T(8,128)(2,1)}, bf16[512,1024]{1,0:T(8,128)(2,1)}, u32[]{:S(2)}, u32[]{:S(2)}) %collective-permute-start.10) | collective-permute-done | bytes 1048608 | tf_op jit(solution)/shard_map/ppermute | solution.py:464
  192.8 14.9 %collective-permute-start.7 = (bf16[512,1024]{1,0:T(8,128)(2,1)S(1)}, bf16[512,1024]{1,0:T(8,128)(2,1)}, u32[]{:S(2)}, u32[]{:S(2)}) collective-permute-start(bf16[512,1024]{1,0:T(8,128)(2,1)S(1)} %collective-permute-done.4.own_second_ref), channel_id=1, source_target_pairs={{0,8},{2,10},{4,12},{6,14},{8,16},{10,18},{12,20},{14,22},{16,24},... | collective-permute-start | bytes 3145736 | tf_op jit(solution)/shard_map/ppermute | solution.py:468
  208.8 42.6 %collective-permute-done.7.own_second_ref = bf16[512,1024]{1,0:T(8,128)(2,1)} collective-permute-done((bf16[512,1024]{1,0:T(8,128)(2,1)S(1)}, bf16[512,1024]{1,0:T(8,128)(2,1)}, u32[]{:S(2)}, u32[]{:S(2)}) %collective-permute-start.7) | collective-permute-done | bytes 1048608 | tf_op jit(solution)/shard_map/ppermute | solution.py:468
  251.4 6.8 collective-permute-start.13
  263.3 6.9 all-to-all-start.1
  270.2 4.2 fusion.118
  274.5 12.9 %all-to-all-done.1 = f32[16,4,512]{2,1,0:T(4,128)S(1)} async-done(((f32[16,4,512]{2,1,0:T(4,128)}), f32[16,4,512]{2,1,0:T(4,128)S(1)}, u32[]{:S(2)}, u32[]{:S(2)}) %all-to-all-start.1) | async-done | bytes 131104 | tf_op jit(solution)/shard_map/all_to_all | solution.py:772
  290.5 35.7 %grad_rows.1.dh_ref = bf16[4,1280,512]{2,1,0:T(8,128)(2,1)} custom-call(s32[16]{0:T(128)} %fusion.99.block_ids, s32[16,4,1,512]{3,2,1,0:T(1,128)} %broadcast_in_dim.86.place_ref, bf16[4,512,2048]{2,1,0:T(8,128)(2,1)} %down_ref.9, bf16[16,2,512,1024]{3,2,1,0:T(8,128)(2,1)} %bitcast.239), custom_call_target="tpu_custom_call" | custom-call | flops 42949672960 | bytes 47185920 | tf_op jit(solution)/shard_map/grad_rows/pallas_call | solution.py:349
  330.3 30.6 %experts.4 = (bf16[2,2,544,1024]{3,2,1,0:T(8,128)(2,1)}, bf16[2,2,544,1024]{3,2,1,0:T(8,128)(2,1)}, bf16[4,320,512]{2,1,0:T(8,128)(2,1)}) custom-call(s32[2]{0:T(128)} %pad_add_fusion.flip_ref, s32[4,4,1,512]{3,2,1,0:T(1,128)} %broadcast_in_dim.87.place_ref, f32[4,4,1,512]{3,2,1,0:T(1,128)} %copy.88.gate_ref, s32[4,512,4]{2,1,0:T(8,128)} %get-tuple-element.584.target_ref, ...), custom_call_target="tpu_custom_call" | custom-call | flops 24159191040 | bytes 33554432 | tf_op jit(solution)/shard_map/experts/pallas_call | solution.py:383
  366.9 30.6 %experts.5 = (bf16[2,2,544,1024]{3,2,1,0:T(8,128)(2,1)}, bf16[2,2,544,1024]{3,2,1,0:T(8,128)(2,1)}, bf16[4,320,512]{2,1,0:T(8,128)(2,1)}) custom-call(s32[2]{0:T(128)} %pad_add_fusion.flip_ref, s32[4,4,1,512]{3,2,1,0:T(1,128)} %broadcast_in_dim.89.place_ref, f32[4,4,1,512]{3,2,1,0:T(1,128)} %copy.89.gate_ref, s32[4,512,4]{2,1,0:T(8,128)} %get-tuple-element.583.target_ref, ...), custom_call_target="tpu_custom_call" | custom-call | flops 24159191040 | bytes 33554432 | tf_op jit(solution)/shard_map/experts/pallas_call | solution.py:383
  402.0 3.5 fusion.37
  405.6 30.8 %experts.6 = (bf16[2,2,544,1024]{3,2,1,0:T(8,128)(2,1)}, bf16[2,2,544,1024]{3,2,1,0:T(8,128)(2,1)}, bf16[4,320,512]{2,1,0:T(8,128)(2,1)}) custom-call(s32[2]{0:T(128)} %pad_add_fusion.flip_ref, s32[4,4,1,512]{3,2,1,0:T(1,128)} %broadcast_in_dim.91.place_ref, f32[4,4,1,512]{3,2,1,0:T(1,128)} %copy.90.gate_ref, s32[4,512,4]{2,1,0:T(8,128)} %get-tuple-element.582.target_ref, ...), custom_call_target="tpu_custom_call" | custom-call | flops 24159191040 | bytes 33554432 | tf_op jit(solution)/shard_map/experts/pallas_call | solution.py:383
  451.7 30.9 %experts.7 = (bf16[2,2,544,1024]{3,2,1,0:T(8,128)(2,1)}, bf16[2,2,544,1024]{3,2,1,0:T(8,128)(2,1)}, bf16[4,320,512]{2,1,0:T(8,128)(2,1)}) custom-call(s32[2]{0:T(128)} %pad_add_fusion.flip_ref, s32[4,4,1,512]{3,2,1,0:T(1,128)} %broadcast_in_dim.93.place_ref, f32[4,4,1,512]{3,2,1,0:T(1,128)} %broadcast_in_dim.94.gate_ref, ...), custom_call_target="tpu_custom_call" | custom-call | flops 24159191040 | bytes 33554432 | tf_op jit(solution)/shard_map/experts/pallas_call | solution.py:383
  482.6 3.6 fusion.11
  498.7 16.0 %outputs.4 = (bf16[2,2,512,1024]{3,2,1,0:T(8,128)(2,1)}, bf16[2,2,512,1024]{3,2,1,0:T(8,128)(2,1)}) custom-call(s32[2]{0:T(128)} %pad_add_fusion.flip_ref, s32[4,512,4]{2,1,0:T(8,128)} %get-tuple-element.584.target_ref, bf16[4,512,2048]{2,1,0:T(8,128)(2,1)} %down_ref.9, bf16[4,320,512]{2,1,0:T(8,128)(2,1)} %get-tuple-element.393.hidden_ref), custom_call_target="tpu_custom_call" | custom-call | flops 10737418240 | bytes 16777216 | tf_op jit(solution)/shard_map/outputs/pallas_call | solution.py:434
  518.6 8.7 collective-permute-done.45
  527.3 22.8 %collective-permute-done.44 = bf16[544,1024]{1,0:T(8,128)(2,1)} collective-permute-done((bf16[544,1024]{1,0:T(8,128)(2,1)}, bf16[544,1024]{1,0:T(8,128)(2,1)}, u32[]{:S(2)}, u32[]{:S(2)}) %collective-permute-start.44) | collective-permute-done | bytes 1114144 | tf_op jit(solution)/shard_map/ppermute | solution.py:468
  556.5 3.6 fusion.6
  560.2 15.8 %outputs.5 = (bf16[2,2,512,1024]{3,2,1,0:T(8,128)(2,1)}, bf16[2,2,512,1024]{3,2,1,0:T(8,128)(2,1)}) custom-call(s32[2]{0:T(128)} %pad_add_fusion.flip_ref, s32[4,512,4]{2,1,0:T(8,128)} %get-tuple-element.582.target_ref, bf16[4,512,2048]{2,1,0:T(8,128)(2,1)} %down_ref.9, bf16[4,320,512]{2,1,0:T(8,128)(2,1)} %get-tuple-element.409.hidden_ref), custom_call_target="tpu_custom_call" | custom-call | flops 10737418240 | bytes 16777216 | tf_op jit(solution)/shard_map/outputs/pallas_call | solution.py:434
  576.0 4.1 collective-permute-done.47
  582.7 6.2 collective-permute-done.49
  596.5 3.5 fusion.46
  602.4 15.8 %outputs.6 = (bf16[2,2,512,1024]{3,2,1,0:T(8,128)(2,1)}, bf16[2,2,512,1024]{3,2,1,0:T(8,128)(2,1)}) custom-call(s32[2]{0:T(128)} %pad_add_fusion.flip_ref, s32[4,512,4]{2,1,0:T(8,128)} %get-tuple-element.581.target_ref, bf16[4,512,2048]{2,1,0:T(8,128)(2,1)} %down_ref.9, bf16[4,320,512]{2,1,0:T(8,128)(2,1)} %get-tuple-element.427.hidden_ref), custom_call_target="tpu_custom_call" | custom-call | flops 10737418240 | bytes 16777216 | tf_op jit(solution)/shard_map/outputs/pallas_call | solution.py:434
  621.7 4.0 collective-permute-done.52
  629.8 15.8 %outputs.7 = (bf16[2,2,512,1024]{3,2,1,0:T(8,128)(2,1)}, bf16[2,2,512,1024]{3,2,1,0:T(8,128)(2,1)}) custom-call(s32[2]{0:T(128)} %pad_add_fusion.flip_ref, s32[4,512,4]{2,1,0:T(8,128)} %get-tuple-element.583.target_ref, bf16[4,512,2048]{2,1,0:T(8,128)(2,1)} %down_ref.9, bf16[4,320,512]{2,1,0:T(8,128)(2,1)} %get-tuple-element.444.hidden_ref), custom_call_target="tpu_custom_call" | custom-call | flops 10737418240 | bytes 16777216 | tf_op jit(solution)/shard_map/outputs/pallas_call | solution.py:434
  645.6 7.3 collective-permute-done.55
  668.8 21.3 %collective-permute-done.60 = f32[512,1]{0,1:T(1,128)S(1)} collective-permute-done((f32[512,1]{0,1:T(1,128)S(1)}, f32[512,1]{0,1:T(1,128)S(1)}, u32[]{:S(2)}, u32[]{:S(2)}) %collective-permute-start.60) | collective-permute-done | bytes 2080 | tf_op jit(solution)/shard_map/ppermute | solution.py:472
  694.7 21.2 %collective-permute-done.62 = bf16[512,1024]{1,0:T(8,128)(2,1)S(1)} collective-permute-done((bf16[512,1024]{1,0:T(8,128)(2,1)S(1)}, bf16[512,1024]{1,0:T(8,128)(2,1)S(1)}, u32[]{:S(2)}, u32[]{:S(2)}) %collective-permute-start.62) | collective-permute-done | bytes 1048608 | tf_op jit(solution)/shard_map/ppermute | solution.py:464
  715.9 4.0 fusion.22
  722.1 21.9 %collective-permute-done.64 = bf16[512,1024]{1,0:T(8,128)(2,1)S(1)} collective-permute-done((bf16[512,1024]{1,0:T(8,128)(2,1)S(1)}, bf16[512,1024]{1,0:T(8,128)(2,1)S(1)}, u32[]{:S(2)}, u32[]{:S(2)}) %collective-permute-start.64) | collective-permute-done | bytes 1048608 | tf_op jit(solution)/shard_map/ppermute | solution.py:468
  747.3 4.0 fusion.51
  755.0 22.4 %attend_back.1 = (bf16[512,1024]{1,0:T(8,128)(2,1)}, bf16[512,1024]{1,0:T(8,128)(2,1)}, bf16[512,1024]{1,0:T(8,128)(2,1)}) custom-call(f32[512,1024]{1,0:T(8,128)} %convolution_add_fusion.2.raw_q, f32[512,1024]{1,0:T(8,128)} %convolution_add_fusion.1.raw_k, bf16[512,1024]{1,0:T(8,128)(2,1)} %get-tuple-element.486.queries, ...), custom_call_target="tpu_custom_call" | custom-call | flops 2684354560 | bytes 4194304 | tf_op jit(solution)/shard_map/attend_back/pallas_call | solution.py:105
  800.3 4.4 fusion.122
  804.7 4.4 fusion.123
  809.2 6.1 add_add_fusion
  817.3 11.6 %collective-permute-done.69 = bf16[512,1024]{1,0:T(8,128)(2,1)S(1)} collective-permute-done((bf16[512,1024]{1,0:T(8,128)(2,1)S(1)}, bf16[512,1024]{1,0:T(8,128)(2,1)S(1)}, u32[]{:S(2)}, u32[]{:S(2)}) %collective-permute-start.69) | collective-permute-done | bytes 1048608 | tf_op jit(solution)/shard_map/ppermute | solution.py:468
  836.0 22.0 %collective-permute-done.70 = bf16[512,1024]{1,0:T(8,128)(2,1)S(1)} collective-permute-done((bf16[512,1024]{1,0:T(8,128)(2,1)S(1)}, bf16[512,1024]{1,0:T(8,128)(2,1)S(1)}, u32[]{:S(2)}, u32[]{:S(2)}) %collective-permute-start.70) | collective-permute-done | bytes 1048608 | tf_op jit(solution)/shard_map/ppermute | solution.py:464
  860.5 13.4 %collective-permute-done.72 = bf16[512,1024]{1,0:T(8,128)(2,1)S(1)} collective-permute-done((bf16[512,1024]{1,0:T(8,128)(2,1)S(1)}, bf16[512,1024]{1,0:T(8,128)(2,1)S(1)}, u32[]{:S(2)}, u32[]{:S(2)}) %collective-permute-start.72) | collective-permute-done | bytes 1048608 | tf_op jit(solution)/shard_map/ppermute | solution.py:468
  881.1 9.6 %collective-permute-done.76 = f32[512,1]{0,1:T(1,128)S(1)} collective-permute-done((f32[512,1]{0,1:T(1,128)S(1)}, f32[512,1]{0,1:T(1,128)S(1)}, u32[]{:S(2)}, u32[]{:S(2)}) %collective-permute-start.76) | collective-permute-done | bytes 2080 | tf_op jit(solution)/shard_map/ppermute | solution.py:472
  892.7 6.6 collective-permute-done.73
  901.1 5.9 fusion
  910.9 3.5 copy.93
  (433 shorter events, 207.7 us)
Async XLA Ops:
  7.2 283.3 %all-gather.5.cloned.1.call-start = ((), (), s32[]{:S(2)}) async-start(), calls=%async_computation.2 | async-start | bytes 34603008 | tf_op jit(solution)/shard_map/all_gather | solution.py:594
  99.7 38.5 %collective-permute-start.6 = (bf16[512,1024]{1,0:T(8,128)(2,1)S(1)}, bf16[512,1024]{1,0:T(8,128)(2,1)S(1)}, u32[]{:S(2)}, u32[]{:S(2)}) collective-permute-start(bf16[512,1024]{1,0:T(8,128)(2,1)S(1)} %multiply_convert_fusion.own_first_ref), channel_id=1, source_target_pairs={{0,4},{2,6},{4,0},{6,2},{8,12},{10,14},{12,8},{14,10},{16,20},{18,... | collective-permute-start | bytes 3145736 | tf_op jit(solution)/shard_map/ppermute | solution.py:464
  101.2 36.9 %collective-permute-start.5 = (bf16[512,1024]{1,0:T(8,128)(2,1)S(1)}, bf16[512,1024]{1,0:T(8,128)(2,1)S(1)}, u32[]{:S(2)}, u32[]{:S(2)}) collective-permute-start(bf16[512,1024]{1,0:T(8,128)(2,1)S(1)} %multiply_convert_fusion.own_first_ref), channel_id=1, source_target_pairs={{0,2},{2,0},{4,6},{6,4},{8,10},{10,8},{12,14},{14,12},{16,18},{18,... | collective-permute-start | bytes 3145736 | tf_op jit(solution)/shard_map/ppermute | solution.py:464
  101.2 41.0 %collective-permute-start.4 = (bf16[512,1024]{1,0:T(8,128)(2,1)S(1)}, bf16[512,1024]{1,0:T(8,128)(2,1)S(1)}, u32[]{:S(2)}, u32[]{:S(2)}) collective-permute-start(bf16[512,1024]{1,0:T(8,128)(2,1)S(1)} %multiply_convert_fusion.own_first_ref), channel_id=1, source_target_pairs={{0,1},{1,0},{2,3},{3,2},{4,5},{5,4},{6,7},{7,6},{8,9},{9,8},{10,11... | collective-permute-start | bytes 3145736 | tf_op jit(solution)/shard_map/ppermute | solution.py:472
  101.8 43.2 %collective-permute-start.3 = (bf16[512,1024]{1,0:T(8,128)(2,1)S(1)}, bf16[512,1024]{1,0:T(8,128)(2,1)}, u32[]{:S(2)}, u32[]{:S(2)}) collective-permute-start(bf16[512,1024]{1,0:T(8,128)(2,1)S(1)} %multiply_convert_fusion.own_first_ref), channel_id=1, source_target_pairs={{0,8},{2,10},{4,12},{6,14},{8,16},{10,18},{12,20},{14,22},{16,24},... | collective-permute-start | bytes 3145736 | tf_op jit(solution)/shard_map/ppermute | solution.py:468
  145.0 47.7 %collective-permute-start.10 = (bf16[512,1024]{1,0:T(8,128)(2,1)}, bf16[512,1024]{1,0:T(8,128)(2,1)}, u32[]{:S(2)}, u32[]{:S(2)}) collective-permute-start(bf16[512,1024]{1,0:T(8,128)(2,1)} %collective-permute-done.3.own_first_ref), channel_id=1, source_target_pairs={{0,4},{2,6},{4,0},{6,2},{8,12},{10,14},{12,8},{14,10},{16,20},{18,... | collective-permute-start | bytes 3145736 | tf_op jit(solution)/shard_map/ppermute | solution.py:464
  145.0 63.7 %collective-permute-start.8 = (bf16[512,1024]{1,0:T(8,128)(2,1)}, bf16[512,1024]{1,0:T(8,128)(2,1)S(1)}, u32[]{:S(2)}, u32[]{:S(2)}) collective-permute-start(bf16[512,1024]{1,0:T(8,128)(2,1)} %collective-permute-done.3.own_first_ref), channel_id=1, source_target_pairs={{0,2},{2,0},{4,6},{6,4},{8,10},{10,8},{12,14},{14,12},{16,18},{18,... | collective-permute-start | bytes 3145736 | tf_op jit(solution)/shard_map/ppermute | solution.py:464
  145.0 63.7 %collective-permute-start.12 = (bf16[512,1024]{1,0:T(8,128)(2,1)S(1)}, bf16[512,1024]{1,0:T(8,128)(2,1)S(1)}, u32[]{:S(2)}, u32[]{:S(2)}) collective-permute-start(bf16[512,1024]{1,0:T(8,128)(2,1)S(1)} %collective-permute-done.6.across_first_ref), channel_id=1, source_target_pairs={{0,2},{2,0},{4,6},{6,4},{8,10},{10,8},{12,14},{14,12},{16,18},{18,... | collective-permute-start | bytes 3145736 | tf_op jit(solution)/shard_map/ppermute | solution.py:464
  145.6 63.2 %collective-permute-start.11 = (bf16[512,1024]{1,0:T(8,128)(2,1)S(1)}, bf16[512,1024]{1,0:T(8,128)(2,1)}, u32[]{:S(2)}, u32[]{:S(2)}) collective-permute-start(bf16[512,1024]{1,0:T(8,128)(2,1)S(1)} %collective-permute-done.6.across_first_ref), channel_id=1, source_target_pairs={{0,1},{1,0},{2,3},{3,2},{4,5},{5,4},{6,7},{7,6},{8,9},{9,8},{10,11... | collective-permute-start | bytes 3145736 | tf_op jit(solution)/shard_map/ppermute | solution.py:472
  147.0 61.8 %collective-permute-start.9 = (bf16[512,1024]{1,0:T(8,128)(2,1)S(1)}, bf16[512,1024]{1,0:T(8,128)(2,1)S(1)}, u32[]{:S(2)}, u32[]{:S(2)}) collective-permute-start(bf16[512,1024]{1,0:T(8,128)(2,1)S(1)} %collective-permute-done.4.own_second_ref), channel_id=1, source_target_pairs={{0,2},{2,0},{4,6},{6,4},{8,10},{10,8},{12,14},{14,12},{16,18},{18,... | collective-permute-start | bytes 3145736 | tf_op jit(solution)/shard_map/ppermute | solution.py:464
  192.8 58.6 %collective-permute-start.7 = (bf16[512,1024]{1,0:T(8,128)(2,1)S(1)}, bf16[512,1024]{1,0:T(8,128)(2,1)}, u32[]{:S(2)}, u32[]{:S(2)}) collective-permute-start(bf16[512,1024]{1,0:T(8,128)(2,1)S(1)} %collective-permute-done.4.own_second_ref), channel_id=1, source_target_pairs={{0,8},{2,10},{4,12},{6,14},{8,16},{10,18},{12,20},{14,22},{16,24},... | collective-permute-start | bytes 3145736 | tf_op jit(solution)/shard_map/ppermute | solution.py:468
  251.4 36.6 %collective-permute-start.13 = (bf16[512,1024]{1,0:T(8,128)(2,1)}, bf16[512,1024]{1,0:T(8,128)(2,1)S(1)}, u32[]{:S(2)}, u32[]{:S(2)}) collective-permute-start(bf16[512,1024]{1,0:T(8,128)(2,1)} %collective-permute-done.3.own_first_ref), channel_id=1, source_target_pairs={{0,8},{2,10},{4,12},{6,14},{8,16},{10,18},{12,20},{14,22},{16,24},... | collective-permute-start | bytes 3145736 | tf_op jit(solution)/shard_map/ppermute | solution.py:468
  270.2 630.9 %all-gather.7.cloned.1.call-start = ((), (), s32[]{:S(2)}) async-start(), calls=%async_computation.3 | async-start | bytes 6127616 | tf_op jit(solution)/shard_map/all_gather | solution.py:916
  288.1 38.2 %collective-permute-start.20 = (bf16[512,1024]{1,0:T(8,128)(2,1)S(1)}, bf16[512,1024]{1,0:T(8,128)(2,1)}, u32[]{:S(2)}, u32[]{:S(2)}) collective-permute-start(bf16[512,1024]{1,0:T(8,128)(2,1)S(1)} %collective-permute-done.13.own_first_ref), channel_id=1, source_target_pairs={{0,4},{2,6},{4,0},{6,2},{8,12},{10,14},{12,8},{14,10},{16,20},{18,... | collective-permute-start | bytes 3145736 | tf_op jit(solution)/shard_map/ppermute | solution.py:464
  289.3 36.9 %collective-permute-start.19 = (bf16[512,1024]{1,0:T(8,128)(2,1)S(1)}, bf16[512,1024]{1,0:T(8,128)(2,1)}, u32[]{:S(2)}, u32[]{:S(2)}) collective-permute-start(bf16[512,1024]{1,0:T(8,128)(2,1)S(1)} %collective-permute-done.13.own_first_ref), channel_id=1, source_target_pairs={{0,2},{2,0},{4,6},{6,4},{8,10},{10,8},{12,14},{14,12},{16,18},{18,... | collective-permute-start | bytes 3145736 | tf_op jit(solution)/shard_map/ppermute | solution.py:464
  289.3 36.9 %collective-permute-start.18 = (bf16[512,1024]{1,0:T(8,128)(2,1)}, bf16[512,1024]{1,0:T(8,128)(2,1)}, u32[]{:S(2)}, u32[]{:S(2)}) collective-permute-start(bf16[512,1024]{1,0:T(8,128)(2,1)} %collective-permute-done.7.own_second_ref), channel_id=1, source_target_pairs={{0,8},{2,10},{4,12},{6,14},{8,16},{10,18},{12,20},{14,22},{16,24},... | collective-permute-start | bytes 3145736 | tf_op jit(solution)/shard_map/ppermute | solution.py:468
  290.3 36.0 %collective-permute-start.21 = (bf16[512,1024]{1,0:T(8,128)(2,1)}, bf16[512,1024]{1,0:T(8,128)(2,1)}, u32[]{:S(2)}, u32[]{:S(2)}) collective-permute-start(bf16[512,1024]{1,0:T(8,128)(2,1)} %collective-permute-done.15.across_second_ref), channel_id=1, source_target_pairs={{0,2},{2,0},{4,6},{6,4},{8,10},{10,8},{12,14},{14,12},{16,18},{18,... | collective-permute-start | bytes 3145736 | tf_op jit(solution)/shard_map/ppermute | solution.py:464
  326.2 34.7 %collective-permute-start.25 = (bf16[512,1024]{1,0:T(8,128)(2,1)}, bf16[512,1024]{1,0:T(8,128)(2,1)S(1)}, u32[]{:S(2)}, u32[]{:S(2)}) collective-permute-start(bf16[512,1024]{1,0:T(8,128)(2,1)} %collective-permute-done.20.across_first_ref), channel_id=1, source_target_pairs={{0,2},{2,0},{4,6},{6,4},{8,10},{10,8},{12,14},{14,12},{16,18},{18,... | collective-permute-start | bytes 3145736 | tf_op jit(solution)/shard_map/ppermute | solution.py:464
  326.6 34.3 %collective-permute-start.24 = (bf16[512,1024]{1,0:T(8,128)(2,1)}, bf16[512,1024]{1,0:T(8,128)(2,1)S(1)}, u32[]{:S(2)}, u32[]{:S(2)}) collective-permute-start(bf16[512,1024]{1,0:T(8,128)(2,1)} %collective-permute-done.20.across_first_ref), channel_id=1, source_target_pairs={{0,1},{1,0},{2,3},{3,2},{4,5},{5,4},{6,7},{7,6},{8,9},{9,8},{10,11... | collective-permute-start | bytes 3145736 | tf_op jit(solution)/shard_map/ppermute | solution.py:472
  330.2 30.7 %collective-permute-start.22 = (bf16[512,1024]{1,0:T(8,128)(2,1)S(1)}, bf16[512,1024]{1,0:T(8,128)(2,1)S(1)}, u32[]{:S(2)}, u32[]{:S(2)}) collective-permute-start(bf16[512,1024]{1,0:T(8,128)(2,1)S(1)} %collective-permute-done.13.own_first_ref), channel_id=1, source_target_pairs={{0,8},{2,10},{4,12},{6,14},{8,16},{10,18},{12,20},{14,22},{16,24},... | collective-permute-start | bytes 3145736 | tf_op jit(solution)/shard_map/ppermute | solution.py:468
  330.3 30.6 %collective-permute-start.23 = (bf16[512,1024]{1,0:T(8,128)(2,1)}, bf16[512,1024]{1,0:T(8,128)(2,1)S(1)}, u32[]{:S(2)}, u32[]{:S(2)}) collective-permute-start(bf16[512,1024]{1,0:T(8,128)(2,1)} %collective-permute-done.18.own_second_ref), channel_id=1, source_target_pairs={{0,2},{2,0},{4,6},{6,4},{8,10},{10,8},{12,14},{14,12},{16,18},{18,... | collective-permute-start | bytes 3145736 | tf_op jit(solution)/shard_map/ppermute | solution.py:464
  362.8 34.7 %collective-permute-start.30 = (bf16[2,2,544,1024]{3,2,1,0:T(8,128)(2,1)}, bf16[2,2,544,1024]{3,2,1,0:T(8,128)(2,1)S(1)}, u32[]{:S(2)}, u32[]{:S(2)}) collective-permute-start(bf16[2,2,544,1024]{3,2,1,0:T(8,128)(2,1)} %get-tuple-element.345), channel_id=1, source_target_pairs={{0,2},{2,0},{4,6},{6,4},{8,10},{10,8},{12,14},{14,12},{16,18},{18,... | collective-permute-start | bytes 13369352 | tf_op jit(solution)/shard_map/ppermute | solution.py:464
  364.6 32.9 %collective-permute-start.28 = (bf16[512,1024]{1,0:T(8,128)(2,1)}, bf16[512,1024]{1,0:T(8,128)(2,1)}, u32[]{:S(2)}, u32[]{:S(2)}) collective-permute-start(bf16[512,1024]{1,0:T(8,128)(2,1)} %copy-done.76), channel_id=1, source_target_pairs={{0,4},{2,6},{4,0},{6,2},{8,12},{10,14},{12,8},{14,10},{16,20},{18,... | collective-permute-start | bytes 3145736 | tf_op jit(solution)/shard_map/ppermute | solution.py:464
  365.4 32.2 %collective-permute-start.27 = (bf16[512,1024]{1,0:T(8,128)(2,1)}, bf16[512,1024]{1,0:T(8,128)(2,1)S(1)}, u32[]{:S(2)}, u32[]{:S(2)}) collective-permute-start(bf16[512,1024]{1,0:T(8,128)(2,1)} %copy-done.76), channel_id=1, source_target_pairs={{0,2},{2,0},{4,6},{6,4},{8,10},{10,8},{12,14},{14,12},{16,18},{18,... | collective-permute-start | bytes 3145736 | tf_op jit(solution)/shard_map/ppermute | solution.py:464
  365.4 32.1 %collective-permute-start.26 = (bf16[512,1024]{1,0:T(8,128)(2,1)}, bf16[512,1024]{1,0:T(8,128)(2,1)}, u32[]{:S(2)}, u32[]{:S(2)}) collective-permute-start(bf16[512,1024]{1,0:T(8,128)(2,1)} %collective-permute-done.18.own_second_ref), channel_id=1, source_target_pairs={{0,8},{2,10},{4,12},{6,14},{8,16},{10,18},{12,20},{14,22},{16,24},... | collective-permute-start | bytes 3145736 | tf_op jit(solution)/shard_map/ppermute | solution.py:468
  366.6 30.9 %collective-permute-start.29 = (bf16[512,1024]{1,0:T(8,128)(2,1)}, bf16[512,1024]{1,0:T(8,128)(2,1)S(1)}, u32[]{:S(2)}, u32[]{:S(2)}) collective-permute-start(bf16[512,1024]{1,0:T(8,128)(2,1)} %copy-done.80), channel_id=1, source_target_pairs={{0,2},{2,0},{4,6},{6,4},{8,10},{10,8},{12,14},{14,12},{16,18},{18,... | collective-permute-start | bytes 3145736 | tf_op jit(solution)/shard_map/ppermute | solution.py:464
  397.6 38.9 %collective-permute-start.34 = (bf16[2,2,544,1024]{3,2,1,0:T(8,128)(2,1)}, bf16[2,2,544,1024]{3,2,1,0:T(8,128)(2,1)}, u32[]{:S(2)}, u32[]{:S(2)}) collective-permute-start(bf16[2,2,544,1024]{3,2,1,0:T(8,128)(2,1)} %get-tuple-element.364), channel_id=1, source_target_pairs={{0,2},{2,0},{4,6},{6,4},{8,10},{10,8},{12,14},{14,12},{16,18},{18,... | collective-permute-start | bytes 13369352 | tf_op jit(solution)/shard_map/ppermute | solution.py:464
  400.1 36.3 %collective-permute-start.32 = (bf16[512,1024]{1,0:T(8,128)(2,1)}, bf16[512,1024]{1,0:T(8,128)(2,1)}, u32[]{:S(2)}, u32[]{:S(2)}) collective-permute-start(bf16[512,1024]{1,0:T(8,128)(2,1)} %collective-permute-done.26.own_second_ref), channel_id=1, source_target_pairs={{0,4},{2,6},{4,0},{6,2},{8,12},{10,14},{12,8},{14,10},{16,20},{18,... | collective-permute-start | bytes 3145736 | tf_op jit(solution)/shard_map/ppermute | solution.py:464
  401.4 35.0 %collective-permute-start.31 = (bf16[512,1024]{1,0:T(8,128)(2,1)}, bf16[512,1024]{1,0:T(8,128)(2,1)}, u32[]{:S(2)}, u32[]{:S(2)}) collective-permute-start(bf16[512,1024]{1,0:T(8,128)(2,1)} %collective-permute-done.26.own_second_ref), channel_id=1, source_target_pairs={{0,2},{2,0},{4,6},{6,4},{8,10},{10,8},{12,14},{14,12},{16,18},{18,... | collective-permute-start | bytes 3145736 | tf_op jit(solution)/shard_map/ppermute | solution.py:464
  401.5 35.0 %collective-permute-start.33 = (bf16[512,1024]{1,0:T(8,128)(2,1)}, bf16[512,1024]{1,0:T(8,128)(2,1)}, u32[]{:S(2)}, u32[]{:S(2)}) collective-permute-start(bf16[512,1024]{1,0:T(8,128)(2,1)} %collective-permute-done.28.across_first_ref), channel_id=1, source_target_pairs={{0,2},{2,0},{4,6},{6,4},{8,10},{10,8},{12,14},{14,12},{16,18},{18,... | collective-permute-start | bytes 3145736 | tf_op jit(solution)/shard_map/ppermute | solution.py:464
  405.5 30.9 %collective-permute-start.35 = (bf16[544,1024]{1,0:T(8,128)(2,1)S(1)}, bf16[544,1024]{1,0:T(8,128)(2,1)S(1)}, u32[]{:S(2)}, u32[]{:S(2)}) collective-permute-start(bf16[544,1024]{1,0:T(8,128)(2,1)S(1)} %get-tuple-element.558), channel_id=1, source_target_pairs={{0,1},{1,0},{2,3},{3,2},{4,5},{5,4},{6,7},{7,6},{8,9},{9,8},{10,11... | collective-permute-start | bytes 3342344 | tf_op jit(solution)/shard_map/ppermute | solution.py:472
  436.5 49.8 %collective-permute-start.37 = (bf16[2,2,544,1024]{3,2,1,0:T(8,128)(2,1)}, bf16[2,2,544,1024]{3,2,1,0:T(8,128)(2,1)}, u32[]{:S(2)}, u32[]{:S(2)}) collective-permute-start(bf16[2,2,544,1024]{3,2,1,0:T(8,128)(2,1)} %get-tuple-element.382), channel_id=1, source_target_pairs={{0,2},{2,0},{4,6},{6,4},{8,10},{10,8},{12,14},{14,12},{16,18},{18,... | collective-permute-start | bytes 13369352 | tf_op jit(solution)/shard_map/ppermute | solution.py:464
  441.3 44.9 %collective-permute-start.40 = (bf16[544,1024]{1,0:T(8,128)(2,1)}, bf16[544,1024]{1,0:T(8,128)(2,1)S(1)}, u32[]{:S(2)}, u32[]{:S(2)}) collective-permute-start(bf16[544,1024]{1,0:T(8,128)(2,1)} %fusion.40), channel_id=1, source_target_pairs={{0,8},{2,10},{4,12},{6,14},{8,16},{10,18},{12,20},{14,22},{16,24},... | collective-permute-start | bytes 3342344 | tf_op jit(solution)/shard_map/ppermute | solution.py:468
  446.6 36.0 %collective-permute-start.39 = (bf16[544,1024]{1,0:T(8,128)(2,1)}, bf16[544,1024]{1,0:T(8,128)(2,1)}, u32[]{:S(2)}, u32[]{:S(2)}) collective-permute-start(bf16[544,1024]{1,0:T(8,128)(2,1)} %add_convert_fusion.10), channel_id=1, source_target_pairs={{0,4},{2,6},{4,0},{6,2},{8,12},{10,14},{12,8},{14,10},{16,20},{18,... | collective-permute-start | bytes 3342344 | tf_op jit(solution)/shard_map/ppermute | solution.py:464
  449.6 36.6 %collective-permute-start.38 = (bf16[544,1024]{1,0:T(8,128)(2,1)S(1)}, bf16[544,1024]{1,0:T(8,128)(2,1)}, u32[]{:S(2)}, u32[]{:S(2)}) collective-permute-start(bf16[544,1024]{1,0:T(8,128)(2,1)S(1)} %get-tuple-element.556), channel_id=1, source_target_pairs={{0,1},{1,0},{2,3},{3,2},{4,5},{5,4},{6,7},{7,6},{8,9},{9,8},{10,11... | collective-permute-start | bytes 3342344 | tf_op jit(solution)/shard_map/ppermute | solution.py:472
  486.2 63.8 %collective-permute-start.41 = (bf16[2,2,544,1024]{3,2,1,0:T(8,128)(2,1)}, bf16[2,2,544,1024]{3,2,1,0:T(8,128)(2,1)}, u32[]{:S(2)}, u32[]{:S(2)}) collective-permute-start(bf16[2,2,544,1024]{3,2,1,0:T(8,128)(2,1)} %get-tuple-element.396), channel_id=1, source_target_pairs={{0,2},{2,0},{4,6},{6,4},{8,10},{10,8},{12,14},{14,12},{16,18},{18,... | collective-permute-start | bytes 13369352 | tf_op jit(solution)/shard_map/ppermute | solution.py:464
  498.6 51.4 %collective-permute-start.44 = (bf16[544,1024]{1,0:T(8,128)(2,1)}, bf16[544,1024]{1,0:T(8,128)(2,1)}, u32[]{:S(2)}, u32[]{:S(2)}) collective-permute-start(bf16[544,1024]{1,0:T(8,128)(2,1)} %fusion.11), channel_id=1, source_target_pairs={{0,8},{2,10},{4,12},{6,14},{8,16},{10,18},{12,20},{14,22},{16,24},... | collective-permute-start | bytes 3342344 | tf_op jit(solution)/shard_map/ppermute | solution.py:468
  498.7 51.4 %collective-permute-start.42 = (bf16[544,1024]{1,0:T(8,128)(2,1)S(1)}, bf16[544,1024]{1,0:T(8,128)(2,1)}, u32[]{:S(2)}, u32[]{:S(2)}) collective-permute-start(bf16[544,1024]{1,0:T(8,128)(2,1)S(1)} %get-tuple-element.554), channel_id=1, source_target_pairs={{0,1},{1,0},{2,3},{3,2},{4,5},{5,4},{6,7},{7,6},{8,9},{9,8},{10,11... | collective-permute-start | bytes 3342344 | tf_op jit(solution)/shard_map/ppermute | solution.py:472
  550.1 38.9 %collective-permute-start.48 = (bf16[2,2,512,1024]{3,2,1,0:T(8,128)(2,1)}, bf16[2,2,512,1024]{3,2,1,0:T(8,128)(2,1)}, u32[]{:S(2)}, u32[]{:S(2)}) collective-permute-start(bf16[2,2,512,1024]{3,2,1,0:T(8,128)(2,1)} %get-tuple-element.420), channel_id=1, source_target_pairs={{0,2},{2,0},{4,6},{6,4},{8,10},{10,8},{12,14},{14,12},{16,18},{18,... | collective-permute-start | bytes 12582920 | tf_op jit(solution)/shard_map/ppermute | solution.py:464
  588.9 36.7 %collective-permute-start.51 = (bf16[2,2,512,1024]{3,2,1,0:T(8,128)(2,1)}, bf16[2,2,512,1024]{3,2,1,0:T(8,128)(2,1)}, u32[]{:S(2)}, u32[]{:S(2)}) collective-permute-start(bf16[2,2,512,1024]{3,2,1,0:T(8,128)(2,1)} %get-tuple-element.436), channel_id=1, source_target_pairs={{0,2},{2,0},{4,6},{6,4},{8,10},{10,8},{12,14},{14,12},{16,18},{18,... | collective-permute-start | bytes 12582920 | tf_op jit(solution)/shard_map/ppermute | solution.py:464
  625.6 33.0 %collective-permute-start.54 = (bf16[2,2,512,1024]{3,2,1,0:T(8,128)(2,1)}, bf16[2,2,512,1024]{3,2,1,0:T(8,128)(2,1)}, u32[]{:S(2)}, u32[]{:S(2)}) collective-permute-start(bf16[2,2,512,1024]{3,2,1,0:T(8,128)(2,1)} %get-tuple-element.448), channel_id=1, source_target_pairs={{0,2},{2,0},{4,6},{6,4},{8,10},{10,8},{12,14},{14,12},{16,18},{18,... | collective-permute-start | bytes 12582920 | tf_op jit(solution)/shard_map/ppermute | solution.py:464
  658.6 33.6 %collective-permute-start.58 = (bf16[2,2,512,1024]{3,2,1,0:T(8,128)(2,1)}, bf16[2,2,512,1024]{3,2,1,0:T(8,128)(2,1)}, u32[]{:S(2)}, u32[]{:S(2)}) collective-permute-start(bf16[2,2,512,1024]{3,2,1,0:T(8,128)(2,1)} %get-tuple-element.459), channel_id=1, source_target_pairs={{0,2},{2,0},{4,6},{6,4},{8,10},{10,8},{12,14},{14,12},{16,18},{18,... | collective-permute-start | bytes 12582920 | tf_op jit(solution)/shard_map/ppermute | solution.py:464
  662.0 30.2 %collective-permute-start.61 = (bf16[512,1024]{1,0:T(8,128)(2,1)S(1)}, bf16[512,1024]{1,0:T(8,128)(2,1)S(1)}, u32[]{:S(2)}, u32[]{:S(2)}) collective-permute-start(bf16[512,1024]{1,0:T(8,128)(2,1)S(1)} %fusion.49), channel_id=1, source_target_pairs={{0,8},{2,10},{4,12},{6,14},{8,16},{10,18},{12,20},{14,22},{16,24},... | collective-permute-start | bytes 3145736 | tf_op jit(solution)/shard_map/ppermute | solution.py:468
  745.7 32.3 %collective-permute-start.66 = (bf16[512,1024]{1,0:T(8,128)(2,1)}, bf16[512,1024]{1,0:T(8,128)(2,1)S(1)}, u32[]{:S(2)}, u32[]{:S(2)}) collective-permute-start(bf16[512,1024]{1,0:T(8,128)(2,1)} %fusion.26), channel_id=1, source_target_pairs={{0,8},{2,10},{4,12},{6,14},{8,16},{10,18},{12,20},{14,22},{16,24},... | collective-permute-start | bytes 3145736 | tf_op jit(solution)/shard_map/ppermute | solution.py:468
  794.7 34.2 %collective-permute-start.69 = (bf16[512,1024]{1,0:T(8,128)(2,1)S(1)}, bf16[512,1024]{1,0:T(8,128)(2,1)S(1)}, u32[]{:S(2)}, u32[]{:S(2)}) collective-permute-start(bf16[512,1024]{1,0:T(8,128)(2,1)S(1)} %add_convert_fusion.19), channel_id=1, source_target_pairs={{0,8},{2,10},{4,12},{6,14},{8,16},{10,18},{12,20},{14,22},{16,24},... | collective-permute-start | bytes 3145736 | tf_op jit(solution)/shard_map/ppermute | solution.py:468
  798.5 30.5 %collective-permute-start.67 = (bf16[512,1024]{1,0:T(8,128)(2,1)S(1)}, bf16[512,1024]{1,0:T(8,128)(2,1)S(1)}, u32[]{:S(2)}, u32[]{:S(2)}) collective-permute-start(bf16[512,1024]{1,0:T(8,128)(2,1)S(1)} %get-tuple-element.560), channel_id=1, source_target_pairs={{0,1},{1,0},{2,3},{3,2},{4,5},{5,4},{6,7},{7,6},{8,9},{9,8},{10,11... | collective-permute-start | bytes 3145736 | tf_op jit(solution)/shard_map/ppermute | solution.py:472
  829.5 30.4 %collective-permute-start.71 = (bf16[512,1024]{1,0:T(8,128)(2,1)S(1)}, bf16[512,1024]{1,0:T(8,128)(2,1)S(1)}, u32[]{:S(2)}, u32[]{:S(2)}) collective-permute-start(bf16[512,1024]{1,0:T(8,128)(2,1)S(1)} %select_convert_fusion), channel_id=1, source_target_pairs={{0,1},{1,0},{2,3},{3,2},{4,5},{5,4},{6,7},{7,6},{8,9},{9,8},{10,11... | collective-permute-start | bytes 3145736 | tf_op jit(solution)/shard_map/ppermute | solution.py:472
  834.6 39.3 %collective-permute-start.72 = (bf16[512,1024]{1,0:T(8,128)(2,1)S(1)}, bf16[512,1024]{1,0:T(8,128)(2,1)S(1)}, u32[]{:S(2)}, u32[]{:S(2)}) collective-permute-start(bf16[512,1024]{1,0:T(8,128)(2,1)S(1)} %fusion.21), channel_id=1, source_target_pairs={{0,8},{2,10},{4,12},{6,14},{8,16},{10,18},{12,20},{14,22},{16,24},... | collective-permute-start | bytes 3145736 | tf_op jit(solution)/shard_map/ppermute | solution.py:468
  (118 other events, 2243.7 us)
Sparse Core Ops, SparseCore 0:
  11.1 255.0 all-gather.4
  789.1 85.7 all-gather.6

commit v4 on v3

--- a/solution.py
+++ b/solution.py
@@ -236,7 +236,10 @@
     buffer_ref,
     rows_ref,
     dgate_ref,
+    wg_buffer,
+    wu_buffer,
     sems,
+    weight_sems,
 ):
     block_refs = [
         own_first_ref,
@@ -252,9 +255,20 @@
     half = buffer_ref.shape[3]
     toks = buffer_ref.shape[2]
 
+    def weight_copies(e):
+        return (
+            pltpu.make_async_copy(wg_ref.at[e], wg_buffer.at[e], weight_sems.at[e, 0]),
+            pltpu.make_async_copy(wu_ref.at[e], wu_buffer.at[e], weight_sems.at[e, 1]),
+        )
+
     @pl.when(step == 0)
     def _():
         start_blocks(block_refs, buffer_ref, sems, flip_ref[0])
+
+    @pl.when(step < experts)
+    def _():
+        for copy in weight_copies(step):
+            copy.start()
 
     @pl.when(step < QUAD)
     def _():
@@ -266,12 +280,14 @@
     @pl.when(jnp.logical_and(step >= QUAD, step < QUAD + experts))
     def _():
         e = step - QUAD
+        for copy in weight_copies(e):
+            copy.wait()
         first = rows_ref[e, 0].reshape(QUAD * cap, half)
         second = rows_ref[e, 1].reshape(QUAD * cap, half)
-        pre_gate = jnp.dot(first, wg_ref[0, :half], preferred_element_type=jnp.float32)
-        pre_gate += jnp.dot(second, wg_ref[0, half:], preferred_element_type=jnp.float32)
-        pre_up = jnp.dot(first, wu_ref[0, :half], preferred_element_type=jnp.float32)
-        pre_up += jnp.dot(second, wu_ref[0, half:], preferred_element_type=jnp.float32)
+        pre_gate = jnp.dot(first, wg_buffer[e, :half], preferred_element_type=jnp.float32)
+        pre_gate += jnp.dot(second, wg_buffer[e, half:], preferred_element_type=jnp.float32)
+        pre_up = jnp.dot(first, wu_buffer[e, :half], preferred_element_type=jnp.float32)
+        pre_up += jnp.dot(second, wu_buffer[e, half:], preferred_element_type=jnp.float32)
         sig = lax.logistic(pre_gate)
         silu = pre_gate * sig
         act = silu * pre_up
@@ -295,8 +311,8 @@
         d_up = (d_hidden * silu).astype(half_type)
         d_gate = (d_hidden * pre_up * (sig * (1.0 + pre_gate * (1.0 - sig)))).astype(half_type)
         for h in range(2):
-            d_in = nt_dot(d_gate, wg_ref[0, h * half : (h + 1) * half])
-            d_in += nt_dot(d_up, wu_ref[0, h * half : (h + 1) * half])
+            d_in = nt_dot(d_gate, wg_buffer[e, h * half : (h + 1) * half])
+            d_in += nt_dot(d_up, wu_buffer[e, h * half : (h + 1) * half])
             rows_ref[e, h] = d_in.astype(half_type).reshape(QUAD, cap, half)
 
     for which, out_ref in ((0, send_ref), (1, keep_ref)):
@@ -309,16 +325,37 @@
             add_gates(dgate_ref, out_ref, b, flip_ref[1], experts)
 
 
-def output_kernel(experts, cap, flip_ref, target_ref, down_ref, hidden_ref, send_ref, keep_ref, rows_ref):
+def output_kernel(
+    experts,
+    cap,
+    flip_ref,
+    target_ref,
+    down_ref,
+    hidden_ref,
+    send_ref,
+    keep_ref,
+    rows_ref,
+    down_buffer,
+    weight_sems,
+):
     step = pl.program_id(0)
     half = rows_ref.shape[4]
 
+    def weight_copy(e):
+        return pltpu.make_async_copy(down_ref.at[e], down_buffer.at[e], weight_sems.at[e])
+
+    @pl.when(step == 0)
+    def _():
+        for e in range(experts):
+            weight_copy(e).start()
+
     @pl.when(step < experts)
     def _():
+        weight_copy(step).wait()
         for h in range(2):
             out = jnp.dot(
-                hidden_ref[0],
-                down_ref[0, :, h * half : (h + 1) * half],
+                hidden_ref[step],
+                down_buffer[step, :, h * half : (h + 1) * half],
                 preferred_element_type=jnp.float32,
             )
             rows_ref[step, h] = out.astype(half_type).reshape(QUAD, cap, half)
@@ -394,8 +431,8 @@
                 whole(place.shape),
                 whole(gate.shape),
                 whole(target.shape),
-                per_step(gate_w.shape, QUAD, experts),
-                per_step(up_w.shape, QUAD, experts),
+                pl.BlockSpec(memory_space=pl.ANY),
+                pl.BlockSpec(memory_space=pl.ANY),
                 pl.BlockSpec(
                     (1, rows, hidden_units),
                     lambda i, *_: (jnp.clip(i - QUAD, 0, experts - 1), group, 0),
@@ -411,7 +448,10 @@
                 pltpu.VMEM((QUAD, 2, toks, half), half_type),
                 pltpu.VMEM((experts, 2, QUAD, cap, half), half_type),
                 pltpu.VMEM((experts, QUAD, 1, toks), jnp.float32),
+                pltpu.VMEM(gate_w.shape, half_type),
+                pltpu.VMEM(up_w.shape, half_type),
                 pltpu.SemaphoreType.DMA((QUAD, 2)),
+                pltpu.SemaphoreType.DMA((experts, 2)),
             ],
         ),
         compiler_params=pltpu.CompilerParams(
@@ -442,11 +482,15 @@
             grid=(QUAD + experts,),
             in_specs=[
                 whole(target.shape),
-                per_step(down.shape, 0, experts),
-                per_step(hidden.shape, 0, experts),
+                pl.BlockSpec(memory_space=pl.ANY),
+                whole(hidden.shape),
             ],
             out_specs=(per_step(blocks, experts, 2), per_step(blocks, experts + 2, 2)),
-            scratch_shapes=[pltpu.VMEM((experts, 2, QUAD, cap, half), half_type)],
+            scratch_shapes=[
+                pltpu.VMEM((experts, 2, QUAD, cap, half), half_type),
+                pltpu.VMEM(down.shape, half_type),
+                pltpu.SemaphoreType.DMA((experts,)),
+            ],
         ),
         compiler_params=pltpu.CompilerParams(
             dimension_semantics=("arbitrary",), vmem_limit_bytes=VMEM_LIMIT
@@ -690,13 +734,14 @@
     own0, own1, core0, core1 = ([None] * quads for _ in range(4))
     af, asec, ff, fs = ([None] * quads for _ in range(4))
     d_raw = [None]
-    sides_by_tensor = [pair and j != quads - 1 for j in range(quads)]
     hidden = [None] * quads
 
     def make_sums():
         return {
-            name: [None] * quads for name in ("send", "keep", "got", "near", "side_got", "first")
+            name: [None] * quads for name in ("send", "keep", "got", "near", "side_got", "arrived")
         }
+
+    flat_groups = {"grads": (), "outs": (2,)} if pair else {"grads": range(4), "outs": range(4)}
 
     grads, outs = make_sums(), make_sums()
 
@@ -712,7 +757,7 @@
 
     def send_rest(j):
         asec[j] = (
-            other_side(af[j]) if sides_by_tensor[j] else swap(own1[j], data_count, 2)
+            other_side(af[j]) if pair else swap(own1[j], data_count, 2)
         )
         core1[j] = swap(own1[j], data_count, 1)
         ff[j] = swap(af[j], data_count, 1)
@@ -727,24 +772,30 @@
     def run_outputs(k):
         outs["send"][k], outs["keep"][k] = outputs_of(k, hidden[k])
 
+    def is_flat(sums, k):
+        return k in flat_groups["grads" if sums is grads else "outs"]
+
     def sum_cores(sums, k):
         sums["got"][k] = swap(sums["send"][k], data_count, 1)
 
     def sum_sides(sums, k):
         keep, got = sums["keep"][k], sums["got"][k]
         away = plus(keep[1, 1], got[1, 1])
-        sums["side_got"][k] = other_side(away) if pair else swap(away, data_count, 2)
+        sums["side_got"][k] = swap(away, data_count, 2) if is_flat(sums, k) else other_side(away)
         sums["near"][k] = plus(keep[1, 0], got[1, 0])
 
     def sum_across(sums, k):
-        keep, got, near = sums["keep"][k], sums["got"][k], sums["near"][k]
-        if pair:
+        near = sums["near"][k]
+        if not is_flat(sums, k):
             near = plus(near, sums["side_got"][k])
-        sums["first"][k] = plus(keep[0, 0], got[0, 0], swap(near, data_count, 2))
+        sums["arrived"][k] = swap(near, data_count, 2)
+
+    def first_of(sums, k):
+        return [sums["keep"][k][0, 0], sums["got"][k][0, 0], sums["arrived"][k]]
 
     def second_of(sums, k):
         terms = [sums["keep"][k][0, 1], sums["got"][k][0, 1]]
-        return terms if pair else terms + [sums["side_got"][k]]
+        return terms + [sums["side_got"][k]] if is_flat(sums, k) else terms
 
     def onward_sum(*terms):
         return onward(plus(*terms), data_count)
@@ -765,81 +816,86 @@
     send_across(0)
     step_end()
     gates_t = gates_of(own0[0], own1[0])
+    gates_all = lax.all_to_all(
+        gates_t.reshape(data_count, local_experts, tok_count), "dp", 0, 0, tiled=True
+    )[order]
     move_second(0)
     send_rest(0)
     send_across(1)
-    (gates_t,) = step_end(gates_t)
-    gates_all = lax.all_to_all(
-        gates_t.reshape(data_count, local_experts, tok_count), "dp", 0, 0, tiled=True
-    )[order]
+    gates_t, gates_all = step_end(gates_t, gates_all)
     move_first(1)
     send_rest(1)
     send_last(0)
+    d_raw[0] = call_grad_rows(
+        order, place_all[:, :, None, :], expert_down_weight, g_all, capacity
+    )
     step_end()
     move_second(1)
     send_across(2)
     send_last(1)
-    d_raw[0] = call_grad_rows(
-        order, place_all[:, :, None, :], expert_down_weight, g_all, capacity
-    )
-    (gates_all,) = step_end(gates_all)
+    run_experts(1)
+    step_end()
     move_first(2)
     send_rest(2)
-    run_experts(1)
+    sum_cores(grads, 1)
+    run_experts(0)
     step_end()
     move_second(2)
     send_across(3)
     send_last(2)
-    sum_cores(grads, 1)
-    run_experts(0)
-    step_end()
-    send_rest(3)
     sum_sides(grads, 1)
     sum_cores(grads, 0)
     run_experts(2)
     step_end()
+    second = onward_sum(*second_of(grads, 1))
+    send_rest(3)
+    sum_across(grads, 1)
+    sum_cores(grads, 2)
+    run_outputs(1)
+    (second,) = step_end(second)
     send_last(3)
-    sum_across(grads, 1)
-    sum_sides(grads, 0)
-    sum_cores(grads, 2)
-    second = onward_sum(*second_of(grads, 1))
+    sum_sides(grads, 2)
+    second = onward_sum(second, *second_of(grads, 2))
     run_experts(3)
     (second,) = step_end(second)
-    sum_sides(grads, 2)
-    sum_across(grads, 0)
+    first = onward_sum(*first_of(grads, 1))
+    sum_across(grads, 2)
+    sum_sides(grads, 0)
     sum_cores(grads, 3)
-    first = onward(grads["first"][1], data_count)
-    second = onward_sum(second, *second_of(grads, 2))
-    run_outputs(1)
-    first, second = step_end(first, second)
-    sum_sides(grads, 3)
-    sum_across(grads, 2)
-    second = onward_sum(second, *second_of(grads, 3))
     sum_cores(outs, 1)
     run_outputs(2)
     first, second = step_end(first, second)
-    first = onward_sum(first, grads["first"][2])
-    second = plus(second, *second_of(grads, 0))
+    first = onward_sum(first, *first_of(grads, 2))
+    sum_sides(grads, 3)
+    sum_across(grads, 0)
+    sum_cores(outs, 2)
+    run_outputs(3)
+    if pair:
+        second = plus(second, *second_of(grads, 3))
+    first, second = step_end(first, second)
+    if not pair:
+        second = plus(second, *second_of(grads, 3))
+    second = onward(second, data_count)
     sum_across(grads, 3)
-    sum_cores(outs, 2)
+    sum_cores(outs, 3)
     sum_sides(outs, 1)
-    run_outputs(3)
-    first, second = step_end(first, second)
-    first = onward_sum(first, grads["first"][3])
-    sum_cores(outs, 3)
+    run_outputs(0)
+    first, second = step_end(first, plus(second, *second_of(grads, 0)))
+    first = onward_sum(first, *first_of(grads, 3))
+    sum_cores(outs, 0)
     sum_across(outs, 1)
-    run_outputs(0)
     if pair:
         from_other = other_side(second).astype(jnp.float32)
-        grad_moe_cols = first.astype(jnp.float32) + grads["first"][0].astype(jnp.float32) + from_other
+        grad_moe_cols = first.astype(jnp.float32) + from_other
+        for term in first_of(grads, 0):
+            grad_moe_cols += term.astype(jnp.float32)
     else:
-        first = plus(first, grads["first"][0])
+        first = plus(first, *first_of(grads, 0))
         grad_gates = tensor_sum(first[tok_count:])
         grad_moe_cols = own_columns(from_sides(first[:tok_count], second[:tok_count]))
         grad_moe_cols = jnp.pad(grad_moe_cols, ((0, 0), (0, half_width - col_width)))
         grad_moe_cols = jnp.concatenate([grad_moe_cols, grad_gates], axis=0)
     (grad_moe_cols,) = step_end(grad_moe_cols)
-    sum_cores(outs, 0)
     sum_sides(outs, 2)
     out_second = onward_sum(*second_of(outs, 1))
     d_gate_home = grad_moe_cols[tok_count:].reshape(expert_total, tok_count)
@@ -865,13 +921,12 @@
         - mixed_cols * (mixed_scale * mixed_scale * mixed_scale * (along / MODEL_WIDTH))
     )
     branch_cols = grad_mixed_cols.astype(half_type)
-    branch_cols, out_second = step_end(branch_cols, out_second)
+    grad_branch = from_sides(*both_halves(branch_cols))
+    grad_branch, out_second = step_end(grad_branch, out_second)
+    out_first = onward_sum(*first_of(outs, 1))
     sum_across(outs, 2)
     out_second = onward_sum(out_second, *second_of(outs, 2))
-    grad_branch = from_sides(*both_halves(branch_cols))
-    grad_branch, out_second = step_end(grad_branch, out_second)
     sum_sides(outs, 3)
-    out_first = onward(outs["first"][1], data_count)
 
     grad_latent_out = nt_dot(grad_branch, out_up_rows).astype(half_type)
     grad_up_out = lax.dot_general(
@@ -892,10 +947,10 @@
         head_shared,
         3,
     )
-    grad_raw, out_first = step_end(grad_raw, out_first)
+    grad_raw, out_first, out_second = step_end(grad_raw, out_first, out_second)
+    out_first = onward_sum(out_first, *first_of(outs, 2))
     sum_sides(outs, 0)
     sum_across(outs, 3)
-    out_first = onward_sum(out_first, outs["first"][2])
     latent_parts = jnp.concatenate([nt_dot(grad_raw[p], up_rows[p]) for p in range(3)], axis=1)
     grad_latent = tensor_sum(latent_parts.astype(half_type)).astype(half_type)
     grad_up = [
@@ -935,11 +990,11 @@
     grad_normed_part += nt_dot(grad_raw[2], w_proj[2])
     grad_normed_mine, grad_normed_other = split_columns(grad_normed_part)
     grad_normed_other, out_first = step_end(grad_normed_other, out_first)
+    out_second = onward_sum(out_second, *second_of(outs, 3))
     sum_across(outs, 0)
-    out_second = onward_sum(out_second, *second_of(outs, 3))
     grad_normed_cols = join_columns(grad_normed_mine, grad_normed_other)
     grad_normed_cols, out_second = step_end(grad_normed_cols, out_second)
-    out_first = plus(onward_sum(out_first, outs["first"][3]), outs["first"][0])
+    out_first = plus(onward_sum(out_first, *first_of(outs, 3)), *first_of(outs, 0))
     out_second = plus(out_second, *second_of(outs, 0))
     if pair:
         moe_cols = out_first.astype(jnp.float32) + other_side(out_second).astype(jnp.float32)

time: 934 us -> 882 us (0.944)
  waiting for transfers between devices: 359 us -> 321 us
    ppermute x37, waiting for transfers between devices: 138 us -> 51.4 us  [swap(): return lax.ppermute(values, 'dp', [(i, i ^ bit) for i in range(data_count)])]
    all_gather x1, waiting for transfers between devices: 0.01 us -> 54.2 us  [local(): g_all = lax.all_gather(cotangent, ('dp', 'tensor'), axis=0)]
    ppermute x18, waiting for transfers between devices: 139 us -> 120 us  [onward(): lax.ppermute(values, 'dp', [(i, (i + QUAD) % data_count) for i in range(d...]
    ppermute x22, waiting for transfers between devices: 68.5 us -> 86.3 us  [other_side(): return lax.ppermute(values, 'tensor', [(0, 1), (1, 0)])]
    ppermute x18, starting transfers between devices: 34.1 us -> 23.4 us  [onward(): lax.ppermute(values, 'dp', [(i, (i + QUAD) % data_count) for i in range(d...]
    convert_element_type x35 -> x29, other arithmetic: 89 us -> 78.9 us  [plus(): return total.astype(half_type)]
  transfers between devices with their start and end apart: 81 -> 81, of which waited for: 26 -> 29; matrix products, arithmetic and copies ran while one was open for 18% -> 18% of each run, Pallas kernels for 29% -> 30%
where the time goes in v4:
time: 882 us; the launch traced here: 872 us
  waiting for transfers between devices  321 us (36%)
  Pallas kernels  261 us (30%)
  other arithmetic  100 us (11%)
  starting transfers between devices  86.6 us (10%)
  matrix products  57.3 us (6%)
  local copies, waits for them, and re-layouts  29.1 us (3%)
  between operations  16.6 us (2%)
    ppermute x18, waiting for transfers between devices, onward(): lax.ppermute(values, 'dp', [(i, (i + QUAD) % data_count) for i in range(d...  120 us
    pallas_call x4, Pallas kernels, call_experts(): pl.pallas_call(functools.partial(expert_kernel, experts, cap), out_shape=...  118 us
    ppermute x22, waiting for transfers between devices, other_side(): return lax.ppermute(values, 'tensor', [(0, 1), (1, 0)])  86.3 us
    convert_element_type x29, other arithmetic, plus(): return total.astype(half_type)  78.9 us
    pallas_call x4, Pallas kernels, call_output(): pl.pallas_call(functools.partial(output_kernel, experts, cap), out_shape=...  64.8 us
    all_gather x1, waiting for transfers between devices, local(): g_all = lax.all_gather(cotangent, ('dp', 'tensor'), axis=0)  54.2 us
    ppermute x37, waiting for transfers between devices, swap(): return lax.ppermute(values, 'dp', [(i, i ^ bit) for i in range(data_count)])  51.4 us
    pallas_call x2, Pallas kernels, call_heads(): pl.pallas_call(kernel, out_shape=[jax.ShapeDtypeStruct((toks, width), hal...  41.6 us
  transfers between devices with their start and end apart: 81, of which 29 were waited for; matrix products, arithmetic and copies ran while one was open for 18% of the time, Pallas kernels for 30%

profile of v4, /device:TPU:0, one launch (start us, length us, event | category | flops | bytes accessed | tf_op | source)
XLA Modules:
  0.0 871.9 jit_solution(11236736842385524918)
XLA Ops:
  10.4 7.4 all-to-all-start
  42.6 19.2 %attend.1 = (bf16[512,1024]{1,0:T(8,128)(2,1)}, bf16[512,1024]{1,0:T(8,128)(2,1)}, bf16[512,1024]{1,0:T(8,128)(2,1)}, bf16[512,1024]{1,0:T(8,128)(2,1)}) custom-call(f32[512,1024]{1,0:T(8,128)} %convolution_add_fusion.2.raw_q, f32[512,1024]{1,0:T(8,128)} %convolution_add_fusion.1.raw_k, f32[512,1024]{1,0:T(8,128)} %convolution_add_fusion.raw_v, ...), custom_call_target="tpu_custom_call" | custom-call | flops 2684354560 | bytes 4194304 | tf_op jit(solution)/shard_map/attend/pallas_call | solution.py:105
  61.9 3.6 fusion.127
  70.2 24.5 %collective-permute-done.1 = bf16[512,16]{0,1:T(8,128)(2,1)S(1)} collective-permute-done((bf16[512,16]{0,1:T(8,128)(2,1)S(1)}, bf16[512,16]{0,1:T(8,128)(2,1)S(1)}, u32[]{:S(2)}, u32[]{:S(2)}) %collective-permute-start.1) | collective-permute-done | bytes 16416 | tf_op jit(solution)/shard_map/ppermute | solution.py:516
  103.3 37.4 %collective-permute-done.3.own_first_ref = bf16[512,1024]{1,0:T(8,128)(2,1)} collective-permute-done((bf16[512,1024]{1,0:T(8,128)(2,1)S(1)}, bf16[512,1024]{1,0:T(8,128)(2,1)}, u32[]{:S(2)}, u32[]{:S(2)}) %collective-permute-start.3) | collective-permute-done | bytes 1048608 | tf_op jit(solution)/shard_map/ppermute | solution.py:512
  143.6 7.6 collective-permute-start.7
  151.2 37.5 %collective-permute-done.10.across_first_ref = bf16[512,1024]{1,0:T(8,128)(2,1)} collective-permute-done((bf16[512,1024]{1,0:T(8,128)(2,1)}, bf16[512,1024]{1,0:T(8,128)(2,1)}, u32[]{:S(2)}, u32[]{:S(2)}) %collective-permute-start.10) | collective-permute-done | bytes 1048608 | tf_op jit(solution)/shard_map/ppermute | solution.py:508
  190.4 12.8 %all-to-all-start.1 = ((f32[16,4,512]{2,1,0:T(4,128)}), f32[16,4,512]{2,1,0:T(4,128)S(1)}, u32[]{:S(2)}, u32[]{:S(2)}) async-start(f32[16,4,512]{2,1,0:T(4,128)} %reshape.325), calls=%async_computation.1 | async-start | bytes 262144 | tf_op jit(solution)/shard_map/all_to_all | solution.py:819
  204.6 9.0 %all-to-all-done.1 = f32[16,4,512]{2,1,0:T(4,128)S(1)} async-done(((f32[16,4,512]{2,1,0:T(4,128)}), f32[16,4,512]{2,1,0:T(4,128)S(1)}, u32[]{:S(2)}, u32[]{:S(2)}) %all-to-all-start.1) | async-done | bytes 131104 | tf_op jit(solution)/shard_map/all_to_all | solution.py:819
  216.4 54.2 %all-gather.5.cloned.1.call-done = bf16[16384,1024]{1,0:T(8,128)(2,1)} async-done(((bf16[512,1024]{1,0:T(8,128)(2,1)}), bf16[16384,1024]{1,0:T(8,128)(2,1)}) %all-gather.5.cloned.1.call-update) | async-done | bytes 33554448 | tf_op jit(solution)/shard_map/all_gather | solution.py:638
  270.6 36.3 %grad_rows.1.dh_ref = bf16[4,1280,512]{2,1,0:T(8,128)(2,1)} custom-call(s32[16]{0:T(128)} %fusion.105.block_ids, s32[16,4,1,512]{3,2,1,0:T(1,128)} %broadcast_in_dim.86.place_ref, bf16[4,512,2048]{2,1,0:T(8,128)(2,1)} %down_ref.9, bf16[16,2,512,1024]{3,2,1,0:T(8,128)(2,1)} %bitcast.251), custom_call_target="tpu_custom_call" | custom-call | flops 42949672960 | bytes 47185920 | tf_op jit(solution)/shard_map/grad_rows/pallas_call | solution.py:386
  313.4 29.5 %experts.4 = (bf16[2,2,544,1024]{3,2,1,0:T(8,128)(2,1)}, bf16[2,2,544,1024]{3,2,1,0:T(8,128)(2,1)}, bf16[4,320,512]{2,1,0:T(8,128)(2,1)}) custom-call(s32[2]{0:T(128)} %pad_add_fusion.flip_ref, s32[4,4,1,512]{3,2,1,0:T(1,128)} %broadcast_in_dim.87.place_ref, f32[4,4,1,512]{3,2,1,0:T(1,128)} %copy.88.gate_ref, s32[4,512,4]{2,1,0:T(8,128)} %get-tuple-element.576.target_ref, ...), custom_call_target="tpu_custom_call" | custom-call | flops 24159191040 | bytes 33554432 | tf_op jit(solution)/shard_map/experts/pallas_call | solution.py:420
  347.1 29.8 %experts.5 = (bf16[2,2,544,1024]{3,2,1,0:T(8,128)(2,1)}, bf16[2,2,544,1024]{3,2,1,0:T(8,128)(2,1)}, bf16[4,320,512]{2,1,0:T(8,128)(2,1)}) custom-call(s32[2]{0:T(128)} %pad_add_fusion.flip_ref, s32[4,4,1,512]{3,2,1,0:T(1,128)} %broadcast_in_dim.89.place_ref, f32[4,4,1,512]{3,2,1,0:T(1,128)} %copy.89.gate_ref, s32[4,512,4]{2,1,0:T(8,128)} %get-tuple-element.575.target_ref, ...), custom_call_target="tpu_custom_call" | custom-call | flops 24159191040 | bytes 33554432 | tf_op jit(solution)/shard_map/experts/pallas_call | solution.py:420
  382.9 3.5 collective-permute-done.30.far_second_ref
  386.7 29.7 %experts.6 = (bf16[2,2,544,1024]{3,2,1,0:T(8,128)(2,1)}, bf16[2,2,544,1024]{3,2,1,0:T(8,128)(2,1)}, bf16[4,320,512]{2,1,0:T(8,128)(2,1)}) custom-call(s32[2]{0:T(128)} %pad_add_fusion.flip_ref, s32[4,4,1,512]{3,2,1,0:T(1,128)} %broadcast_in_dim.91.place_ref, f32[4,4,1,512]{3,2,1,0:T(1,128)} %copy.90.gate_ref, s32[4,512,4]{2,1,0:T(8,128)} %get-tuple-element.574.target_ref, ...), custom_call_target="tpu_custom_call" | custom-call | flops 24159191040 | bytes 33554432 | tf_op jit(solution)/shard_map/experts/pallas_call | solution.py:420
  419.7 3.5 collective-permute-start.38
  426.0 16.1 %outputs.4 = (bf16[2,2,512,1024]{3,2,1,0:T(8,128)(2,1)}, bf16[2,2,512,1024]{3,2,1,0:T(8,128)(2,1)}) custom-call(s32[2]{0:T(128)} %pad_add_fusion.flip_ref, s32[4,512,4]{2,1,0:T(8,128)} %get-tuple-element.576.target_ref, bf16[4,512,2048]{2,1,0:T(8,128)(2,1)} %down_ref.9, bf16[4,320,512]{2,1,0:T(8,128)(2,1)} %get-tuple-element.344.hidden_ref), custom_call_target="tpu_custom_call" | custom-call | flops 10737418240 | bytes 16777216 | tf_op jit(solution)/shard_map/outputs/pallas_call | solution.py:474
  442.2 8.1 collective-permute-done.34.across_second_ref
  460.0 29.2 %experts.7 = (bf16[2,2,544,1024]{3,2,1,0:T(8,128)(2,1)}, bf16[2,2,544,1024]{3,2,1,0:T(8,128)(2,1)}, bf16[4,320,512]{2,1,0:T(8,128)(2,1)}) custom-call(s32[2]{0:T(128)} %pad_add_fusion.flip_ref, s32[4,4,1,512]{3,2,1,0:T(1,128)} %broadcast_in_dim.93.place_ref, f32[4,4,1,512]{3,2,1,0:T(1,128)} %broadcast_in_dim.94.gate_ref, ...), custom_call_target="tpu_custom_call" | custom-call | flops 24159191040 | bytes 33554432 | tf_op jit(solution)/shard_map/experts/pallas_call | solution.py:420
  497.5 3.5 fusion.48
  502.8 16.1 %outputs.5 = (bf16[2,2,512,1024]{3,2,1,0:T(8,128)(2,1)}, bf16[2,2,512,1024]{3,2,1,0:T(8,128)(2,1)}) custom-call(s32[2]{0:T(128)} %pad_add_fusion.flip_ref, s32[4,512,4]{2,1,0:T(8,128)} %get-tuple-element.574.target_ref, bf16[4,512,2048]{2,1,0:T(8,128)(2,1)} %down_ref.9, bf16[4,320,512]{2,1,0:T(8,128)(2,1)} %get-tuple-element.380.hidden_ref), custom_call_target="tpu_custom_call" | custom-call | flops 10737418240 | bytes 16777216 | tf_op jit(solution)/shard_map/outputs/pallas_call | solution.py:474
  523.4 3.8 collective-permute-done.43
  527.2 4.2 fusion.11
  542.9 16.3 %outputs.6 = (bf16[2,2,512,1024]{3,2,1,0:T(8,128)(2,1)}, bf16[2,2,512,1024]{3,2,1,0:T(8,128)(2,1)}) custom-call(s32[2]{0:T(128)} %pad_add_fusion.flip_ref, s32[4,512,4]{2,1,0:T(8,128)} %get-tuple-element.573.target_ref, bf16[4,512,2048]{2,1,0:T(8,128)(2,1)} %down_ref.9, bf16[4,320,512]{2,1,0:T(8,128)(2,1)} %get-tuple-element.399.hidden_ref), custom_call_target="tpu_custom_call" | custom-call | flops 10737418240 | bytes 16777216 | tf_op jit(solution)/shard_map/outputs/pallas_call | solution.py:474
  561.4 3.6 collective-permute-done.47
  564.9 3.9 collective-permute-start.54
  568.9 4.1 fusion.52
  578.2 16.2 %outputs.7 = (bf16[2,2,512,1024]{3,2,1,0:T(8,128)(2,1)}, bf16[2,2,512,1024]{3,2,1,0:T(8,128)(2,1)}) custom-call(s32[2]{0:T(128)} %pad_add_fusion.flip_ref, s32[4,512,4]{2,1,0:T(8,128)} %get-tuple-element.575.target_ref, bf16[4,512,2048]{2,1,0:T(8,128)(2,1)} %down_ref.9, bf16[4,320,512]{2,1,0:T(8,128)(2,1)} %get-tuple-element.417.hidden_ref), custom_call_target="tpu_custom_call" | custom-call | flops 10737418240 | bytes 16777216 | tf_op jit(solution)/shard_map/outputs/pallas_call | solution.py:474
  598.6 5.3 collective-permute-done.51
  609.7 25.6 %collective-permute-done.57 = bf16[544,1024]{1,0:T(8,128)(2,1)S(1)} collective-permute-done((bf16[544,1024]{1,0:T(8,128)(2,1)S(1)}, bf16[544,1024]{1,0:T(8,128)(2,1)S(1)}, u32[]{:S(2)}, u32[]{:S(2)}) %collective-permute-start.57) | collective-permute-done | bytes 1114144 | tf_op jit(solution)/shard_map/ppermute | solution.py:512
  635.3 4.6 fusion.5
  647.0 3.7 fusion.122
  653.0 3.5 fusion.54
  657.2 17.1 %collective-permute-done.61 = bf16[512,1024]{1,0:T(8,128)(2,1)S(1)} collective-permute-done((bf16[512,1024]{1,0:T(8,128)(2,1)S(1)}, bf16[512,1024]{1,0:T(8,128)(2,1)S(1)}, u32[]{:S(2)}, u32[]{:S(2)}) %collective-permute-start.61) | collective-permute-done | bytes 1048608 | tf_op jit(solution)/shard_map/ppermute | solution.py:516
  674.7 3.5 collective-permute-done.62
  690.0 4.0 fusion.57
  699.9 22.4 %attend_back.1 = (bf16[512,1024]{1,0:T(8,128)(2,1)}, bf16[512,1024]{1,0:T(8,128)(2,1)}, bf16[512,1024]{1,0:T(8,128)(2,1)}) custom-call(f32[512,1024]{1,0:T(8,128)} %convolution_add_fusion.2.raw_q, f32[512,1024]{1,0:T(8,128)} %convolution_add_fusion.1.raw_k, bf16[512,1024]{1,0:T(8,128)(2,1)} %get-tuple-element.475.queries, ...), custom_call_target="tpu_custom_call" | custom-call | flops 2684354560 | bytes 4194304 | tf_op jit(solution)/shard_map/attend_back/pallas_call | solution.py:105
  722.8 7.1 collective-permute-done.65
  750.5 4.5 fusion.128
  755.0 4.3 fusion.129
  759.3 6.1 add_add_fusion
  765.6 11.9 %collective-permute-done.69 = bf16[512,1024]{1,0:T(8,128)(2,1)S(1)} collective-permute-done((bf16[512,1024]{1,0:T(8,128)(2,1)S(1)}, bf16[512,1024]{1,0:T(8,128)(2,1)S(1)}, u32[]{:S(2)}, u32[]{:S(2)}) %collective-permute-start.69) | collective-permute-done | bytes 1048608 | tf_op jit(solution)/shard_map/ppermute | solution.py:512
  784.3 8.8 %collective-permute-done.71 = bf16[512,1024]{1,0:T(8,128)(2,1)S(1)} collective-permute-done((bf16[512,1024]{1,0:T(8,128)(2,1)S(1)}, bf16[512,1024]{1,0:T(8,128)(2,1)S(1)}, u32[]{:S(2)}, u32[]{:S(2)}) %collective-permute-start.71) | collective-permute-done | bytes 1048608 | tf_op jit(solution)/shard_map/ppermute | solution.py:516
  793.7 30.0 %collective-permute-done.72 = bf16[512,1024]{1,0:T(8,128)(2,1)S(1)} collective-permute-done((bf16[512,1024]{1,0:T(8,128)(2,1)S(1)}, bf16[512,1024]{1,0:T(8,128)(2,1)S(1)}, u32[]{:S(2)}, u32[]{:S(2)}) %collective-permute-start.72) | collective-permute-done | bytes 1048608 | tf_op jit(solution)/shard_map/ppermute | solution.py:512
  832.9 10.7 %collective-permute-done.76 = f32[512,1]{0,1:T(1,128)S(1)} collective-permute-done((f32[512,1]{0,1:T(1,128)S(1)}, f32[512,1]{0,1:T(1,128)S(1)}, u32[]{:S(2)}, u32[]{:S(2)}) %collective-permute-start.76) | collective-permute-done | bytes 2080 | tf_op jit(solution)/shard_map/ppermute | solution.py:516
  845.7 3.5 add_convert_fusion.13
  849.2 5.9 fusion
  859.0 3.5 copy.93
  (407 shorter events, 198.7 us)
Async XLA Ops:
  7.2 263.4 %all-gather.5.cloned.1.call-start = ((), (), s32[]{:S(2)}) async-start(), calls=%async_computation.2 | async-start | bytes 34603008 | tf_op jit(solution)/shard_map/all_gather | solution.py:638
  99.7 40.9 %collective-permute-start.3 = (bf16[512,1024]{1,0:T(8,128)(2,1)S(1)}, bf16[512,1024]{1,0:T(8,128)(2,1)}, u32[]{:S(2)}, u32[]{:S(2)}) collective-permute-start(bf16[512,1024]{1,0:T(8,128)(2,1)S(1)} %multiply_convert_fusion.own_first_ref), channel_id=1, source_target_pairs={{0,8},{2,10},{4,12},{6,14},{8,16},{10,18},{12,20},{14,22},{16,24},... | collective-permute-start | bytes 3145736 | tf_op jit(solution)/shard_map/ppermute | solution.py:512
  101.2 39.4 %collective-permute-start.4 = (bf16[512,1024]{1,0:T(8,128)(2,1)S(1)}, bf16[512,1024]{1,0:T(8,128)(2,1)S(1)}, u32[]{:S(2)}, u32[]{:S(2)}) collective-permute-start(bf16[512,1024]{1,0:T(8,128)(2,1)S(1)} %multiply_convert_fusion.own_first_ref), channel_id=1, source_target_pairs={{0,1},{1,0},{2,3},{3,2},{4,5},{5,4},{6,7},{7,6},{8,9},{9,8},{10,11... | collective-permute-start | bytes 3145736 | tf_op jit(solution)/shard_map/ppermute | solution.py:516
  101.8 38.9 %collective-permute-start.5 = (bf16[512,1024]{1,0:T(8,128)(2,1)S(1)}, bf16[512,1024]{1,0:T(8,128)(2,1)S(1)}, u32[]{:S(2)}, u32[]{:S(2)}) collective-permute-start(bf16[512,1024]{1,0:T(8,128)(2,1)S(1)} %multiply_convert_fusion.own_first_ref), channel_id=1, source_target_pairs={{0,2},{2,0},{4,6},{6,4},{8,10},{10,8},{12,14},{14,12},{16,18},{18,... | collective-permute-start | bytes 3145736 | tf_op jit(solution)/shard_map/ppermute | solution.py:508
  101.8 38.9 %collective-permute-start.6 = (bf16[512,1024]{1,0:T(8,128)(2,1)S(1)}, bf16[512,1024]{1,0:T(8,128)(2,1)}, u32[]{:S(2)}, u32[]{:S(2)}) collective-permute-start(bf16[512,1024]{1,0:T(8,128)(2,1)S(1)} %multiply_convert_fusion.own_first_ref), channel_id=1, source_target_pairs={{0,4},{2,6},{4,0},{6,2},{8,12},{10,14},{12,8},{14,10},{16,20},{18,... | collective-permute-start | bytes 3145736 | tf_op jit(solution)/shard_map/ppermute | solution.py:508
  140.6 48.0 %collective-permute-start.10 = (bf16[512,1024]{1,0:T(8,128)(2,1)}, bf16[512,1024]{1,0:T(8,128)(2,1)}, u32[]{:S(2)}, u32[]{:S(2)}) collective-permute-start(bf16[512,1024]{1,0:T(8,128)(2,1)} %collective-permute-done.3.own_first_ref), channel_id=1, source_target_pairs={{0,4},{2,6},{4,0},{6,2},{8,12},{10,14},{12,8},{14,10},{16,20},{18,... | collective-permute-start | bytes 3145736 | tf_op jit(solution)/shard_map/ppermute | solution.py:508
  141.8 72.4 %collective-permute-start.11 = (bf16[512,1024]{1,0:T(8,128)(2,1)}, bf16[512,1024]{1,0:T(8,128)(2,1)}, u32[]{:S(2)}, u32[]{:S(2)}) collective-permute-start(bf16[512,1024]{1,0:T(8,128)(2,1)} %collective-permute-done.6.across_first_ref), channel_id=1, source_target_pairs={{0,1},{1,0},{2,3},{3,2},{4,5},{5,4},{6,7},{7,6},{8,9},{9,8},{10,11... | collective-permute-start | bytes 3145736 | tf_op jit(solution)/shard_map/ppermute | solution.py:516
  143.0 71.2 %collective-permute-start.12 = (bf16[512,1024]{1,0:T(8,128)(2,1)}, bf16[512,1024]{1,0:T(8,128)(2,1)}, u32[]{:S(2)}, u32[]{:S(2)}) collective-permute-start(bf16[512,1024]{1,0:T(8,128)(2,1)} %collective-permute-done.6.across_first_ref), channel_id=1, source_target_pairs={{0,2},{2,0},{4,6},{6,4},{8,10},{10,8},{12,14},{14,12},{16,18},{18,... | collective-permute-start | bytes 3145736 | tf_op jit(solution)/shard_map/ppermute | solution.py:508
  143.0 71.2 %collective-permute-start.8 = (bf16[512,1024]{1,0:T(8,128)(2,1)}, bf16[512,1024]{1,0:T(8,128)(2,1)}, u32[]{:S(2)}, u32[]{:S(2)}) collective-permute-start(bf16[512,1024]{1,0:T(8,128)(2,1)} %collective-permute-done.3.own_first_ref), channel_id=1, source_target_pairs={{0,2},{2,0},{4,6},{6,4},{8,10},{10,8},{12,14},{14,12},{16,18},{18,... | collective-permute-start | bytes 3145736 | tf_op jit(solution)/shard_map/ppermute | solution.py:508
  143.6 70.7 %collective-permute-start.7 = (bf16[512,1024]{1,0:T(8,128)(2,1)S(1)}, bf16[512,1024]{1,0:T(8,128)(2,1)}, u32[]{:S(2)}, u32[]{:S(2)}) collective-permute-start(bf16[512,1024]{1,0:T(8,128)(2,1)S(1)} %collective-permute-done.4.own_second_ref), channel_id=1, source_target_pairs={{0,8},{2,10},{4,12},{6,14},{8,16},{10,18},{12,20},{14,22},{16,24},... | collective-permute-start | bytes 3145736 | tf_op jit(solution)/shard_map/ppermute | solution.py:512
  203.2 646.0 %all-gather.7.cloned.1.call-start = ((), (), s32[]{:S(2)}) async-start(), calls=%async_computation.3 | async-start | bytes 6127616 | tf_op jit(solution)/shard_map/all_gather | solution.py:971
  214.3 92.6 %collective-permute-start.15 = (bf16[512,1024]{1,0:T(8,128)(2,1)}, bf16[512,1024]{1,0:T(8,128)(2,1)}, u32[]{:S(2)}, u32[]{:S(2)}) collective-permute-start(bf16[512,1024]{1,0:T(8,128)(2,1)} %collective-permute-done.10.across_first_ref), channel_id=1, source_target_pairs={{0,1},{1,0},{2,3},{3,2},{4,5},{5,4},{6,7},{7,6},{8,9},{9,8},{10,11... | collective-permute-start | bytes 3145736 | tf_op jit(solution)/shard_map/ppermute | solution.py:516
  215.8 91.0 %collective-permute-start.16 = (bf16[512,1024]{1,0:T(8,128)(2,1)}, bf16[512,1024]{1,0:T(8,128)(2,1)}, u32[]{:S(2)}, u32[]{:S(2)}) collective-permute-start(bf16[512,1024]{1,0:T(8,128)(2,1)} %collective-permute-done.10.across_first_ref), channel_id=1, source_target_pairs={{0,2},{2,0},{4,6},{6,4},{8,10},{10,8},{12,14},{14,12},{16,18},{18,... | collective-permute-start | bytes 3145736 | tf_op jit(solution)/shard_map/ppermute | solution.py:508
  215.8 91.0 %collective-permute-start.13 = (bf16[512,1024]{1,0:T(8,128)(2,1)}, bf16[512,1024]{1,0:T(8,128)(2,1)S(1)}, u32[]{:S(2)}, u32[]{:S(2)}) collective-permute-start(bf16[512,1024]{1,0:T(8,128)(2,1)} %collective-permute-done.3.own_first_ref), channel_id=1, source_target_pairs={{0,8},{2,10},{4,12},{6,14},{8,16},{10,18},{12,20},{14,22},{16,24},... | collective-permute-start | bytes 3145736 | tf_op jit(solution)/shard_map/ppermute | solution.py:512
  215.9 91.0 %collective-permute-start.14 = (bf16[512,1024]{1,0:T(8,128)(2,1)}, bf16[512,1024]{1,0:T(8,128)(2,1)}, u32[]{:S(2)}, u32[]{:S(2)}) collective-permute-start(bf16[512,1024]{1,0:T(8,128)(2,1)} %collective-permute-done.7.own_second_ref), channel_id=1, source_target_pairs={{0,2},{2,0},{4,6},{6,4},{8,10},{10,8},{12,14},{14,12},{16,18},{18,... | collective-permute-start | bytes 3145736 | tf_op jit(solution)/shard_map/ppermute | solution.py:508
  216.4 90.5 %collective-permute-start.17 = (bf16[512,1024]{1,0:T(8,128)(2,1)}, bf16[512,1024]{1,0:T(8,128)(2,1)S(1)}, u32[]{:S(2)}, u32[]{:S(2)}) collective-permute-start(bf16[512,1024]{1,0:T(8,128)(2,1)} %collective-permute-done.11.across_second_ref), channel_id=1, source_target_pairs={{0,2},{2,0},{4,6},{6,4},{8,10},{10,8},{12,14},{14,12},{16,18},{18,... | collective-permute-start | bytes 3145736 | tf_op jit(solution)/shard_map/ppermute | solution.py:508
  311.4 31.4 %collective-permute-start.19 = (bf16[512,1024]{1,0:T(8,128)(2,1)S(1)}, bf16[512,1024]{1,0:T(8,128)(2,1)S(1)}, u32[]{:S(2)}, u32[]{:S(2)}) collective-permute-start(bf16[512,1024]{1,0:T(8,128)(2,1)S(1)} %collective-permute-done.13.own_first_ref), channel_id=1, source_target_pairs={{0,2},{2,0},{4,6},{6,4},{8,10},{10,8},{12,14},{14,12},{16,18},{18,... | collective-permute-start | bytes 3145736 | tf_op jit(solution)/shard_map/ppermute | solution.py:508
  311.7 31.2 %collective-permute-start.20 = (bf16[512,1024]{1,0:T(8,128)(2,1)S(1)}, bf16[512,1024]{1,0:T(8,128)(2,1)S(1)}, u32[]{:S(2)}, u32[]{:S(2)}) collective-permute-start(bf16[512,1024]{1,0:T(8,128)(2,1)S(1)} %collective-permute-done.13.own_first_ref), channel_id=1, source_target_pairs={{0,4},{2,6},{4,0},{6,2},{8,12},{10,14},{12,8},{14,10},{16,20},{18,... | collective-permute-start | bytes 3145736 | tf_op jit(solution)/shard_map/ppermute | solution.py:508
  313.1 29.7 %collective-permute-start.18 = (bf16[512,1024]{1,0:T(8,128)(2,1)}, bf16[512,1024]{1,0:T(8,128)(2,1)}, u32[]{:S(2)}, u32[]{:S(2)}) collective-permute-start(bf16[512,1024]{1,0:T(8,128)(2,1)} %collective-permute-done.7.own_second_ref), channel_id=1, source_target_pairs={{0,8},{2,10},{4,12},{6,14},{8,16},{10,18},{12,20},{14,22},{16,24},... | collective-permute-start | bytes 3145736 | tf_op jit(solution)/shard_map/ppermute | solution.py:512
  342.9 34.1 %collective-permute-start.26 = (bf16[2,2,544,1024]{3,2,1,0:T(8,128)(2,1)}, bf16[2,2,544,1024]{3,2,1,0:T(8,128)(2,1)}, u32[]{:S(2)}, u32[]{:S(2)}) collective-permute-start(bf16[2,2,544,1024]{3,2,1,0:T(8,128)(2,1)} %get-tuple-element.317), channel_id=1, source_target_pairs={{0,2},{2,0},{4,6},{6,4},{8,10},{10,8},{12,14},{14,12},{16,18},{18,... | collective-permute-start | bytes 13369352 | tf_op jit(solution)/shard_map/ppermute | solution.py:508
  344.4 32.6 %collective-permute-start.24 = (bf16[512,1024]{1,0:T(8,128)(2,1)S(1)}, bf16[512,1024]{1,0:T(8,128)(2,1)}, u32[]{:S(2)}, u32[]{:S(2)}) collective-permute-start(bf16[512,1024]{1,0:T(8,128)(2,1)S(1)} %collective-permute-done.20.across_first_ref), channel_id=1, source_target_pairs={{0,1},{1,0},{2,3},{3,2},{4,5},{5,4},{6,7},{7,6},{8,9},{9,8},{10,11... | collective-permute-start | bytes 3145736 | tf_op jit(solution)/shard_map/ppermute | solution.py:516
  345.9 31.1 %collective-permute-start.25 = (bf16[512,1024]{1,0:T(8,128)(2,1)S(1)}, bf16[512,1024]{1,0:T(8,128)(2,1)}, u32[]{:S(2)}, u32[]{:S(2)}) collective-permute-start(bf16[512,1024]{1,0:T(8,128)(2,1)S(1)} %collective-permute-done.20.across_first_ref), channel_id=1, source_target_pairs={{0,2},{2,0},{4,6},{6,4},{8,10},{10,8},{12,14},{14,12},{16,18},{18,... | collective-permute-start | bytes 3145736 | tf_op jit(solution)/shard_map/ppermute | solution.py:508
  345.9 31.0 %collective-permute-start.22 = (bf16[512,1024]{1,0:T(8,128)(2,1)S(1)}, bf16[512,1024]{1,0:T(8,128)(2,1)}, u32[]{:S(2)}, u32[]{:S(2)}) collective-permute-start(bf16[512,1024]{1,0:T(8,128)(2,1)S(1)} %collective-permute-done.13.own_first_ref), channel_id=1, source_target_pairs={{0,8},{2,10},{4,12},{6,14},{8,16},{10,18},{12,20},{14,22},{16,24},... | collective-permute-start | bytes 3145736 | tf_op jit(solution)/shard_map/ppermute | solution.py:512
  347.0 30.0 %collective-permute-start.23 = (bf16[512,1024]{1,0:T(8,128)(2,1)}, bf16[512,1024]{1,0:T(8,128)(2,1)}, u32[]{:S(2)}, u32[]{:S(2)}) collective-permute-start(bf16[512,1024]{1,0:T(8,128)(2,1)} %collective-permute-done.18.own_second_ref), channel_id=1, source_target_pairs={{0,2},{2,0},{4,6},{6,4},{8,10},{10,8},{12,14},{14,12},{16,18},{18,... | collective-permute-start | bytes 3145736 | tf_op jit(solution)/shard_map/ppermute | solution.py:508
  377.0 39.4 %collective-permute-start.31 = (bf16[2,2,544,1024]{3,2,1,0:T(8,128)(2,1)}, bf16[2,2,544,1024]{3,2,1,0:T(8,128)(2,1)}, u32[]{:S(2)}, u32[]{:S(2)}) collective-permute-start(bf16[2,2,544,1024]{3,2,1,0:T(8,128)(2,1)} %get-tuple-element.332), channel_id=1, source_target_pairs={{0,2},{2,0},{4,6},{6,4},{8,10},{10,8},{12,14},{14,12},{16,18},{18,... | collective-permute-start | bytes 13369352 | tf_op jit(solution)/shard_map/ppermute | solution.py:508
  378.8 37.5 %collective-permute-start.28 = (bf16[512,1024]{1,0:T(8,128)(2,1)}, bf16[512,1024]{1,0:T(8,128)(2,1)}, u32[]{:S(2)}, u32[]{:S(2)}) collective-permute-start(bf16[512,1024]{1,0:T(8,128)(2,1)} %collective-permute-done.22.own_first_ref), channel_id=1, source_target_pairs={{0,2},{2,0},{4,6},{6,4},{8,10},{10,8},{12,14},{14,12},{16,18},{18,... | collective-permute-start | bytes 3145736 | tf_op jit(solution)/shard_map/ppermute | solution.py:508
  379.2 37.2 %collective-permute-start.29 = (bf16[512,1024]{1,0:T(8,128)(2,1)}, bf16[512,1024]{1,0:T(8,128)(2,1)}, u32[]{:S(2)}, u32[]{:S(2)}) collective-permute-start(bf16[512,1024]{1,0:T(8,128)(2,1)} %collective-permute-done.22.own_first_ref), channel_id=1, source_target_pairs={{0,4},{2,6},{4,0},{6,2},{8,12},{10,14},{12,8},{14,10},{16,20},{18,... | collective-permute-start | bytes 3145736 | tf_op jit(solution)/shard_map/ppermute | solution.py:508
  382.5 33.9 %collective-permute-start.32 = (bf16[544,1024]{1,0:T(8,128)(2,1)S(1)}, bf16[544,1024]{1,0:T(8,128)(2,1)S(1)}, u32[]{:S(2)}, u32[]{:S(2)}) collective-permute-start(bf16[544,1024]{1,0:T(8,128)(2,1)S(1)} %get-tuple-element.552), channel_id=1, source_target_pairs={{0,1},{1,0},{2,3},{3,2},{4,5},{5,4},{6,7},{7,6},{8,9},{9,8},{10,11... | collective-permute-start | bytes 3342344 | tf_op jit(solution)/shard_map/ppermute | solution.py:516
  386.4 29.9 %collective-permute-start.27 = (bf16[512,1024]{1,0:T(8,128)(2,1)}, bf16[512,1024]{1,0:T(8,128)(2,1)}, u32[]{:S(2)}, u32[]{:S(2)}) collective-permute-start(bf16[512,1024]{1,0:T(8,128)(2,1)} %collective-permute-done.18.own_second_ref), channel_id=1, source_target_pairs={{0,8},{2,10},{4,12},{6,14},{8,16},{10,18},{12,20},{14,22},{16,24},... | collective-permute-start | bytes 3145736 | tf_op jit(solution)/shard_map/ppermute | solution.py:512
  416.4 34.7 %collective-permute-start.36 = (bf16[2,2,544,1024]{3,2,1,0:T(8,128)(2,1)}, bf16[2,2,544,1024]{3,2,1,0:T(8,128)(2,1)}, u32[]{:S(2)}, u32[]{:S(2)}) collective-permute-start(bf16[2,2,544,1024]{3,2,1,0:T(8,128)(2,1)} %get-tuple-element.346), channel_id=1, source_target_pairs={{0,2},{2,0},{4,6},{6,4},{8,10},{10,8},{12,14},{14,12},{16,18},{18,... | collective-permute-start | bytes 13369352 | tf_op jit(solution)/shard_map/ppermute | solution.py:508
  419.7 30.6 %collective-permute-start.38 = (bf16[544,1024]{1,0:T(8,128)(2,1)}, bf16[544,1024]{1,0:T(8,128)(2,1)S(1)}, u32[]{:S(2)}, u32[]{:S(2)}) collective-permute-start(bf16[544,1024]{1,0:T(8,128)(2,1)} %fusion.44), channel_id=1, source_target_pairs={{0,8},{2,10},{4,12},{6,14},{8,16},{10,18},{12,20},{14,22},{16,24},... | collective-permute-start | bytes 3342344 | tf_op jit(solution)/shard_map/ppermute | solution.py:512
  455.7 33.5 %collective-permute-start.41 = (bf16[544,1024]{1,0:T(8,128)(2,1)}, bf16[544,1024]{1,0:T(8,128)(2,1)S(1)}, u32[]{:S(2)}, u32[]{:S(2)}) collective-permute-start(bf16[544,1024]{1,0:T(8,128)(2,1)} %fusion.12), channel_id=1, source_target_pairs={{0,8},{2,10},{4,12},{6,14},{8,16},{10,18},{12,20},{14,22},{16,24},... | collective-permute-start | bytes 3342344 | tf_op jit(solution)/shard_map/ppermute | solution.py:512
  459.5 29.8 %collective-permute-start.40 = (bf16[544,1024]{1,0:T(8,128)(2,1)S(1)}, bf16[544,1024]{1,0:T(8,128)(2,1)}, u32[]{:S(2)}, u32[]{:S(2)}) collective-permute-start(bf16[544,1024]{1,0:T(8,128)(2,1)S(1)} %get-tuple-element.550), channel_id=1, source_target_pairs={{0,1},{1,0},{2,3},{3,2},{4,5},{5,4},{6,7},{7,6},{8,9},{9,8},{10,11... | collective-permute-start | bytes 3342344 | tf_op jit(solution)/shard_map/ppermute | solution.py:516
  489.3 37.9 %collective-permute-start.42 = (bf16[2,2,544,1024]{3,2,1,0:T(8,128)(2,1)}, bf16[2,2,544,1024]{3,2,1,0:T(8,128)(2,1)}, u32[]{:S(2)}, u32[]{:S(2)}) collective-permute-start(bf16[2,2,544,1024]{3,2,1,0:T(8,128)(2,1)} %get-tuple-element.382), channel_id=1, source_target_pairs={{0,2},{2,0},{4,6},{6,4},{8,10},{10,8},{12,14},{14,12},{16,18},{18,... | collective-permute-start | bytes 13369352 | tf_op jit(solution)/shard_map/ppermute | solution.py:508
  489.3 37.9 %collective-permute-start.45 = (bf16[2,2,512,1024]{3,2,1,0:T(8,128)(2,1)}, bf16[2,2,512,1024]{3,2,1,0:T(8,128)(2,1)}, u32[]{:S(2)}, u32[]{:S(2)}) collective-permute-start(bf16[2,2,512,1024]{3,2,1,0:T(8,128)(2,1)} %get-tuple-element.393), channel_id=1, source_target_pairs={{0,2},{2,0},{4,6},{6,4},{8,10},{10,8},{12,14},{14,12},{16,18},{18,... | collective-permute-start | bytes 12582920 | tf_op jit(solution)/shard_map/ppermute | solution.py:508
  527.2 37.7 %collective-permute-start.49 = (bf16[2,2,512,1024]{3,2,1,0:T(8,128)(2,1)}, bf16[2,2,512,1024]{3,2,1,0:T(8,128)(2,1)}, u32[]{:S(2)}, u32[]{:S(2)}) collective-permute-start(bf16[2,2,512,1024]{3,2,1,0:T(8,128)(2,1)} %get-tuple-element.409), channel_id=1, source_target_pairs={{0,2},{2,0},{4,6},{6,4},{8,10},{10,8},{12,14},{14,12},{16,18},{18,... | collective-permute-start | bytes 12582920 | tf_op jit(solution)/shard_map/ppermute | solution.py:508
  564.9 38.9 %collective-permute-start.52 = (bf16[2,2,512,1024]{3,2,1,0:T(8,128)(2,1)}, bf16[2,2,512,1024]{3,2,1,0:T(8,128)(2,1)}, u32[]{:S(2)}, u32[]{:S(2)}) collective-permute-start(bf16[2,2,512,1024]{3,2,1,0:T(8,128)(2,1)} %get-tuple-element.426), channel_id=1, source_target_pairs={{0,2},{2,0},{4,6},{6,4},{8,10},{10,8},{12,14},{14,12},{16,18},{18,... | collective-permute-start | bytes 12582920 | tf_op jit(solution)/shard_map/ppermute | solution.py:508
  564.9 29.4 %collective-permute-start.54 = (bf16[544,1024]{1,0:T(8,128)(2,1)S(1)}, bf16[544,1024]{1,0:T(8,128)(2,1)}, u32[]{:S(2)}, u32[]{:S(2)}) collective-permute-start(bf16[544,1024]{1,0:T(8,128)(2,1)S(1)} %copy-done.29), channel_id=1, source_target_pairs={{0,8},{2,10},{4,12},{6,14},{8,16},{10,18},{12,20},{14,22},{16,24},... | collective-permute-start | bytes 3342344 | tf_op jit(solution)/shard_map/ppermute | solution.py:512
  603.9 36.0 %collective-permute-start.55 = (bf16[2,2,512,1024]{3,2,1,0:T(8,128)(2,1)S(1)}, bf16[2,2,512,1024]{3,2,1,0:T(8,128)(2,1)}, u32[]{:S(2)}, u32[]{:S(2)}) collective-permute-start(bf16[2,2,512,1024]{3,2,1,0:T(8,128)(2,1)S(1)} %copy-done.66), channel_id=1, source_target_pairs={{0,2},{2,0},{4,6},{6,4},{8,10},{10,8},{12,14},{14,12},{16,18},{18,... | collective-permute-start | bytes 12582920 | tf_op jit(solution)/shard_map/ppermute | solution.py:508
  608.9 31.0 %collective-permute-start.56 = (bf16[512,1024]{1,0:T(8,128)(2,1)S(1)}, bf16[512,1024]{1,0:T(8,128)(2,1)S(1)}, u32[]{:S(2)}, u32[]{:S(2)}) collective-permute-start(bf16[512,1024]{1,0:T(8,128)(2,1)S(1)} %add_convert_fusion.24), channel_id=1, source_target_pairs={{0,4},{2,6},{4,0},{6,2},{8,12},{10,14},{12,8},{14,10},{16,20},{18,... | collective-permute-start | bytes 3145736 | tf_op jit(solution)/shard_map/ppermute | solution.py:508
  682.9 39.9 %collective-permute-start.66 = (bf16[512,1024]{1,0:T(8,128)(2,1)}, bf16[512,1024]{1,0:T(8,128)(2,1)}, u32[]{:S(2)}, u32[]{:S(2)}) collective-permute-start(bf16[512,1024]{1,0:T(8,128)(2,1)} %fusion.31), channel_id=1, source_target_pairs={{0,8},{2,10},{4,12},{6,14},{8,16},{10,18},{12,20},{14,22},{16,24},... | collective-permute-start | bytes 3145736 | tf_op jit(solution)/shard_map/ppermute | solution.py:512
  685.9 44.1 %collective-permute-start.65 = (bf16[512,1024]{1,0:T(8,128)(2,1)}, bf16[512,1024]{1,0:T(8,128)(2,1)}, u32[]{:S(2)}, u32[]{:S(2)}) collective-permute-start(bf16[512,1024]{1,0:T(8,128)(2,1)} %fusion.32), channel_id=1, source_target_pairs={{0,8},{2,10},{4,12},{6,14},{8,16},{10,18},{12,20},{14,22},{16,24},... | collective-permute-start | bytes 3145736 | tf_op jit(solution)/shard_map/ppermute | solution.py:512
  694.0 36.0 %collective-permute-start.63 = (bf16[512,1024]{1,0:T(8,128)(2,1)}, bf16[512,1024]{1,0:T(8,128)(2,1)}, u32[]{:S(2)}, u32[]{:S(2)}) collective-permute-start(bf16[512,1024]{1,0:T(8,128)(2,1)} %get-tuple-element.556), channel_id=1, source_target_pairs={{0,1},{1,0},{2,3},{3,2},{4,5},{5,4},{6,7},{7,6},{8,9},{9,8},{10,11... | collective-permute-start | bytes 3145736 | tf_op jit(solution)/shard_map/ppermute | solution.py:516
  695.6 34.4 %collective-permute-start.64 = (bf16[512,1024]{1,0:T(8,128)(2,1)}, bf16[512,1024]{1,0:T(8,128)(2,1)}, u32[]{:S(2)}, u32[]{:S(2)}) collective-permute-start(bf16[512,1024]{1,0:T(8,128)(2,1)} %get-tuple-element.472), channel_id=1, source_target_pairs={{0,4},{2,6},{4,0},{6,2},{8,12},{10,14},{12,8},{14,10},{16,20},{18,... | collective-permute-start | bytes 3145736 | tf_op jit(solution)/shard_map/ppermute | solution.py:508
  742.6 34.8 %collective-permute-start.69 = (bf16[512,1024]{1,0:T(8,128)(2,1)S(1)}, bf16[512,1024]{1,0:T(8,128)(2,1)S(1)}, u32[]{:S(2)}, u32[]{:S(2)}) collective-permute-start(bf16[512,1024]{1,0:T(8,128)(2,1)S(1)} %fusion.29), channel_id=1, source_target_pairs={{0,8},{2,10},{4,12},{6,14},{8,16},{10,18},{12,20},{14,22},{16,24},... | collective-permute-start | bytes 3145736 | tf_op jit(solution)/shard_map/ppermute | solution.py:512
  744.6 32.9 %collective-permute-start.68 = (bf16[512,1024]{1,0:T(8,128)(2,1)S(1)}, bf16[512,1024]{1,0:T(8,128)(2,1)S(1)}, u32[]{:S(2)}, u32[]{:S(2)}) collective-permute-start(bf16[512,1024]{1,0:T(8,128)(2,1)S(1)} %add_convert_fusion.15), channel_id=1, source_target_pairs={{0,4},{2,6},{4,0},{6,2},{8,12},{10,14},{12,8},{14,10},{16,20},{18,... | collective-permute-start | bytes 3145736 | tf_op jit(solution)/shard_map/ppermute | solution.py:508
  782.5 41.2 %collective-permute-start.72 = (bf16[512,1024]{1,0:T(8,128)(2,1)S(1)}, bf16[512,1024]{1,0:T(8,128)(2,1)S(1)}, u32[]{:S(2)}, u32[]{:S(2)}) collective-permute-start(bf16[512,1024]{1,0:T(8,128)(2,1)S(1)} %fusion.27), channel_id=1, source_target_pairs={{0,8},{2,10},{4,12},{6,14},{8,16},{10,18},{12,20},{14,22},{16,24},... | collective-permute-start | bytes 3145736 | tf_op jit(solution)/shard_map/ppermute | solution.py:512
  783.0 40.7 %collective-permute-start.70 = (bf16[512,1024]{1,0:T(8,128)(2,1)S(1)}, bf16[512,1024]{1,0:T(8,128)(2,1)S(1)}, u32[]{:S(2)}, u32[]{:S(2)}) collective-permute-start(bf16[512,1024]{1,0:T(8,128)(2,1)S(1)} %add_convert_fusion.14), channel_id=1, source_target_pairs={{0,4},{2,6},{4,0},{6,2},{8,12},{10,14},{12,8},{14,10},{16,20},{18,... | collective-permute-start | bytes 3145736 | tf_op jit(solution)/shard_map/ppermute | solution.py:508
  (108 other events, 2190.5 us)
Sparse Core Ops, SparseCore 0:
  11.1 259.3 all-gather.4
  739.5 87.0 all-gather.6

commit v5 on v4

--- a/solution.py
+++ b/solution.py
@@ -139,6 +139,7 @@
         [jnp.where(slot == place_ref[b, e], 1.0, 0.0) for e in range(experts)], axis=0
     ).astype(half_type)
     half = rows_ref.shape[4]
+
     for h in range(rows_ref.shape[1]):
         for start in range(0, half, tile):
             rows = jnp.dot(
@@ -159,6 +160,7 @@
         hit = jnp.logical_or(hit, lane == target[:, e : e + 1])
     spread = jnp.where(hit, 1.0, 0.0).astype(half_type)
     half = rows_ref.shape[4]
+
     for h in range(2):
         for start in range(0, half, tile):
             rows = jnp.concatenate(
@@ -738,7 +740,7 @@
 
     def make_sums():
         return {
-            name: [None] * quads for name in ("send", "keep", "got", "near", "side_got", "arrived")
+            name: [None] * quads for name in ("send", "keep", "got", "side_got", "arrived")
         }
 
     flat_groups = {"grads": (), "outs": (2,)} if pair else {"grads": range(4), "outs": range(4)}
@@ -782,13 +784,12 @@
         keep, got = sums["keep"][k], sums["got"][k]
         away = plus(keep[1, 1], got[1, 1])
         sums["side_got"][k] = swap(away, data_count, 2) if is_flat(sums, k) else other_side(away)
-        sums["near"][k] = plus(keep[1, 0], got[1, 0])
 
     def sum_across(sums, k):
-        near = sums["near"][k]
+        near = [sums["keep"][k][1, 0], sums["got"][k][1, 0]]
         if not is_flat(sums, k):
-            near = plus(near, sums["side_got"][k])
-        sums["arrived"][k] = swap(near, data_count, 2)
+            near.append(sums["side_got"][k])
+        sums["arrived"][k] = swap(plus(*near), data_count, 2)
 
     def first_of(sums, k):
         return [sums["keep"][k][0, 0], sums["got"][k][0, 0], sums["arrived"][k]]
@@ -822,7 +823,7 @@
     move_second(0)
     send_rest(0)
     send_across(1)
-    gates_t, gates_all = step_end(gates_t, gates_all)
+    gates_t, gates_all, g_all = step_end(gates_t, gates_all, g_all)
     move_first(1)
     send_rest(1)
     send_last(0)
@@ -993,7 +994,15 @@
     out_second = onward_sum(out_second, *second_of(outs, 3))
     sum_across(outs, 0)
     grad_normed_cols = join_columns(grad_normed_mine, grad_normed_other)
-    grad_normed_cols, out_second = step_end(grad_normed_cols, out_second)
+    grad_normed_cols += jnp.dot(
+        grad_latent, columns_of(down_rows), preferred_element_type=jnp.float32
+    )
+    attention_gain_cols = columns_of(attention_norm_gain[None, :])
+    hidden_cols = columns_of(layer_input).astype(jnp.float32)
+    along_in = tensor_sum(
+        jnp.sum(hidden_cols * attention_gain_cols * grad_normed_cols, axis=1, keepdims=True)
+    )
+    along_in, out_second = step_end(along_in, out_second)
     out_first = plus(onward_sum(out_first, *first_of(outs, 3)), *first_of(outs, 0))
     out_second = plus(out_second, *second_of(outs, 0))
     if pair:
@@ -1001,14 +1010,6 @@
     else:
         moe_cols = own_columns(from_sides(out_first, out_second))
     layer_out = (mixed_cols + moe_cols).astype(half_type)
-    grad_normed_cols += jnp.dot(
-        grad_latent, columns_of(down_rows), preferred_element_type=jnp.float32
-    )
-    attention_gain_cols = columns_of(attention_norm_gain[None, :])
-    hidden_cols = columns_of(layer_input).astype(jnp.float32)
-    along_in = tensor_sum(
-        jnp.sum(hidden_cols * attention_gain_cols * grad_normed_cols, axis=1, keepdims=True)
-    )
     grad_input = (
         grad_mixed_cols
         + attention_gain_cols * hidden_scale * grad_normed_cols

time: 882 us -> 864 us (0.980)
  waiting for transfers between devices: 321 us -> 303 us
    all_gather x1, waiting for transfers between devices: 54.2 us -> 33.3 us  [local(): g_all = lax.all_gather(cotangent, ('dp', 'tensor'), axis=0)]
    ppermute x18, waiting for transfers between devices: 120 us -> 131 us  [onward(): lax.ppermute(values, 'dp', [(i, (i + QUAD) % data_count) for i in range(d...]
    convert_element_type x29 -> x30, other arithmetic: 78.9 us -> 78.9 us  [plus(): return total.astype(half_type)]
  transfers between devices with their start and end apart: 81 -> 81, of which waited for: 29 -> 30; matrix products, arithmetic and copies ran while one was open for 18% -> 18% of each run, Pallas kernels for 30% -> 31%
where the time goes in v5:
time: 864 us; the launch traced here: 854 us
  waiting for transfers between devices  303 us (35%)
  Pallas kernels  261 us (30%)
  other arithmetic  99.3 us (11%)
  starting transfers between devices  82.7 us (10%)
  matrix products  60.1 us (7%)
  local copies, waits for them, and re-layouts  30.6 us (4%)
  between operations  16.6 us (2%)
    ppermute x18, waiting for transfers between devices, onward(): lax.ppermute(values, 'dp', [(i, (i + QUAD) % data_count) for i in range(d...  131 us
    pallas_call x4, Pallas kernels, call_experts(): pl.pallas_call(functools.partial(expert_kernel, experts, cap), out_shape=...  118 us
    convert_element_type x30, other arithmetic, plus(): return total.astype(half_type)  78.9 us
    ppermute x22, waiting for transfers between devices, other_side(): return lax.ppermute(values, 'tensor', [(0, 1), (1, 0)])  77.7 us
    pallas_call x4, Pallas kernels, call_output(): pl.pallas_call(functools.partial(output_kernel, experts, cap), out_shape=...  65.3 us
    ppermute x37, waiting for transfers between devices, swap(): return lax.ppermute(values, 'dp', [(i, i ^ bit) for i in range(data_count)])  53.5 us
    pallas_call x2, Pallas kernels, call_heads(): pl.pallas_call(kernel, out_shape=[jax.ShapeDtypeStruct((toks, width), hal...  41.6 us
    pallas_call x1, Pallas kernels, call_grad_rows(): pl.pallas_call(functools.partial(grad_rows_kernel, experts, cap), out_sha...  36.3 us
  transfers between devices with their start and end apart: 81, of which 30 were waited for; matrix products, arithmetic and copies ran while one was open for 18% of the time, Pallas kernels for 31%

profile of v5, /device:TPU:0, one launch (start us, length us, event | category | flops | bytes accessed | tf_op | source)
XLA Modules:
  0.0 854.0 jit_solution(1313059179209293152)
XLA Ops:
  10.4 7.4 all-to-all-start
  42.7 19.2 %attend.1 = (bf16[512,1024]{1,0:T(8,128)(2,1)}, bf16[512,1024]{1,0:T(8,128)(2,1)}, bf16[512,1024]{1,0:T(8,128)(2,1)}, bf16[512,1024]{1,0:T(8,128)(2,1)}) custom-call(f32[512,1024]{1,0:T(8,128)} %convolution_add_fusion.2.raw_q, f32[512,1024]{1,0:T(8,128)} %convolution_add_fusion.1.raw_k, f32[512,1024]{1,0:T(8,128)} %convolution_add_fusion.raw_v, ...), custom_call_target="tpu_custom_call" | custom-call | flops 2684354560 | bytes 4194304 | tf_op jit(solution)/shard_map/attend/pallas_call | solution.py:105
  61.9 3.6 fusion.127
  70.3 24.5 %collective-permute-done.1 = bf16[512,16]{0,1:T(8,128)(2,1)S(1)} collective-permute-done((bf16[512,16]{0,1:T(8,128)(2,1)S(1)}, bf16[512,16]{0,1:T(8,128)(2,1)S(1)}, u32[]{:S(2)}, u32[]{:S(2)}) %collective-permute-start.1) | collective-permute-done | bytes 16416 | tf_op jit(solution)/shard_map/ppermute | solution.py:518
  103.5 37.4 %collective-permute-done.3.own_first_ref = bf16[512,1024]{1,0:T(8,128)(2,1)} collective-permute-done((bf16[512,1024]{1,0:T(8,128)(2,1)S(1)}, bf16[512,1024]{1,0:T(8,128)(2,1)}, u32[]{:S(2)}, u32[]{:S(2)}) %collective-permute-start.3) | collective-permute-done | bytes 1048608 | tf_op jit(solution)/shard_map/ppermute | solution.py:514
  144.0 7.4 collective-permute-start.7
  151.5 37.4 %collective-permute-done.10.across_first_ref = bf16[512,1024]{1,0:T(8,128)(2,1)S(1)} collective-permute-done((bf16[512,1024]{1,0:T(8,128)(2,1)}, bf16[512,1024]{1,0:T(8,128)(2,1)S(1)}, u32[]{:S(2)}, u32[]{:S(2)}) %collective-permute-start.10) | collective-permute-done | bytes 1048608 | tf_op jit(solution)/shard_map/ppermute | solution.py:510
  191.6 14.6 %all-to-all-start.1 = ((f32[16,4,512]{2,1,0:T(4,128)}), f32[16,4,512]{2,1,0:T(4,128)S(1)}, u32[]{:S(2)}, u32[]{:S(2)}) async-start(f32[16,4,512]{2,1,0:T(4,128)} %reshape.318), calls=%async_computation.1 | async-start | bytes 262144 | tf_op jit(solution)/shard_map/all_to_all | solution.py:820
  207.5 6.7 all-to-all-done.1
  214.9 33.3 %all-gather.5.cloned.1.call-done = bf16[16384,1024]{1,0:T(8,128)(2,1)} async-done(((bf16[512,1024]{1,0:T(8,128)(2,1)}), bf16[16384,1024]{1,0:T(8,128)(2,1)}) %all-gather.5.cloned.1.call-update) | async-done | bytes 33554448 | tf_op jit(solution)/shard_map/all_gather | solution.py:640
  250.1 36.3 %grad_rows.1.dh_ref = bf16[4,1280,512]{2,1,0:T(8,128)(2,1)} custom-call(s32[16]{0:T(128)} %fusion.105.block_ids, s32[16,4,1,512]{3,2,1,0:T(1,128)} %broadcast_in_dim.86.place_ref, bf16[4,512,2048]{2,1,0:T(8,128)(2,1)} %down_ref.9, bf16[16,2,512,1024]{3,2,1,0:T(8,128)(2,1)} %bitcast.265), custom_call_target="tpu_custom_call" | custom-call | flops 42949672960 | bytes 47185920 | tf_op jit(solution)/shard_map/grad_rows/pallas_call | solution.py:388
  294.1 29.5 %experts.4 = (bf16[2,2,544,1024]{3,2,1,0:T(8,128)(2,1)}, bf16[2,2,544,1024]{3,2,1,0:T(8,128)(2,1)}, bf16[4,320,512]{2,1,0:T(8,128)(2,1)}) custom-call(s32[2]{0:T(128)} %pad_add_fusion.flip_ref, s32[4,4,1,512]{3,2,1,0:T(1,128)} %broadcast_in_dim.87.place_ref, f32[4,4,1,512]{3,2,1,0:T(1,128)} %copy.88.gate_ref, s32[4,512,4]{2,1,0:T(8,128)} %get-tuple-element.546.target_ref, ...), custom_call_target="tpu_custom_call" | custom-call | flops 24159191040 | bytes 33554432 | tf_op jit(solution)/shard_map/experts/pallas_call | solution.py:422
  327.6 29.8 %experts.5 = (bf16[2,2,544,1024]{3,2,1,0:T(8,128)(2,1)}, bf16[2,2,544,1024]{3,2,1,0:T(8,128)(2,1)}, bf16[4,320,512]{2,1,0:T(8,128)(2,1)}) custom-call(s32[2]{0:T(128)} %pad_add_fusion.flip_ref, s32[4,4,1,512]{3,2,1,0:T(1,128)} %broadcast_in_dim.89.place_ref, f32[4,4,1,512]{3,2,1,0:T(1,128)} %copy.89.gate_ref, s32[4,512,4]{2,1,0:T(8,128)} %get-tuple-element.545.target_ref, ...), custom_call_target="tpu_custom_call" | custom-call | flops 24159191040 | bytes 33554432 | tf_op jit(solution)/shard_map/experts/pallas_call | solution.py:422
  363.1 5.3 collective-permute-done.30.far_second_ref
  370.4 29.6 %experts.6 = (bf16[2,2,544,1024]{3,2,1,0:T(8,128)(2,1)}, bf16[2,2,544,1024]{3,2,1,0:T(8,128)(2,1)}, bf16[4,320,512]{2,1,0:T(8,128)(2,1)}) custom-call(s32[2]{0:T(128)} %pad_add_fusion.flip_ref, s32[4,4,1,512]{3,2,1,0:T(1,128)} %broadcast_in_dim.91.place_ref, f32[4,4,1,512]{3,2,1,0:T(1,128)} %copy.90.gate_ref, s32[4,512,4]{2,1,0:T(8,128)} %get-tuple-element.544.target_ref, ...), custom_call_target="tpu_custom_call" | custom-call | flops 24159191040 | bytes 33554432 | tf_op jit(solution)/shard_map/experts/pallas_call | solution.py:422
  409.7 16.1 %outputs.4 = (bf16[2,2,512,1024]{3,2,1,0:T(8,128)(2,1)}, bf16[2,2,512,1024]{3,2,1,0:T(8,128)(2,1)}) custom-call(s32[2]{0:T(128)} %pad_add_fusion.flip_ref, s32[4,512,4]{2,1,0:T(8,128)} %get-tuple-element.546.target_ref, bf16[4,512,2048]{2,1,0:T(8,128)(2,1)} %down_ref.9, bf16[4,320,512]{2,1,0:T(8,128)(2,1)} %get-tuple-element.338.hidden_ref), custom_call_target="tpu_custom_call" | custom-call | flops 10737418240 | bytes 16777216 | tf_op jit(solution)/shard_map/outputs/pallas_call | solution.py:476
  425.9 6.2 collective-permute-done.34.across_second_ref
  434.7 3.3 fusion.12
  443.3 29.4 %experts.7 = (bf16[2,2,544,1024]{3,2,1,0:T(8,128)(2,1)}, bf16[2,2,544,1024]{3,2,1,0:T(8,128)(2,1)}, bf16[4,320,512]{2,1,0:T(8,128)(2,1)}) custom-call(s32[2]{0:T(128)} %pad_add_fusion.flip_ref, s32[4,4,1,512]{3,2,1,0:T(1,128)} %broadcast_in_dim.93.place_ref, f32[4,4,1,512]{3,2,1,0:T(1,128)} %broadcast_in_dim.94.gate_ref, ...), custom_call_target="tpu_custom_call" | custom-call | flops 24159191040 | bytes 33554432 | tf_op jit(solution)/shard_map/experts/pallas_call | solution.py:422
  478.0 3.3 fusion.16
  485.7 16.4 %outputs.5 = (bf16[2,2,512,1024]{3,2,1,0:T(8,128)(2,1)}, bf16[2,2,512,1024]{3,2,1,0:T(8,128)(2,1)}) custom-call(s32[2]{0:T(128)} %pad_add_fusion.flip_ref, s32[4,512,4]{2,1,0:T(8,128)} %get-tuple-element.544.target_ref, bf16[4,512,2048]{2,1,0:T(8,128)(2,1)} %down_ref.9, bf16[4,320,512]{2,1,0:T(8,128)(2,1)} %get-tuple-element.373.hidden_ref), custom_call_target="tpu_custom_call" | custom-call | flops 10737418240 | bytes 16777216 | tf_op jit(solution)/shard_map/outputs/pallas_call | solution.py:476
  507.9 3.5 collective-permute-done.43
  511.4 3.9 fusion.11
  527.1 16.2 %outputs.6 = (bf16[2,2,512,1024]{3,2,1,0:T(8,128)(2,1)}, bf16[2,2,512,1024]{3,2,1,0:T(8,128)(2,1)}) custom-call(s32[2]{0:T(128)} %pad_add_fusion.flip_ref, s32[4,512,4]{2,1,0:T(8,128)} %get-tuple-element.543.target_ref, bf16[4,512,2048]{2,1,0:T(8,128)(2,1)} %down_ref.9, bf16[4,320,512]{2,1,0:T(8,128)(2,1)} %get-tuple-element.391.hidden_ref), custom_call_target="tpu_custom_call" | custom-call | flops 10737418240 | bytes 16777216 | tf_op jit(solution)/shard_map/outputs/pallas_call | solution.py:476
  544.3 3.3 collective-permute-done.48
  547.6 3.7 collective-permute-done.47
  555.1 3.3 fusion.13
  559.0 16.6 %outputs.7 = (bf16[2,2,512,1024]{3,2,1,0:T(8,128)(2,1)}, bf16[2,2,512,1024]{3,2,1,0:T(8,128)(2,1)}) custom-call(s32[2]{0:T(128)} %pad_add_fusion.flip_ref, s32[4,512,4]{2,1,0:T(8,128)} %get-tuple-element.545.target_ref, bf16[4,512,2048]{2,1,0:T(8,128)(2,1)} %down_ref.9, bf16[4,320,512]{2,1,0:T(8,128)(2,1)} %get-tuple-element.408.hidden_ref), custom_call_target="tpu_custom_call" | custom-call | flops 10737418240 | bytes 16777216 | tf_op jit(solution)/shard_map/outputs/pallas_call | solution.py:476
  575.7 4.6 collective-permute-done.54
  593.4 23.1 %collective-permute-done.57 = bf16[544,1024]{1,0:T(8,128)(2,1)S(1)} collective-permute-done((bf16[544,1024]{1,0:T(8,128)(2,1)S(1)}, bf16[544,1024]{1,0:T(8,128)(2,1)S(1)}, u32[]{:S(2)}, u32[]{:S(2)}) %collective-permute-start.57) | collective-permute-done | bytes 1114144 | tf_op jit(solution)/shard_map/ppermute | solution.py:514
  616.5 4.6 fusion.5
  628.2 3.7 fusion.122
  638.0 17.5 %collective-permute-done.61 = bf16[512,1024]{1,0:T(8,128)(2,1)S(1)} collective-permute-done((bf16[512,1024]{1,0:T(8,128)(2,1)S(1)}, bf16[512,1024]{1,0:T(8,128)(2,1)S(1)}, u32[]{:S(2)}, u32[]{:S(2)}) %collective-permute-start.61) | collective-permute-done | bytes 1048608 | tf_op jit(solution)/shard_map/ppermute | solution.py:518
  656.0 4.2 collective-permute-done.62
  677.7 3.4 add_convert_fusion.7.grad
  681.2 22.4 %attend_back.1 = (bf16[512,1024]{1,0:T(8,128)(2,1)}, bf16[512,1024]{1,0:T(8,128)(2,1)}, bf16[512,1024]{1,0:T(8,128)(2,1)}) custom-call(f32[512,1024]{1,0:T(8,128)} %convolution_add_fusion.2.raw_q, f32[512,1024]{1,0:T(8,128)} %convolution_add_fusion.1.raw_k, bf16[512,1024]{1,0:T(8,128)(2,1)} %get-tuple-element.463.queries, ...), custom_call_target="tpu_custom_call" | custom-call | flops 2684354560 | bytes 4194304 | tf_op jit(solution)/shard_map/attend_back/pallas_call | solution.py:105
  704.1 8.9 %collective-permute-done.65 = bf16[512,1024]{1,0:T(8,128)(2,1)} collective-permute-done((bf16[512,1024]{1,0:T(8,128)(2,1)}, bf16[512,1024]{1,0:T(8,128)(2,1)}, u32[]{:S(2)}, u32[]{:S(2)}) %collective-permute-start.65) | collective-permute-done | bytes 1048608 | tf_op jit(solution)/shard_map/ppermute | solution.py:514
  731.3 6.9 fusion.128
  738.2 4.4 fusion.129
  742.6 5.9 add_add_fusion
  748.7 11.8 %collective-permute-done.69 = bf16[512,1024]{1,0:T(8,128)(2,1)S(1)} collective-permute-done((bf16[512,1024]{1,0:T(8,128)(2,1)S(1)}, bf16[512,1024]{1,0:T(8,128)(2,1)S(1)}, u32[]{:S(2)}, u32[]{:S(2)}) %collective-permute-start.69) | collective-permute-done | bytes 1048608 | tf_op jit(solution)/shard_map/ppermute | solution.py:514
  766.5 10.8 %collective-permute-done.71 = bf16[512,1024]{1,0:T(8,128)(2,1)S(1)} collective-permute-done((bf16[512,1024]{1,0:T(8,128)(2,1)S(1)}, bf16[512,1024]{1,0:T(8,128)(2,1)S(1)}, u32[]{:S(2)}, u32[]{:S(2)}) %collective-permute-start.71) | collective-permute-done | bytes 1048608 | tf_op jit(solution)/shard_map/ppermute | solution.py:518
  778.6 3.3 collective-permute-done.73
  782.0 25.4 %collective-permute-done.74 = bf16[512,1024]{1,0:T(8,128)(2,1)S(1)} collective-permute-done((bf16[512,1024]{1,0:T(8,128)(2,1)S(1)}, bf16[512,1024]{1,0:T(8,128)(2,1)S(1)}, u32[]{:S(2)}, u32[]{:S(2)}) %collective-permute-start.74) | collective-permute-done | bytes 1048608 | tf_op jit(solution)/shard_map/ppermute | solution.py:514
  815.7 12.2 %collective-permute-done.75 = bf16[512,1024]{1,0:T(8,128)(2,1)S(1)} collective-permute-done((bf16[512,1024]{1,0:T(8,128)(2,1)S(1)}, bf16[512,1024]{1,0:T(8,128)(2,1)S(1)}, u32[]{:S(2)}, u32[]{:S(2)}) %collective-permute-start.75) | collective-permute-done | bytes 1048608 | tf_op jit(solution)/shard_map/ppermute | solution.py:514
  827.8 3.5 add_convert_fusion.5
  831.3 5.9 fusion
  841.0 3.5 copy.93
  (402 shorter events, 204.6 us)
Async XLA Ops:
  7.2 241.0 %all-gather.5.cloned.1.call-start = ((), (), s32[]{:S(2)}) async-start(), calls=%async_computation.2 | async-start | bytes 34603008 | tf_op jit(solution)/shard_map/all_gather | solution.py:640
  65.7 29.0 %collective-permute-start = (bf16[512,1024]{1,0:T(8,128)(2,1)S(1)}, bf16[512,1024]{1,0:T(8,128)(2,1)S(1)}, u32[]{:S(2)}, u32[]{:S(2)}) collective-permute-start(bf16[512,1024]{1,0:T(8,128)(2,1)S(1)} %select_convert_fusion.1), channel_id=1, source_target_pairs={{0,1},{1,0},{2,3},{3,2},{4,5},{5,4},{6,7},{7,6},{8,9},{9,8},{10,11... | collective-permute-start | bytes 3145736 | tf_op jit(solution)/shard_map/ppermute | solution.py:518
  99.9 40.9 %collective-permute-start.3 = (bf16[512,1024]{1,0:T(8,128)(2,1)S(1)}, bf16[512,1024]{1,0:T(8,128)(2,1)}, u32[]{:S(2)}, u32[]{:S(2)}) collective-permute-start(bf16[512,1024]{1,0:T(8,128)(2,1)S(1)} %multiply_convert_fusion.own_first_ref), channel_id=1, source_target_pairs={{0,8},{2,10},{4,12},{6,14},{8,16},{10,18},{12,20},{14,22},{16,24},... | collective-permute-start | bytes 3145736 | tf_op jit(solution)/shard_map/ppermute | solution.py:514
  101.4 39.4 %collective-permute-start.4 = (bf16[512,1024]{1,0:T(8,128)(2,1)S(1)}, bf16[512,1024]{1,0:T(8,128)(2,1)S(1)}, u32[]{:S(2)}, u32[]{:S(2)}) collective-permute-start(bf16[512,1024]{1,0:T(8,128)(2,1)S(1)} %multiply_convert_fusion.own_first_ref), channel_id=1, source_target_pairs={{0,1},{1,0},{2,3},{3,2},{4,5},{5,4},{6,7},{7,6},{8,9},{9,8},{10,11... | collective-permute-start | bytes 3145736 | tf_op jit(solution)/shard_map/ppermute | solution.py:518
  102.0 38.8 %collective-permute-start.5 = (bf16[512,1024]{1,0:T(8,128)(2,1)S(1)}, bf16[512,1024]{1,0:T(8,128)(2,1)S(1)}, u32[]{:S(2)}, u32[]{:S(2)}) collective-permute-start(bf16[512,1024]{1,0:T(8,128)(2,1)S(1)} %multiply_convert_fusion.own_first_ref), channel_id=1, source_target_pairs={{0,2},{2,0},{4,6},{6,4},{8,10},{10,8},{12,14},{14,12},{16,18},{18,... | collective-permute-start | bytes 3145736 | tf_op jit(solution)/shard_map/ppermute | solution.py:510
  102.0 38.9 %collective-permute-start.6 = (bf16[512,1024]{1,0:T(8,128)(2,1)S(1)}, bf16[512,1024]{1,0:T(8,128)(2,1)S(1)}, u32[]{:S(2)}, u32[]{:S(2)}) collective-permute-start(bf16[512,1024]{1,0:T(8,128)(2,1)S(1)} %multiply_convert_fusion.own_first_ref), channel_id=1, source_target_pairs={{0,4},{2,6},{4,0},{6,2},{8,12},{10,14},{12,8},{14,10},{16,20},{18,... | collective-permute-start | bytes 3145736 | tf_op jit(solution)/shard_map/ppermute | solution.py:510
  140.9 48.0 %collective-permute-start.10 = (bf16[512,1024]{1,0:T(8,128)(2,1)}, bf16[512,1024]{1,0:T(8,128)(2,1)S(1)}, u32[]{:S(2)}, u32[]{:S(2)}) collective-permute-start(bf16[512,1024]{1,0:T(8,128)(2,1)} %collective-permute-done.3.own_first_ref), channel_id=1, source_target_pairs={{0,4},{2,6},{4,0},{6,2},{8,12},{10,14},{12,8},{14,10},{16,20},{18,... | collective-permute-start | bytes 3145736 | tf_op jit(solution)/shard_map/ppermute | solution.py:510
  142.3 72.5 %collective-permute-start.11 = (bf16[512,1024]{1,0:T(8,128)(2,1)S(1)}, bf16[512,1024]{1,0:T(8,128)(2,1)}, u32[]{:S(2)}, u32[]{:S(2)}) collective-permute-start(bf16[512,1024]{1,0:T(8,128)(2,1)S(1)} %collective-permute-done.6.across_first_ref), channel_id=1, source_target_pairs={{0,1},{1,0},{2,3},{3,2},{4,5},{5,4},{6,7},{7,6},{8,9},{9,8},{10,11... | collective-permute-start | bytes 3145736 | tf_op jit(solution)/shard_map/ppermute | solution.py:518
  143.5 71.3 %collective-permute-start.12 = (bf16[512,1024]{1,0:T(8,128)(2,1)S(1)}, bf16[512,1024]{1,0:T(8,128)(2,1)}, u32[]{:S(2)}, u32[]{:S(2)}) collective-permute-start(bf16[512,1024]{1,0:T(8,128)(2,1)S(1)} %collective-permute-done.6.across_first_ref), channel_id=1, source_target_pairs={{0,2},{2,0},{4,6},{6,4},{8,10},{10,8},{12,14},{14,12},{16,18},{18,... | collective-permute-start | bytes 3145736 | tf_op jit(solution)/shard_map/ppermute | solution.py:510
  143.5 71.3 %collective-permute-start.8 = (bf16[512,1024]{1,0:T(8,128)(2,1)}, bf16[512,1024]{1,0:T(8,128)(2,1)}, u32[]{:S(2)}, u32[]{:S(2)}) collective-permute-start(bf16[512,1024]{1,0:T(8,128)(2,1)} %collective-permute-done.3.own_first_ref), channel_id=1, source_target_pairs={{0,2},{2,0},{4,6},{6,4},{8,10},{10,8},{12,14},{14,12},{16,18},{18,... | collective-permute-start | bytes 3145736 | tf_op jit(solution)/shard_map/ppermute | solution.py:510
  144.0 70.8 %collective-permute-start.7 = (bf16[512,1024]{1,0:T(8,128)(2,1)S(1)}, bf16[512,1024]{1,0:T(8,128)(2,1)}, u32[]{:S(2)}, u32[]{:S(2)}) collective-permute-start(bf16[512,1024]{1,0:T(8,128)(2,1)S(1)} %collective-permute-done.4.own_second_ref), channel_id=1, source_target_pairs={{0,8},{2,10},{4,12},{6,14},{8,16},{10,18},{12,20},{14,22},{16,24},... | collective-permute-start | bytes 3145736 | tf_op jit(solution)/shard_map/ppermute | solution.py:514
  206.2 625.1 %all-gather.7.cloned.1.call-start = ((), (), s32[]{:S(2)}) async-start(), calls=%async_computation.3 | async-start | bytes 6127616 | tf_op jit(solution)/shard_map/all_gather | solution.py:972
  248.1 38.3 %collective-permute-start.15 = (bf16[512,1024]{1,0:T(8,128)(2,1)}, bf16[512,1024]{1,0:T(8,128)(2,1)}, u32[]{:S(2)}, u32[]{:S(2)}) collective-permute-start(bf16[512,1024]{1,0:T(8,128)(2,1)} %copy-done.63), channel_id=1, source_target_pairs={{0,1},{1,0},{2,3},{3,2},{4,5},{5,4},{6,7},{7,6},{8,9},{9,8},{10,11... | collective-permute-start | bytes 3145736 | tf_op jit(solution)/shard_map/ppermute | solution.py:518
  249.6 36.8 %collective-permute-start.16 = (bf16[512,1024]{1,0:T(8,128)(2,1)}, bf16[512,1024]{1,0:T(8,128)(2,1)}, u32[]{:S(2)}, u32[]{:S(2)}) collective-permute-start(bf16[512,1024]{1,0:T(8,128)(2,1)} %copy-done.63), channel_id=1, source_target_pairs={{0,2},{2,0},{4,6},{6,4},{8,10},{10,8},{12,14},{14,12},{16,18},{18,... | collective-permute-start | bytes 3145736 | tf_op jit(solution)/shard_map/ppermute | solution.py:510
  249.6 36.8 %collective-permute-start.13 = (bf16[512,1024]{1,0:T(8,128)(2,1)}, bf16[512,1024]{1,0:T(8,128)(2,1)S(1)}, u32[]{:S(2)}, u32[]{:S(2)}) collective-permute-start(bf16[512,1024]{1,0:T(8,128)(2,1)} %collective-permute-done.3.own_first_ref), channel_id=1, source_target_pairs={{0,8},{2,10},{4,12},{6,14},{8,16},{10,18},{12,20},{14,22},{16,24},... | collective-permute-start | bytes 3145736 | tf_op jit(solution)/shard_map/ppermute | solution.py:514
  249.6 36.8 %collective-permute-start.14 = (bf16[512,1024]{1,0:T(8,128)(2,1)}, bf16[512,1024]{1,0:T(8,128)(2,1)}, u32[]{:S(2)}, u32[]{:S(2)}) collective-permute-start(bf16[512,1024]{1,0:T(8,128)(2,1)} %collective-permute-done.7.own_second_ref), channel_id=1, source_target_pairs={{0,2},{2,0},{4,6},{6,4},{8,10},{10,8},{12,14},{14,12},{16,18},{18,... | collective-permute-start | bytes 3145736 | tf_op jit(solution)/shard_map/ppermute | solution.py:510
  250.1 36.3 %collective-permute-start.17 = (bf16[512,1024]{1,0:T(8,128)(2,1)}, bf16[512,1024]{1,0:T(8,128)(2,1)}, u32[]{:S(2)}, u32[]{:S(2)}) collective-permute-start(bf16[512,1024]{1,0:T(8,128)(2,1)} %collective-permute-done.11.across_second_ref), channel_id=1, source_target_pairs={{0,2},{2,0},{4,6},{6,4},{8,10},{10,8},{12,14},{14,12},{16,18},{18,... | collective-permute-start | bytes 3145736 | tf_op jit(solution)/shard_map/ppermute | solution.py:510
  291.0 32.6 %collective-permute-start.19 = (bf16[512,1024]{1,0:T(8,128)(2,1)S(1)}, bf16[512,1024]{1,0:T(8,128)(2,1)S(1)}, u32[]{:S(2)}, u32[]{:S(2)}) collective-permute-start(bf16[512,1024]{1,0:T(8,128)(2,1)S(1)} %collective-permute-done.13.own_first_ref), channel_id=1, source_target_pairs={{0,2},{2,0},{4,6},{6,4},{8,10},{10,8},{12,14},{14,12},{16,18},{18,... | collective-permute-start | bytes 3145736 | tf_op jit(solution)/shard_map/ppermute | solution.py:510
  291.1 32.4 %collective-permute-start.20 = (bf16[512,1024]{1,0:T(8,128)(2,1)S(1)}, bf16[512,1024]{1,0:T(8,128)(2,1)S(1)}, u32[]{:S(2)}, u32[]{:S(2)}) collective-permute-start(bf16[512,1024]{1,0:T(8,128)(2,1)S(1)} %collective-permute-done.13.own_first_ref), channel_id=1, source_target_pairs={{0,4},{2,6},{4,0},{6,2},{8,12},{10,14},{12,8},{14,10},{16,20},{18,... | collective-permute-start | bytes 3145736 | tf_op jit(solution)/shard_map/ppermute | solution.py:510
  293.1 30.5 %collective-permute-start.18 = (bf16[512,1024]{1,0:T(8,128)(2,1)}, bf16[512,1024]{1,0:T(8,128)(2,1)}, u32[]{:S(2)}, u32[]{:S(2)}) collective-permute-start(bf16[512,1024]{1,0:T(8,128)(2,1)} %collective-permute-done.7.own_second_ref), channel_id=1, source_target_pairs={{0,8},{2,10},{4,12},{6,14},{8,16},{10,18},{12,20},{14,22},{16,24},... | collective-permute-start | bytes 3145736 | tf_op jit(solution)/shard_map/ppermute | solution.py:514
  323.6 33.9 %collective-permute-start.26 = (bf16[2,2,544,1024]{3,2,1,0:T(8,128)(2,1)}, bf16[2,2,544,1024]{3,2,1,0:T(8,128)(2,1)}, u32[]{:S(2)}, u32[]{:S(2)}) collective-permute-start(bf16[2,2,544,1024]{3,2,1,0:T(8,128)(2,1)} %get-tuple-element.311), channel_id=1, source_target_pairs={{0,2},{2,0},{4,6},{6,4},{8,10},{10,8},{12,14},{14,12},{16,18},{18,... | collective-permute-start | bytes 13369352 | tf_op jit(solution)/shard_map/ppermute | solution.py:510
  325.1 32.3 %collective-permute-start.24 = (bf16[512,1024]{1,0:T(8,128)(2,1)S(1)}, bf16[512,1024]{1,0:T(8,128)(2,1)}, u32[]{:S(2)}, u32[]{:S(2)}) collective-permute-start(bf16[512,1024]{1,0:T(8,128)(2,1)S(1)} %collective-permute-done.20.across_first_ref), channel_id=1, source_target_pairs={{0,1},{1,0},{2,3},{3,2},{4,5},{5,4},{6,7},{7,6},{8,9},{9,8},{10,11... | collective-permute-start | bytes 3145736 | tf_op jit(solution)/shard_map/ppermute | solution.py:518
  325.6 31.8 %collective-permute-start.25 = (bf16[512,1024]{1,0:T(8,128)(2,1)S(1)}, bf16[512,1024]{1,0:T(8,128)(2,1)}, u32[]{:S(2)}, u32[]{:S(2)}) collective-permute-start(bf16[512,1024]{1,0:T(8,128)(2,1)S(1)} %collective-permute-done.20.across_first_ref), channel_id=1, source_target_pairs={{0,2},{2,0},{4,6},{6,4},{8,10},{10,8},{12,14},{14,12},{16,18},{18,... | collective-permute-start | bytes 3145736 | tf_op jit(solution)/shard_map/ppermute | solution.py:510
  325.7 31.7 %collective-permute-start.22 = (bf16[512,1024]{1,0:T(8,128)(2,1)S(1)}, bf16[512,1024]{1,0:T(8,128)(2,1)}, u32[]{:S(2)}, u32[]{:S(2)}) collective-permute-start(bf16[512,1024]{1,0:T(8,128)(2,1)S(1)} %collective-permute-done.13.own_first_ref), channel_id=1, source_target_pairs={{0,8},{2,10},{4,12},{6,14},{8,16},{10,18},{12,20},{14,22},{16,24},... | collective-permute-start | bytes 3145736 | tf_op jit(solution)/shard_map/ppermute | solution.py:514
  327.5 30.0 %collective-permute-start.23 = (bf16[512,1024]{1,0:T(8,128)(2,1)}, bf16[512,1024]{1,0:T(8,128)(2,1)}, u32[]{:S(2)}, u32[]{:S(2)}) collective-permute-start(bf16[512,1024]{1,0:T(8,128)(2,1)} %collective-permute-done.18.own_second_ref), channel_id=1, source_target_pairs={{0,2},{2,0},{4,6},{6,4},{8,10},{10,8},{12,14},{14,12},{16,18},{18,... | collective-permute-start | bytes 3145736 | tf_op jit(solution)/shard_map/ppermute | solution.py:510
  357.5 42.7 %collective-permute-start.31 = (bf16[2,2,544,1024]{3,2,1,0:T(8,128)(2,1)}, bf16[2,2,544,1024]{3,2,1,0:T(8,128)(2,1)}, u32[]{:S(2)}, u32[]{:S(2)}) collective-permute-start(bf16[2,2,544,1024]{3,2,1,0:T(8,128)(2,1)} %get-tuple-element.326), channel_id=1, source_target_pairs={{0,2},{2,0},{4,6},{6,4},{8,10},{10,8},{12,14},{14,12},{16,18},{18,... | collective-permute-start | bytes 13369352 | tf_op jit(solution)/shard_map/ppermute | solution.py:510
  359.3 40.8 %collective-permute-start.28 = (bf16[512,1024]{1,0:T(8,128)(2,1)}, bf16[512,1024]{1,0:T(8,128)(2,1)S(1)}, u32[]{:S(2)}, u32[]{:S(2)}) collective-permute-start(bf16[512,1024]{1,0:T(8,128)(2,1)} %collective-permute-done.22.own_first_ref), channel_id=1, source_target_pairs={{0,2},{2,0},{4,6},{6,4},{8,10},{10,8},{12,14},{14,12},{16,18},{18,... | collective-permute-start | bytes 3145736 | tf_op jit(solution)/shard_map/ppermute | solution.py:510
  359.6 40.5 %collective-permute-start.29 = (bf16[512,1024]{1,0:T(8,128)(2,1)}, bf16[512,1024]{1,0:T(8,128)(2,1)}, u32[]{:S(2)}, u32[]{:S(2)}) collective-permute-start(bf16[512,1024]{1,0:T(8,128)(2,1)} %collective-permute-done.22.own_first_ref), channel_id=1, source_target_pairs={{0,4},{2,6},{4,0},{6,2},{8,12},{10,14},{12,8},{14,10},{16,20},{18,... | collective-permute-start | bytes 3145736 | tf_op jit(solution)/shard_map/ppermute | solution.py:510
  361.4 38.7 %collective-permute-start.32 = (bf16[544,1024]{1,0:T(8,128)(2,1)S(1)}, bf16[544,1024]{1,0:T(8,128)(2,1)S(1)}, u32[]{:S(2)}, u32[]{:S(2)}) collective-permute-start(bf16[544,1024]{1,0:T(8,128)(2,1)S(1)} %fusion.49), channel_id=1, source_target_pairs={{0,1},{1,0},{2,3},{3,2},{4,5},{5,4},{6,7},{7,6},{8,9},{9,8},{10,11... | collective-permute-start | bytes 3342344 | tf_op jit(solution)/shard_map/ppermute | solution.py:518
  368.4 31.7 %collective-permute-start.27 = (bf16[512,1024]{1,0:T(8,128)(2,1)}, bf16[512,1024]{1,0:T(8,128)(2,1)}, u32[]{:S(2)}, u32[]{:S(2)}) collective-permute-start(bf16[512,1024]{1,0:T(8,128)(2,1)} %collective-permute-done.18.own_second_ref), channel_id=1, source_target_pairs={{0,8},{2,10},{4,12},{6,14},{8,16},{10,18},{12,20},{14,22},{16,24},... | collective-permute-start | bytes 3145736 | tf_op jit(solution)/shard_map/ppermute | solution.py:514
  400.1 33.3 %collective-permute-start.36 = (bf16[2,2,544,1024]{3,2,1,0:T(8,128)(2,1)}, bf16[2,2,544,1024]{3,2,1,0:T(8,128)(2,1)}, u32[]{:S(2)}, u32[]{:S(2)}) collective-permute-start(bf16[2,2,544,1024]{3,2,1,0:T(8,128)(2,1)} %get-tuple-element.340), channel_id=1, source_target_pairs={{0,2},{2,0},{4,6},{6,4},{8,10},{10,8},{12,14},{14,12},{16,18},{18,... | collective-permute-start | bytes 13369352 | tf_op jit(solution)/shard_map/ppermute | solution.py:510
  437.9 34.8 %collective-permute-start.41 = (bf16[544,1024]{1,0:T(8,128)(2,1)}, bf16[544,1024]{1,0:T(8,128)(2,1)S(1)}, u32[]{:S(2)}, u32[]{:S(2)}) collective-permute-start(bf16[544,1024]{1,0:T(8,128)(2,1)} %fusion.12), channel_id=1, source_target_pairs={{0,8},{2,10},{4,12},{6,14},{8,16},{10,18},{12,20},{14,22},{16,24},... | collective-permute-start | bytes 3342344 | tf_op jit(solution)/shard_map/ppermute | solution.py:514
  441.8 31.0 %collective-permute-start.40 = (bf16[544,1024]{1,0:T(8,128)(2,1)}, bf16[544,1024]{1,0:T(8,128)(2,1)S(1)}, u32[]{:S(2)}, u32[]{:S(2)}) collective-permute-start(bf16[544,1024]{1,0:T(8,128)(2,1)} %fusion.51), channel_id=1, source_target_pairs={{0,1},{1,0},{2,3},{3,2},{4,5},{5,4},{6,7},{7,6},{8,9},{9,8},{10,11... | collective-permute-start | bytes 3342344 | tf_op jit(solution)/shard_map/ppermute | solution.py:518
  472.8 38.6 %collective-permute-start.42 = (bf16[2,2,544,1024]{3,2,1,0:T(8,128)(2,1)}, bf16[2,2,544,1024]{3,2,1,0:T(8,128)(2,1)}, u32[]{:S(2)}, u32[]{:S(2)}) collective-permute-start(bf16[2,2,544,1024]{3,2,1,0:T(8,128)(2,1)} %get-tuple-element.375), channel_id=1, source_target_pairs={{0,2},{2,0},{4,6},{6,4},{8,10},{10,8},{12,14},{14,12},{16,18},{18,... | collective-permute-start | bytes 13369352 | tf_op jit(solution)/shard_map/ppermute | solution.py:510
  472.9 38.5 %collective-permute-start.45 = (bf16[2,2,512,1024]{3,2,1,0:T(8,128)(2,1)}, bf16[2,2,512,1024]{3,2,1,0:T(8,128)(2,1)}, u32[]{:S(2)}, u32[]{:S(2)}) collective-permute-start(bf16[2,2,512,1024]{3,2,1,0:T(8,128)(2,1)} %get-tuple-element.385), channel_id=1, source_target_pairs={{0,2},{2,0},{4,6},{6,4},{8,10},{10,8},{12,14},{14,12},{16,18},{18,... | collective-permute-start | bytes 12582920 | tf_op jit(solution)/shard_map/ppermute | solution.py:510
  511.4 39.9 %collective-permute-start.49 = (bf16[2,2,512,1024]{3,2,1,0:T(8,128)(2,1)}, bf16[2,2,512,1024]{3,2,1,0:T(8,128)(2,1)}, u32[]{:S(2)}, u32[]{:S(2)}) collective-permute-start(bf16[2,2,512,1024]{3,2,1,0:T(8,128)(2,1)} %get-tuple-element.400), channel_id=1, source_target_pairs={{0,2},{2,0},{4,6},{6,4},{8,10},{10,8},{12,14},{14,12},{16,18},{18,... | collective-permute-start | bytes 12582920 | tf_op jit(solution)/shard_map/ppermute | solution.py:510
  515.3 29.0 %collective-permute-start.50 = (bf16[544,1024]{1,0:T(8,128)(2,1)}, bf16[544,1024]{1,0:T(8,128)(2,1)S(1)}, u32[]{:S(2)}, u32[]{:S(2)}) collective-permute-start(bf16[544,1024]{1,0:T(8,128)(2,1)} %fusion.11), channel_id=1, source_target_pairs={{0,8},{2,10},{4,12},{6,14},{8,16},{10,18},{12,20},{14,22},{16,24},... | collective-permute-start | bytes 3342344 | tf_op jit(solution)/shard_map/ppermute | solution.py:514
  551.3 33.7 %collective-permute-start.52 = (bf16[2,2,512,1024]{3,2,1,0:T(8,128)(2,1)}, bf16[2,2,512,1024]{3,2,1,0:T(8,128)(2,1)}, u32[]{:S(2)}, u32[]{:S(2)}) collective-permute-start(bf16[2,2,512,1024]{3,2,1,0:T(8,128)(2,1)} %get-tuple-element.416), channel_id=1, source_target_pairs={{0,2},{2,0},{4,6},{6,4},{8,10},{10,8},{12,14},{14,12},{16,18},{18,... | collective-permute-start | bytes 12582920 | tf_op jit(solution)/shard_map/ppermute | solution.py:510
  585.1 36.0 %collective-permute-start.55 = (bf16[2,2,512,1024]{3,2,1,0:T(8,128)(2,1)S(1)}, bf16[2,2,512,1024]{3,2,1,0:T(8,128)(2,1)}, u32[]{:S(2)}, u32[]{:S(2)}) collective-permute-start(bf16[2,2,512,1024]{3,2,1,0:T(8,128)(2,1)S(1)} %copy-done.59), channel_id=1, source_target_pairs={{0,2},{2,0},{4,6},{6,4},{8,10},{10,8},{12,14},{14,12},{16,18},{18,... | collective-permute-start | bytes 12582920 | tf_op jit(solution)/shard_map/ppermute | solution.py:510
  665.9 38.1 %collective-permute-start.66 = (bf16[512,1024]{1,0:T(8,128)(2,1)}, bf16[512,1024]{1,0:T(8,128)(2,1)}, u32[]{:S(2)}, u32[]{:S(2)}) collective-permute-start(bf16[512,1024]{1,0:T(8,128)(2,1)} %fusion.35), channel_id=1, source_target_pairs={{0,8},{2,10},{4,12},{6,14},{8,16},{10,18},{12,20},{14,22},{16,24},... | collective-permute-start | bytes 3145736 | tf_op jit(solution)/shard_map/ppermute | solution.py:514
  670.7 42.2 %collective-permute-start.65 = (bf16[512,1024]{1,0:T(8,128)(2,1)}, bf16[512,1024]{1,0:T(8,128)(2,1)}, u32[]{:S(2)}, u32[]{:S(2)}) collective-permute-start(bf16[512,1024]{1,0:T(8,128)(2,1)} %fusion.38), channel_id=1, source_target_pairs={{0,8},{2,10},{4,12},{6,14},{8,16},{10,18},{12,20},{14,22},{16,24},... | collective-permute-start | bytes 3145736 | tf_op jit(solution)/shard_map/ppermute | solution.py:514
  673.5 39.4 %collective-permute-start.64 = (bf16[512,1024]{1,0:T(8,128)(2,1)}, bf16[512,1024]{1,0:T(8,128)(2,1)}, u32[]{:S(2)}, u32[]{:S(2)}) collective-permute-start(bf16[512,1024]{1,0:T(8,128)(2,1)} %fusion.58), channel_id=1, source_target_pairs={{0,4},{2,6},{4,0},{6,2},{8,12},{10,14},{12,8},{14,10},{16,20},{18,... | collective-permute-start | bytes 3145736 | tf_op jit(solution)/shard_map/ppermute | solution.py:510
  677.2 35.7 %collective-permute-start.63 = (bf16[512,1024]{1,0:T(8,128)(2,1)}, bf16[512,1024]{1,0:T(8,128)(2,1)}, u32[]{:S(2)}, u32[]{:S(2)}) collective-permute-start(bf16[512,1024]{1,0:T(8,128)(2,1)} %fusion.57), channel_id=1, source_target_pairs={{0,1},{1,0},{2,3},{3,2},{4,5},{5,4},{6,7},{7,6},{8,9},{9,8},{10,11... | collective-permute-start | bytes 3145736 | tf_op jit(solution)/shard_map/ppermute | solution.py:518
  725.6 34.9 %collective-permute-start.69 = (bf16[512,1024]{1,0:T(8,128)(2,1)S(1)}, bf16[512,1024]{1,0:T(8,128)(2,1)S(1)}, u32[]{:S(2)}, u32[]{:S(2)}) collective-permute-start(bf16[512,1024]{1,0:T(8,128)(2,1)S(1)} %fusion.33), channel_id=1, source_target_pairs={{0,8},{2,10},{4,12},{6,14},{8,16},{10,18},{12,20},{14,22},{16,24},... | collective-permute-start | bytes 3145736 | tf_op jit(solution)/shard_map/ppermute | solution.py:514
  728.3 32.2 %collective-permute-start.68 = (bf16[512,1024]{1,0:T(8,128)(2,1)S(1)}, bf16[512,1024]{1,0:T(8,128)(2,1)S(1)}, u32[]{:S(2)}, u32[]{:S(2)}) collective-permute-start(bf16[512,1024]{1,0:T(8,128)(2,1)S(1)} %fusion.37), channel_id=1, source_target_pairs={{0,4},{2,6},{4,0},{6,2},{8,12},{10,14},{12,8},{14,10},{16,20},{18,... | collective-permute-start | bytes 3145736 | tf_op jit(solution)/shard_map/ppermute | solution.py:510
  730.7 29.9 %collective-permute-start.67 = (bf16[512,1024]{1,0:T(8,128)(2,1)S(1)}, bf16[512,1024]{1,0:T(8,128)(2,1)S(1)}, u32[]{:S(2)}, u32[]{:S(2)}) collective-permute-start(bf16[512,1024]{1,0:T(8,128)(2,1)S(1)} %fusion.59), channel_id=1, source_target_pairs={{0,1},{1,0},{2,3},{3,2},{4,5},{5,4},{6,7},{7,6},{8,9},{9,8},{10,11... | collective-permute-start | bytes 3145736 | tf_op jit(solution)/shard_map/ppermute | solution.py:518
  762.8 44.6 %collective-permute-start.74 = (bf16[512,1024]{1,0:T(8,128)(2,1)S(1)}, bf16[512,1024]{1,0:T(8,128)(2,1)S(1)}, u32[]{:S(2)}, u32[]{:S(2)}) collective-permute-start(bf16[512,1024]{1,0:T(8,128)(2,1)S(1)} %fusion.31), channel_id=1, source_target_pairs={{0,8},{2,10},{4,12},{6,14},{8,16},{10,18},{12,20},{14,22},{16,24},... | collective-permute-start | bytes 3145736 | tf_op jit(solution)/shard_map/ppermute | solution.py:514
  764.9 42.5 %collective-permute-start.70 = (bf16[512,1024]{1,0:T(8,128)(2,1)S(1)}, bf16[512,1024]{1,0:T(8,128)(2,1)S(1)}, u32[]{:S(2)}, u32[]{:S(2)}) collective-permute-start(bf16[512,1024]{1,0:T(8,128)(2,1)S(1)} %fusion.36), channel_id=1, source_target_pairs={{0,4},{2,6},{4,0},{6,2},{8,12},{10,14},{12,8},{14,10},{16,20},{18,... | collective-permute-start | bytes 3145736 | tf_op jit(solution)/shard_map/ppermute | solution.py:510
  (105 other events, 1995.4 us)
Sparse Core Ops, SparseCore 0:
  11.1 236.9 all-gather.4
  722.5 85.2 all-gather.6

commit v6 on v5

--- a/solution.py
+++ b/solution.py
@@ -780,16 +780,20 @@
     def sum_cores(sums, k):
         sums["got"][k] = swap(sums["send"][k], data_count, 1)
 
-    def sum_sides(sums, k):
-        keep, got = sums["keep"][k], sums["got"][k]
-        away = plus(keep[1, 1], got[1, 1])
+    def away_of(sums, k):
+        return plus(sums["keep"][k][1, 1], sums["got"][k][1, 1])
+
+    def near_of(sums, k):
+        near = [sums["keep"][k][1, 0], sums["got"][k][1, 0]]
+        return plus(*near) if is_flat(sums, k) else plus(*near, sums["side_got"][k])
+
+    def sum_sides(sums, k, away=None):
+        away = away_of(sums, k) if away is None else away
         sums["side_got"][k] = swap(away, data_count, 2) if is_flat(sums, k) else other_side(away)
 
-    def sum_across(sums, k):
-        near = [sums["keep"][k][1, 0], sums["got"][k][1, 0]]
-        if not is_flat(sums, k):
-            near.append(sums["side_got"][k])
-        sums["arrived"][k] = swap(plus(*near), data_count, 2)
+    def sum_across(sums, k, near=None):
+        near = near_of(sums, k) if near is None else near
+        sums["arrived"][k] = swap(near, data_count, 2)
 
     def first_of(sums, k):
         return [sums["keep"][k][0, 0], sums["got"][k][0, 0], sums["arrived"][k]]
@@ -896,9 +900,12 @@
         grad_moe_cols = own_columns(from_sides(first[:tok_count], second[:tok_count]))
         grad_moe_cols = jnp.pad(grad_moe_cols, ((0, 0), (0, half_width - col_width)))
         grad_moe_cols = jnp.concatenate([grad_moe_cols, grad_gates], axis=0)
-    (grad_moe_cols,) = step_end(grad_moe_cols)
+    out_second = plus(*second_of(outs, 1))
+    grad_moe_cols, out_second = step_end(grad_moe_cols, out_second)
     sum_sides(outs, 2)
-    out_second = onward_sum(*second_of(outs, 1))
+    out_second = onward(out_second, data_count)
+    out_first = onward_sum(*first_of(outs, 1))
+    near_next, away_next = near_of(outs, 2), away_of(outs, 3)
     d_gate_home = grad_moe_cols[tok_count:].reshape(expert_total, tok_count)
     grad_moe_cols = grad_moe_cols[:tok_count, :col_width]
 
@@ -923,11 +930,13 @@
     )
     branch_cols = grad_mixed_cols.astype(half_type)
     grad_branch = from_sides(*both_halves(branch_cols))
-    grad_branch, out_second = step_end(grad_branch, out_second)
-    out_first = onward_sum(*first_of(outs, 1))
-    sum_across(outs, 2)
+    grad_branch, out_first, out_second, near_next, away_next = step_end(
+        grad_branch, out_first, out_second, near_next, away_next
+    )
+    sum_across(outs, 2, near_next)
     out_second = onward_sum(out_second, *second_of(outs, 2))
-    sum_sides(outs, 3)
+    sum_sides(outs, 3, away_next)
+    away_next = away_of(outs, 0)
 
     grad_latent_out = nt_dot(grad_branch, out_up_rows).astype(half_type)
     grad_up_out = lax.dot_general(
@@ -948,10 +957,13 @@
         head_shared,
         3,
     )
-    grad_raw, out_first, out_second = step_end(grad_raw, out_first, out_second)
+    grad_raw, out_first, out_second, away_next = step_end(
+        grad_raw, out_first, out_second, away_next
+    )
     out_first = onward_sum(out_first, *first_of(outs, 2))
-    sum_sides(outs, 0)
+    sum_sides(outs, 0, away_next)
     sum_across(outs, 3)
+    out_second = plus(out_second, *second_of(outs, 3))
     latent_parts = jnp.concatenate([nt_dot(grad_raw[p], up_rows[p]) for p in range(3)], axis=1)
     grad_latent = tensor_sum(latent_parts.astype(half_type)).astype(half_type)
     grad_up = [
@@ -978,6 +990,7 @@
     def rows_at(i):
         return adapter_sums[:, i * ADAPTER_RANK : (i + 1) * ADAPTER_RANK]
 
+    sum_down_out, sum_up_out = rows_at(0).transpose(0, 2, 1), rows_at(1)
     sum_up_qkv = jnp.stack([rows_at(2 + p) for p in range(3)])
     sum_down_qkv = jnp.stack(
         [
@@ -990,8 +1003,8 @@
     grad_normed_part += nt_dot(grad_raw[1], w_proj[1])
     grad_normed_part += nt_dot(grad_raw[2], w_proj[2])
     grad_normed_mine, grad_normed_other = split_columns(grad_normed_part)
-    grad_normed_other, out_first = step_end(grad_normed_other, out_first)
-    out_second = onward_sum(out_second, *second_of(outs, 3))
+    grad_normed_other, out_first, out_second = step_end(grad_normed_other, out_first, out_second)
+    out_second = onward(out_second, data_count)
     sum_across(outs, 0)
     grad_normed_cols = join_columns(grad_normed_mine, grad_normed_other)
     grad_normed_cols += jnp.dot(
@@ -1003,7 +1016,11 @@
         jnp.sum(hidden_cols * attention_gain_cols * grad_normed_cols, axis=1, keepdims=True)
     )
     along_in, out_second = step_end(along_in, out_second)
-    out_first = plus(onward_sum(out_first, *first_of(outs, 3)), *first_of(outs, 0))
+    out_first = onward_sum(out_first, *first_of(outs, 3))
+    out_first, sum_down_qkv, sum_up_qkv, sum_down_out, sum_up_out = fence(
+        out_first, sum_down_qkv, sum_up_qkv, sum_down_out, sum_up_out
+    )
+    out_first = plus(out_first, *first_of(outs, 0))
     out_second = plus(out_second, *second_of(outs, 0))
     if pair:
         moe_cols = out_first.astype(jnp.float32) + other_side(out_second).astype(jnp.float32)
@@ -1020,8 +1037,8 @@
         grad_input,
         sum_down_qkv,
         sum_up_qkv,
-        rows_at(0).transpose(0, 2, 1),
-        rows_at(1),
+        sum_down_out,
+        sum_up_out,
     )
 
 

time: 864 us -> 864 us (level)
  starting transfers between devices: 82.7 us -> 94 us
    ppermute x37, waiting for transfers between devices: 53.5 us -> 65.9 us  [swap(): return lax.ppermute(values, 'dp', [(i, i ^ bit) for i in range(data_count)])]
    ppermute x22, waiting for transfers between devices: 77.7 us -> 65.4 us  [other_side(): return lax.ppermute(values, 'tensor', [(0, 1), (1, 0)])]
    convert_element_type x30 -> x28, other arithmetic: 78.9 us -> 76.4 us  [plus(): return total.astype(half_type)]
  transfers between devices with their start and end apart: 81 -> 81, of which waited for: 30 -> 30; matrix products, arithmetic and copies ran while one was open for 18% -> 19% of each run, Pallas kernels for 31% -> 31%
where the time goes in v6:
time: 864 us; the launch traced here: 854 us
  waiting for transfers between devices  295 us (34%)
  Pallas kernels  261 us (30%)
  other arithmetic  97.8 us (11%)
  starting transfers between devices  94 us (11%)
  matrix products  58 us (7%)
  local copies, waits for them, and re-layouts  31.6 us (4%)
  between operations  16.6 us (2%)
    ppermute x18, waiting for transfers between devices, onward(): lax.ppermute(values, 'dp', [(i, (i + QUAD) % data_count) for i in range(d...  123 us
    pallas_call x4, Pallas kernels, call_experts(): pl.pallas_call(functools.partial(expert_kernel, experts, cap), out_shape=...  118 us
    convert_element_type x28, other arithmetic, plus(): return total.astype(half_type)  76.4 us
    ppermute x37, waiting for transfers between devices, swap(): return lax.ppermute(values, 'dp', [(i, i ^ bit) for i in range(data_count)])  65.9 us
    ppermute x22, waiting for transfers between devices, other_side(): return lax.ppermute(values, 'tensor', [(0, 1), (1, 0)])  65.4 us
    pallas_call x4, Pallas kernels, call_output(): pl.pallas_call(functools.partial(output_kernel, experts, cap), out_shape=...  65.2 us
    pallas_call x2, Pallas kernels, call_heads(): pl.pallas_call(kernel, out_shape=[jax.ShapeDtypeStruct((toks, width), hal...  41.6 us
    pallas_call x1, Pallas kernels, call_grad_rows(): pl.pallas_call(functools.partial(grad_rows_kernel, experts, cap), out_sha...  36.3 us
  transfers between devices with their start and end apart: 81, of which 30 were waited for; matrix products, arithmetic and copies ran while one was open for 19% of the time, Pallas kernels for 31%

profile of v6, /device:TPU:0, one launch (start us, length us, event | category | flops | bytes accessed | tf_op | source)
XLA Modules:
  0.0 854.2 jit_solution(560061504778434573)
XLA Ops:
  10.4 7.4 all-to-all-start
  42.6 19.2 %attend.1 = (bf16[512,1024]{1,0:T(8,128)(2,1)}, bf16[512,1024]{1,0:T(8,128)(2,1)}, bf16[512,1024]{1,0:T(8,128)(2,1)}, bf16[512,1024]{1,0:T(8,128)(2,1)}) custom-call(f32[512,1024]{1,0:T(8,128)} %convolution_add_fusion.2.raw_q, f32[512,1024]{1,0:T(8,128)} %convolution_add_fusion.1.raw_k, f32[512,1024]{1,0:T(8,128)} %convolution_add_fusion.raw_v, ...), custom_call_target="tpu_custom_call" | custom-call | flops 2684354560 | bytes 4194304 | tf_op jit(solution)/shard_map/attend/pallas_call | solution.py:105
  61.9 3.6 fusion.127
  70.2 24.6 %collective-permute-done.1 = bf16[512,16]{0,1:T(8,128)(2,1)S(1)} collective-permute-done((bf16[512,16]{0,1:T(8,128)(2,1)S(1)}, bf16[512,16]{0,1:T(8,128)(2,1)S(1)}, u32[]{:S(2)}, u32[]{:S(2)}) %collective-permute-start.1) | collective-permute-done | bytes 16416 | tf_op jit(solution)/shard_map/ppermute | solution.py:518
  103.4 37.4 %collective-permute-done.3.own_first_ref = bf16[512,1024]{1,0:T(8,128)(2,1)} collective-permute-done((bf16[512,1024]{1,0:T(8,128)(2,1)S(1)}, bf16[512,1024]{1,0:T(8,128)(2,1)}, u32[]{:S(2)}, u32[]{:S(2)}) %collective-permute-start.3) | collective-permute-done | bytes 1048608 | tf_op jit(solution)/shard_map/ppermute | solution.py:514
  143.9 7.5 collective-permute-start.7
  151.5 37.3 %collective-permute-done.10.across_first_ref = bf16[512,1024]{1,0:T(8,128)(2,1)S(1)} collective-permute-done((bf16[512,1024]{1,0:T(8,128)(2,1)}, bf16[512,1024]{1,0:T(8,128)(2,1)S(1)}, u32[]{:S(2)}, u32[]{:S(2)}) %collective-permute-start.10) | collective-permute-done | bytes 1048608 | tf_op jit(solution)/shard_map/ppermute | solution.py:510
  191.6 14.6 %all-to-all-start.1 = ((f32[16,4,512]{2,1,0:T(4,128)}), f32[16,4,512]{2,1,0:T(4,128)S(1)}, u32[]{:S(2)}, u32[]{:S(2)}) async-start(f32[16,4,512]{2,1,0:T(4,128)} %reshape.318), calls=%async_computation.1 | async-start | bytes 262144 | tf_op jit(solution)/shard_map/all_to_all | solution.py:824
  207.6 6.6 all-to-all-done.1
  214.8 33.3 %all-gather.5.cloned.1.call-done = bf16[16384,1024]{1,0:T(8,128)(2,1)} async-done(((bf16[512,1024]{1,0:T(8,128)(2,1)}), bf16[16384,1024]{1,0:T(8,128)(2,1)}) %all-gather.5.cloned.1.call-update) | async-done | bytes 33554448 | tf_op jit(solution)/shard_map/all_gather | solution.py:640
  250.6 36.3 %grad_rows.1.dh_ref = bf16[4,1280,512]{2,1,0:T(8,128)(2,1)} custom-call(s32[16]{0:T(128)} %fusion.105.block_ids, s32[16,4,1,512]{3,2,1,0:T(1,128)} %broadcast_in_dim.86.place_ref, bf16[4,512,2048]{2,1,0:T(8,128)(2,1)} %down_ref.9, bf16[16,2,512,1024]{3,2,1,0:T(8,128)(2,1)} %bitcast.265), custom_call_target="tpu_custom_call" | custom-call | flops 42949672960 | bytes 47185920 | tf_op jit(solution)/shard_map/grad_rows/pallas_call | solution.py:388
  293.9 29.5 %experts.4 = (bf16[2,2,544,1024]{3,2,1,0:T(8,128)(2,1)}, bf16[2,2,544,1024]{3,2,1,0:T(8,128)(2,1)}, bf16[4,320,512]{2,1,0:T(8,128)(2,1)}) custom-call(s32[2]{0:T(128)} %pad_add_fusion.flip_ref, s32[4,4,1,512]{3,2,1,0:T(1,128)} %broadcast_in_dim.87.place_ref, f32[4,4,1,512]{3,2,1,0:T(1,128)} %copy.88.gate_ref, s32[4,512,4]{2,1,0:T(8,128)} %get-tuple-element.566.target_ref, ...), custom_call_target="tpu_custom_call" | custom-call | flops 24159191040 | bytes 33554432 | tf_op jit(solution)/shard_map/experts/pallas_call | solution.py:422
  327.6 29.8 %experts.5 = (bf16[2,2,544,1024]{3,2,1,0:T(8,128)(2,1)}, bf16[2,2,544,1024]{3,2,1,0:T(8,128)(2,1)}, bf16[4,320,512]{2,1,0:T(8,128)(2,1)}) custom-call(s32[2]{0:T(128)} %pad_add_fusion.flip_ref, s32[4,4,1,512]{3,2,1,0:T(1,128)} %broadcast_in_dim.89.place_ref, f32[4,4,1,512]{3,2,1,0:T(1,128)} %copy.89.gate_ref, s32[4,512,4]{2,1,0:T(8,128)} %get-tuple-element.565.target_ref, ...), custom_call_target="tpu_custom_call" | custom-call | flops 24159191040 | bytes 33554432 | tf_op jit(solution)/shard_map/experts/pallas_call | solution.py:422
  363.3 5.1 collective-permute-done.30.far_second_ref
  370.3 29.6 %experts.6 = (bf16[2,2,544,1024]{3,2,1,0:T(8,128)(2,1)}, bf16[2,2,544,1024]{3,2,1,0:T(8,128)(2,1)}, bf16[4,320,512]{2,1,0:T(8,128)(2,1)}) custom-call(s32[2]{0:T(128)} %pad_add_fusion.flip_ref, s32[4,4,1,512]{3,2,1,0:T(1,128)} %broadcast_in_dim.91.place_ref, f32[4,4,1,512]{3,2,1,0:T(1,128)} %copy.90.gate_ref, s32[4,512,4]{2,1,0:T(8,128)} %get-tuple-element.564.target_ref, ...), custom_call_target="tpu_custom_call" | custom-call | flops 24159191040 | bytes 33554432 | tf_op jit(solution)/shard_map/experts/pallas_call | solution.py:422
  409.6 16.1 %outputs.4 = (bf16[2,2,512,1024]{3,2,1,0:T(8,128)(2,1)}, bf16[2,2,512,1024]{3,2,1,0:T(8,128)(2,1)}) custom-call(s32[2]{0:T(128)} %pad_add_fusion.flip_ref, s32[4,512,4]{2,1,0:T(8,128)} %get-tuple-element.566.target_ref, bf16[4,512,2048]{2,1,0:T(8,128)(2,1)} %down_ref.9, bf16[4,320,512]{2,1,0:T(8,128)(2,1)} %get-tuple-element.346.hidden_ref), custom_call_target="tpu_custom_call" | custom-call | flops 10737418240 | bytes 16777216 | tf_op jit(solution)/shard_map/outputs/pallas_call | solution.py:476
  425.7 6.5 collective-permute-done.34.across_second_ref
  434.6 3.3 fusion.12
  443.3 29.4 %experts.7 = (bf16[2,2,544,1024]{3,2,1,0:T(8,128)(2,1)}, bf16[2,2,544,1024]{3,2,1,0:T(8,128)(2,1)}, bf16[4,320,512]{2,1,0:T(8,128)(2,1)}) custom-call(s32[2]{0:T(128)} %pad_add_fusion.flip_ref, s32[4,4,1,512]{3,2,1,0:T(1,128)} %broadcast_in_dim.93.place_ref, f32[4,4,1,512]{3,2,1,0:T(1,128)} %broadcast_in_dim.94.gate_ref, ...), custom_call_target="tpu_custom_call" | custom-call | flops 24159191040 | bytes 33554432 | tf_op jit(solution)/shard_map/experts/pallas_call | solution.py:422
  485.7 16.3 %outputs.5 = (bf16[2,2,512,1024]{3,2,1,0:T(8,128)(2,1)}, bf16[2,2,512,1024]{3,2,1,0:T(8,128)(2,1)}) custom-call(s32[2]{0:T(128)} %pad_add_fusion.flip_ref, s32[4,512,4]{2,1,0:T(8,128)} %get-tuple-element.564.target_ref, bf16[4,512,2048]{2,1,0:T(8,128)(2,1)} %down_ref.9, bf16[4,320,512]{2,1,0:T(8,128)(2,1)} %get-tuple-element.381.hidden_ref), custom_call_target="tpu_custom_call" | custom-call | flops 10737418240 | bytes 16777216 | tf_op jit(solution)/shard_map/outputs/pallas_call | solution.py:476
  507.7 3.5 collective-permute-done.43
  511.3 3.9 fusion.11
  527.0 16.2 %outputs.6 = (bf16[2,2,512,1024]{3,2,1,0:T(8,128)(2,1)}, bf16[2,2,512,1024]{3,2,1,0:T(8,128)(2,1)}) custom-call(s32[2]{0:T(128)} %pad_add_fusion.flip_ref, s32[4,512,4]{2,1,0:T(8,128)} %get-tuple-element.563.target_ref, bf16[4,512,2048]{2,1,0:T(8,128)(2,1)} %down_ref.9, bf16[4,320,512]{2,1,0:T(8,128)(2,1)} %get-tuple-element.399.hidden_ref), custom_call_target="tpu_custom_call" | custom-call | flops 10737418240 | bytes 16777216 | tf_op jit(solution)/shard_map/outputs/pallas_call | solution.py:476
  544.2 3.4 collective-permute-done.48
  547.6 3.6 collective-permute-done.47
  558.9 16.5 %outputs.7 = (bf16[2,2,512,1024]{3,2,1,0:T(8,128)(2,1)}, bf16[2,2,512,1024]{3,2,1,0:T(8,128)(2,1)}) custom-call(s32[2]{0:T(128)} %pad_add_fusion.flip_ref, s32[4,512,4]{2,1,0:T(8,128)} %get-tuple-element.565.target_ref, bf16[4,512,2048]{2,1,0:T(8,128)(2,1)} %down_ref.9, bf16[4,320,512]{2,1,0:T(8,128)(2,1)} %get-tuple-element.416.hidden_ref), custom_call_target="tpu_custom_call" | custom-call | flops 10737418240 | bytes 16777216 | tf_op jit(solution)/shard_map/outputs/pallas_call | solution.py:476
  575.5 4.7 collective-permute-done.54
  595.0 21.5 %collective-permute-done.57 = bf16[544,1024]{1,0:T(8,128)(2,1)S(1)} collective-permute-done((bf16[544,1024]{1,0:T(8,128)(2,1)S(1)}, bf16[544,1024]{1,0:T(8,128)(2,1)S(1)}, u32[]{:S(2)}, u32[]{:S(2)}) %collective-permute-start.57) | collective-permute-done | bytes 1114144 | tf_op jit(solution)/shard_map/ppermute | solution.py:514
  616.4 4.6 fusion.5
  629.1 3.6 fusion.122
  637.0 3.5 fusion.57
  645.5 10.7 %collective-permute-done.61 = bf16[512,1024]{1,0:T(8,128)(2,1)S(1)} collective-permute-done((bf16[512,1024]{1,0:T(8,128)(2,1)S(1)}, bf16[512,1024]{1,0:T(8,128)(2,1)S(1)}, u32[]{:S(2)}, u32[]{:S(2)}) %collective-permute-start.61) | collective-permute-done | bytes 1048608 | tf_op jit(solution)/shard_map/ppermute | solution.py:518
  656.5 7.9 collective-permute-done.62
  664.4 19.5 %collective-permute-done.63 = bf16[512,1024]{1,0:T(8,128)(2,1)S(1)} collective-permute-done((bf16[512,1024]{1,0:T(8,128)(2,1)S(1)}, bf16[512,1024]{1,0:T(8,128)(2,1)S(1)}, u32[]{:S(2)}, u32[]{:S(2)}) %collective-permute-start.63) | collective-permute-done | bytes 1048608 | tf_op jit(solution)/shard_map/ppermute | solution.py:514
  688.5 3.4 add_convert_fusion.7.grad
  693.2 22.4 %attend_back.1 = (bf16[512,1024]{1,0:T(8,128)(2,1)}, bf16[512,1024]{1,0:T(8,128)(2,1)}, bf16[512,1024]{1,0:T(8,128)(2,1)}) custom-call(f32[512,1024]{1,0:T(8,128)} %convolution_add_fusion.2.raw_q, f32[512,1024]{1,0:T(8,128)} %convolution_add_fusion.1.raw_k, bf16[512,1024]{1,0:T(8,128)(2,1)} %get-tuple-element.471.queries, ...), custom_call_target="tpu_custom_call" | custom-call | flops 2684354560 | bytes 4194304 | tf_op jit(solution)/shard_map/attend_back/pallas_call | solution.py:105
  732.4 3.5 fusion.31
  738.8 4.4 fusion.128
  743.2 4.3 fusion.129
  747.6 6.1 add_add_fusion
  753.9 12.4 %collective-permute-done.69 = bf16[512,1024]{1,0:T(8,128)(2,1)S(1)} collective-permute-done((bf16[512,1024]{1,0:T(8,128)(2,1)S(1)}, bf16[512,1024]{1,0:T(8,128)(2,1)S(1)}, u32[]{:S(2)}, u32[]{:S(2)}) %collective-permute-start.69) | collective-permute-done | bytes 1048608 | tf_op jit(solution)/shard_map/ppermute | solution.py:514
  772.4 9.0 %collective-permute-done.71 = bf16[512,1024]{1,0:T(8,128)(2,1)S(1)} collective-permute-done((bf16[512,1024]{1,0:T(8,128)(2,1)S(1)}, bf16[512,1024]{1,0:T(8,128)(2,1)S(1)}, u32[]{:S(2)}, u32[]{:S(2)}) %collective-permute-start.71) | collective-permute-done | bytes 1048608 | tf_op jit(solution)/shard_map/ppermute | solution.py:518
  786.1 13.4 %collective-permute-done.70 = bf16[512,1024]{1,0:T(8,128)(2,1)S(1)} collective-permute-done((bf16[512,1024]{1,0:T(8,128)(2,1)S(1)}, bf16[512,1024]{1,0:T(8,128)(2,1)S(1)}, u32[]{:S(2)}, u32[]{:S(2)}) %collective-permute-start.70) | collective-permute-done | bytes 1048608 | tf_op jit(solution)/shard_map/ppermute | solution.py:510
  799.5 12.0 %collective-permute-done.74 = bf16[512,1024]{1,0:T(8,128)(2,1)S(1)} collective-permute-done((bf16[512,1024]{1,0:T(8,128)(2,1)S(1)}, bf16[512,1024]{1,0:T(8,128)(2,1)S(1)}, u32[]{:S(2)}, u32[]{:S(2)}) %collective-permute-start.74) | collective-permute-done | bytes 1048608 | tf_op jit(solution)/shard_map/ppermute | solution.py:514
  823.0 5.9 fusion
  830.8 3.9 collective-permute-done.75
  834.7 3.5 copy.93
  842.4 4.5 add_convert_fusion.5
  (420 shorter events, 212.3 us)
Async XLA Ops:
  7.2 241.0 %all-gather.5.cloned.1.call-start = ((), (), s32[]{:S(2)}) async-start(), calls=%async_computation.2 | async-start | bytes 34603008 | tf_op jit(solution)/shard_map/all_gather | solution.py:640
  10.4 28.8 %all-to-all-start = ((s32[16,5,512]{2,1,0:T(8,128)}), s32[16,5,512]{2,1,0:T(8,128)S(1)}, u32[]{:S(2)}, u32[]{:S(2)}) async-start(s32[16,5,512]{2,1,0:T(8,128)} %concatenate.31), calls=%async_computation | async-start | bytes 524288 | tf_op jit(solution)/shard_map/all_to_all | solution.py:600
  65.7 29.1 %collective-permute-start = (bf16[512,1024]{1,0:T(8,128)(2,1)S(1)}, bf16[512,1024]{1,0:T(8,128)(2,1)S(1)}, u32[]{:S(2)}, u32[]{:S(2)}) collective-permute-start(bf16[512,1024]{1,0:T(8,128)(2,1)S(1)} %select_convert_fusion.1), channel_id=1, source_target_pairs={{0,1},{1,0},{2,3},{3,2},{4,5},{5,4},{6,7},{7,6},{8,9},{9,8},{10,11... | collective-permute-start | bytes 3145736 | tf_op jit(solution)/shard_map/ppermute | solution.py:518
  99.9 40.9 %collective-permute-start.3 = (bf16[512,1024]{1,0:T(8,128)(2,1)S(1)}, bf16[512,1024]{1,0:T(8,128)(2,1)}, u32[]{:S(2)}, u32[]{:S(2)}) collective-permute-start(bf16[512,1024]{1,0:T(8,128)(2,1)S(1)} %multiply_convert_fusion.own_first_ref), channel_id=1, source_target_pairs={{0,8},{2,10},{4,12},{6,14},{8,16},{10,18},{12,20},{14,22},{16,24},... | collective-permute-start | bytes 3145736 | tf_op jit(solution)/shard_map/ppermute | solution.py:514
  101.4 39.4 %collective-permute-start.4 = (bf16[512,1024]{1,0:T(8,128)(2,1)S(1)}, bf16[512,1024]{1,0:T(8,128)(2,1)S(1)}, u32[]{:S(2)}, u32[]{:S(2)}) collective-permute-start(bf16[512,1024]{1,0:T(8,128)(2,1)S(1)} %multiply_convert_fusion.own_first_ref), channel_id=1, source_target_pairs={{0,1},{1,0},{2,3},{3,2},{4,5},{5,4},{6,7},{7,6},{8,9},{9,8},{10,11... | collective-permute-start | bytes 3145736 | tf_op jit(solution)/shard_map/ppermute | solution.py:518
  101.9 38.8 %collective-permute-start.5 = (bf16[512,1024]{1,0:T(8,128)(2,1)S(1)}, bf16[512,1024]{1,0:T(8,128)(2,1)S(1)}, u32[]{:S(2)}, u32[]{:S(2)}) collective-permute-start(bf16[512,1024]{1,0:T(8,128)(2,1)S(1)} %multiply_convert_fusion.own_first_ref), channel_id=1, source_target_pairs={{0,2},{2,0},{4,6},{6,4},{8,10},{10,8},{12,14},{14,12},{16,18},{18,... | collective-permute-start | bytes 3145736 | tf_op jit(solution)/shard_map/ppermute | solution.py:510
  101.9 38.9 %collective-permute-start.6 = (bf16[512,1024]{1,0:T(8,128)(2,1)S(1)}, bf16[512,1024]{1,0:T(8,128)(2,1)S(1)}, u32[]{:S(2)}, u32[]{:S(2)}) collective-permute-start(bf16[512,1024]{1,0:T(8,128)(2,1)S(1)} %multiply_convert_fusion.own_first_ref), channel_id=1, source_target_pairs={{0,4},{2,6},{4,0},{6,2},{8,12},{10,14},{12,8},{14,10},{16,20},{18,... | collective-permute-start | bytes 3145736 | tf_op jit(solution)/shard_map/ppermute | solution.py:510
  140.8 48.0 %collective-permute-start.10 = (bf16[512,1024]{1,0:T(8,128)(2,1)}, bf16[512,1024]{1,0:T(8,128)(2,1)S(1)}, u32[]{:S(2)}, u32[]{:S(2)}) collective-permute-start(bf16[512,1024]{1,0:T(8,128)(2,1)} %collective-permute-done.3.own_first_ref), channel_id=1, source_target_pairs={{0,4},{2,6},{4,0},{6,2},{8,12},{10,14},{12,8},{14,10},{16,20},{18,... | collective-permute-start | bytes 3145736 | tf_op jit(solution)/shard_map/ppermute | solution.py:510
  142.2 72.6 %collective-permute-start.11 = (bf16[512,1024]{1,0:T(8,128)(2,1)S(1)}, bf16[512,1024]{1,0:T(8,128)(2,1)}, u32[]{:S(2)}, u32[]{:S(2)}) collective-permute-start(bf16[512,1024]{1,0:T(8,128)(2,1)S(1)} %collective-permute-done.6.across_first_ref), channel_id=1, source_target_pairs={{0,1},{1,0},{2,3},{3,2},{4,5},{5,4},{6,7},{7,6},{8,9},{9,8},{10,11... | collective-permute-start | bytes 3145736 | tf_op jit(solution)/shard_map/ppermute | solution.py:518
  143.4 71.4 %collective-permute-start.12 = (bf16[512,1024]{1,0:T(8,128)(2,1)S(1)}, bf16[512,1024]{1,0:T(8,128)(2,1)}, u32[]{:S(2)}, u32[]{:S(2)}) collective-permute-start(bf16[512,1024]{1,0:T(8,128)(2,1)S(1)} %collective-permute-done.6.across_first_ref), channel_id=1, source_target_pairs={{0,2},{2,0},{4,6},{6,4},{8,10},{10,8},{12,14},{14,12},{16,18},{18,... | collective-permute-start | bytes 3145736 | tf_op jit(solution)/shard_map/ppermute | solution.py:510
  143.4 71.4 %collective-permute-start.8 = (bf16[512,1024]{1,0:T(8,128)(2,1)}, bf16[512,1024]{1,0:T(8,128)(2,1)}, u32[]{:S(2)}, u32[]{:S(2)}) collective-permute-start(bf16[512,1024]{1,0:T(8,128)(2,1)} %collective-permute-done.3.own_first_ref), channel_id=1, source_target_pairs={{0,2},{2,0},{4,6},{6,4},{8,10},{10,8},{12,14},{14,12},{16,18},{18,... | collective-permute-start | bytes 3145736 | tf_op jit(solution)/shard_map/ppermute | solution.py:510
  143.9 70.9 %collective-permute-start.7 = (bf16[512,1024]{1,0:T(8,128)(2,1)S(1)}, bf16[512,1024]{1,0:T(8,128)(2,1)}, u32[]{:S(2)}, u32[]{:S(2)}) collective-permute-start(bf16[512,1024]{1,0:T(8,128)(2,1)S(1)} %collective-permute-done.4.own_second_ref), channel_id=1, source_target_pairs={{0,8},{2,10},{4,12},{6,14},{8,16},{10,18},{12,20},{14,22},{16,24},... | collective-permute-start | bytes 3145736 | tf_op jit(solution)/shard_map/ppermute | solution.py:514
  206.2 616.8 %all-gather.7.cloned.1.call-start = ((), (), s32[]{:S(2)}) async-start(), calls=%async_computation.3 | async-start | bytes 6127616 | tf_op jit(solution)/shard_map/all_gather | solution.py:984
  248.1 38.7 %collective-permute-start.15 = (bf16[512,1024]{1,0:T(8,128)(2,1)}, bf16[512,1024]{1,0:T(8,128)(2,1)}, u32[]{:S(2)}, u32[]{:S(2)}) collective-permute-start(bf16[512,1024]{1,0:T(8,128)(2,1)} %copy-done.73), channel_id=1, source_target_pairs={{0,1},{1,0},{2,3},{3,2},{4,5},{5,4},{6,7},{7,6},{8,9},{9,8},{10,11... | collective-permute-start | bytes 3145736 | tf_op jit(solution)/shard_map/ppermute | solution.py:518
  250.1 36.8 %collective-permute-start.16 = (bf16[512,1024]{1,0:T(8,128)(2,1)}, bf16[512,1024]{1,0:T(8,128)(2,1)}, u32[]{:S(2)}, u32[]{:S(2)}) collective-permute-start(bf16[512,1024]{1,0:T(8,128)(2,1)} %copy-done.73), channel_id=1, source_target_pairs={{0,2},{2,0},{4,6},{6,4},{8,10},{10,8},{12,14},{14,12},{16,18},{18,... | collective-permute-start | bytes 3145736 | tf_op jit(solution)/shard_map/ppermute | solution.py:510
  250.1 36.8 %collective-permute-start.13 = (bf16[512,1024]{1,0:T(8,128)(2,1)}, bf16[512,1024]{1,0:T(8,128)(2,1)S(1)}, u32[]{:S(2)}, u32[]{:S(2)}) collective-permute-start(bf16[512,1024]{1,0:T(8,128)(2,1)} %collective-permute-done.3.own_first_ref), channel_id=1, source_target_pairs={{0,8},{2,10},{4,12},{6,14},{8,16},{10,18},{12,20},{14,22},{16,24},... | collective-permute-start | bytes 3145736 | tf_op jit(solution)/shard_map/ppermute | solution.py:514
  250.1 36.8 %collective-permute-start.14 = (bf16[512,1024]{1,0:T(8,128)(2,1)}, bf16[512,1024]{1,0:T(8,128)(2,1)}, u32[]{:S(2)}, u32[]{:S(2)}) collective-permute-start(bf16[512,1024]{1,0:T(8,128)(2,1)} %collective-permute-done.7.own_second_ref), channel_id=1, source_target_pairs={{0,2},{2,0},{4,6},{6,4},{8,10},{10,8},{12,14},{14,12},{16,18},{18,... | collective-permute-start | bytes 3145736 | tf_op jit(solution)/shard_map/ppermute | solution.py:510
  250.6 36.3 %collective-permute-start.17 = (bf16[512,1024]{1,0:T(8,128)(2,1)}, bf16[512,1024]{1,0:T(8,128)(2,1)}, u32[]{:S(2)}, u32[]{:S(2)}) collective-permute-start(bf16[512,1024]{1,0:T(8,128)(2,1)} %collective-permute-done.11.across_second_ref), channel_id=1, source_target_pairs={{0,2},{2,0},{4,6},{6,4},{8,10},{10,8},{12,14},{14,12},{16,18},{18,... | collective-permute-start | bytes 3145736 | tf_op jit(solution)/shard_map/ppermute | solution.py:510
  291.4 32.0 %collective-permute-start.19 = (bf16[512,1024]{1,0:T(8,128)(2,1)S(1)}, bf16[512,1024]{1,0:T(8,128)(2,1)S(1)}, u32[]{:S(2)}, u32[]{:S(2)}) collective-permute-start(bf16[512,1024]{1,0:T(8,128)(2,1)S(1)} %collective-permute-done.13.own_first_ref), channel_id=1, source_target_pairs={{0,2},{2,0},{4,6},{6,4},{8,10},{10,8},{12,14},{14,12},{16,18},{18,... | collective-permute-start | bytes 3145736 | tf_op jit(solution)/shard_map/ppermute | solution.py:510
  291.5 31.9 %collective-permute-start.20 = (bf16[512,1024]{1,0:T(8,128)(2,1)S(1)}, bf16[512,1024]{1,0:T(8,128)(2,1)S(1)}, u32[]{:S(2)}, u32[]{:S(2)}) collective-permute-start(bf16[512,1024]{1,0:T(8,128)(2,1)S(1)} %collective-permute-done.13.own_first_ref), channel_id=1, source_target_pairs={{0,4},{2,6},{4,0},{6,2},{8,12},{10,14},{12,8},{14,10},{16,20},{18,... | collective-permute-start | bytes 3145736 | tf_op jit(solution)/shard_map/ppermute | solution.py:510
  292.9 30.5 %collective-permute-start.18 = (bf16[512,1024]{1,0:T(8,128)(2,1)}, bf16[512,1024]{1,0:T(8,128)(2,1)}, u32[]{:S(2)}, u32[]{:S(2)}) collective-permute-start(bf16[512,1024]{1,0:T(8,128)(2,1)} %collective-permute-done.7.own_second_ref), channel_id=1, source_target_pairs={{0,8},{2,10},{4,12},{6,14},{8,16},{10,18},{12,20},{14,22},{16,24},... | collective-permute-start | bytes 3145736 | tf_op jit(solution)/shard_map/ppermute | solution.py:514
  323.5 34.0 %collective-permute-start.26 = (bf16[2,2,544,1024]{3,2,1,0:T(8,128)(2,1)}, bf16[2,2,544,1024]{3,2,1,0:T(8,128)(2,1)}, u32[]{:S(2)}, u32[]{:S(2)}) collective-permute-start(bf16[2,2,544,1024]{3,2,1,0:T(8,128)(2,1)} %get-tuple-element.319), channel_id=1, source_target_pairs={{0,2},{2,0},{4,6},{6,4},{8,10},{10,8},{12,14},{14,12},{16,18},{18,... | collective-permute-start | bytes 13369352 | tf_op jit(solution)/shard_map/ppermute | solution.py:510
  325.0 32.4 %collective-permute-start.24 = (bf16[512,1024]{1,0:T(8,128)(2,1)S(1)}, bf16[512,1024]{1,0:T(8,128)(2,1)}, u32[]{:S(2)}, u32[]{:S(2)}) collective-permute-start(bf16[512,1024]{1,0:T(8,128)(2,1)S(1)} %collective-permute-done.20.across_first_ref), channel_id=1, source_target_pairs={{0,1},{1,0},{2,3},{3,2},{4,5},{5,4},{6,7},{7,6},{8,9},{9,8},{10,11... | collective-permute-start | bytes 3145736 | tf_op jit(solution)/shard_map/ppermute | solution.py:518
  325.5 32.0 %collective-permute-start.25 = (bf16[512,1024]{1,0:T(8,128)(2,1)S(1)}, bf16[512,1024]{1,0:T(8,128)(2,1)}, u32[]{:S(2)}, u32[]{:S(2)}) collective-permute-start(bf16[512,1024]{1,0:T(8,128)(2,1)S(1)} %collective-permute-done.20.across_first_ref), channel_id=1, source_target_pairs={{0,2},{2,0},{4,6},{6,4},{8,10},{10,8},{12,14},{14,12},{16,18},{18,... | collective-permute-start | bytes 3145736 | tf_op jit(solution)/shard_map/ppermute | solution.py:510
  325.5 31.9 %collective-permute-start.22 = (bf16[512,1024]{1,0:T(8,128)(2,1)S(1)}, bf16[512,1024]{1,0:T(8,128)(2,1)}, u32[]{:S(2)}, u32[]{:S(2)}) collective-permute-start(bf16[512,1024]{1,0:T(8,128)(2,1)S(1)} %collective-permute-done.13.own_first_ref), channel_id=1, source_target_pairs={{0,8},{2,10},{4,12},{6,14},{8,16},{10,18},{12,20},{14,22},{16,24},... | collective-permute-start | bytes 3145736 | tf_op jit(solution)/shard_map/ppermute | solution.py:514
  327.4 30.0 %collective-permute-start.23 = (bf16[512,1024]{1,0:T(8,128)(2,1)}, bf16[512,1024]{1,0:T(8,128)(2,1)}, u32[]{:S(2)}, u32[]{:S(2)}) collective-permute-start(bf16[512,1024]{1,0:T(8,128)(2,1)} %collective-permute-done.18.own_second_ref), channel_id=1, source_target_pairs={{0,2},{2,0},{4,6},{6,4},{8,10},{10,8},{12,14},{14,12},{16,18},{18,... | collective-permute-start | bytes 3145736 | tf_op jit(solution)/shard_map/ppermute | solution.py:510
  357.4 42.6 %collective-permute-start.31 = (bf16[2,2,544,1024]{3,2,1,0:T(8,128)(2,1)}, bf16[2,2,544,1024]{3,2,1,0:T(8,128)(2,1)}, u32[]{:S(2)}, u32[]{:S(2)}) collective-permute-start(bf16[2,2,544,1024]{3,2,1,0:T(8,128)(2,1)} %get-tuple-element.334), channel_id=1, source_target_pairs={{0,2},{2,0},{4,6},{6,4},{8,10},{10,8},{12,14},{14,12},{16,18},{18,... | collective-permute-start | bytes 13369352 | tf_op jit(solution)/shard_map/ppermute | solution.py:510
  359.3 40.7 %collective-permute-start.28 = (bf16[512,1024]{1,0:T(8,128)(2,1)}, bf16[512,1024]{1,0:T(8,128)(2,1)S(1)}, u32[]{:S(2)}, u32[]{:S(2)}) collective-permute-start(bf16[512,1024]{1,0:T(8,128)(2,1)} %collective-permute-done.22.own_first_ref), channel_id=1, source_target_pairs={{0,2},{2,0},{4,6},{6,4},{8,10},{10,8},{12,14},{14,12},{16,18},{18,... | collective-permute-start | bytes 3145736 | tf_op jit(solution)/shard_map/ppermute | solution.py:510
  359.6 40.4 %collective-permute-start.29 = (bf16[512,1024]{1,0:T(8,128)(2,1)}, bf16[512,1024]{1,0:T(8,128)(2,1)}, u32[]{:S(2)}, u32[]{:S(2)}) collective-permute-start(bf16[512,1024]{1,0:T(8,128)(2,1)} %collective-permute-done.22.own_first_ref), channel_id=1, source_target_pairs={{0,4},{2,6},{4,0},{6,2},{8,12},{10,14},{12,8},{14,10},{16,20},{18,... | collective-permute-start | bytes 3145736 | tf_op jit(solution)/shard_map/ppermute | solution.py:510
  361.5 38.5 %collective-permute-start.32 = (bf16[544,1024]{1,0:T(8,128)(2,1)S(1)}, bf16[544,1024]{1,0:T(8,128)(2,1)S(1)}, u32[]{:S(2)}, u32[]{:S(2)}) collective-permute-start(bf16[544,1024]{1,0:T(8,128)(2,1)S(1)} %fusion.49), channel_id=1, source_target_pairs={{0,1},{1,0},{2,3},{3,2},{4,5},{5,4},{6,7},{7,6},{8,9},{9,8},{10,11... | collective-permute-start | bytes 3342344 | tf_op jit(solution)/shard_map/ppermute | solution.py:518
  368.4 31.6 %collective-permute-start.27 = (bf16[512,1024]{1,0:T(8,128)(2,1)}, bf16[512,1024]{1,0:T(8,128)(2,1)}, u32[]{:S(2)}, u32[]{:S(2)}) collective-permute-start(bf16[512,1024]{1,0:T(8,128)(2,1)} %collective-permute-done.18.own_second_ref), channel_id=1, source_target_pairs={{0,8},{2,10},{4,12},{6,14},{8,16},{10,18},{12,20},{14,22},{16,24},... | collective-permute-start | bytes 3145736 | tf_op jit(solution)/shard_map/ppermute | solution.py:514
  400.0 33.3 %collective-permute-start.36 = (bf16[2,2,544,1024]{3,2,1,0:T(8,128)(2,1)}, bf16[2,2,544,1024]{3,2,1,0:T(8,128)(2,1)}, u32[]{:S(2)}, u32[]{:S(2)}) collective-permute-start(bf16[2,2,544,1024]{3,2,1,0:T(8,128)(2,1)} %get-tuple-element.348), channel_id=1, source_target_pairs={{0,2},{2,0},{4,6},{6,4},{8,10},{10,8},{12,14},{14,12},{16,18},{18,... | collective-permute-start | bytes 13369352 | tf_op jit(solution)/shard_map/ppermute | solution.py:510
  437.8 34.9 %collective-permute-start.41 = (bf16[544,1024]{1,0:T(8,128)(2,1)}, bf16[544,1024]{1,0:T(8,128)(2,1)S(1)}, u32[]{:S(2)}, u32[]{:S(2)}) collective-permute-start(bf16[544,1024]{1,0:T(8,128)(2,1)} %fusion.12), channel_id=1, source_target_pairs={{0,8},{2,10},{4,12},{6,14},{8,16},{10,18},{12,20},{14,22},{16,24},... | collective-permute-start | bytes 3342344 | tf_op jit(solution)/shard_map/ppermute | solution.py:514
  441.7 31.0 %collective-permute-start.40 = (bf16[544,1024]{1,0:T(8,128)(2,1)}, bf16[544,1024]{1,0:T(8,128)(2,1)S(1)}, u32[]{:S(2)}, u32[]{:S(2)}) collective-permute-start(bf16[544,1024]{1,0:T(8,128)(2,1)} %fusion.51), channel_id=1, source_target_pairs={{0,1},{1,0},{2,3},{3,2},{4,5},{5,4},{6,7},{7,6},{8,9},{9,8},{10,11... | collective-permute-start | bytes 3342344 | tf_op jit(solution)/shard_map/ppermute | solution.py:518
  472.7 38.6 %collective-permute-start.42 = (bf16[2,2,544,1024]{3,2,1,0:T(8,128)(2,1)}, bf16[2,2,544,1024]{3,2,1,0:T(8,128)(2,1)}, u32[]{:S(2)}, u32[]{:S(2)}) collective-permute-start(bf16[2,2,544,1024]{3,2,1,0:T(8,128)(2,1)} %get-tuple-element.383), channel_id=1, source_target_pairs={{0,2},{2,0},{4,6},{6,4},{8,10},{10,8},{12,14},{14,12},{16,18},{18,... | collective-permute-start | bytes 13369352 | tf_op jit(solution)/shard_map/ppermute | solution.py:510
  472.8 38.5 %collective-permute-start.45 = (bf16[2,2,512,1024]{3,2,1,0:T(8,128)(2,1)}, bf16[2,2,512,1024]{3,2,1,0:T(8,128)(2,1)}, u32[]{:S(2)}, u32[]{:S(2)}) collective-permute-start(bf16[2,2,512,1024]{3,2,1,0:T(8,128)(2,1)} %get-tuple-element.393), channel_id=1, source_target_pairs={{0,2},{2,0},{4,6},{6,4},{8,10},{10,8},{12,14},{14,12},{16,18},{18,... | collective-permute-start | bytes 12582920 | tf_op jit(solution)/shard_map/ppermute | solution.py:510
  511.3 40.0 %collective-permute-start.49 = (bf16[2,2,512,1024]{3,2,1,0:T(8,128)(2,1)}, bf16[2,2,512,1024]{3,2,1,0:T(8,128)(2,1)}, u32[]{:S(2)}, u32[]{:S(2)}) collective-permute-start(bf16[2,2,512,1024]{3,2,1,0:T(8,128)(2,1)} %get-tuple-element.408), channel_id=1, source_target_pairs={{0,2},{2,0},{4,6},{6,4},{8,10},{10,8},{12,14},{14,12},{16,18},{18,... | collective-permute-start | bytes 12582920 | tf_op jit(solution)/shard_map/ppermute | solution.py:510
  515.2 29.0 %collective-permute-start.50 = (bf16[544,1024]{1,0:T(8,128)(2,1)}, bf16[544,1024]{1,0:T(8,128)(2,1)S(1)}, u32[]{:S(2)}, u32[]{:S(2)}) collective-permute-start(bf16[544,1024]{1,0:T(8,128)(2,1)} %fusion.11), channel_id=1, source_target_pairs={{0,8},{2,10},{4,12},{6,14},{8,16},{10,18},{12,20},{14,22},{16,24},... | collective-permute-start | bytes 3342344 | tf_op jit(solution)/shard_map/ppermute | solution.py:514
  551.3 33.7 %collective-permute-start.52 = (bf16[2,2,512,1024]{3,2,1,0:T(8,128)(2,1)}, bf16[2,2,512,1024]{3,2,1,0:T(8,128)(2,1)}, u32[]{:S(2)}, u32[]{:S(2)}) collective-permute-start(bf16[2,2,512,1024]{3,2,1,0:T(8,128)(2,1)} %get-tuple-element.424), channel_id=1, source_target_pairs={{0,2},{2,0},{4,6},{6,4},{8,10},{10,8},{12,14},{14,12},{16,18},{18,... | collective-permute-start | bytes 12582920 | tf_op jit(solution)/shard_map/ppermute | solution.py:510
  551.3 28.9 %collective-permute-start.54 = (bf16[544,1024]{1,0:T(8,128)(2,1)S(1)}, bf16[544,1024]{1,0:T(8,128)(2,1)}, u32[]{:S(2)}, u32[]{:S(2)}) collective-permute-start(bf16[544,1024]{1,0:T(8,128)(2,1)S(1)} %fusion.9), channel_id=1, source_target_pairs={{0,8},{2,10},{4,12},{6,14},{8,16},{10,18},{12,20},{14,22},{16,24},... | collective-permute-start | bytes 3342344 | tf_op jit(solution)/shard_map/ppermute | solution.py:514
  585.0 36.1 %collective-permute-start.55 = (bf16[2,2,512,1024]{3,2,1,0:T(8,128)(2,1)S(1)}, bf16[2,2,512,1024]{3,2,1,0:T(8,128)(2,1)}, u32[]{:S(2)}, u32[]{:S(2)}) collective-permute-start(bf16[2,2,512,1024]{3,2,1,0:T(8,128)(2,1)S(1)} %copy-done.69), channel_id=1, source_target_pairs={{0,2},{2,0},{4,6},{6,4},{8,10},{10,8},{12,14},{14,12},{16,18},{18,... | collective-permute-start | bytes 12582920 | tf_op jit(solution)/shard_map/ppermute | solution.py:510
  641.2 42.7 %collective-permute-start.63 = (bf16[512,1024]{1,0:T(8,128)(2,1)S(1)}, bf16[512,1024]{1,0:T(8,128)(2,1)S(1)}, u32[]{:S(2)}, u32[]{:S(2)}) collective-permute-start(bf16[512,1024]{1,0:T(8,128)(2,1)S(1)} %fusion.55), channel_id=1, source_target_pairs={{0,8},{2,10},{4,12},{6,14},{8,16},{10,18},{12,20},{14,22},{16,24},... | collective-permute-start | bytes 3145736 | tf_op jit(solution)/shard_map/ppermute | solution.py:514
  686.1 33.1 %collective-permute-start.66 = (bf16[512,1024]{1,0:T(8,128)(2,1)S(1)}, bf16[512,1024]{1,0:T(8,128)(2,1)S(1)}, u32[]{:S(2)}, u32[]{:S(2)}) collective-permute-start(bf16[512,1024]{1,0:T(8,128)(2,1)S(1)} %fusion.35), channel_id=1, source_target_pairs={{0,8},{2,10},{4,12},{6,14},{8,16},{10,18},{12,20},{14,22},{16,24},... | collective-permute-start | bytes 3145736 | tf_op jit(solution)/shard_map/ppermute | solution.py:514
  732.0 34.2 %collective-permute-start.69 = (bf16[512,1024]{1,0:T(8,128)(2,1)S(1)}, bf16[512,1024]{1,0:T(8,128)(2,1)S(1)}, u32[]{:S(2)}, u32[]{:S(2)}) collective-permute-start(bf16[512,1024]{1,0:T(8,128)(2,1)S(1)} %fusion.33), channel_id=1, source_target_pairs={{0,8},{2,10},{4,12},{6,14},{8,16},{10,18},{12,20},{14,22},{16,24},... | collective-permute-start | bytes 3145736 | tf_op jit(solution)/shard_map/ppermute | solution.py:514
  736.0 30.2 %collective-permute-start.68 = (bf16[512,1024]{1,0:T(8,128)(2,1)S(1)}, bf16[512,1024]{1,0:T(8,128)(2,1)S(1)}, u32[]{:S(2)}, u32[]{:S(2)}) collective-permute-start(bf16[512,1024]{1,0:T(8,128)(2,1)S(1)} %get-tuple-element.549), channel_id=1, source_target_pairs={{0,4},{2,6},{4,0},{6,2},{8,12},{10,14},{12,8},{14,10},{16,20},{18,... | collective-permute-start | bytes 3145736 | tf_op jit(solution)/shard_map/ppermute | solution.py:510
  737.4 28.8 %collective-permute-start.67 = (bf16[512,1024]{1,0:T(8,128)(2,1)S(1)}, bf16[512,1024]{1,0:T(8,128)(2,1)S(1)}, u32[]{:S(2)}, u32[]{:S(2)}) collective-permute-start(bf16[512,1024]{1,0:T(8,128)(2,1)S(1)} %copy-done.28), channel_id=1, source_target_pairs={{0,1},{1,0},{2,3},{3,2},{4,5},{5,4},{6,7},{7,6},{8,9},{9,8},{10,11... | collective-permute-start | bytes 3145736 | tf_op jit(solution)/shard_map/ppermute | solution.py:518
  770.5 29.0 %collective-permute-start.70 = (bf16[512,1024]{1,0:T(8,128)(2,1)S(1)}, bf16[512,1024]{1,0:T(8,128)(2,1)S(1)}, u32[]{:S(2)}, u32[]{:S(2)}) collective-permute-start(bf16[512,1024]{1,0:T(8,128)(2,1)S(1)} %fusion.36), channel_id=1, source_target_pairs={{0,4},{2,6},{4,0},{6,2},{8,12},{10,14},{12,8},{14,10},{16,20},{18,... | collective-permute-start | bytes 3145736 | tf_op jit(solution)/shard_map/ppermute | solution.py:510
  772.3 39.2 %collective-permute-start.74 = (bf16[512,1024]{1,0:T(8,128)(2,1)S(1)}, bf16[512,1024]{1,0:T(8,128)(2,1)S(1)}, u32[]{:S(2)}, u32[]{:S(2)}) collective-permute-start(bf16[512,1024]{1,0:T(8,128)(2,1)S(1)} %get-tuple-element.502), channel_id=1, source_target_pairs={{0,8},{2,10},{4,12},{6,14},{8,16},{10,18},{12,20},{14,22},{16,24},... | collective-permute-start | bytes 3145736 | tf_op jit(solution)/shard_map/ppermute | solution.py:514
  (115 other events, 2053.8 us)
Sparse Core Ops, SparseCore 0:
  11.1 236.9 all-gather.4
  728.8 85.5 all-gather.6

commit v7 on v6

--- a/solution.py
+++ b/solution.py
@@ -930,8 +930,8 @@
     )
     branch_cols = grad_mixed_cols.astype(half_type)
     grad_branch = from_sides(*both_halves(branch_cols))
-    grad_branch, out_first, out_second, near_next, away_next = step_end(
-        grad_branch, out_first, out_second, near_next, away_next
+    grad_branch, out_second, near_next, away_next = step_end(
+        grad_branch, out_second, near_next, away_next
     )
     sum_across(outs, 2, near_next)
     out_second = onward_sum(out_second, *second_of(outs, 2))

time: 864 us -> 855 us (0.990)
  starting transfers between devices: 94 us -> 84.7 us
    ppermute x18, waiting for transfers between devices: 123 us -> 109 us  [onward(): lax.ppermute(values, 'dp', [(i, (i + QUAD) % data_count) for i in range(d...]
  transfers between devices with their start and end apart: 81 -> 81, of which waited for: 30 -> 32; matrix products, arithmetic and copies ran while one was open for 19% -> 20% of each run, Pallas kernels for 31% -> 31%
where the time goes in v7:
time: 855 us; the launch traced here: 845 us
  waiting for transfers between devices  293 us (34%)
  Pallas kernels  261 us (31%)
  other arithmetic  99.4 us (12%)
  starting transfers between devices  84.7 us (10%)
  matrix products  58 us (7%)
  local copies, waits for them, and re-layouts  31.6 us (4%)
  between operations  16.6 us (2%)
    pallas_call x4, Pallas kernels, call_experts(): pl.pallas_call(functools.partial(expert_kernel, experts, cap), out_shape=...  118 us
    ppermute x18, waiting for transfers between devices, onward(): lax.ppermute(values, 'dp', [(i, (i + QUAD) % data_count) for i in range(d...  109 us
    convert_element_type x28, other arithmetic, plus(): return total.astype(half_type)  78.1 us
    ppermute x22, waiting for transfers between devices, other_side(): return lax.ppermute(values, 'tensor', [(0, 1), (1, 0)])  73.4 us
    ppermute x37, waiting for transfers between devices, swap(): return lax.ppermute(values, 'dp', [(i, i ^ bit) for i in range(data_count)])  70.5 us
    pallas_call x4, Pallas kernels, call_output(): pl.pallas_call(functools.partial(output_kernel, experts, cap), out_shape=...  65.3 us
    pallas_call x2, Pallas kernels, call_heads(): pl.pallas_call(kernel, out_shape=[jax.ShapeDtypeStruct((toks, width), hal...  41.6 us
    pallas_call x1, Pallas kernels, call_grad_rows(): pl.pallas_call(functools.partial(grad_rows_kernel, experts, cap), out_sha...  36.3 us
  transfers between devices with their start and end apart: 81, of which 32 were waited for; matrix products, arithmetic and copies ran while one was open for 20% of the time, Pallas kernels for 31%

profile of v7, /device:TPU:0, one launch (start us, length us, event | category | flops | bytes accessed | tf_op | source)
XLA Modules:
  0.0 844.8 jit_solution(2075829673592053680)
XLA Ops:
  10.4 7.4 all-to-all-start
  42.6 19.2 %attend.1 = (bf16[512,1024]{1,0:T(8,128)(2,1)}, bf16[512,1024]{1,0:T(8,128)(2,1)}, bf16[512,1024]{1,0:T(8,128)(2,1)}, bf16[512,1024]{1,0:T(8,128)(2,1)}) custom-call(f32[512,1024]{1,0:T(8,128)} %convolution_add_fusion.2.raw_q, f32[512,1024]{1,0:T(8,128)} %convolution_add_fusion.1.raw_k, f32[512,1024]{1,0:T(8,128)} %convolution_add_fusion.raw_v, ...), custom_call_target="tpu_custom_call" | custom-call | flops 2684354560 | bytes 4194304 | tf_op jit(solution)/shard_map/attend/pallas_call | solution.py:105
  61.9 3.6 fusion.127
  70.2 24.5 %collective-permute-done.1 = bf16[512,16]{0,1:T(8,128)(2,1)S(1)} collective-permute-done((bf16[512,16]{0,1:T(8,128)(2,1)S(1)}, bf16[512,16]{0,1:T(8,128)(2,1)S(1)}, u32[]{:S(2)}, u32[]{:S(2)}) %collective-permute-start.1) | collective-permute-done | bytes 16416 | tf_op jit(solution)/shard_map/ppermute | solution.py:518
  103.4 37.4 %collective-permute-done.3.own_first_ref = bf16[512,1024]{1,0:T(8,128)(2,1)} collective-permute-done((bf16[512,1024]{1,0:T(8,128)(2,1)S(1)}, bf16[512,1024]{1,0:T(8,128)(2,1)}, u32[]{:S(2)}, u32[]{:S(2)}) %collective-permute-start.3) | collective-permute-done | bytes 1048608 | tf_op jit(solution)/shard_map/ppermute | solution.py:514
  144.0 7.5 collective-permute-start.7
  151.5 37.3 %collective-permute-done.10.across_first_ref = bf16[512,1024]{1,0:T(8,128)(2,1)S(1)} collective-permute-done((bf16[512,1024]{1,0:T(8,128)(2,1)}, bf16[512,1024]{1,0:T(8,128)(2,1)S(1)}, u32[]{:S(2)}, u32[]{:S(2)}) %collective-permute-start.10) | collective-permute-done | bytes 1048608 | tf_op jit(solution)/shard_map/ppermute | solution.py:510
  191.6 14.6 %all-to-all-start.1 = ((f32[16,4,512]{2,1,0:T(4,128)}), f32[16,4,512]{2,1,0:T(4,128)S(1)}, u32[]{:S(2)}, u32[]{:S(2)}) async-start(f32[16,4,512]{2,1,0:T(4,128)} %reshape.318), calls=%async_computation.1 | async-start | bytes 262144 | tf_op jit(solution)/shard_map/all_to_all | solution.py:824
  207.6 6.6 all-to-all-done.1
  214.8 33.3 %all-gather.5.cloned.1.call-done = bf16[16384,1024]{1,0:T(8,128)(2,1)} async-done(((bf16[512,1024]{1,0:T(8,128)(2,1)}), bf16[16384,1024]{1,0:T(8,128)(2,1)}) %all-gather.5.cloned.1.call-update) | async-done | bytes 33554448 | tf_op jit(solution)/shard_map/all_gather | solution.py:640
  250.1 36.3 %grad_rows.1.dh_ref = bf16[4,1280,512]{2,1,0:T(8,128)(2,1)} custom-call(s32[16]{0:T(128)} %fusion.105.block_ids, s32[16,4,1,512]{3,2,1,0:T(1,128)} %broadcast_in_dim.86.place_ref, bf16[4,512,2048]{2,1,0:T(8,128)(2,1)} %down_ref.9, bf16[16,2,512,1024]{3,2,1,0:T(8,128)(2,1)} %bitcast.265), custom_call_target="tpu_custom_call" | custom-call | flops 42949672960 | bytes 47185920 | tf_op jit(solution)/shard_map/grad_rows/pallas_call | solution.py:388
  294.1 29.5 %experts.4 = (bf16[2,2,544,1024]{3,2,1,0:T(8,128)(2,1)}, bf16[2,2,544,1024]{3,2,1,0:T(8,128)(2,1)}, bf16[4,320,512]{2,1,0:T(8,128)(2,1)}) custom-call(s32[2]{0:T(128)} %pad_add_fusion.flip_ref, s32[4,4,1,512]{3,2,1,0:T(1,128)} %broadcast_in_dim.87.place_ref, f32[4,4,1,512]{3,2,1,0:T(1,128)} %copy.88.gate_ref, s32[4,512,4]{2,1,0:T(8,128)} %get-tuple-element.564.target_ref, ...), custom_call_target="tpu_custom_call" | custom-call | flops 24159191040 | bytes 33554432 | tf_op jit(solution)/shard_map/experts/pallas_call | solution.py:422
  327.6 29.7 %experts.5 = (bf16[2,2,544,1024]{3,2,1,0:T(8,128)(2,1)}, bf16[2,2,544,1024]{3,2,1,0:T(8,128)(2,1)}, bf16[4,320,512]{2,1,0:T(8,128)(2,1)}) custom-call(s32[2]{0:T(128)} %pad_add_fusion.flip_ref, s32[4,4,1,512]{3,2,1,0:T(1,128)} %broadcast_in_dim.89.place_ref, f32[4,4,1,512]{3,2,1,0:T(1,128)} %copy.89.gate_ref, s32[4,512,4]{2,1,0:T(8,128)} %get-tuple-element.563.target_ref, ...), custom_call_target="tpu_custom_call" | custom-call | flops 24159191040 | bytes 33554432 | tf_op jit(solution)/shard_map/experts/pallas_call | solution.py:422
  363.1 5.3 collective-permute-done.30.far_second_ref
  370.4 29.7 %experts.6 = (bf16[2,2,544,1024]{3,2,1,0:T(8,128)(2,1)}, bf16[2,2,544,1024]{3,2,1,0:T(8,128)(2,1)}, bf16[4,320,512]{2,1,0:T(8,128)(2,1)}) custom-call(s32[2]{0:T(128)} %pad_add_fusion.flip_ref, s32[4,4,1,512]{3,2,1,0:T(1,128)} %broadcast_in_dim.91.place_ref, f32[4,4,1,512]{3,2,1,0:T(1,128)} %copy.90.gate_ref, s32[4,512,4]{2,1,0:T(8,128)} %get-tuple-element.562.target_ref, ...), custom_call_target="tpu_custom_call" | custom-call | flops 24159191040 | bytes 33554432 | tf_op jit(solution)/shard_map/experts/pallas_call | solution.py:422
  409.7 16.2 %outputs.4 = (bf16[2,2,512,1024]{3,2,1,0:T(8,128)(2,1)}, bf16[2,2,512,1024]{3,2,1,0:T(8,128)(2,1)}) custom-call(s32[2]{0:T(128)} %pad_add_fusion.flip_ref, s32[4,512,4]{2,1,0:T(8,128)} %get-tuple-element.564.target_ref, bf16[4,512,2048]{2,1,0:T(8,128)(2,1)} %down_ref.9, bf16[4,320,512]{2,1,0:T(8,128)(2,1)} %get-tuple-element.345.hidden_ref), custom_call_target="tpu_custom_call" | custom-call | flops 10737418240 | bytes 16777216 | tf_op jit(solution)/shard_map/outputs/pallas_call | solution.py:476
  425.9 6.3 collective-permute-done.34.across_second_ref
  443.4 29.4 %experts.7 = (bf16[2,2,544,1024]{3,2,1,0:T(8,128)(2,1)}, bf16[2,2,544,1024]{3,2,1,0:T(8,128)(2,1)}, bf16[4,320,512]{2,1,0:T(8,128)(2,1)}) custom-call(s32[2]{0:T(128)} %pad_add_fusion.flip_ref, s32[4,4,1,512]{3,2,1,0:T(1,128)} %broadcast_in_dim.93.place_ref, f32[4,4,1,512]{3,2,1,0:T(1,128)} %broadcast_in_dim.94.gate_ref, ...), custom_call_target="tpu_custom_call" | custom-call | flops 24159191040 | bytes 33554432 | tf_op jit(solution)/shard_map/experts/pallas_call | solution.py:422
  485.8 16.4 %outputs.5 = (bf16[2,2,512,1024]{3,2,1,0:T(8,128)(2,1)}, bf16[2,2,512,1024]{3,2,1,0:T(8,128)(2,1)}) custom-call(s32[2]{0:T(128)} %pad_add_fusion.flip_ref, s32[4,512,4]{2,1,0:T(8,128)} %get-tuple-element.562.target_ref, bf16[4,512,2048]{2,1,0:T(8,128)(2,1)} %down_ref.9, bf16[4,320,512]{2,1,0:T(8,128)(2,1)} %get-tuple-element.380.hidden_ref), custom_call_target="tpu_custom_call" | custom-call | flops 10737418240 | bytes 16777216 | tf_op jit(solution)/shard_map/outputs/pallas_call | solution.py:476
  507.9 3.5 collective-permute-done.43
  511.4 3.9 fusion.11
  527.1 16.2 %outputs.6 = (bf16[2,2,512,1024]{3,2,1,0:T(8,128)(2,1)}, bf16[2,2,512,1024]{3,2,1,0:T(8,128)(2,1)}) custom-call(s32[2]{0:T(128)} %pad_add_fusion.flip_ref, s32[4,512,4]{2,1,0:T(8,128)} %get-tuple-element.561.target_ref, bf16[4,512,2048]{2,1,0:T(8,128)(2,1)} %down_ref.9, bf16[4,320,512]{2,1,0:T(8,128)(2,1)} %get-tuple-element.398.hidden_ref), custom_call_target="tpu_custom_call" | custom-call | flops 10737418240 | bytes 16777216 | tf_op jit(solution)/shard_map/outputs/pallas_call | solution.py:476
  544.3 3.3 collective-permute-done.48
  547.6 3.7 collective-permute-done.47
  559.1 16.6 %outputs.7 = (bf16[2,2,512,1024]{3,2,1,0:T(8,128)(2,1)}, bf16[2,2,512,1024]{3,2,1,0:T(8,128)(2,1)}) custom-call(s32[2]{0:T(128)} %pad_add_fusion.flip_ref, s32[4,512,4]{2,1,0:T(8,128)} %get-tuple-element.563.target_ref, bf16[4,512,2048]{2,1,0:T(8,128)(2,1)} %down_ref.9, bf16[4,320,512]{2,1,0:T(8,128)(2,1)} %get-tuple-element.415.hidden_ref), custom_call_target="tpu_custom_call" | custom-call | flops 10737418240 | bytes 16777216 | tf_op jit(solution)/shard_map/outputs/pallas_call | solution.py:476
  575.6 4.6 collective-permute-done.54
  594.9 21.6 %collective-permute-done.57 = bf16[544,1024]{1,0:T(8,128)(2,1)S(1)} collective-permute-done((bf16[544,1024]{1,0:T(8,128)(2,1)S(1)}, bf16[544,1024]{1,0:T(8,128)(2,1)S(1)}, u32[]{:S(2)}, u32[]{:S(2)}) %collective-permute-start.57) | collective-permute-done | bytes 1114144 | tf_op jit(solution)/shard_map/ppermute | solution.py:514
  616.5 4.6 fusion.5
  629.2 3.7 fusion.122
  634.4 3.5 fusion.57
  646.5 9.9 %collective-permute-done.61 = bf16[512,1024]{1,0:T(8,128)(2,1)S(1)} collective-permute-done((bf16[512,1024]{1,0:T(8,128)(2,1)S(1)}, bf16[512,1024]{1,0:T(8,128)(2,1)S(1)}, u32[]{:S(2)}, u32[]{:S(2)}) %collective-permute-start.61) | collective-permute-done | bytes 1048608 | tf_op jit(solution)/shard_map/ppermute | solution.py:518
  656.6 4.4 collective-permute-done.59
  661.0 5.5 collective-permute-done.62
  671.0 3.4 add_convert_fusion.7.grad
  676.3 22.4 %attend_back.1 = (bf16[512,1024]{1,0:T(8,128)(2,1)}, bf16[512,1024]{1,0:T(8,128)(2,1)}, bf16[512,1024]{1,0:T(8,128)(2,1)}) custom-call(f32[512,1024]{1,0:T(8,128)} %convolution_add_fusion.2.raw_q, f32[512,1024]{1,0:T(8,128)} %convolution_add_fusion.1.raw_k, bf16[512,1024]{1,0:T(8,128)(2,1)} %get-tuple-element.470.queries, ...), custom_call_target="tpu_custom_call" | custom-call | flops 2684354560 | bytes 4194304 | tf_op jit(solution)/shard_map/attend_back/pallas_call | solution.py:105
  702.3 6.1 collective-permute-done.66
  721.4 4.1 fusion.31
  727.2 4.4 fusion.128
  731.7 4.3 fusion.129
  736.0 6.1 add_add_fusion
  742.3 13.4 %collective-permute-done.69 = bf16[512,1024]{1,0:T(8,128)(2,1)S(1)} collective-permute-done((bf16[512,1024]{1,0:T(8,128)(2,1)S(1)}, bf16[512,1024]{1,0:T(8,128)(2,1)S(1)}, u32[]{:S(2)}, u32[]{:S(2)}) %collective-permute-start.69) | collective-permute-done | bytes 1048608 | tf_op jit(solution)/shard_map/ppermute | solution.py:514
  759.6 15.3 %collective-permute-done.71 = bf16[512,1024]{1,0:T(8,128)(2,1)S(1)} collective-permute-done((bf16[512,1024]{1,0:T(8,128)(2,1)S(1)}, bf16[512,1024]{1,0:T(8,128)(2,1)S(1)}, u32[]{:S(2)}, u32[]{:S(2)}) %collective-permute-start.71) | collective-permute-done | bytes 1048608 | tf_op jit(solution)/shard_map/ppermute | solution.py:518
  779.6 12.7 %collective-permute-done.70 = bf16[512,1024]{1,0:T(8,128)(2,1)S(1)} collective-permute-done((bf16[512,1024]{1,0:T(8,128)(2,1)S(1)}, bf16[512,1024]{1,0:T(8,128)(2,1)S(1)}, u32[]{:S(2)}, u32[]{:S(2)}) %collective-permute-start.70) | collective-permute-done | bytes 1048608 | tf_op jit(solution)/shard_map/ppermute | solution.py:510
  792.3 11.5 %collective-permute-done.74 = bf16[512,1024]{1,0:T(8,128)(2,1)S(1)} collective-permute-done((bf16[512,1024]{1,0:T(8,128)(2,1)S(1)}, bf16[512,1024]{1,0:T(8,128)(2,1)S(1)}, u32[]{:S(2)}, u32[]{:S(2)}) %collective-permute-start.74) | collective-permute-done | bytes 1048608 | tf_op jit(solution)/shard_map/ppermute | solution.py:514
  812.7 5.9 fusion
  820.4 4.8 collective-permute-done.75
  825.2 3.5 copy.93
  833.0 4.5 add_convert_fusion.5
  (416 shorter events, 211.0 us)
Async XLA Ops:
  7.2 240.9 %all-gather.5.cloned.1.call-start = ((), (), s32[]{:S(2)}) async-start(), calls=%async_computation.2 | async-start | bytes 34603008 | tf_op jit(solution)/shard_map/all_gather | solution.py:640
  65.7 29.1 %collective-permute-start = (bf16[512,1024]{1,0:T(8,128)(2,1)S(1)}, bf16[512,1024]{1,0:T(8,128)(2,1)S(1)}, u32[]{:S(2)}, u32[]{:S(2)}) collective-permute-start(bf16[512,1024]{1,0:T(8,128)(2,1)S(1)} %select_convert_fusion.1), channel_id=1, source_target_pairs={{0,1},{1,0},{2,3},{3,2},{4,5},{5,4},{6,7},{7,6},{8,9},{9,8},{10,11... | collective-permute-start | bytes 3145736 | tf_op jit(solution)/shard_map/ppermute | solution.py:518
  99.9 40.9 %collective-permute-start.3 = (bf16[512,1024]{1,0:T(8,128)(2,1)S(1)}, bf16[512,1024]{1,0:T(8,128)(2,1)}, u32[]{:S(2)}, u32[]{:S(2)}) collective-permute-start(bf16[512,1024]{1,0:T(8,128)(2,1)S(1)} %multiply_convert_fusion.own_first_ref), channel_id=1, source_target_pairs={{0,8},{2,10},{4,12},{6,14},{8,16},{10,18},{12,20},{14,22},{16,24},... | collective-permute-start | bytes 3145736 | tf_op jit(solution)/shard_map/ppermute | solution.py:514
  101.4 39.4 %collective-permute-start.4 = (bf16[512,1024]{1,0:T(8,128)(2,1)S(1)}, bf16[512,1024]{1,0:T(8,128)(2,1)S(1)}, u32[]{:S(2)}, u32[]{:S(2)}) collective-permute-start(bf16[512,1024]{1,0:T(8,128)(2,1)S(1)} %multiply_convert_fusion.own_first_ref), channel_id=1, source_target_pairs={{0,1},{1,0},{2,3},{3,2},{4,5},{5,4},{6,7},{7,6},{8,9},{9,8},{10,11... | collective-permute-start | bytes 3145736 | tf_op jit(solution)/shard_map/ppermute | solution.py:518
  102.0 38.8 %collective-permute-start.5 = (bf16[512,1024]{1,0:T(8,128)(2,1)S(1)}, bf16[512,1024]{1,0:T(8,128)(2,1)S(1)}, u32[]{:S(2)}, u32[]{:S(2)}) collective-permute-start(bf16[512,1024]{1,0:T(8,128)(2,1)S(1)} %multiply_convert_fusion.own_first_ref), channel_id=1, source_target_pairs={{0,2},{2,0},{4,6},{6,4},{8,10},{10,8},{12,14},{14,12},{16,18},{18,... | collective-permute-start | bytes 3145736 | tf_op jit(solution)/shard_map/ppermute | solution.py:510
  102.0 38.9 %collective-permute-start.6 = (bf16[512,1024]{1,0:T(8,128)(2,1)S(1)}, bf16[512,1024]{1,0:T(8,128)(2,1)S(1)}, u32[]{:S(2)}, u32[]{:S(2)}) collective-permute-start(bf16[512,1024]{1,0:T(8,128)(2,1)S(1)} %multiply_convert_fusion.own_first_ref), channel_id=1, source_target_pairs={{0,4},{2,6},{4,0},{6,2},{8,12},{10,14},{12,8},{14,10},{16,20},{18,... | collective-permute-start | bytes 3145736 | tf_op jit(solution)/shard_map/ppermute | solution.py:510
  140.8 48.0 %collective-permute-start.10 = (bf16[512,1024]{1,0:T(8,128)(2,1)}, bf16[512,1024]{1,0:T(8,128)(2,1)S(1)}, u32[]{:S(2)}, u32[]{:S(2)}) collective-permute-start(bf16[512,1024]{1,0:T(8,128)(2,1)} %collective-permute-done.3.own_first_ref), channel_id=1, source_target_pairs={{0,4},{2,6},{4,0},{6,2},{8,12},{10,14},{12,8},{14,10},{16,20},{18,... | collective-permute-start | bytes 3145736 | tf_op jit(solution)/shard_map/ppermute | solution.py:510
  142.2 72.6 %collective-permute-start.11 = (bf16[512,1024]{1,0:T(8,128)(2,1)S(1)}, bf16[512,1024]{1,0:T(8,128)(2,1)}, u32[]{:S(2)}, u32[]{:S(2)}) collective-permute-start(bf16[512,1024]{1,0:T(8,128)(2,1)S(1)} %collective-permute-done.6.across_first_ref), channel_id=1, source_target_pairs={{0,1},{1,0},{2,3},{3,2},{4,5},{5,4},{6,7},{7,6},{8,9},{9,8},{10,11... | collective-permute-start | bytes 3145736 | tf_op jit(solution)/shard_map/ppermute | solution.py:518
  143.5 71.3 %collective-permute-start.12 = (bf16[512,1024]{1,0:T(8,128)(2,1)S(1)}, bf16[512,1024]{1,0:T(8,128)(2,1)}, u32[]{:S(2)}, u32[]{:S(2)}) collective-permute-start(bf16[512,1024]{1,0:T(8,128)(2,1)S(1)} %collective-permute-done.6.across_first_ref), channel_id=1, source_target_pairs={{0,2},{2,0},{4,6},{6,4},{8,10},{10,8},{12,14},{14,12},{16,18},{18,... | collective-permute-start | bytes 3145736 | tf_op jit(solution)/shard_map/ppermute | solution.py:510
  143.5 71.3 %collective-permute-start.8 = (bf16[512,1024]{1,0:T(8,128)(2,1)}, bf16[512,1024]{1,0:T(8,128)(2,1)}, u32[]{:S(2)}, u32[]{:S(2)}) collective-permute-start(bf16[512,1024]{1,0:T(8,128)(2,1)} %collective-permute-done.3.own_first_ref), channel_id=1, source_target_pairs={{0,2},{2,0},{4,6},{6,4},{8,10},{10,8},{12,14},{14,12},{16,18},{18,... | collective-permute-start | bytes 3145736 | tf_op jit(solution)/shard_map/ppermute | solution.py:510
  144.0 70.8 %collective-permute-start.7 = (bf16[512,1024]{1,0:T(8,128)(2,1)S(1)}, bf16[512,1024]{1,0:T(8,128)(2,1)}, u32[]{:S(2)}, u32[]{:S(2)}) collective-permute-start(bf16[512,1024]{1,0:T(8,128)(2,1)S(1)} %collective-permute-done.4.own_second_ref), channel_id=1, source_target_pairs={{0,8},{2,10},{4,12},{6,14},{8,16},{10,18},{12,20},{14,22},{16,24},... | collective-permute-start | bytes 3145736 | tf_op jit(solution)/shard_map/ppermute | solution.py:514
  206.2 606.5 %all-gather.7.cloned.1.call-start = ((), (), s32[]{:S(2)}) async-start(), calls=%async_computation.3 | async-start | bytes 6127616 | tf_op jit(solution)/shard_map/all_gather | solution.py:984
  248.1 38.2 %collective-permute-start.15 = (bf16[512,1024]{1,0:T(8,128)(2,1)}, bf16[512,1024]{1,0:T(8,128)(2,1)}, u32[]{:S(2)}, u32[]{:S(2)}) collective-permute-start(bf16[512,1024]{1,0:T(8,128)(2,1)} %copy-done.71), channel_id=1, source_target_pairs={{0,1},{1,0},{2,3},{3,2},{4,5},{5,4},{6,7},{7,6},{8,9},{9,8},{10,11... | collective-permute-start | bytes 3145736 | tf_op jit(solution)/shard_map/ppermute | solution.py:518
  249.6 36.8 %collective-permute-start.16 = (bf16[512,1024]{1,0:T(8,128)(2,1)}, bf16[512,1024]{1,0:T(8,128)(2,1)}, u32[]{:S(2)}, u32[]{:S(2)}) collective-permute-start(bf16[512,1024]{1,0:T(8,128)(2,1)} %copy-done.71), channel_id=1, source_target_pairs={{0,2},{2,0},{4,6},{6,4},{8,10},{10,8},{12,14},{14,12},{16,18},{18,... | collective-permute-start | bytes 3145736 | tf_op jit(solution)/shard_map/ppermute | solution.py:510
  249.6 36.8 %collective-permute-start.13 = (bf16[512,1024]{1,0:T(8,128)(2,1)}, bf16[512,1024]{1,0:T(8,128)(2,1)S(1)}, u32[]{:S(2)}, u32[]{:S(2)}) collective-permute-start(bf16[512,1024]{1,0:T(8,128)(2,1)} %collective-permute-done.3.own_first_ref), channel_id=1, source_target_pairs={{0,8},{2,10},{4,12},{6,14},{8,16},{10,18},{12,20},{14,22},{16,24},... | collective-permute-start | bytes 3145736 | tf_op jit(solution)/shard_map/ppermute | solution.py:514
  249.6 36.8 %collective-permute-start.14 = (bf16[512,1024]{1,0:T(8,128)(2,1)}, bf16[512,1024]{1,0:T(8,128)(2,1)}, u32[]{:S(2)}, u32[]{:S(2)}) collective-permute-start(bf16[512,1024]{1,0:T(8,128)(2,1)} %collective-permute-done.7.own_second_ref), channel_id=1, source_target_pairs={{0,2},{2,0},{4,6},{6,4},{8,10},{10,8},{12,14},{14,12},{16,18},{18,... | collective-permute-start | bytes 3145736 | tf_op jit(solution)/shard_map/ppermute | solution.py:510
  250.1 36.3 %collective-permute-start.17 = (bf16[512,1024]{1,0:T(8,128)(2,1)}, bf16[512,1024]{1,0:T(8,128)(2,1)}, u32[]{:S(2)}, u32[]{:S(2)}) collective-permute-start(bf16[512,1024]{1,0:T(8,128)(2,1)} %collective-permute-done.11.across_second_ref), channel_id=1, source_target_pairs={{0,2},{2,0},{4,6},{6,4},{8,10},{10,8},{12,14},{14,12},{16,18},{18,... | collective-permute-start | bytes 3145736 | tf_op jit(solution)/shard_map/ppermute | solution.py:510
  291.0 32.6 %collective-permute-start.19 = (bf16[512,1024]{1,0:T(8,128)(2,1)S(1)}, bf16[512,1024]{1,0:T(8,128)(2,1)S(1)}, u32[]{:S(2)}, u32[]{:S(2)}) collective-permute-start(bf16[512,1024]{1,0:T(8,128)(2,1)S(1)} %collective-permute-done.13.own_first_ref), channel_id=1, source_target_pairs={{0,2},{2,0},{4,6},{6,4},{8,10},{10,8},{12,14},{14,12},{16,18},{18,... | collective-permute-start | bytes 3145736 | tf_op jit(solution)/shard_map/ppermute | solution.py:510
  291.1 32.4 %collective-permute-start.20 = (bf16[512,1024]{1,0:T(8,128)(2,1)S(1)}, bf16[512,1024]{1,0:T(8,128)(2,1)S(1)}, u32[]{:S(2)}, u32[]{:S(2)}) collective-permute-start(bf16[512,1024]{1,0:T(8,128)(2,1)S(1)} %collective-permute-done.13.own_first_ref), channel_id=1, source_target_pairs={{0,4},{2,6},{4,0},{6,2},{8,12},{10,14},{12,8},{14,10},{16,20},{18,... | collective-permute-start | bytes 3145736 | tf_op jit(solution)/shard_map/ppermute | solution.py:510
  293.0 30.5 %collective-permute-start.18 = (bf16[512,1024]{1,0:T(8,128)(2,1)}, bf16[512,1024]{1,0:T(8,128)(2,1)}, u32[]{:S(2)}, u32[]{:S(2)}) collective-permute-start(bf16[512,1024]{1,0:T(8,128)(2,1)} %collective-permute-done.7.own_second_ref), channel_id=1, source_target_pairs={{0,8},{2,10},{4,12},{6,14},{8,16},{10,18},{12,20},{14,22},{16,24},... | collective-permute-start | bytes 3145736 | tf_op jit(solution)/shard_map/ppermute | solution.py:514
  323.6 33.9 %collective-permute-start.26 = (bf16[2,2,544,1024]{3,2,1,0:T(8,128)(2,1)}, bf16[2,2,544,1024]{3,2,1,0:T(8,128)(2,1)}, u32[]{:S(2)}, u32[]{:S(2)}) collective-permute-start(bf16[2,2,544,1024]{3,2,1,0:T(8,128)(2,1)} %get-tuple-element.318), channel_id=1, source_target_pairs={{0,2},{2,0},{4,6},{6,4},{8,10},{10,8},{12,14},{14,12},{16,18},{18,... | collective-permute-start | bytes 13369352 | tf_op jit(solution)/shard_map/ppermute | solution.py:510
  325.1 32.3 %collective-permute-start.24 = (bf16[512,1024]{1,0:T(8,128)(2,1)S(1)}, bf16[512,1024]{1,0:T(8,128)(2,1)}, u32[]{:S(2)}, u32[]{:S(2)}) collective-permute-start(bf16[512,1024]{1,0:T(8,128)(2,1)S(1)} %collective-permute-done.20.across_first_ref), channel_id=1, source_target_pairs={{0,1},{1,0},{2,3},{3,2},{4,5},{5,4},{6,7},{7,6},{8,9},{9,8},{10,11... | collective-permute-start | bytes 3145736 | tf_op jit(solution)/shard_map/ppermute | solution.py:518
  325.6 31.8 %collective-permute-start.25 = (bf16[512,1024]{1,0:T(8,128)(2,1)S(1)}, bf16[512,1024]{1,0:T(8,128)(2,1)}, u32[]{:S(2)}, u32[]{:S(2)}) collective-permute-start(bf16[512,1024]{1,0:T(8,128)(2,1)S(1)} %collective-permute-done.20.across_first_ref), channel_id=1, source_target_pairs={{0,2},{2,0},{4,6},{6,4},{8,10},{10,8},{12,14},{14,12},{16,18},{18,... | collective-permute-start | bytes 3145736 | tf_op jit(solution)/shard_map/ppermute | solution.py:510
  325.7 31.7 %collective-permute-start.22 = (bf16[512,1024]{1,0:T(8,128)(2,1)S(1)}, bf16[512,1024]{1,0:T(8,128)(2,1)}, u32[]{:S(2)}, u32[]{:S(2)}) collective-permute-start(bf16[512,1024]{1,0:T(8,128)(2,1)S(1)} %collective-permute-done.13.own_first_ref), channel_id=1, source_target_pairs={{0,8},{2,10},{4,12},{6,14},{8,16},{10,18},{12,20},{14,22},{16,24},... | collective-permute-start | bytes 3145736 | tf_op jit(solution)/shard_map/ppermute | solution.py:514
  327.5 30.0 %collective-permute-start.23 = (bf16[512,1024]{1,0:T(8,128)(2,1)}, bf16[512,1024]{1,0:T(8,128)(2,1)}, u32[]{:S(2)}, u32[]{:S(2)}) collective-permute-start(bf16[512,1024]{1,0:T(8,128)(2,1)} %collective-permute-done.18.own_second_ref), channel_id=1, source_target_pairs={{0,2},{2,0},{4,6},{6,4},{8,10},{10,8},{12,14},{14,12},{16,18},{18,... | collective-permute-start | bytes 3145736 | tf_op jit(solution)/shard_map/ppermute | solution.py:510
  357.5 42.7 %collective-permute-start.31 = (bf16[2,2,544,1024]{3,2,1,0:T(8,128)(2,1)}, bf16[2,2,544,1024]{3,2,1,0:T(8,128)(2,1)}, u32[]{:S(2)}, u32[]{:S(2)}) collective-permute-start(bf16[2,2,544,1024]{3,2,1,0:T(8,128)(2,1)} %get-tuple-element.333), channel_id=1, source_target_pairs={{0,2},{2,0},{4,6},{6,4},{8,10},{10,8},{12,14},{14,12},{16,18},{18,... | collective-permute-start | bytes 13369352 | tf_op jit(solution)/shard_map/ppermute | solution.py:510
  359.3 40.8 %collective-permute-start.28 = (bf16[512,1024]{1,0:T(8,128)(2,1)}, bf16[512,1024]{1,0:T(8,128)(2,1)S(1)}, u32[]{:S(2)}, u32[]{:S(2)}) collective-permute-start(bf16[512,1024]{1,0:T(8,128)(2,1)} %collective-permute-done.22.own_first_ref), channel_id=1, source_target_pairs={{0,2},{2,0},{4,6},{6,4},{8,10},{10,8},{12,14},{14,12},{16,18},{18,... | collective-permute-start | bytes 3145736 | tf_op jit(solution)/shard_map/ppermute | solution.py:510
  359.6 40.5 %collective-permute-start.29 = (bf16[512,1024]{1,0:T(8,128)(2,1)}, bf16[512,1024]{1,0:T(8,128)(2,1)}, u32[]{:S(2)}, u32[]{:S(2)}) collective-permute-start(bf16[512,1024]{1,0:T(8,128)(2,1)} %collective-permute-done.22.own_first_ref), channel_id=1, source_target_pairs={{0,4},{2,6},{4,0},{6,2},{8,12},{10,14},{12,8},{14,10},{16,20},{18,... | collective-permute-start | bytes 3145736 | tf_op jit(solution)/shard_map/ppermute | solution.py:510
  361.4 38.7 %collective-permute-start.32 = (bf16[544,1024]{1,0:T(8,128)(2,1)S(1)}, bf16[544,1024]{1,0:T(8,128)(2,1)S(1)}, u32[]{:S(2)}, u32[]{:S(2)}) collective-permute-start(bf16[544,1024]{1,0:T(8,128)(2,1)S(1)} %fusion.49), channel_id=1, source_target_pairs={{0,1},{1,0},{2,3},{3,2},{4,5},{5,4},{6,7},{7,6},{8,9},{9,8},{10,11... | collective-permute-start | bytes 3342344 | tf_op jit(solution)/shard_map/ppermute | solution.py:518
  368.4 31.7 %collective-permute-start.27 = (bf16[512,1024]{1,0:T(8,128)(2,1)}, bf16[512,1024]{1,0:T(8,128)(2,1)}, u32[]{:S(2)}, u32[]{:S(2)}) collective-permute-start(bf16[512,1024]{1,0:T(8,128)(2,1)} %collective-permute-done.18.own_second_ref), channel_id=1, source_target_pairs={{0,8},{2,10},{4,12},{6,14},{8,16},{10,18},{12,20},{14,22},{16,24},... | collective-permute-start | bytes 3145736 | tf_op jit(solution)/shard_map/ppermute | solution.py:514
  400.1 33.3 %collective-permute-start.36 = (bf16[2,2,544,1024]{3,2,1,0:T(8,128)(2,1)}, bf16[2,2,544,1024]{3,2,1,0:T(8,128)(2,1)}, u32[]{:S(2)}, u32[]{:S(2)}) collective-permute-start(bf16[2,2,544,1024]{3,2,1,0:T(8,128)(2,1)} %get-tuple-element.347), channel_id=1, source_target_pairs={{0,2},{2,0},{4,6},{6,4},{8,10},{10,8},{12,14},{14,12},{16,18},{18,... | collective-permute-start | bytes 13369352 | tf_op jit(solution)/shard_map/ppermute | solution.py:510
  438.0 34.8 %collective-permute-start.41 = (bf16[544,1024]{1,0:T(8,128)(2,1)}, bf16[544,1024]{1,0:T(8,128)(2,1)S(1)}, u32[]{:S(2)}, u32[]{:S(2)}) collective-permute-start(bf16[544,1024]{1,0:T(8,128)(2,1)} %fusion.12), channel_id=1, source_target_pairs={{0,8},{2,10},{4,12},{6,14},{8,16},{10,18},{12,20},{14,22},{16,24},... | collective-permute-start | bytes 3342344 | tf_op jit(solution)/shard_map/ppermute | solution.py:514
  441.8 30.9 %collective-permute-start.40 = (bf16[544,1024]{1,0:T(8,128)(2,1)}, bf16[544,1024]{1,0:T(8,128)(2,1)S(1)}, u32[]{:S(2)}, u32[]{:S(2)}) collective-permute-start(bf16[544,1024]{1,0:T(8,128)(2,1)} %fusion.51), channel_id=1, source_target_pairs={{0,1},{1,0},{2,3},{3,2},{4,5},{5,4},{6,7},{7,6},{8,9},{9,8},{10,11... | collective-permute-start | bytes 3342344 | tf_op jit(solution)/shard_map/ppermute | solution.py:518
  472.8 38.6 %collective-permute-start.42 = (bf16[2,2,544,1024]{3,2,1,0:T(8,128)(2,1)}, bf16[2,2,544,1024]{3,2,1,0:T(8,128)(2,1)}, u32[]{:S(2)}, u32[]{:S(2)}) collective-permute-start(bf16[2,2,544,1024]{3,2,1,0:T(8,128)(2,1)} %get-tuple-element.382), channel_id=1, source_target_pairs={{0,2},{2,0},{4,6},{6,4},{8,10},{10,8},{12,14},{14,12},{16,18},{18,... | collective-permute-start | bytes 13369352 | tf_op jit(solution)/shard_map/ppermute | solution.py:510
  472.9 38.5 %collective-permute-start.45 = (bf16[2,2,512,1024]{3,2,1,0:T(8,128)(2,1)}, bf16[2,2,512,1024]{3,2,1,0:T(8,128)(2,1)}, u32[]{:S(2)}, u32[]{:S(2)}) collective-permute-start(bf16[2,2,512,1024]{3,2,1,0:T(8,128)(2,1)} %get-tuple-element.392), channel_id=1, source_target_pairs={{0,2},{2,0},{4,6},{6,4},{8,10},{10,8},{12,14},{14,12},{16,18},{18,... | collective-permute-start | bytes 12582920 | tf_op jit(solution)/shard_map/ppermute | solution.py:510
  511.4 39.9 %collective-permute-start.49 = (bf16[2,2,512,1024]{3,2,1,0:T(8,128)(2,1)}, bf16[2,2,512,1024]{3,2,1,0:T(8,128)(2,1)}, u32[]{:S(2)}, u32[]{:S(2)}) collective-permute-start(bf16[2,2,512,1024]{3,2,1,0:T(8,128)(2,1)} %get-tuple-element.407), channel_id=1, source_target_pairs={{0,2},{2,0},{4,6},{6,4},{8,10},{10,8},{12,14},{14,12},{16,18},{18,... | collective-permute-start | bytes 12582920 | tf_op jit(solution)/shard_map/ppermute | solution.py:510
  515.3 29.0 %collective-permute-start.50 = (bf16[544,1024]{1,0:T(8,128)(2,1)}, bf16[544,1024]{1,0:T(8,128)(2,1)S(1)}, u32[]{:S(2)}, u32[]{:S(2)}) collective-permute-start(bf16[544,1024]{1,0:T(8,128)(2,1)} %fusion.11), channel_id=1, source_target_pairs={{0,8},{2,10},{4,12},{6,14},{8,16},{10,18},{12,20},{14,22},{16,24},... | collective-permute-start | bytes 3342344 | tf_op jit(solution)/shard_map/ppermute | solution.py:514
  551.3 33.7 %collective-permute-start.52 = (bf16[2,2,512,1024]{3,2,1,0:T(8,128)(2,1)}, bf16[2,2,512,1024]{3,2,1,0:T(8,128)(2,1)}, u32[]{:S(2)}, u32[]{:S(2)}) collective-permute-start(bf16[2,2,512,1024]{3,2,1,0:T(8,128)(2,1)} %get-tuple-element.423), channel_id=1, source_target_pairs={{0,2},{2,0},{4,6},{6,4},{8,10},{10,8},{12,14},{14,12},{16,18},{18,... | collective-permute-start | bytes 12582920 | tf_op jit(solution)/shard_map/ppermute | solution.py:510
  551.3 28.9 %collective-permute-start.54 = (bf16[544,1024]{1,0:T(8,128)(2,1)S(1)}, bf16[544,1024]{1,0:T(8,128)(2,1)}, u32[]{:S(2)}, u32[]{:S(2)}) collective-permute-start(bf16[544,1024]{1,0:T(8,128)(2,1)S(1)} %fusion.9), channel_id=1, source_target_pairs={{0,8},{2,10},{4,12},{6,14},{8,16},{10,18},{12,20},{14,22},{16,24},... | collective-permute-start | bytes 3342344 | tf_op jit(solution)/shard_map/ppermute | solution.py:514
  585.1 36.1 %collective-permute-start.55 = (bf16[2,2,512,1024]{3,2,1,0:T(8,128)(2,1)S(1)}, bf16[2,2,512,1024]{3,2,1,0:T(8,128)(2,1)}, u32[]{:S(2)}, u32[]{:S(2)}) collective-permute-start(bf16[2,2,512,1024]{3,2,1,0:T(8,128)(2,1)S(1)} %copy-done.67), channel_id=1, source_target_pairs={{0,2},{2,0},{4,6},{6,4},{8,10},{10,8},{12,14},{14,12},{16,18},{18,... | collective-permute-start | bytes 12582920 | tf_op jit(solution)/shard_map/ppermute | solution.py:510
  642.3 59.9 %collective-permute-start.65 = (bf16[512,1024]{1,0:T(8,128)(2,1)}, bf16[512,1024]{1,0:T(8,128)(2,1)S(1)}, u32[]{:S(2)}, u32[]{:S(2)}) collective-permute-start(bf16[512,1024]{1,0:T(8,128)(2,1)} %fusion.38), channel_id=1, source_target_pairs={{0,8},{2,10},{4,12},{6,14},{8,16},{10,18},{12,20},{14,22},{16,24},... | collective-permute-start | bytes 3145736 | tf_op jit(solution)/shard_map/ppermute | solution.py:514
  668.7 39.7 %collective-permute-start.66 = (bf16[512,1024]{1,0:T(8,128)(2,1)S(1)}, bf16[512,1024]{1,0:T(8,128)(2,1)}, u32[]{:S(2)}, u32[]{:S(2)}) collective-permute-start(bf16[512,1024]{1,0:T(8,128)(2,1)S(1)} %fusion.35), channel_id=1, source_target_pairs={{0,8},{2,10},{4,12},{6,14},{8,16},{10,18},{12,20},{14,22},{16,24},... | collective-permute-start | bytes 3145736 | tf_op jit(solution)/shard_map/ppermute | solution.py:514
  674.5 33.9 %collective-permute-start.63 = (bf16[512,1024]{1,0:T(8,128)(2,1)S(1)}, bf16[512,1024]{1,0:T(8,128)(2,1)}, u32[]{:S(2)}, u32[]{:S(2)}) collective-permute-start(bf16[512,1024]{1,0:T(8,128)(2,1)S(1)} %fusion.58), channel_id=1, source_target_pairs={{0,1},{1,0},{2,3},{3,2},{4,5},{5,4},{6,7},{7,6},{8,9},{9,8},{10,11... | collective-permute-start | bytes 3145736 | tf_op jit(solution)/shard_map/ppermute | solution.py:518
  675.0 33.4 %collective-permute-start.64 = (bf16[512,1024]{1,0:T(8,128)(2,1)}, bf16[512,1024]{1,0:T(8,128)(2,1)S(1)}, u32[]{:S(2)}, u32[]{:S(2)}) collective-permute-start(bf16[512,1024]{1,0:T(8,128)(2,1)} %get-tuple-element.469), channel_id=1, source_target_pairs={{0,4},{2,6},{4,0},{6,2},{8,12},{10,14},{12,8},{14,10},{16,20},{18,... | collective-permute-start | bytes 3145736 | tf_op jit(solution)/shard_map/ppermute | solution.py:510
  721.1 34.5 %collective-permute-start.69 = (bf16[512,1024]{1,0:T(8,128)(2,1)S(1)}, bf16[512,1024]{1,0:T(8,128)(2,1)S(1)}, u32[]{:S(2)}, u32[]{:S(2)}) collective-permute-start(bf16[512,1024]{1,0:T(8,128)(2,1)S(1)} %fusion.33), channel_id=1, source_target_pairs={{0,8},{2,10},{4,12},{6,14},{8,16},{10,18},{12,20},{14,22},{16,24},... | collective-permute-start | bytes 3145736 | tf_op jit(solution)/shard_map/ppermute | solution.py:514
  725.5 30.2 %collective-permute-start.68 = (bf16[512,1024]{1,0:T(8,128)(2,1)S(1)}, bf16[512,1024]{1,0:T(8,128)(2,1)S(1)}, u32[]{:S(2)}, u32[]{:S(2)}) collective-permute-start(bf16[512,1024]{1,0:T(8,128)(2,1)S(1)} %get-tuple-element.547), channel_id=1, source_target_pairs={{0,4},{2,6},{4,0},{6,2},{8,12},{10,14},{12,8},{14,10},{16,20},{18,... | collective-permute-start | bytes 3145736 | tf_op jit(solution)/shard_map/ppermute | solution.py:510
  758.2 34.0 %collective-permute-start.70 = (bf16[512,1024]{1,0:T(8,128)(2,1)S(1)}, bf16[512,1024]{1,0:T(8,128)(2,1)S(1)}, u32[]{:S(2)}, u32[]{:S(2)}) collective-permute-start(bf16[512,1024]{1,0:T(8,128)(2,1)S(1)} %fusion.36), channel_id=1, source_target_pairs={{0,4},{2,6},{4,0},{6,2},{8,12},{10,14},{12,8},{14,10},{16,20},{18,... | collective-permute-start | bytes 3145736 | tf_op jit(solution)/shard_map/ppermute | solution.py:510
  759.6 44.2 %collective-permute-start.74 = (bf16[512,1024]{1,0:T(8,128)(2,1)S(1)}, bf16[512,1024]{1,0:T(8,128)(2,1)S(1)}, u32[]{:S(2)}, u32[]{:S(2)}) collective-permute-start(bf16[512,1024]{1,0:T(8,128)(2,1)S(1)} %get-tuple-element.500), channel_id=1, source_target_pairs={{0,8},{2,10},{4,12},{6,14},{8,16},{10,18},{12,20},{14,22},{16,24},... | collective-permute-start | bytes 3145736 | tf_op jit(solution)/shard_map/ppermute | solution.py:514
  (113 other events, 2064.6 us)
Sparse Core Ops, SparseCore 0:
  11.1 236.9 all-gather.4
  717.9 87.0 all-gather.6
